TPU v7x, 32 devices: a whole 2x2x4 slice. The times are simulated.
32 devices in a mesh: seq: 8 (over y, x, core), fsdp: 4 (over z).
Axes of the slice: x: 2, y: 2, z: 4, core: 2. Of those that a mesh axis runs over, the one named last changes fastest.
Arguments:
- tokens: bfloat16 [4, 4096, 2048], P('fsdp', 'seq'), may hold values from -6 to 6
- doc_starts: int32 [4, 4096], P('fsdp', 'seq'), may hold values from 0 to 1, as said below
- gain_attn: bfloat16 [2048], P(('seq', 'fsdp')), may hold values from 0.5 to 1.5
- w_query: bfloat16 [2048, 2048], P(('seq', 'fsdp')), may hold values from -0.125 to 0.125
- w_key: bfloat16 [2048, 256], P(('seq', 'fsdp')), may hold values from -0.125 to 0.125
- w_value: bfloat16 [2048, 256], P(('seq', 'fsdp')), may hold values from -0.125 to 0.125
- w_out: bfloat16 [2048, 2048], P(('seq', 'fsdp')), may hold values from -1 to 1
- gain_ffn: bfloat16 [2048], P(('seq', 'fsdp')), may hold values from 0.5 to 1.5
- w_gate: bfloat16 [2048, 5632], P(('seq', 'fsdp')), may hold values from -0.125 to 0.125
- w_up: bfloat16 [2048, 5632], P(('seq', 'fsdp')), may hold values from -0.125 to 0.125
- w_down: bfloat16 [5632, 2048], P(('seq', 'fsdp')), may hold values from -0.078125 to 0.078125
- cotangent: bfloat16 [4, 4096, 2048], P('fsdp', 'seq'), may hold values from -6 to 6
Outputs:
- output: bfloat16 [4, 4096, 2048], P('fsdp', 'seq')
- grad_tokens: float32 [4, 4096, 2048], P('fsdp', 'seq')
- grad_gain_attn: float32 [2048], P(('seq', 'fsdp'))
- grad_query: float32 [2048, 2048], P(('seq', 'fsdp'))
- grad_key: float32 [2048, 256], P(('seq', 'fsdp'))
- grad_value: float32 [2048, 256], P(('seq', 'fsdp'))
- grad_out: float32 [2048, 2048], P(('seq', 'fsdp'))
- grad_gain_ffn: float32 [2048], P(('seq', 'fsdp'))
- grad_gate: float32 [2048, 5632], P(('seq', 'fsdp'))
- grad_up: float32 [2048, 5632], P(('seq', 'fsdp'))
- grad_down: float32 [5632, 2048], P(('seq', 'fsdp'))
Inputs may be any that keep to these rules, and one draw needn't show every extreme that they name: `doc_starts`: position 0 of every stream begins a document whatever its entry; one stream or more holds a document of 3072 positions or more.
All inputs are finite; a program needn't handle non-finite values.
Results may differ from a plain program's by a relative error of at most 0.015.
Values may be sent and summed in bfloat16 or wider, within the bound.
A program may use at most 384 MiB of HBM per device.

v0:
```python
import math

import jax
import jax.numpy as jnp
from jax import lax
from jax.sharding import PartitionSpec as P

H = 32
KV = 4
HD = 64


epsilon = 1e-05


def entering(part, axis, combine, identity):
    place = lax.axis_index(axis)
    gathered = jax.tree.map(lambda a: lax.all_gather(a, axis), part)
    state = jax.tree.map(lambda a, e: jnp.zeros_like(a) + jnp.asarray(e, a.dtype), part, identity)

    def one(step, state):
        return combine(
            state, jax.tree.map(lambda a: lax.dynamic_index_in_dim(a, step, 0, False), gathered)
        )

    return lax.fori_loop(0, place, one, state)


def rotary_tables(places, head_width):
    half_width = head_width // 2
    frequency = jnp.exp(
        jnp.arange(half_width, dtype=jnp.float32) * (-2.0 * math.log(10000.0) / head_width)
    )
    angles = places.astype(jnp.float32)[..., None] * frequency
    return (jnp.cos(angles), jnp.sin(angles))


def rotate(values, cosine, sine):
    half_width = values.shape[-1] // 2
    first_half = values[..., :half_width]
    second_half = values[..., half_width:]
    cos_part = cosine[..., None, :]
    sin_part = sine[..., None, :]
    return jnp.concatenate(
        [
            first_half * cos_part - second_half * sin_part,
            second_half * cos_part + first_half * sin_part,
        ],
        axis=-1,
    )


def unrotate(gradient, cosine, sine):
    half_width = gradient.shape[-1] // 2
    first_half = gradient[..., :half_width]
    second_half = gradient[..., half_width:]
    cos_part = cosine[..., None, :]
    sin_part = sine[..., None, :]
    return jnp.concatenate(
        [
            first_half * cos_part + second_half * sin_part,
            second_half * cos_part - first_half * sin_part,
        ],
        axis=-1,
    )


def prefix_combine(earlier, later):
    return (earlier[0] + later[0], jnp.maximum(earlier[1], later[1]))


def gather_attention(gain_attn, w_query, w_key, w_value, w_out):
    return (
        lax.all_gather(gain_attn, ("seq", "fsdp"), axis=0, tiled=True),
        lax.all_gather(w_query, ("seq", "fsdp"), axis=0, tiled=True),
        lax.all_gather(w_key, ("seq", "fsdp"), axis=0, tiled=True),
        lax.all_gather(w_value, ("seq", "fsdp"), axis=0, tiled=True),
        lax.all_gather(w_out, ("seq", "fsdp"), axis=0, tiled=True),
    )


def gather_feedforward(gain_ffn, w_gate, w_up, w_down):
    return (
        lax.all_gather(gain_ffn, ("seq", "fsdp"), axis=0, tiled=True),
        lax.all_gather(w_gate, ("seq", "fsdp"), axis=0, tiled=True),
        lax.all_gather(w_up, ("seq", "fsdp"), axis=0, tiled=True),
        lax.all_gather(w_down, ("seq", "fsdp"), axis=0, tiled=True),
    )


def reduce_terms(terms):
    return lax.psum_scatter(terms, ("seq", "fsdp"), scatter_dimension=0, tiled=True)


def block_logits(query_all, key_all, segment_all, first_row, block_rows, length):
    stream_start = first_row // length * length
    query_block = lax.dynamic_slice_in_dim(query_all, first_row, block_rows, 0)
    query_segment = lax.dynamic_slice_in_dim(segment_all, first_row, block_rows, 0)
    query_place = first_row - stream_start + jnp.arange(block_rows, dtype=jnp.int32)
    key_place = jnp.arange(length, dtype=jnp.int32)
    allowed = (key_place[None, :] <= query_place[:, None]) & (
        segment_all[None, :] == query_segment[:, None]
    )
    score_scale = query_all.shape[2] ** (-0.5)
    logits = (
        jnp.einsum("qhd,khd->hqk", query_block, key_all, preferred_element_type=jnp.float32)
        * score_scale
    )
    logits = jnp.where(allowed[None], logits, -1000000000.0)
    return (query_block, key_all, stream_start, logits)


def attend_forward(query_all, key_all, value_all, segment_all, length):
    total_rows, head_count, head_width = query_all.shape
    block_rows = min(512, length)

    def one_block(first_row):
        query_block, key_block, stream_start, logits = block_logits(
            query_all, key_all, segment_all, first_row, block_rows, length
        )
        row_max = jnp.max(logits, axis=-1, keepdims=True)
        weights = jnp.exp(logits - row_max)
        denominator = jnp.sum(weights, axis=-1, keepdims=True)
        probability = (weights / denominator).astype(jnp.bfloat16)
        attended = jnp.einsum(
            "hqk,khd->qhd", probability, value_all, preferred_element_type=jnp.float32
        )
        return (attended.astype(jnp.bfloat16), (row_max + jnp.log(denominator))[..., 0])

    first_rows = jnp.arange(total_rows // block_rows, dtype=jnp.int32) * block_rows
    attended, log_sums = lax.map(one_block, first_rows)
    return (attended.reshape(total_rows, head_count * head_width), log_sums)


def attend_backward(query_all, key_all, value_all, segment_all, length, log_sums, grad_all):
    total_rows, head_count, head_width = query_all.shape
    block_rows = min(512, length)
    score_scale = head_width ** (-0.5)

    def one_block(running, block_data):
        first_row, log_block = block_data
        key_grad, value_grad = running
        query_block, key_block, stream_start, logits = block_logits(
            query_all, key_all, segment_all, first_row, block_rows, length
        )
        grad_block = lax.dynamic_slice_in_dim(grad_all, first_row, block_rows, 0)
        probability = jnp.exp(logits - log_block[..., None])
        probability_low = probability.astype(jnp.bfloat16)
        grad_probs = jnp.einsum(
            "qhd,khd->hqk", grad_block, value_all, preferred_element_type=jnp.float32
        )
        grad_logits = probability * (
            grad_probs - jnp.sum(probability * grad_probs, axis=-1, keepdims=True)
        )
        grad_logits = grad_logits.astype(jnp.bfloat16)
        query_grad = (
            jnp.einsum("hqk,khd->qhd", grad_logits, key_block, preferred_element_type=jnp.float32)
            * score_scale
        )
        key_step = (
            jnp.einsum("hqk,qhd->khd", grad_logits, query_block, preferred_element_type=jnp.float32)
            * score_scale
        )
        value_step = jnp.einsum(
            "hqk,qhd->khd", probability_low, grad_block, preferred_element_type=jnp.float32
        )
        key_grad = key_grad + key_step
        value_grad = value_grad + value_step
        return ((key_grad, value_grad), query_grad)

    first_rows = jnp.arange(total_rows // block_rows, dtype=jnp.int32) * block_rows
    zero_grads = jnp.zeros((total_rows, head_count, head_width), jnp.float32)
    (key_grad, value_grad), query_grad = lax.scan(
        one_block, (zero_grads, zero_grads), (first_rows, log_sums)
    )
    return (query_grad.reshape(total_rows, head_count, head_width), key_grad, value_grad)


def body(
    tokens,
    doc_starts,
    gain_attn,
    w_query,
    w_key,
    w_value,
    w_out,
    gain_ffn,
    w_gate,
    w_up,
    w_down,
    cotangent,
):
    streams, local_len, model_width = tokens.shape
    seq_count = lax.axis_size("seq")
    length = local_len * seq_count
    head_count = H
    kv_count = KV
    head_width = HD
    head_group = head_count // seq_count
    row_count = streams * local_len
    positions = lax.axis_index("seq") * local_len + jnp.arange(local_len, dtype=jnp.int32)
    doc_flags = jnp.where((doc_starts != 0) | (positions[None, :] == 0), 1, 0).astype(jnp.int32)
    counts = jnp.cumsum(doc_flags, axis=1)
    last_start = lax.cummax(jnp.where(doc_flags == 1, positions[None, :], 0), axis=1)
    zero_pair = (jnp.zeros((streams,), jnp.int32), jnp.zeros((streams,), jnp.int32))
    before_count, before_last = entering(
        (counts[:, -1], last_start[:, -1]), "seq", prefix_combine, zero_pair
    )
    segment = counts + before_count[:, None]
    rotary_place = positions[None, :] - jnp.maximum(last_start, before_last[:, None])
    segment_all = lax.all_gather(segment, "seq", axis=1, tiled=True).reshape(streams * length)
    cosine, sine = rotary_tables(rotary_place, head_width)
    inputs = tokens.astype(jnp.float32).reshape(row_count, model_width)
    scale_attn = lax.rsqrt(jnp.mean(inputs * inputs, axis=-1, keepdims=True) + epsilon)
    gain_one, query_w, key_w, value_w, out_w = gather_attention(
        gain_attn, w_query, w_key, w_value, w_out
    )
    normed_attn = (inputs * scale_attn * gain_one.astype(jnp.float32)).astype(jnp.bfloat16)
    queries = jnp.dot(normed_attn, query_w, preferred_element_type=jnp.float32).reshape(
        streams, local_len, head_count, head_width
    )
    keys = jnp.dot(normed_attn, key_w, preferred_element_type=jnp.float32).reshape(
        streams, local_len, kv_count, head_width
    )
    values_new = jnp.dot(normed_attn, value_w, preferred_element_type=jnp.float32).reshape(
        streams, local_len, kv_count, head_width
    )
    query_rot = rotate(queries, cosine, sine).astype(jnp.bfloat16)
    key_rot = rotate(keys, cosine, sine).astype(jnp.bfloat16)
    key_value = jnp.concatenate([key_rot, values_new.astype(jnp.bfloat16)], axis=-1)
    key_value = jnp.repeat(key_value, head_count // kv_count, axis=2)
    copies = key_value.shape[2] // seq_count
    query_send = query_rot.reshape(streams, local_len, seq_count, head_group * head_width)
    query_heads, pair_heads = (
        lax.all_to_all(query_send, "seq", split_axis=2, concat_axis=1, tiled=True),
        lax.all_to_all(key_value, "seq", split_axis=2, concat_axis=1, tiled=True),
    )
    query_all = query_heads.reshape(streams * length, head_group, head_width)
    pair_all = pair_heads.reshape(streams * length, copies, 2 * head_width)
    key_all = pair_all[..., :head_width]
    value_all = pair_all[..., head_width:]
    attended, log_sums = attend_forward(query_all, key_all, value_all, segment_all, length)
    attended_send = attended.reshape(streams, length, 1, head_group * head_width)
    attended_tokens = lax.all_to_all(
        attended_send, "seq", split_axis=1, concat_axis=2, tiled=True
    ).reshape(row_count, head_count * head_width)
    hidden_one = inputs + jnp.dot(attended_tokens, out_w, preferred_element_type=jnp.float32)
    scale_ffn = lax.rsqrt(jnp.mean(hidden_one * hidden_one, axis=-1, keepdims=True) + epsilon)
    gain_two, gate_w, up_w, down_w = gather_feedforward(gain_ffn, w_gate, w_up, w_down)
    normed_ffn = (hidden_one * scale_ffn * gain_two.astype(jnp.float32)).astype(jnp.bfloat16)
    gate_proj = jnp.dot(normed_ffn, gate_w, preferred_element_type=jnp.float32)
    up_proj = jnp.dot(normed_ffn, up_w, preferred_element_type=jnp.float32)
    sigmoid_gate = jax.nn.sigmoid(gate_proj)
    silu_gate = gate_proj * sigmoid_gate
    activation = (silu_gate * up_proj).astype(jnp.bfloat16)
    output = (hidden_one + jnp.dot(activation, down_w, preferred_element_type=jnp.float32)).astype(
        jnp.bfloat16
    )
    grad_output = cotangent.reshape(row_count, model_width)
    gain_two, gate_w, up_w, down_w = gather_feedforward(gain_ffn, w_gate, w_up, w_down)
    grad_act = jnp.einsum("td,fd->tf", grad_output, down_w, preferred_element_type=jnp.float32)
    grad_gate = (
        grad_act * up_proj * sigmoid_gate * (1.0 + gate_proj * (1.0 - sigmoid_gate))
    ).astype(jnp.bfloat16)
    grad_up = (grad_act * silu_gate).astype(jnp.bfloat16)
    term_gate = jnp.einsum("td,tf->df", normed_ffn, grad_gate, preferred_element_type=jnp.float32)
    term_up = jnp.einsum("td,tf->df", normed_ffn, grad_up, preferred_element_type=jnp.float32)
    term_down = jnp.einsum("tf,td->fd", activation, grad_output, preferred_element_type=jnp.float32)
    grad_normed = jnp.einsum("tf,df->td", grad_gate, gate_w, preferred_element_type=jnp.float32)
    grad_normed = grad_normed + jnp.einsum(
        "tf,df->td", grad_up, up_w, preferred_element_type=jnp.float32
    )
    unit_ffn = hidden_one * scale_ffn
    term_gain_two = jnp.sum(grad_normed * unit_ffn, axis=0)
    grad_hat = grad_normed * gain_two.astype(jnp.float32)
    grad_hidden = grad_output.astype(jnp.float32) + scale_ffn * (
        grad_hat - unit_ffn * jnp.mean(grad_hat * unit_ffn, axis=-1, keepdims=True)
    )
    ffn_sums = reduce_terms((term_gate, term_up, term_down, term_gain_two))
    grad_branch = grad_hidden.astype(jnp.bfloat16)
    gain_one, query_w, key_w, value_w, out_w = gather_attention(
        gain_attn, w_query, w_key, w_value, w_out
    )
    term_out = jnp.einsum(
        "te,td->ed", attended_tokens, grad_branch, preferred_element_type=jnp.float32
    )
    grad_attended = jnp.einsum(
        "td,ed->te", grad_branch, out_w, preferred_element_type=jnp.float32
    ).astype(jnp.bfloat16)
    grad_send = grad_attended.reshape(streams, local_len, seq_count, head_group * head_width)
    grad_heads = lax.all_to_all(grad_send, "seq", split_axis=2, concat_axis=1, tiled=True).reshape(
        streams * length, head_group, head_width
    )
    query_grad, key_grad, value_grad = attend_backward(
        query_all, key_all, value_all, segment_all, length, log_sums, grad_heads
    )
    pair_grad = jnp.concatenate([key_grad, value_grad], axis=-1)
    query_return = query_grad.reshape(streams, length, 1, head_group * head_width)
    pair_return = pair_grad.reshape(streams, length, copies, 2 * head_width)
    query_back, pair_back = (
        lax.all_to_all(
            query_return.astype(jnp.bfloat16), "seq", split_axis=1, concat_axis=2, tiled=True
        ).astype(query_return.dtype),
        lax.all_to_all(
            pair_return.astype(jnp.bfloat16), "seq", split_axis=1, concat_axis=2, tiled=True
        ).astype(pair_return.dtype),
    )
    query_back = query_back.reshape(streams, local_len, head_count, head_width)
    pair_back = jnp.sum(pair_back.reshape(streams, local_len, kv_count, -1, 2 * head_width), axis=3)
    grad_query_rows = (
        unrotate(query_back, cosine, sine)
        .astype(jnp.bfloat16)
        .reshape(row_count, head_count * head_width)
    )
    grad_key_rows = (
        unrotate(pair_back[..., :head_width], cosine, sine)
        .astype(jnp.bfloat16)
        .reshape(row_count, kv_count * head_width)
    )
    grad_value_rows = (
        pair_back[..., head_width:].astype(jnp.bfloat16).reshape(row_count, kv_count * head_width)
    )
    term_query = jnp.einsum(
        "td,te->de", normed_attn, grad_query_rows, preferred_element_type=jnp.float32
    )
    term_key = jnp.einsum(
        "td,te->de", normed_attn, grad_key_rows, preferred_element_type=jnp.float32
    )
    term_value = jnp.einsum(
        "td,te->de", normed_attn, grad_value_rows, preferred_element_type=jnp.float32
    )
    grad_first = jnp.einsum(
        "te,de->td", grad_query_rows, query_w, preferred_element_type=jnp.float32
    )
    grad_first = grad_first + jnp.einsum(
        "te,de->td", grad_key_rows, key_w, preferred_element_type=jnp.float32
    )
    grad_first = grad_first + jnp.einsum(
        "te,de->td", grad_value_rows, value_w, preferred_element_type=jnp.float32
    )
    unit_attn = inputs * scale_attn
    term_gain_one = jnp.sum(grad_first * unit_attn, axis=0)
    grad_hat_one = grad_first * gain_one.astype(jnp.float32)
    grad_input = grad_hidden + scale_attn * (
        grad_hat_one - unit_attn * jnp.mean(grad_hat_one * unit_attn, axis=-1, keepdims=True)
    )
    attn_sums = reduce_terms((term_query, term_key, term_value, term_out, term_gain_one))
    return (
        output.reshape(streams, local_len, model_width),
        grad_input.reshape(streams, local_len, model_width),
        attn_sums[4],
        attn_sums[0],
        attn_sums[1],
        attn_sums[2],
        attn_sums[3],
        ffn_sums[3],
        ffn_sums[0],
        ffn_sums[1],
        ffn_sums[2],
    )


def solution(mesh):
    placed = (
        P("fsdp", "seq", None),
        P("fsdp", "seq"),
        P(("seq", "fsdp")),
        P(("seq", "fsdp"), None),
        P(("seq", "fsdp"), None),
        P(("seq", "fsdp"), None),
        P(("seq", "fsdp"), None),
        P(("seq", "fsdp")),
        P(("seq", "fsdp"), None),
        P(("seq", "fsdp"), None),
        P(("seq", "fsdp"), None),
        P("fsdp", "seq", None),
    )
    return jax.shard_map(
        body,
        mesh=mesh,
        in_specs=placed,
        out_specs=(
            P("fsdp", "seq", None),
            P("fsdp", "seq", None),
            P(("seq", "fsdp")),
            P(("seq", "fsdp"), None),
            P(("seq", "fsdp"), None),
            P(("seq", "fsdp"), None),
            P(("seq", "fsdp"), None),
            P(("seq", "fsdp")),
            P(("seq", "fsdp"), None),
            P(("seq", "fsdp"), None),
            P(("seq", "fsdp"), None),
        ),
        check_vma=False,
    )
```

profile of v0, /device:TPU:0, one launch (start us, length us, event | category | flops | bytes accessed | tf_op | source)
XLA Modules:
  0.0 6015.1 jit_solution(5665313782535262937)
XLA Ops:
  30.9 39.7 all-reduce.8
  74.7 48.7 all-gather.10.cloned.1.call-done
  136.4 86.6 %all-gather.8.cloned.1.call-done = bf16[2048,2048]{1,0:T(8,128)(2,1)} async-done(((bf16[64,2048]{1,0:T(8,128)(2,1)}), bf16[2048,2048]{1,0:T(8,128)(2,1)}) %all-gather.8.cloned.1.call-update) | async-done | bytes 8388624 | tf_op jit(solution)/shard_map/all_gather | solution.py:75
  249.9 37.3 all_gather.47
  310.5 455.6 %while.44 = (s32[]{:T(128)}, bf16[8,512,4,64]{1,3,2,0:T(8,128)(2,1)}, f32[8,4,512]{2,1,0:T(4,128)}, s32[8]{0:T(128)S(1)}, s32[1,4096]{1,0:T(1,128)S(1)}, /*index...) while((s32[]{:T(128)}, ...), condition=%wide.region_10.11_spmd, body=%wide.region_7.10_spmd.sunk | while | flops 2254567936 | bytes 122251664 | solution.py:131
  373.8 18.4 fusion.162
  520.5 18.2 fusion.164
  789.0 32.1 reduce.10
  827.9 26.6 all-to-all-done.2
  877.0 19.8 fusion.93
  896.8 19.1 fusion.94
  915.9 28.5 multiply_convert_fusion.1
  944.3 19.6 fusion.95
  963.9 19.5 multiply_reduce_fusion.1
  1000.6 26.5 all-to-all-done.3
  1037.4 953.9 %while.45 = (s32[]{:T(128)}, f32[4096,4,64]{0,2,1:T(8,128)}, f32[4096,4,64]{0,2,1:T(8,128)}, bf16[8,512,4,64]{1,3,2,0:T(8,128)(2,1)}, s32[8]{0:T(128)S(1)}, /*in...) while((s32[]{:T(128)}, f32[4096,4,64]{0,2,1:T(8,128)}, ...), condition=%wide.region_15.16_spmd.clone, body=%wide.region_13.15_spmd.clone.sunk | while | flops 5506202112 | bytes 293161408 | solution.py:173
  1059.9 29.4 multiply_reduce_fusion.5
  1089.3 27.6 multiply_convert_fusion.6
  1177.0 29.4 multiply_reduce_fusion.5
  1206.4 27.6 multiply_convert_fusion.6
  1246.3 17.7 fusion.177
  1296.5 29.4 multiply_reduce_fusion.5
  1325.9 27.6 multiply_convert_fusion.6
  1365.8 17.7 fusion.177
  1416.0 29.4 multiply_reduce_fusion.5
  1445.4 27.6 multiply_convert_fusion.6
  1485.3 17.7 fusion.177
  1535.4 29.4 multiply_reduce_fusion.5
  1564.8 27.6 multiply_convert_fusion.6
  1654.9 29.4 multiply_reduce_fusion.5
  1684.3 27.6 multiply_convert_fusion.6
  1774.4 29.4 multiply_reduce_fusion.5
  1803.8 27.6 multiply_convert_fusion.6
  1893.8 29.4 multiply_reduce_fusion.5
  1923.2 27.6 multiply_convert_fusion.6
  2013.1 51.6 all_to_all.78
  2118.1 22.9 reduce.11
  2146.8 32.9 all_to_all.79
  2209.9 23.9 fusion.98
  2234.0 23.9 fusion.99
  2258.0 23.9 fusion.56
  2281.9 19.9 fusion.55
  2314.6 37.2 all-reduce.7
  2359.5 359.3 %reduce-scatter.14.cloned.1.call-done = f32[64,2048]{1,0:T(8,128)} async-done(((f32[2048,2048]{1,0:T(8,128)}), f32[64,2048]{1,0:T(8,128)}) %reduce-scatter.14.cloned.1.call-update) | async-done | bytes 524304 | tf_op jit(solution)/shard_map/reduce_scatter | solution.py:92
  2718.8 365.0 %reduce-scatter.8.cloned.1.call-done = f32[64,2048]{1,0:T(8,128)} async-done(((f32[2048,2048]{1,0:T(8,128)}), f32[64,2048]{1,0:T(8,128)}) %reduce-scatter.8.cloned.1.call-update) | async-done | bytes 524304 | tf_op jit(solution)/shard_map/reduce_scatter | solution.py:92
  3083.8 973.1 %reduce-scatter.16.cloned.1.call-done = f32[64,5632]{1,0:T(8,128)} async-done(((f32[2048,5632]{1,0:T(8,128)}), f32[64,5632]{1,0:T(8,128)}) %reduce-scatter.16.cloned.1.call-update) | async-done | bytes 1441808 | tf_op jit(solution)/shard_map/reduce_scatter | solution.py:92
  4056.9 975.7 %reduce-scatter.18.cloned.1.call-done = f32[64,5632]{1,0:T(8,128)} async-done(((f32[2048,5632]{1,0:T(8,128)}), f32[64,5632]{1,0:T(8,128)}) %reduce-scatter.18.cloned.1.call-update) | async-done | bytes 1441808 | tf_op jit(solution)/shard_map/reduce_scatter | solution.py:92
  5032.6 975.5 %reduce-scatter.20.cloned.1.call-done = f32[176,2048]{1,0:T(8,128)} async-done(((f32[5632,2048]{1,0:T(8,128)}), f32[176,2048]{1,0:T(8,128)}) %reduce-scatter.20.cloned.1.call-update) | async-done | bytes 1441808 | tf_op jit(solution)/shard_map/reduce_scatter | solution.py:92
  (380 shorter events, 1090.6 us)
Async XLA Ops:
  7.2 66.0 %all-gather.12.cloned.1.call-start = ((), (), s32[]{:S(2)}) async-start(), calls=%async_computation.15 | async-start | bytes 1081344 | tf_op jit(solution)/shard_map/all_gather | solution.py:77
  7.9 115.4 %all-gather.10.cloned.1.call-start = ((), (), s32[]{:S(2)}) async-start(), calls=%async_computation.14 | async-start | bytes 1081344 | tf_op jit(solution)/shard_map/all_gather | solution.py:76
  8.7 214.4 %all-gather.8.cloned.1.call-start = ((), (), s32[]{:S(2)}) async-start(), calls=%async_computation.13 | async-start | bytes 8650752 | tf_op jit(solution)/shard_map/all_gather | solution.py:75
  9.4 857.3 %all-gather.14.cloned.1.call-start = ((), (), s32[]{:S(2)}) async-start(), calls=%async_computation.16 | async-start | bytes 8650752 | tf_op jit(solution)/shard_map/all_gather | solution.py:78
  10.0 115.6 %copy-start.4 = (bf16[1,512,2048]{2,1,0:T(8,128)(2,1)S(1)}, bf16[1,512,2048]{2,1,0:T(8,128)(2,1)}, u32[]{:S(2)}) copy-start(bf16[1,512,2048]{2,1,0:T(8,128)(2,1)} %param.18) | copy-start | bytes 6291460
  10.0 867.0 %all-gather.16.cloned.1.call-start = ((), (), s32[]{:S(2)}) async-start(), calls=%async_computation.17 | async-start | bytes 23789568 | tf_op jit(solution)/shard_map/all_gather | solution.py:85
  10.6 886.2 %all-gather.18.cloned.1.call-start = ((), (), s32[]{:S(2)}) async-start(), calls=%async_computation.18 | async-start | bytes 23789568 | tf_op jit(solution)/shard_map/all_gather | solution.py:86
  70.6 164.8 %copy-start.28 = (f32[2048]{0:T(1024)}, f32[2048]{0:T(1024)S(1)}, u32[]{:S(2)}) copy-start(f32[2048]{0:T(1024)S(1)} %convert_element_type.207) | copy-start | bytes 24580
  72.7 162.7 %copy-start.30 = (f32[512]{0:T(512)}, f32[512]{0:T(512)S(1)}, u32[]{:S(2)}) copy-start(f32[512]{0:T(512)S(1)} %add_rsqrt_fusion.1) | copy-start | bytes 6148
  73.1 169.4 %copy-start.20 = (f32[512,32]{0,1:T(8,128)}, f32[512,32]{0,1:T(8,128)S(1)}, u32[]{:S(2)}) copy-start(f32[512,32]{0,1:T(8,128)S(1)} %get-tuple-element.548) | copy-start | bytes 196612
  73.1 169.4 %copy-start.22 = (f32[512,32]{0,1:T(8,128)}, f32[512,32]{0,1:T(8,128)S(1)}, u32[]{:S(2)}) copy-start(f32[512,32]{0,1:T(8,128)S(1)} %get-tuple-element.549) | copy-start | bytes 196612
  131.9 112.9 %all-to-all-start.1 = ((bf16[1,512,32,128]{3,1,0,2:T(8,128)(2,1)}), bf16[1,512,32,128]{3,1,0,2:T(8,128)(2,1)}, u32[]{:S(2)}, u32[]{:S(2)}) async-start(bf16[1,512,32,128]{3,1,0,2:T(8,128)(2,1)} %bitcast.268), calls=%async_computation.1 | async-start | bytes 8388608 | tf_op jit(solution)/shard_map/all_to_all | solution.py:236
  244.8 57.4 all-to-all-start
  249.1 666.7 %all-gather.20.cloned.1.call-start = ((), (), s32[]{:S(2)}) async-start(), calls=%async_computation.19 | async-start | bytes 23789568 | tf_op jit(solution)/shard_map/all_gather | solution.py:87
  317.9 15.5 copy-start.3
  373.8 18.4 copy-start.3
  432.5 16.0 copy-start.3
  489.8 15.4 copy-start.3
  546.7 15.4 copy-start.3
  602.7 16.0 copy-start.3
  659.5 15.3 copy-start.3
  717.3 15.7 copy-start.3
  766.1 22.4 copy-start
  766.1 22.4 copy-start.14
  766.1 22.4 copy-start.34
  824.3 30.2 all-to-all-start.2
  876.9 19.9 copy-start.16
  963.9 19.5 copy-start.8
  963.9 19.5 copy-start.19
  984.6 9.8 copy-start.9
  996.9 30.2 all-to-all-start.3
  1000.5 1359.0 %reduce-scatter.10.cloned.1.call-start = ((), (), s32[]{:S(2)}) async-start(), calls=%async_computation.21 | async-start | bytes 2162688 | tf_op jit(solution)/shard_map/reduce_scatter | solution.py:92
  1144.6 10.1 copy-start.2
  1264.1 10.1 copy-start.2
  1383.5 10.1 copy-start.2
  1503.0 10.1 copy-start.2
  1622.5 10.1 copy-start.2
  1741.9 10.1 copy-start.2
  1861.4 10.1 copy-start.2
  1980.8 10.1 copy-start.2
  2067.0 9.3 copy-start.23
  2079.0 280.6 %reduce-scatter.12.cloned.1.call-start = ((), (), s32[]{:S(2)}) async-start(), calls=%async_computation.22 | async-start | bytes 2162688 | tf_op jit(solution)/shard_map/reduce_scatter | solution.py:92
  2082.5 636.3 %reduce-scatter.14.cloned.1.call-start = ((), (), s32[]{:S(2)}) async-start(), calls=%async_computation.23 | async-start | bytes 17301504 | tf_op jit(solution)/shard_map/reduce_scatter | solution.py:92
  2095.8 988.1 %reduce-scatter.8.cloned.1.call-start = ((), (), s32[]{:S(2)}) async-start(), calls=%async_computation.20 | async-start | bytes 17301504 | tf_op jit(solution)/shard_map/reduce_scatter | solution.py:92
  2209.8 1847.1 %reduce-scatter.16.cloned.1.call-start = ((), (), s32[]{:S(2)}) async-start(), calls=%async_computation.24 | async-start | bytes 47579136 | tf_op jit(solution)/shard_map/reduce_scatter | solution.py:92
  2233.7 2798.9 %reduce-scatter.18.cloned.1.call-start = ((), (), s32[]{:S(2)}) async-start(), calls=%async_computation.25 | async-start | bytes 47579136 | tf_op jit(solution)/shard_map/reduce_scatter | solution.py:92
  2257.9 3750.2 %reduce-scatter.20.cloned.1.call-start = ((), (), s32[]{:S(2)}) async-start(), calls=%async_computation.26 | async-start | bytes 47579136 | tf_op jit(solution)/shard_map/reduce_scatter | solution.py:92
  2281.9 19.9 copy-start.18
  (20 other events, 100.8 us)
Sparse Core Ops, SparseCore 0:
  11.0 56.5 all-gather.11
  70.5 52.7 all-gather.9
  126.3 96.7 all-gather.7
  225.8 84.9 all-gather.13
  313.6 142.4 all-gather.15
  458.8 142.7 all-gather.17
  604.5 142.7 all-gather.19
  2079.1 135.4 reduce-scatter.9
  2217.5 136.2 reduce-scatter.11
  2356.6 362.1 reduce-scatter.13
  2721.7 362.1 reduce-scatter.7
  3086.6 970.3 reduce-scatter.15
  4059.8 972.7 reduce-scatter.17
  5035.3 972.7 reduce-scatter.19
where the time goes:
time: 6030 us; the launch traced here: 6020 us
  waiting for transfers between devices  3840 us (64%)
  matrix products  1200 us (20%)
  other arithmetic  479 us (8%)
  blocking collectives  208 us (3%)
  local copies, waits for them, and re-layouts  182 us (3%)
  loops' own time  73.8 us (1%)
    reduce_scatter x7, waiting for transfers between devices, reduce_terms(): lax.psum_scatter(terms, ('seq', 'fsdp'), scatter_dimension=0, tiled=True)  3650 us
    dot_general x16, matrix products, block_logits(): jnp.einsum('qhd,khd->hqk', query_block, key_all, preferred_element_type=j...  241 us
    dot_general x8, matrix products, one_block(): jnp.einsum('qhd,khd->hqk', grad_block, value_all, preferred_element_type=...  235 us
    convert_element_type x8, other arithmetic, one_block(): grad_logits = grad_logits.astype(jnp.bfloat16)  221 us
    dot_general x8, matrix products, one_block(): jnp.einsum('hqk,qhd->khd', probability_low, grad_block, preferred_element...  141 us
    dot_general x8, matrix products, one_block(): jnp.einsum('hqk,khd->qhd', probability, value_all, preferred_element_type...  139 us
    reduce_sum x8, other arithmetic, one_block(): denominator = jnp.sum(weights, axis=-1, keepdims=True)  125 us
  transfers between devices with their start and end apart: 18, of which 9 were waited for; matrix products, arithmetic and copies ran while one was open for 13% of the time, Pallas kernels for 0%

commit v1 on v0

v1 whole, which is shorter than its diff:
```python
import functools
import math

import jax
import jax.numpy as jnp
from jax import lax
from jax.experimental import pallas as pl
from jax.experimental.pallas import tpu as pltpu
from jax.sharding import PartitionSpec as P

H = 32
KV = 4
HD = 64
HALF = HD // 2
EPS = 1e-05
NEG = -1e30
BQ = 256
BK = 512
BF = jnp.bfloat16
F32 = jnp.float32
VMEM_LIMIT = 56 * 1024 * 1024


def dot_f32(a, b):
    return jnp.dot(a, b, preferred_element_type=F32)


def heads_wide(block, group):
    return jnp.concatenate([block[h * HD : (h + 1) * HD] for h in range(group)], axis=1)


def heads_tall(block, group):
    width = block.shape[1] // group
    return jnp.concatenate([block[:, h * width : (h + 1) * width] for h in range(group)], axis=0)


def allowed_block(step, block_keys, first_row, block_rows, wide, starts):
    key = step * block_keys + lax.broadcasted_iota(jnp.int32, (block_keys, 1), 0)
    row = first_row + (lax.broadcasted_iota(jnp.int32, (1, wide), 1) & (block_rows - 1))
    return (key <= row) & (key >= starts)


def three_loops(bounds_ref, index, body):
    low, first, second, high = (bounds_ref[index, n] for n in range(4))
    lax.fori_loop(low, first, lambda j, c: body(j, True), None)
    lax.fori_loop(first, second, lambda j, c: body(j, False), None)
    lax.fori_loop(second, high, lambda j, c: body(j, True), None)


def forward_kernel(group, bounds_ref, q_ref, k_ref, vt_ref, start_ref, o_ref, lse_ref, acc, top, total):
    i = pl.program_id(0)
    rows = q_ref.shape[1]
    wide = rows * group
    q4 = heads_wide(q_ref[...], group)
    starts = start_ref[0]
    acc[...] = jnp.zeros_like(acc)
    top[...] = jnp.full_like(top, NEG)
    total[...] = jnp.zeros_like(total)

    def block(j, masked):
        at = pl.multiple_of(j * BK, BK)
        s = dot_f32(k_ref[pl.ds(at, BK), :], q4)
        if masked:
            s = jnp.where(allowed_block(j, BK, i * rows, rows, wide, starts), s, NEG)
        old = top[...]
        new = jnp.maximum(old, jnp.max(s, axis=0, keepdims=True))
        p = jnp.exp(s - new)
        keep = jnp.exp(old - new)
        top[...] = new
        total[...] = total[...] * keep + jnp.sum(p, axis=0, keepdims=True)
        acc[...] = acc[...] * keep + dot_f32(vt_ref[:, pl.ds(at, BK)], p.astype(BF))

    three_loops(bounds_ref, i, block)
    o = acc[...] / total[...]
    o_ref[0] = heads_tall(o, group).astype(BF)
    lse_ref[0] = top[...] + jnp.log(total[...])


def backward_kernel(
    group, bounds_ref, q_ref, k_ref, kt_ref, v_ref, start_ref, o_ref, do_ref, lse_ref,
    dq_ref, dk_ref, dv_ref, acc,
):
    i = pl.program_id(0)
    rows = q_ref.shape[1]
    wide = rows * group
    q4 = heads_wide(q_ref[...], group)
    g4 = heads_wide(do_ref[0], group)
    o4 = heads_wide(o_ref[0], group)
    delta = jnp.sum(g4.astype(F32) * o4.astype(F32), axis=0, keepdims=True)
    q4t = q4.T
    g4t = g4.T
    starts = start_ref[0]
    lse = lse_ref[0]
    acc[...] = jnp.zeros_like(acc)

    @pl.when(i == 0)
    def _():
        dk_ref[...] = jnp.zeros_like(dk_ref)
        dv_ref[...] = jnp.zeros_like(dv_ref)

    def block(j, masked):
        at = pl.multiple_of(j * BK, BK)
        s = dot_f32(k_ref[pl.ds(at, BK), :], q4)
        p = jnp.exp(s - lse)
        if masked:
            p = jnp.where(allowed_block(j, BK, i * rows, rows, wide, starts), p, 0.0)
        dp = dot_f32(v_ref[pl.ds(at, BK), :], g4)
        ds = (p * (dp - delta)).astype(BF)
        dv_ref[pl.ds(at, BK), :] += dot_f32(p.astype(BF), g4t)
        dk_ref[pl.ds(at, BK), :] += dot_f32(ds, q4t)
        acc[...] += dot_f32(kt_ref[:, pl.ds(at, BK)], ds)

    three_loops(bounds_ref, i, block)
    dq_ref[...] = heads_tall(acc[...], group)


def whole_spec(shape):
    return pl.BlockSpec(shape, lambda i, b: (0,) * len(shape))


def attend(bounds, qt, k, vt, starts, group, senders, local):
    length = k.shape[0]
    blocks = length // BQ
    per = local // BQ
    piece = pl.BlockSpec((1, group * HD, BQ), lambda i, b: (i // per, 0, i % per))
    line = pl.BlockSpec((1, 1, group * BQ), lambda i, b: (i, 0, 0))
    return pl.pallas_call(
        functools.partial(forward_kernel, group),
        out_shape=(
            jax.ShapeDtypeStruct((senders, group * HD, local), BF),
            jax.ShapeDtypeStruct((blocks, 1, group * BQ), F32),
        ),
        grid_spec=pltpu.PrefetchScalarGridSpec(
            num_scalar_prefetch=1,
            grid=(blocks,),
            in_specs=[
                pl.BlockSpec((group * HD, BQ), lambda i, b: (0, i)),
                whole_spec((length, HD)),
                whole_spec((HD, length)),
                line,
            ],
            out_specs=(piece, line),
            scratch_shapes=[
                pltpu.VMEM((HD, group * BQ), F32),
                pltpu.VMEM((1, group * BQ), F32),
                pltpu.VMEM((1, group * BQ), F32),
            ],
        ),
        compiler_params=pltpu.CompilerParams(
            dimension_semantics=("arbitrary",), vmem_limit_bytes=VMEM_LIMIT
        ),
        cost_estimate=pl.CostEstimate(
            flops=4 * group * length * length * HD // 2,
            bytes_accessed=4 * group * length * HD * 2,
            transcendentals=group * length * length // 4,
        ),
        name="attend",
    )(bounds, qt, k, vt, starts)


def attend_back(bounds, qt, k, kt, v, starts, o, do, lse, group):
    length = k.shape[0]
    blocks = length // BQ
    senders, _, local = o.shape
    per = local // BQ
    piece = pl.BlockSpec((1, group * HD, BQ), lambda i, b: (i // per, 0, i % per))
    line = pl.BlockSpec((1, 1, group * BQ), lambda i, b: (i, 0, 0))
    flat = pl.BlockSpec((group * HD, BQ), lambda i, b: (0, i))
    return pl.pallas_call(
        functools.partial(backward_kernel, group),
        out_shape=(
            jax.ShapeDtypeStruct((group * HD, length), F32),
            jax.ShapeDtypeStruct((length, HD), F32),
            jax.ShapeDtypeStruct((length, HD), F32),
        ),
        grid_spec=pltpu.PrefetchScalarGridSpec(
            num_scalar_prefetch=1,
            grid=(blocks,),
            in_specs=[
                flat,
                whole_spec((length, HD)),
                whole_spec((HD, length)),
                whole_spec((length, HD)),
                line,
                piece,
                piece,
                line,
            ],
            out_specs=(flat, whole_spec((length, HD)), whole_spec((length, HD))),
            scratch_shapes=[pltpu.VMEM((HD, group * BQ), F32)],
        ),
        compiler_params=pltpu.CompilerParams(
            dimension_semantics=("arbitrary",), vmem_limit_bytes=VMEM_LIMIT
        ),
        cost_estimate=pl.CostEstimate(
            flops=10 * group * length * length * HD // 2,
            bytes_accessed=8 * group * length * HD * 2,
            transcendentals=group * length * length // 4,
        ),
        name="attend_back",
    )(bounds, qt, k, kt, v, starts, o, do, lse)


def ring(axis):
    count = lax.axis_size(axis)
    return [(n, (n + 1) % count) for n in range(count)]


def ring_gather(block, axis):
    count = lax.axis_size(axis)
    me = lax.axis_index(axis)
    pieces = [block]
    for _ in range(count - 1):
        block = lax.ppermute(block, axis, ring(axis))
        pieces.append(block)
    whole = jnp.zeros((count,) + block.shape, block.dtype)
    for back, piece in enumerate(pieces):
        whole = lax.dynamic_update_index_in_dim(whole, piece, (me + count - back) % count, 0)
    return whole


def ring_scatter(terms, axis):
    count = lax.axis_size(axis)
    me = lax.axis_index(axis)

    def pick(back):
        return lax.dynamic_index_in_dim(terms, (me + 2 * count - 1 - back) % count, 0, False)

    state = pick(0)
    for step in range(1, count):
        moved = lax.ppermute(state.astype(BF), axis, ring(axis))
        state = moved.astype(F32) + pick(step).astype(F32)
    return state


def exchange(array):
    return lax.all_to_all(array, "seq", split_axis=0, concat_axis=0, tiled=True)


def document_starts(flags_all):
    length = flags_all.shape[0]
    lanes = 128
    table = flags_all.reshape(length // lanes, lanes)
    place = jnp.arange(length, dtype=jnp.int32).reshape(table.shape)
    marked = jnp.where((table != 0) & (place > 0), place, 0)
    inside = jnp.arange(lanes)[None, :] <= jnp.arange(lanes)[:, None]
    local = jnp.max(jnp.where(inside[None], marked[:, None, :], 0), axis=-1)
    rows = jnp.max(marked, axis=1)
    count = length // lanes
    before = jnp.arange(count)[None, :] < jnp.arange(count)[:, None]
    carried = jnp.max(jnp.where(before, rows[None, :], 0), axis=-1)
    return jnp.maximum(local, carried[:, None]).reshape(length)


def rotate(block, cosine, sine, direction):
    first, second = block[:, :HALF], block[:, HALF:]
    sine = sine * direction
    return jnp.concatenate(
        [first * cosine - second * sine, second * cosine + first * sine], axis=1
    )


def body(
    tokens, doc_starts, gain_attn, w_query, w_key, w_value, w_out, gain_ffn, w_gate, w_up, w_down,
    cotangent,
):
    streams, local, width = tokens.shape
    assert streams == 1
    count = lax.axis_size("seq")
    parts = lax.axis_size("fsdp")
    length = local * count
    group = H // count
    share = (H // KV) // group
    rows = w_query.shape[0]
    hidden = w_gate.shape[1] // count
    group_width = group * HD
    both = ("seq", "fsdp")

    gains = lax.all_gather(jnp.stack([gain_attn, gain_ffn]), both, axis=1, tiled=True)
    gain_one, gain_two = gains[0].astype(F32), gains[1].astype(F32)
    flags = lax.all_gather(doc_starts[0], "seq", axis=0, tiled=True)
    x = tokens[0].astype(F32)
    r1 = lax.rsqrt(jnp.mean(x * x, axis=-1, keepdims=True) + EPS)
    n1 = (x * r1 * gain_one).astype(BF)
    n1_all = lax.all_gather(n1, "seq", axis=0, tiled=True)

    last = document_starts(flags)
    place = (jnp.arange(length, dtype=jnp.int32) - last).astype(F32)
    frequency = jnp.exp(jnp.arange(HALF, dtype=F32) * (-2.0 * math.log(10000.0) / HD))
    angle = frequency[:, None] * place[None, :]
    cosine, sine = jnp.cos(angle), jnp.sin(angle)
    blocks = length // BQ
    by_block = last.reshape(blocks, BQ)
    starts = jnp.tile(by_block, (1, group)).reshape(blocks, 1, group * BQ)
    first_row = jnp.arange(blocks, dtype=jnp.int32) * BQ
    low = by_block[:, 0] // BK
    high = (first_row + BQ + BK - 1) // BK
    begin = jnp.minimum((by_block[:, -1] + BK - 1) // BK, high)
    end = jnp.maximum((first_row + 1) // BK, begin)
    bounds = jnp.stack([low, begin, end, high], axis=1)

    attn_send = jnp.concatenate(
        [
            w_query.reshape(rows, count, group_width),
            jnp.repeat(w_key.reshape(rows, KV, HD), share, axis=1),
            jnp.repeat(w_value.reshape(rows, KV, HD), share, axis=1),
        ],
        axis=2,
    ).transpose(1, 2, 0)
    attn_cols = group_width + 2 * HD
    attn_part = exchange(attn_send)
    attn_t = ring_gather(attn_part, "fsdp").transpose(2, 1, 0, 3).reshape(attn_cols, width)

    ffn_send = jnp.concatenate(
        [w_gate.reshape(rows, count, hidden), w_up.reshape(rows, count, hidden)], axis=0
    ).transpose(1, 0, 2)
    ffn_part = exchange(ffn_send).reshape(count, 2, rows, hidden)
    ffn_w = ring_gather(ffn_part, "fsdp").transpose(2, 1, 0, 3, 4).reshape(2, width, hidden)
    gate_w, up_w = ffn_w[0], ffn_w[1]
    down_w = ring_gather(w_down, "fsdp").reshape(hidden, width)

    projected = jnp.einsum("ed,td->et", attn_t, n1_all, preferred_element_type=F32)
    q_t = rotate(projected[:group_width].reshape(group, HD, length), cosine, sine, 1.0)
    k_t = rotate(projected[group_width : group_width + HD].reshape(1, HD, length), cosine, sine, 1.0)
    q_t = (q_t.astype(BF) * BF(HD**-0.5)).reshape(group_width, length)
    k_t = k_t.astype(BF).reshape(HD, length)
    v_t = projected[group_width + HD :].astype(BF)
    k_n, v_n = k_t.T, v_t.T
    o_heads, lse = attend(bounds, q_t, k_n, v_t, starts, group, count, local)
    o_t = exchange(o_heads).reshape(count * group_width, local)
    out_w = lax.all_gather(w_out, both, axis=0, tiled=True)
    h1 = x + jnp.einsum("et,ed->td", o_t, out_w, preferred_element_type=F32)
    r2 = lax.rsqrt(jnp.mean(h1 * h1, axis=-1, keepdims=True) + EPS)
    n2 = (h1 * r2 * gain_two).astype(BF)
    n2_all = lax.all_gather(n2, "seq", axis=0, tiled=True)
    dy = cotangent[0]
    dy_all = lax.all_gather(dy, "seq", axis=0, tiled=True)

    gate = dot_f32(n2_all, gate_w)
    up = dot_f32(n2_all, up_w)
    sig = jax.nn.sigmoid(gate)
    silu = gate * sig
    act = (silu * up).astype(BF)
    d_act = jnp.einsum("td,fd->tf", dy_all, down_w, preferred_element_type=F32)
    d_gate = (d_act * up * sig * (1.0 + gate * (1.0 - sig))).astype(BF)
    d_up = (d_act * silu).astype(BF)
    dn2_part = jnp.einsum("tf,df->td", d_gate, gate_w, preferred_element_type=F32) + jnp.einsum(
        "tf,df->td", d_up, up_w, preferred_element_type=F32
    )
    dn2 = lax.psum_scatter(dn2_part.astype(BF), "seq", scatter_dimension=0, tiled=True).astype(F32)
    y_part = dot_f32(act, down_w).astype(BF)
    y = lax.psum_scatter(y_part, "seq", scatter_dimension=0, tiled=True).astype(F32)
    output = (h1 + y).astype(BF)

    def by_fsdp(term):
        return term.reshape(count, parts, rows, -1).transpose(1, 0, 2, 3)

    term_gate = jnp.einsum("td,tf->df", n2_all, d_gate, preferred_element_type=F32)
    term_up = jnp.einsum("td,tf->df", n2_all, d_up, preferred_element_type=F32)
    term_down = jnp.einsum("tf,td->fd", act, dy_all, preferred_element_type=F32)
    part_gate = ring_scatter(by_fsdp(term_gate), "fsdp")
    part_up = ring_scatter(by_fsdp(term_up), "fsdp")
    grad_down = ring_scatter(term_down.reshape(parts, hidden // parts, width), "fsdp")

    m2 = h1 * r2
    e2 = dn2 * gain_two
    dh1 = dy.astype(F32) + r2 * (e2 - m2 * jnp.mean(e2 * m2, axis=-1, keepdims=True))
    db = dh1.astype(BF)
    do_t = jnp.einsum("ed,td->et", out_w, db, preferred_element_type=F32).astype(BF)
    do_heads = exchange(do_t.reshape(count, group_width, local))
    term_out = dot_f32(o_t, db).astype(BF)
    part_out = lax.psum_scatter(term_out, "seq", scatter_dimension=0, tiled=True)
    grad_out = ring_scatter(part_out.reshape(parts, rows, width), "fsdp")

    dq_t, dk_n, dv_n = attend_back(
        bounds, q_t, k_n, k_t, v_n, starts, o_heads, do_heads, lse, group
    )
    dq_t = rotate(dq_t.reshape(group, HD, length) * (HD**-0.5), cosine, sine, -1.0)
    dk_t = rotate(dk_n.T.reshape(1, HD, length), cosine, sine, -1.0)
    d_t = jnp.concatenate(
        [
            dq_t.reshape(group_width, length).astype(BF),
            dk_t.reshape(HD, length).astype(BF),
            dv_n.T.astype(BF),
        ],
        axis=0,
    )
    dn1_part = jnp.einsum("et,ed->td", d_t, attn_t, preferred_element_type=F32)
    dn1 = lax.psum_scatter(dn1_part.astype(BF), "seq", scatter_dimension=0, tiled=True).astype(F32)
    term_attn = jnp.einsum("td,et->de", n1_all, d_t, preferred_element_type=F32)
    part_attn = ring_scatter(by_fsdp(term_attn), "fsdp")
    m1 = x * r1
    e1 = dn1 * gain_one
    grad_tokens = dh1 + r1 * (e1 - m1 * jnp.mean(e1 * m1, axis=-1, keepdims=True))

    ffn_back = exchange(jnp.stack([part_gate, part_up], axis=1).astype(BF)).astype(F32)
    grad_gate = ffn_back[:, 0].transpose(1, 0, 2).reshape(rows, count * hidden)
    grad_up = ffn_back[:, 1].transpose(1, 0, 2).reshape(rows, count * hidden)
    attn_back = exchange(part_attn.astype(BF)).astype(F32)
    grad_query = attn_back[:, :, :group_width].transpose(1, 0, 2).reshape(rows, H * HD)
    pair = attn_back[:, :, group_width:].reshape(KV, share, rows, 2 * HD).sum(axis=1)
    grad_key = pair[:, :, :HD].transpose(1, 0, 2).reshape(rows, KV * HD)
    grad_value = pair[:, :, HD:].transpose(1, 0, 2).reshape(rows, KV * HD)

    def along(weight, grad):
        return jnp.sum(weight.astype(F32) * grad, axis=1)

    grad_gain_attn = (
        along(w_query, grad_query) + along(w_key, grad_key) + along(w_value, grad_value)
    ) / gain_attn.astype(F32)
    grad_gain_ffn = (along(w_gate, grad_gate) + along(w_up, grad_up)) / gain_ffn.astype(F32)
    return (
        output[None],
        grad_tokens[None],
        grad_gain_attn,
        grad_query,
        grad_key,
        grad_value,
        grad_out,
        grad_gain_ffn,
        grad_gate,
        grad_up,
        grad_down,
    )


def solution(mesh):
    sheet = P("fsdp", "seq", None)
    line = P(("seq", "fsdp"))
    matrix = P(("seq", "fsdp"), None)
    return jax.shard_map(
        body,
        mesh=mesh,
        in_specs=(
            sheet, P("fsdp", "seq"), line, matrix, matrix, matrix, matrix, line, matrix, matrix,
            matrix, sheet,
        ),
        out_specs=(
            sheet, sheet, line, matrix, matrix, matrix, matrix, line, matrix, matrix, matrix,
        ),
        check_vma=False,
    )
```

time: 6030 us -> 1350 us (0.22)
  waiting for transfers between devices: 3840 us -> 574 us
  matrix products: 1200 us -> 254 us
  other arithmetic: 479 us -> 77.3 us
  Pallas kernels: 0 us -> 165 us
  local copies, waits for them, and re-layouts: 182 us -> 59.8 us
  loops' own time: 73.8 us -> 0 us
    reduce_scatter x7 -> x4, waiting for transfers between devices: 3650 us -> 207 us  [the longest x1 116 us: body(): lax.psum_scatter(y_part, 'seq', scatter_dimension=0, tiled=True).astype(F32)]
    dot_general x77 -> x15, matrix products: 1200 us -> 254 us  [the longest x4 65.6 us: dot_f32(): return jnp.dot(a, b, preferred_element_type=F32)]
    ppermute x0 -> x24, waiting for transfers between devices: none -> 306 us  [the longest x9 168 us: ring_gather(): block = lax.ppermute(block, axis, ring(axis))]
    convert_element_type x15 -> x18, other arithmetic: 224 us -> 23.5 us  [the longest x10 15.6 us: ring_scatter(): moved = lax.ppermute(state.astype(BF), axis, ring(axis))]
    pallas_call x0 -> x2, Pallas kernels: none -> 165 us  [the longest x1 94.5 us: attend_back(): pl.pallas_call(functools.partial(backward_kernel, group), out_shape=(jax....]
    reduce_sum x11 -> x9, other arithmetic: 132 us -> 11.6 us  [the longest x1 3.6 us: body(): jnp.mean(e2 * m2, axis=-1, keepdims=True)]
    all_gather x7 -> x4, waiting for transfers between devices: 135 us -> 26.1 us  [the longest x1 26.1 us: body(): n1_all = lax.all_gather(n1, 'seq', axis=0, tiled=True)]
    unnamed x3 -> x0, blocking collectives: 86.4 us -> none
  transfers between devices with their start and end apart: 18 -> 36, of which waited for: 9 -> 25; matrix products, arithmetic and copies ran while one was open for 13% -> 20% of each run, Pallas kernels for 0% -> 12%
where the time goes in v1:
time: 1350 us; the launch traced here: 1340 us
  waiting for transfers between devices  574 us (43%)
  matrix products  254 us (19%)
  blocking collectives  169 us (13%)
  Pallas kernels  165 us (12%)
  other arithmetic  77.3 us (6%)
  local copies, waits for them, and re-layouts  59.8 us (4%)
  starting transfers between devices  21.1 us (2%)
  between operations  15.6 us (1%)
    ppermute x9, waiting for transfers between devices, ring_gather(): block = lax.ppermute(block, axis, ring(axis))  168 us
    ppermute x15, waiting for transfers between devices, ring_scatter(): moved = lax.ppermute(state.astype(BF), axis, ring(axis))  138 us
    reduce_scatter x1, waiting for transfers between devices, body(): lax.psum_scatter(y_part, 'seq', scatter_dimension=0, tiled=True).astype(F32)  116 us
    pallas_call x1, Pallas kernels, attend_back(): pl.pallas_call(functools.partial(backward_kernel, group), out_shape=(jax....  94.5 us
    reduce_scatter x1, waiting for transfers between devices, body(): lax.psum_scatter(dn2_part.astype(BF), 'seq', scatter_dimension=0, tiled=T...  91.6 us
    all_to_all x2, blocking collectives, exchange(): return lax.all_to_all(array, 'seq', split_axis=0, concat_axis=0, tiled=True)  84 us
    pallas_call x1, Pallas kernels, attend(): pl.pallas_call(functools.partial(forward_kernel, group), out_shape=(jax.S...  70.9 us
    all_gather x1, blocking collectives, body(): lax.all_gather(jnp.stack([gain_attn, gain_ffn]), both, axis=1, tiled=True)  69.3 us
  transfers between devices with their start and end apart: 36, of which 25 were waited for; matrix products, arithmetic and copies ran while one was open for 20% of the time, Pallas kernels for 12%

profile of v1, /device:TPU:0, one launch (start us, length us, event | category | flops | bytes accessed | tf_op | source)
XLA Modules:
  0.0 1335.3 jit_solution(16952722137385291577)
XLA Ops:
  8.1 69.3 %all-gather.2 = bf16[32,64,2]{1,2,0:T(2,128)(2,1)S(1)} all-gather(bf16[1,64,2]{1,2,0:T(2,128)(2,1)S(1)} %maximum_bitcast_fusion.3), channel_id=1, replica_groups=mesh['seq'=8,'fsdp'=4] {'seq','fsdp'}, dimensions={0}, use_global_device_ids=true | all-gather | bytes 8448 | tf_op jit(solution)/shard_map/all_gather | solution.py:279
  87.7 15.5 %all-gather = s32[1,4096]{1,0:T(1,128)S(1)} all-gather(s32[1,512]{1,0:T(1,128)S(1)} %copy-done.48), channel_id=2, replica_groups=mesh['seq'=8,'fsdp'=4] {'seq'}, dimensions={1}, use_global_device_ids=true | all-gather | bytes 18432 | tf_op jit(solution)/shard_map/all_gather | solution.py:281
  112.8 5.7 collective-permute-done
  125.8 5.4 collective-permute-done.1
  135.0 8.0 collective-permute-done.2
  143.9 26.1 %all-gather.8.cloned.1.call-done = bf16[4096,2048]{1,0:T(8,128)(2,1)} async-done(((bf16[512,2048]{1,0:T(8,128)(2,1)}), bf16[4096,2048]{1,0:T(8,128)(2,1)}) %all-gather.8.cloned.1.call-update) | async-done | bytes 16777232 | tf_op jit(solution)/shard_map/all_gather | solution.py:285
  169.9 10.8 fusion.86
  198.9 70.9 %attend.1 = (bf16[8,256,512]{2,1,0:T(8,128)(2,1)}, f32[16,1,1024]{2,1,0:T(1,128)}) custom-call(s32[16,4]{1,0:T(8,128)} %pad_add_fusion.bounds_ref, bf16[256,4096]{1,0:T(8,128)(2,1)} %bitcast.278, bf16[4096,64]{1,0:T(8,128)(2,1)} %copy.166.k_ref, bf16[64,4096]{1,0:T(8,128)(2,1)} %copy.167.vt_ref, s32[16,1,1024]{2,1,0:T(1,128)} %tile.8.start_ref), custom_call_target="tpu_custom_call" | custom-call | flops 8589934592 | bytes 8388608 | tf_op jit(solution)/shard_map/attend/pallas_call | solution.py:127
  274.3 26.6 %all-to-all-done.1 = bf16[8,256,512]{2,1,0:T(8,128)(2,1)} async-done(((bf16[8,256,512]{2,1,0:T(8,128)(2,1)}), bf16[8,256,512]{2,1,0:T(8,128)(2,1)}, u32[]{:S(2)}, u32[]{:S(2)}) %all-to-all-start.1) | async-done | bytes 2097184 | tf_op jit(solution)/shard_map/all_to_all | solution.py:237
  300.9 7.8 multiply_reduce_fusion.1
  316.5 38.5 %all_to_all.30 = bf16[8,128,704]{1,2,0:T(8,128)(2,1)} all-to-all(bf16[8,128,704]{1,2,0:T(8,128)(2,1)S(1)} %copy.168), channel_id=1, replica_groups=mesh['seq'=8,'fsdp'=4] {'seq'}, dimensions={0} | all-to-all | bytes 2883584 | tf_op jit(solution)/shard_map/all_to_all | solution.py:237
  356.8 39.0 %collective-permute-done.3 = bf16[8,2,64,704]{3,2,1,0:T(8,128)(2,1)S(1)} collective-permute-done((bf16[8,2,64,704]{3,2,1,0:T(8,128)(2,1)S(1)}, bf16[8,2,64,704]{3,2,1,0:T(8,128)(2,1)S(1)}, u32[]{:S(2)}, u32[]{:S(2)}) %collective-permute-start.3) | collective-permute-done | bytes 1441824 | tf_op jit(solution)/shard_map/ppermute | solution.py:214
  395.9 15.4 %collective-permute-done.6 = bf16[176,2048]{1,0:T(8,128)(2,1)S(1)} collective-permute-done((bf16[176,2048]{1,0:T(8,128)(2,1)}, bf16[176,2048]{1,0:T(8,128)(2,1)S(1)}, u32[]{:S(2)}, u32[]{:S(2)}) %collective-permute-start.6) | collective-permute-done | bytes 720928 | tf_op jit(solution)/shard_map/ppermute | solution.py:214
  411.9 46.2 %collective-permute-done.7 = bf16[176,2048]{1,0:T(8,128)(2,1)S(1)} collective-permute-done((bf16[176,2048]{1,0:T(8,128)(2,1)S(1)}, bf16[176,2048]{1,0:T(8,128)(2,1)S(1)}, u32[]{:S(2)}, u32[]{:S(2)}) %collective-permute-start.7) | collective-permute-done | bytes 720928 | tf_op jit(solution)/shard_map/ppermute | solution.py:214
  459.2 19.7 %collective-permute-done.8 = bf16[176,2048]{1,0:T(8,128)(2,1)S(1)} collective-permute-done((bf16[176,2048]{1,0:T(8,128)(2,1)S(1)}, bf16[176,2048]{1,0:T(8,128)(2,1)S(1)}, u32[]{:S(2)}, u32[]{:S(2)}) %collective-permute-start.8) | collective-permute-done | bytes 720928 | tf_op jit(solution)/shard_map/ppermute | solution.py:214
  480.6 28.7 %collective-permute-done.5 = bf16[8,2,64,704]{3,2,1,0:T(8,128)(2,1)S(1)} collective-permute-done((bf16[8,2,64,704]{3,2,1,0:T(8,128)(2,1)S(1)}, bf16[8,2,64,704]{3,2,1,0:T(8,128)(2,1)S(1)}, u32[]{:S(2)}, u32[]{:S(2)}) %collective-permute-start.5) | collective-permute-done | bytes 1441824 | tf_op jit(solution)/shard_map/ppermute | solution.py:214
  511.7 18.3 %fusion.88 = f32[4096,704]{0,1:T(8,128)} fusion(bf16[4096,2048]{1,0:T(8,128)(2,1)} %all-gather.12.cloned.1.call-done, bf16[2048,704]{1,0:T(8,128)(2,1)S(1)} %bitcast.268), kind=kOutput, calls=%fused_computation.210 | convolution fusion | flops 11811160064 | bytes 31195136 | tf_op jit(solution)/shard_map/dot_general | solution.py:25
  530.1 19.3 %fusion.87 = f32[4096,704]{0,1:T(8,128)} fusion(bf16[4096,2048]{1,0:T(8,128)(2,1)} %all-gather.12.cloned.1.call-done, bf16[2048,704]{1,0:T(8,128)(2,1)} %bitcast.270), kind=kOutput, calls=%fused_computation.209 | convolution fusion | flops 11811160064 | bytes 31195136 | tf_op jit(solution)/shard_map/dot_general | solution.py:25
  549.4 26.8 %fusion.7 = (bf16[4096,704]{0,1:T(8,128)(2,1)}, bf16[4096,704]{0,1:T(8,128)(2,1)}, bf16[4096,704]{0,1:T(8,128)(2,1)}) fusion(f32[4096,704]{0,1:T(8,128)} %fusion.87, f32[4096,704]{0,1:T(8,128)} %fusion.88, bf16[704,2048]{1,0:T(8,128)(2,1)} %bitcast.272, bf16[1,4096,2048]{2,1,0:T(8,128)(2,1)} %all-gather.14.cloned.1.call-done), kind=kOutput, calls=%fused_computation.12 | convolution fusion | flops 11854413824 | bytes 60030976 | tf_op jit(solution)/shard_map/td,fd->tf/dot_general | solution.py:344
  576.2 22.8 %fusion.89 = f32[4096,2048]{1,0:T(8,128)} fusion(bf16[4096,704]{0,1:T(8,128)(2,1)} %get-tuple-element.24, bf16[2048,704]{1,0:T(8,128)(2,1)} %bitcast.271), kind=kOutput, calls=%fused_computation.211 | convolution fusion | flops 11811160064 | bytes 42205184 | tf_op jit(solution)/shard_map/tf,df->td/dot_general | solution.py:347
  599.0 23.5 %add_convert_fusion = bf16[4096,2048]{1,0:T(8,128)(2,1)} fusion(f32[4096,2048]{1,0:T(8,128)} %fusion.89, bf16[4096,704]{0,1:T(8,128)(2,1)} %get-tuple-element.23, bf16[2048,704]{1,0:T(8,128)(2,1)S(1)} %bitcast.269), kind=kOutput, calls=%fused_computation | convolution fusion | flops 11827937280 | bytes 58982400 | tf_op jit(solution)/shard_map/tf,df->td/dot_general | solution.py:347
  624.4 19.6 %convolution_convert_fusion.1 = bf16[4096,2048]{1,0:T(8,128)(2,1)} fusion(bf16[4096,704]{0,1:T(8,128)(2,1)} %get-tuple-element.25, bf16[704,2048]{1,0:T(8,128)(2,1)S(1)} %bitcast.273), kind=kOutput, calls=%fused_computation.6 | convolution fusion | flops 11819548672 | bytes 25427968 | tf_op jit(solution)/shard_map/dot_general | solution.py:25
  644.0 91.6 %reduce-scatter.7.cloned.1.call-done = bf16[512,2048]{1,0:T(8,128)(2,1)} async-done(((bf16[4096,2048]{1,0:T(8,128)(2,1)}), bf16[512,2048]{1,0:T(8,128)(2,1)}) %reduce-scatter.7.cloned.1.call-update) | async-done | bytes 2097168 | tf_op jit(solution)/shard_map/reduce_scatter | solution.py:350
  739.2 115.8 %reduce-scatter.5.cloned.1.call-done = bf16[512,2048]{1,0:T(8,128)(2,1)} async-done(((bf16[4096,2048]{1,0:T(8,128)(2,1)}), bf16[512,2048]{1,0:T(8,128)(2,1)}) %reduce-scatter.5.cloned.1.call-update) | async-done | bytes 2097168 | tf_op jit(solution)/shard_map/reduce_scatter | solution.py:352
  855.1 5.4 convert_add_fusion.1
  862.4 8.4 convolution_convert_fusion.2
  870.9 10.5 fusion.19
  884.4 45.5 %all_to_all.31.do_ref = bf16[8,256,512]{2,1,0:T(8,128)(2,1)} all-to-all(bf16[8,256,512]{2,1,0:T(8,128)(2,1)S(1)} %bitcast.251), channel_id=1, replica_groups=mesh['seq'=8,'fsdp'=4] {'seq'}, dimensions={0} | all-to-all | bytes 4194304 | tf_op jit(solution)/shard_map/all_to_all | solution.py:237
  930.0 94.5 %attend_back.1 = (f32[256,4096]{1,0:T(8,128)}, f32[4096,64]{1,0:T(8,128)}, f32[4096,64]{1,0:T(8,128)}) custom-call(s32[16,4]{1,0:T(8,128)} %pad_add_fusion.bounds_ref, bf16[256,4096]{1,0:T(8,128)(2,1)} %bitcast.279, bf16[4096,64]{1,0:T(8,128)(2,1)} %copy.166.k_ref, bf16[64,4096]{1,0:T(8,128)(2,1)} %get-tuple-element.40.kt_ref, bf16[4096,64]{1,0:T(8,128)(2,1)} %bitcast.267, ...), custom_call_target="tpu_custom_call" | custom-call | flops 21474836480 | bytes 16777216 | tf_op jit(solution)/shard_map/attend_back/pallas_call | solution.py:169
  1036.1 13.9 %convolution_convert_fusion = bf16[4096,2048]{1,0:T(8,128)(2,1)} fusion(bf16[384,2048]{0,1:T(8,128)(2,1)} %bitcast.11, bf16[64,4096]{1,0:T(8,128)(2,1)S(1)} %copy.178, bf16[64,4096]{1,0:T(8,128)(2,1)S(1)} %maximum_bitcast_fusion.1, bf16[256,4096]{1,0:T(8,128)(2,1)S(1)} %bitcast.280), kind=kOutput, calls=%fused_computation.5 | convolution fusion | flops 6460276736 | bytes 21495808 | tf_op jit(solution)/shard_map/et,ed->td/dot_general | solution.py:388
  1050.1 19.2 %fusion.90 = f32[2048,704]{1,0:T(8,128)S(1)} fusion(bf16[4096,2048]{1,0:T(8,128)(2,1)} %all-gather.12.cloned.1.call-done, bf16[4096,704]{0,1:T(8,128)(2,1)} %get-tuple-element.24), kind=kOutput, calls=%fused_computation.212 | convolution fusion | flops 11811160064 | bytes 28311552 | tf_op jit(solution)/shard_map/td,tf->df/dot_general | solution.py:358
  1069.4 20.6 %fusion.91 = f32[2048,704]{1,0:T(8,128)S(1)} fusion(bf16[4096,2048]{1,0:T(8,128)(2,1)} %all-gather.12.cloned.1.call-done, bf16[4096,704]{0,1:T(8,128)(2,1)} %get-tuple-element.23), kind=kOutput, calls=%fused_computation.213 | convolution fusion | flops 11811160064 | bytes 28311552 | tf_op jit(solution)/shard_map/td,tf->df/dot_general | solution.py:359
  1090.2 19.0 %fusion = f32[704,2048]{1,0:T(8,128)S(1)} fusion(bf16[4096,704]{0,1:T(8,128)(2,1)} %get-tuple-element.25, bf16[1,4096,2048]{2,1,0:T(8,128)(2,1)} %all-gather.14.cloned.1.call-done), kind=kOutput, calls=%fused_computation.1 | convolution fusion | flops 11811160064 | bytes 28311552 | tf_op jit(solution)/shard_map/tf,td->fd/dot_general | solution.py:360
  1119.9 13.9 %collective-permute-done.21 = bf16[176,2048]{1,0:T(8,128)(2,1)} collective-permute-done((bf16[176,2048]{1,0:T(8,128)(2,1)}, bf16[176,2048]{1,0:T(8,128)(2,1)}, u32[]{:S(2)}, u32[]{:S(2)}) %collective-permute-start.21) | collective-permute-done | bytes 720928 | tf_op jit(solution)/shard_map/ppermute | solution.py:231
  1136.3 14.2 %collective-permute-done.16 = bf16[8,64,704]{2,1,0:T(8,128)(2,1)S(1)} collective-permute-done((bf16[8,64,704]{2,1,0:T(8,128)(2,1)S(1)}, bf16[8,64,704]{2,1,0:T(8,128)(2,1)S(1)}, u32[]{:S(2)}, u32[]{:S(2)}) %collective-permute-start.16) | collective-permute-done | bytes 720928 | tf_op jit(solution)/shard_map/ppermute | solution.py:231
  1152.3 15.1 %collective-permute-done.19 = bf16[8,64,704]{2,1,0:T(8,128)(2,1)} collective-permute-done((bf16[8,64,704]{2,1,0:T(8,128)(2,1)S(1)}, bf16[8,64,704]{2,1,0:T(8,128)(2,1)}, u32[]{:S(2)}, u32[]{:S(2)}) %collective-permute-start.19) | collective-permute-done | bytes 720928 | tf_op jit(solution)/shard_map/ppermute | solution.py:231
  1169.3 13.6 %collective-permute-done.22 = bf16[176,2048]{1,0:T(8,128)(2,1)} collective-permute-done((bf16[176,2048]{1,0:T(8,128)(2,1)}, bf16[176,2048]{1,0:T(8,128)(2,1)}, u32[]{:S(2)}, u32[]{:S(2)}) %collective-permute-start.22) | collective-permute-done | bytes 720928 | tf_op jit(solution)/shard_map/ppermute | solution.py:231
  1184.7 15.0 %collective-permute-done.17 = bf16[8,64,704]{2,1,0:T(8,128)(2,1)S(1)} collective-permute-done((bf16[8,64,704]{2,1,0:T(8,128)(2,1)S(1)}, bf16[8,64,704]{2,1,0:T(8,128)(2,1)S(1)}, u32[]{:S(2)}, u32[]{:S(2)}) %collective-permute-start.17) | collective-permute-done | bytes 720928 | tf_op jit(solution)/shard_map/ppermute | solution.py:231
  1201.2 15.2 %collective-permute-done.20 = bf16[8,64,704]{2,1,0:T(8,128)(2,1)S(1)} collective-permute-done((bf16[8,64,704]{2,1,0:T(8,128)(2,1)S(1)}, bf16[8,64,704]{2,1,0:T(8,128)(2,1)S(1)}, u32[]{:S(2)}, u32[]{:S(2)}) %collective-permute-start.20) | collective-permute-done | bytes 720928 | tf_op jit(solution)/shard_map/ppermute | solution.py:231
  1223.6 13.2 fusion.29
  1237.0 13.2 collective-permute-done.9
  1253.4 9.5 collective-permute-done.10
  1272.0 4.9 collective-permute-done.11
  1284.3 6.4 all-to-all-done.4
  1291.9 8.1 collective-permute-done.12
  1302.0 7.3 collective-permute-done.13
  1311.3 7.5 collective-permute-done.14
  1323.5 4.8 fusion.17
  (277 shorter events, 149.4 us)
Async XLA Ops:
  7.2 73.0 %copy-start.1 = (bf16[1,512,2048]{2,1,0:T(8,128)(2,1)S(1)}, bf16[1,512,2048]{2,1,0:T(8,128)(2,1)}, u32[]{:S(2)}) copy-start(bf16[1,512,2048]{2,1,0:T(8,128)(2,1)} %param.12) | copy-start | bytes 6291460
  7.2 162.7 %all-gather.8.cloned.1.call-start = ((), (), s32[]{:S(2)}) async-start(), calls=%async_computation.10 | async-start | bytes 18874368 | tf_op jit(solution)/shard_map/all_gather | solution.py:285
  82.1 192.2 %all-gather.10.cloned.1.call-start = ((), (), s32[]{:S(2)}) async-start(), calls=%async_computation.11 | async-start | bytes 8650752 | tf_op jit(solution)/shard_map/all_gather | solution.py:331
  84.2 20.6 %all-to-all-start = ((bf16[8,384,64]{1,2,0:T(8,128)(2,1)}), bf16[8,384,64]{1,2,0:T(8,128)(2,1)S(1)}, u32[]{:S(2)}, u32[]{:S(2)}) async-start(bf16[8,384,64]{1,2,0:T(8,128)(2,1)} %copy.161), calls=%async_computation | async-start | bytes 786432 | tf_op jit(solution)/shard_map/all_to_all | solution.py:237
  104.8 79.1 %copy-start.27 = (f32[4096]{0:T(1024)}, f32[4096]{0:T(1024)S(1)}, u32[]{:S(2)}) copy-start(f32[4096]{0:T(1024)S(1)} %fusion.62) | copy-start | bytes 49156
  105.3 13.2 collective-permute-start
  108.6 85.8 %copy-start.10 = (f32[32,4096]{1,0:T(8,128)}, f32[32,4096]{1,0:T(8,128)S(1)}, u32[]{:S(2)}) copy-start(f32[32,4096]{1,0:T(8,128)S(1)} %get-tuple-element.46) | copy-start | bytes 1572868
  118.5 12.7 collective-permute-start.1
  131.2 11.9 collective-permute-start.2
  269.9 31.0 %all-to-all-start.1 = ((bf16[8,256,512]{2,1,0:T(8,128)(2,1)}), bf16[8,256,512]{2,1,0:T(8,128)(2,1)}, u32[]{:S(2)}, u32[]{:S(2)}) async-start(bf16[8,256,512]{2,1,0:T(8,128)(2,1)} %get-tuple-element.16.o_ref), calls=%async_computation.1 | async-start | bytes 4194304 | tf_op jit(solution)/shard_map/all_to_all | solution.py:237
  274.2 237.5 %all-gather.12.cloned.1.call-start = ((), (), s32[]{:S(2)}) async-start(), calls=%async_computation.12 | async-start | bytes 18874368 | tf_op jit(solution)/shard_map/all_gather | solution.py:335
  312.4 236.9 %all-gather.14.cloned.1.call-start = ((), (), s32[]{:S(2)}) async-start(), calls=%async_computation.17 | async-start | bytes 18874368 | tf_op jit(solution)/shard_map/all_gather | solution.py:337
  313.0 422.6 %reduce-scatter.7.cloned.1.call-start = ((), (), s32[]{:S(2)}) async-start(), calls=%async_computation.14 | async-start | bytes 18874368 | tf_op jit(solution)/shard_map/reduce_scatter | solution.py:350
  354.9 56.8 %copy-start.23 = (bf16[176,2048]{1,0:T(8,128)(2,1)S(1)}, bf16[176,2048]{1,0:T(8,128)(2,1)}, u32[]{:S(2)}) copy-start(bf16[176,2048]{1,0:T(8,128)(2,1)} %param.22) | copy-start | bytes 2162692
  356.7 39.2 %collective-permute-start.3 = (bf16[8,2,64,704]{3,2,1,0:T(8,128)(2,1)S(1)}, bf16[8,2,64,704]{3,2,1,0:T(8,128)(2,1)S(1)}, u32[]{:S(2)}, u32[]{:S(2)}) collective-permute-start(bf16[8,2,64,704]{3,2,1,0:T(8,128)(2,1)S(1)} %bitcast.252), channel_id=1, source_target_pairs={{0,1},{1,2},{2,3},{3,0},{4,5},{5,6},{6,7},{7,4},{8,9},{9,10},{10,1... | collective-permute-start | bytes 4325384 | tf_op jit(solution)/shard_map/ppermute | solution.py:214
  356.8 54.6 %collective-permute-start.6 = (bf16[176,2048]{1,0:T(8,128)(2,1)}, bf16[176,2048]{1,0:T(8,128)(2,1)S(1)}, u32[]{:S(2)}, u32[]{:S(2)}) collective-permute-start(bf16[176,2048]{1,0:T(8,128)(2,1)} %param.22), channel_id=1, source_target_pairs={{0,1},{1,2},{2,3},{3,0},{4,5},{5,6},{6,7},{7,4},{8,9},{9,10},{10,1... | collective-permute-start | bytes 2162696 | tf_op jit(solution)/shard_map/ppermute | solution.py:214
  395.9 63.1 %collective-permute-start.4 = (bf16[8,2,64,704]{3,2,1,0:T(8,128)(2,1)S(1)}, bf16[8,2,64,704]{3,2,1,0:T(8,128)(2,1)S(1)}, u32[]{:S(2)}, u32[]{:S(2)}) collective-permute-start(bf16[8,2,64,704]{3,2,1,0:T(8,128)(2,1)S(1)} %collective-permute-done.3), channel_id=1, source_target_pairs={{0,1},{1,2},{2,3},{3,0},{4,5},{5,6},{6,7},{7,4},{8,9},{9,10},{10,1... | collective-permute-start | bytes 4325384 | tf_op jit(solution)/shard_map/ppermute | solution.py:214
  411.3 46.7 %collective-permute-start.7 = (bf16[176,2048]{1,0:T(8,128)(2,1)S(1)}, bf16[176,2048]{1,0:T(8,128)(2,1)S(1)}, u32[]{:S(2)}, u32[]{:S(2)}) collective-permute-start(bf16[176,2048]{1,0:T(8,128)(2,1)S(1)} %collective-permute-done.6), channel_id=1, source_target_pairs={{0,1},{1,2},{2,3},{3,0},{4,5},{5,6},{6,7},{7,4},{8,9},{9,10},{10,1... | collective-permute-start | bytes 2162696 | tf_op jit(solution)/shard_map/ppermute | solution.py:214
  458.1 20.9 %collective-permute-start.8 = (bf16[176,2048]{1,0:T(8,128)(2,1)S(1)}, bf16[176,2048]{1,0:T(8,128)(2,1)S(1)}, u32[]{:S(2)}, u32[]{:S(2)}) collective-permute-start(bf16[176,2048]{1,0:T(8,128)(2,1)S(1)} %collective-permute-done.7), channel_id=1, source_target_pairs={{0,1},{1,2},{2,3},{3,0},{4,5},{5,6},{6,7},{7,4},{8,9},{9,10},{10,1... | collective-permute-start | bytes 2162696 | tf_op jit(solution)/shard_map/ppermute | solution.py:214
  459.0 50.2 %collective-permute-start.5 = (bf16[8,2,64,704]{3,2,1,0:T(8,128)(2,1)S(1)}, bf16[8,2,64,704]{3,2,1,0:T(8,128)(2,1)S(1)}, u32[]{:S(2)}, u32[]{:S(2)}) collective-permute-start(bf16[8,2,64,704]{3,2,1,0:T(8,128)(2,1)S(1)} %collective-permute-done.4), channel_id=1, source_target_pairs={{0,1},{1,2},{2,3},{3,0},{4,5},{5,6},{6,7},{7,4},{8,9},{9,10},{10,1... | collective-permute-start | bytes 4325384 | tf_op jit(solution)/shard_map/ppermute | solution.py:214
  622.6 232.5 %reduce-scatter.5.cloned.1.call-start = ((), (), s32[]{:S(2)}) async-start(), calls=%async_computation.13 | async-start | bytes 18874368 | tf_op jit(solution)/shard_map/reduce_scatter | solution.py:352
  643.9 91.7 %copy-start.36 = (f32[1,2048]{1,0:T(1,128)S(1)}, f32[1,2048]{1,0:T(1,128)}, u32[]{:S(2)}) copy-start(f32[1,2048]{1,0:T(1,128)} %get-tuple-element.48) | copy-start | bytes 24580
  643.9 91.7 %copy-start.44 = (f32[512]{0:T(512)S(1)}, f32[512]{0:T(512)}, u32[]{:S(2)}) copy-start(f32[512]{0:T(512)} %copy-done.43) | copy-start | bytes 6148
  644.0 211.1 %copy-start.5 = (bf16[1,512,2048]{2,1,0:T(8,128)(2,1)S(1)}, bf16[1,512,2048]{2,1,0:T(8,128)(2,1)}, u32[]{:S(2)}) copy-start(bf16[1,512,2048]{2,1,0:T(8,128)(2,1)} %param.23) | copy-start | bytes 6291460
  644.0 646.8 %reduce-scatter.11.cloned.1.call-start = ((), (), s32[]{:S(2)}) async-start(), calls=%async_computation.16 | async-start | bytes 9437184 | tf_op jit(solution)/shard_map/reduce_scatter | solution.py:372
  870.8 449.8 %reduce-scatter.9.cloned.1.call-start = ((), (), s32[]{:S(2)}) async-start(), calls=%async_computation.15 | async-start | bytes 18874368 | tf_op jit(solution)/shard_map/reduce_scatter | solution.py:389
  1069.3 43.2 %collective-permute-start.15 = (bf16[8,64,704]{2,1,0:T(8,128)(2,1)S(1)}, bf16[8,64,704]{2,1,0:T(8,128)(2,1)}, u32[]{:S(2)}, u32[]{:S(2)}) collective-permute-start(bf16[8,64,704]{2,1,0:T(8,128)(2,1)S(1)} %fusion.32), channel_id=1, source_target_pairs={{0,1},{1,2},{2,3},{3,0},{4,5},{5,6},{6,7},{7,4},{8,9},{9,10},{10,1... | collective-permute-start | bytes 2162696 | tf_op jit(solution)/shard_map/ppermute | solution.py:231
  1090.1 25.5 %collective-permute-start.18 = (bf16[8,64,704]{2,1,0:T(8,128)(2,1)S(1)}, bf16[8,64,704]{2,1,0:T(8,128)(2,1)}, u32[]{:S(2)}, u32[]{:S(2)}) collective-permute-start(bf16[8,64,704]{2,1,0:T(8,128)(2,1)S(1)} %fusion.35), channel_id=1, source_target_pairs={{0,1},{1,2},{2,3},{3,0},{4,5},{5,6},{6,7},{7,4},{8,9},{9,10},{10,1... | collective-permute-start | bytes 2162696 | tf_op jit(solution)/shard_map/ppermute | solution.py:231
  1112.5 21.2 %collective-permute-start.21 = (bf16[176,2048]{1,0:T(8,128)(2,1)}, bf16[176,2048]{1,0:T(8,128)(2,1)}, u32[]{:S(2)}, u32[]{:S(2)}) collective-permute-start(bf16[176,2048]{1,0:T(8,128)(2,1)} %fusion.46), channel_id=1, source_target_pairs={{0,1},{1,2},{2,3},{3,0},{4,5},{5,6},{6,7},{7,4},{8,9},{9,10},{10,1... | collective-permute-start | bytes 2162696 | tf_op jit(solution)/shard_map/ppermute | solution.py:231
  1114.3 36.1 %collective-permute-start.16 = (bf16[8,64,704]{2,1,0:T(8,128)(2,1)S(1)}, bf16[8,64,704]{2,1,0:T(8,128)(2,1)S(1)}, u32[]{:S(2)}, u32[]{:S(2)}) collective-permute-start(bf16[8,64,704]{2,1,0:T(8,128)(2,1)S(1)} %fusion.26), channel_id=1, source_target_pairs={{0,1},{1,2},{2,3},{3,0},{4,5},{5,6},{6,7},{7,4},{8,9},{9,10},{10,1... | collective-permute-start | bytes 2162696 | tf_op jit(solution)/shard_map/ppermute | solution.py:231
  1117.4 50.0 %collective-permute-start.19 = (bf16[8,64,704]{2,1,0:T(8,128)(2,1)S(1)}, bf16[8,64,704]{2,1,0:T(8,128)(2,1)}, u32[]{:S(2)}, u32[]{:S(2)}) collective-permute-start(bf16[8,64,704]{2,1,0:T(8,128)(2,1)S(1)} %fusion.23), channel_id=1, source_target_pairs={{0,1},{1,2},{2,3},{3,0},{4,5},{5,6},{6,7},{7,4},{8,9},{9,10},{10,1... | collective-permute-start | bytes 2162696 | tf_op jit(solution)/shard_map/ppermute | solution.py:231
  1136.3 46.6 %collective-permute-start.22 = (bf16[176,2048]{1,0:T(8,128)(2,1)}, bf16[176,2048]{1,0:T(8,128)(2,1)}, u32[]{:S(2)}, u32[]{:S(2)}) collective-permute-start(bf16[176,2048]{1,0:T(8,128)(2,1)} %fusion.28), channel_id=1, source_target_pairs={{0,1},{1,2},{2,3},{3,0},{4,5},{5,6},{6,7},{7,4},{8,9},{9,10},{10,1... | collective-permute-start | bytes 2162696 | tf_op jit(solution)/shard_map/ppermute | solution.py:231
  1152.2 47.4 %collective-permute-start.17 = (bf16[8,64,704]{2,1,0:T(8,128)(2,1)S(1)}, bf16[8,64,704]{2,1,0:T(8,128)(2,1)S(1)}, u32[]{:S(2)}, u32[]{:S(2)}) collective-permute-start(bf16[8,64,704]{2,1,0:T(8,128)(2,1)S(1)} %fusion.25), channel_id=1, source_target_pairs={{0,1},{1,2},{2,3},{3,0},{4,5},{5,6},{6,7},{7,4},{8,9},{9,10},{10,1... | collective-permute-start | bytes 2162696 | tf_op jit(solution)/shard_map/ppermute | solution.py:231
  1169.2 47.3 %collective-permute-start.20 = (bf16[8,64,704]{2,1,0:T(8,128)(2,1)S(1)}, bf16[8,64,704]{2,1,0:T(8,128)(2,1)S(1)}, u32[]{:S(2)}, u32[]{:S(2)}) collective-permute-start(bf16[8,64,704]{2,1,0:T(8,128)(2,1)S(1)} %fusion.22), channel_id=1, source_target_pairs={{0,1},{1,2},{2,3},{3,0},{4,5},{5,6},{6,7},{7,4},{8,9},{9,10},{10,1... | collective-permute-start | bytes 2162696 | tf_op jit(solution)/shard_map/ppermute | solution.py:231
  1184.6 65.8 %collective-permute-start.23 = (bf16[176,2048]{1,0:T(8,128)(2,1)S(1)}, bf16[176,2048]{1,0:T(8,128)(2,1)S(1)}, u32[]{:S(2)}, u32[]{:S(2)}) collective-permute-start(bf16[176,2048]{1,0:T(8,128)(2,1)S(1)} %fusion.27), channel_id=1, source_target_pairs={{0,1},{1,2},{2,3},{3,0},{4,5},{5,6},{6,7},{7,4},{8,9},{9,10},{10,1... | collective-permute-start | bytes 2162696 | tf_op jit(solution)/shard_map/ppermute | solution.py:231
  1219.6 33.5 %all-to-all-start.5 = ((bf16[8,2,64,704]{3,2,1,0:T(8,128)(2,1)}), bf16[8,2,64,704]{3,2,1,0:T(8,128)(2,1)S(1)}, u32[]{:S(2)}, u32[]{:S(2)}) async-start(bf16[8,2,64,704]{3,2,1,0:T(8,128)(2,1)} %copy.185), calls=%async_computation.9 | async-start | bytes 3145728 | tf_op jit(solution)/shard_map/all_to_all | solution.py:237
  1236.9 13.3 collective-permute-start.9
  1250.3 12.6 collective-permute-start.10
  1265.0 11.9 collective-permute-start.11
  1278.9 11.7 all-to-all-start.4
  1291.7 8.2 collective-permute-start.12
  1291.9 28.7 %copy-start.2 = (bf16[1,512,2048]{2,1,0:T(8,128)(2,1)S(1)}, bf16[1,512,2048]{2,1,0:T(8,128)(2,1)}, u32[]{:S(2)}) copy-start(bf16[1,512,2048]{2,1,0:T(8,128)(2,1)} %param.12) | copy-start | bytes 6291460
  1291.9 28.7 %copy-start.34 = (f32[1,2048]{1,0:T(1,128)S(1)}, f32[1,2048]{1,0:T(1,128)}, u32[]{:S(2)}) copy-start(f32[1,2048]{1,0:T(1,128)} %copy-done.33) | copy-start | bytes 24580
  1291.9 28.7 %copy-start.42 = (f32[512]{0:T(512)S(1)}, f32[512]{0:T(512)}, u32[]{:S(2)}) copy-start(f32[512]{0:T(512)} %copy-done.41) | copy-start | bytes 6148
  1301.0 8.3 collective-permute-start.13
  1301.2 22.1 %copy-start.20 = (f32[8,8,8,256]{3,2,0,1:T(8,128)}, f32[8,8,8,256]{3,2,0,1:T(8,128)S(1)}, u32[]{:S(2)}) copy-start(f32[8,8,8,256]{3,2,0,1:T(8,128)S(1)} %copy.192) | copy-start | bytes 1572868
  1301.5 21.9 %copy-start.29 = (f32[64,256]{1,0:T(8,128)}, f32[64,256]{1,0:T(8,128)S(1)}, u32[]{:S(2)}) copy-start(f32[64,256]{1,0:T(8,128)S(1)} %reshape.561) | copy-start | bytes 196612
  1310.4 8.4 collective-permute-start.14
  (39 other events, 256.4 us)
Sparse Core Ops, SparseCore 0:
  82.2 87.6 all-gather.7
  172.9 77.4 all-gather.9
  312.6 98.8 all-gather.11
  413.2 89.8 all-gather.13
  622.7 112.8 reduce-scatter.6
  739.0 115.9 reduce-scatter.4
  870.9 86.5 reduce-scatter.10
  1050.2 112.1 reduce-scatter.8

commit v2 on v1

v2 whole, which is shorter than its diff:
```python
import functools
import math

import jax
import jax.numpy as jnp
from jax import lax
from jax.experimental import pallas as pl
from jax.experimental.pallas import tpu as pltpu
from jax.sharding import PartitionSpec as P

H = 32
KV = 4
HD = 64
HALF = HD // 2
EPS = 1e-05
NEG = -1e30
BQ = 256
BK = 512
BF = jnp.bfloat16
F32 = jnp.float32
VMEM_LIMIT = 56 * 1024 * 1024
MESH = pl.DeviceIdType.MESH


def dot_f32(a, b):
    return jnp.dot(a, b, preferred_element_type=F32)


def heads_wide(block, group):
    return jnp.concatenate([block[h * HD : (h + 1) * HD] for h in range(group)], axis=1)


def heads_tall(block, group):
    width = block.shape[1] // group
    return jnp.concatenate([block[:, h * width : (h + 1) * width] for h in range(group)], axis=0)


def allowed_block(step, block_keys, first_row, block_rows, wide, starts):
    key = step * block_keys + lax.broadcasted_iota(jnp.int32, (block_keys, 1), 0)
    row = first_row + (lax.broadcasted_iota(jnp.int32, (1, wide), 1) & (block_rows - 1))
    return (key <= row) & (key >= starts)


def three_loops(bounds_ref, index, body):
    low, first, second, high = (bounds_ref[index, n] for n in range(4))
    lax.fori_loop(low, first, lambda j, c: body(j, True), None)
    lax.fori_loop(first, second, lambda j, c: body(j, False), None)
    lax.fori_loop(second, high, lambda j, c: body(j, True), None)


def turned(block, cosine, sine):
    first, second = block[:HALF], block[HALF:]
    return jnp.concatenate(
        [first * cosine - second * sine, second * cosine + first * sine], axis=0
    )


def turned_back(block, cosine, sine):
    first, second = block[:HALF], block[HALF:]
    return jnp.concatenate(
        [first * cosine + second * sine, second * cosine - first * sine], axis=0
    )


def forward_kernel(
    group, bounds_ref, q_ref, kv_ref, cos_ref, sin_ref, start_ref,
    o_ref, lse_ref, qt_ref, kt_ref, kn_ref, vn_ref, vt, acc, top, total,
):
    i = pl.program_id(0)
    rows = q_ref.shape[1]
    wide = rows * group
    here = pl.ds(pl.multiple_of(i * rows, rows), rows)
    cosine, sine = cos_ref[:, here], sin_ref[:, here]

    @pl.when(i == 0)
    def _():
        for part in range(kv_ref.shape[1] // BK):
            at = pl.ds(part * BK, BK)
            k = turned(kv_ref[:HD, at], cos_ref[:, at], sin_ref[:, at]).astype(BF)
            v = kv_ref[HD:, at].astype(BF)
            kt_ref[:, at] = k
            vt[:, at] = v
            kn_ref[at, :] = k.T
            vn_ref[at, :] = v.T

    heads = [
        turned(q_ref[h * HD : (h + 1) * HD, :], cosine, sine).astype(BF) * BF(HD**-0.5)
        for h in range(group)
    ]
    qt_ref[...] = jnp.concatenate(heads, axis=0)
    q4 = jnp.concatenate(heads, axis=1)
    starts = start_ref[0]
    acc[...] = jnp.zeros_like(acc)
    top[...] = jnp.full_like(top, NEG)
    total[...] = jnp.zeros_like(total)

    def block(j, masked):
        at = pl.multiple_of(j * BK, BK)
        s = dot_f32(kn_ref[pl.ds(at, BK), :], q4)
        if masked:
            s = jnp.where(allowed_block(j, BK, i * rows, rows, wide, starts), s, NEG)
        old = top[...]
        new = jnp.maximum(old, jnp.max(s, axis=0, keepdims=True))
        p = jnp.exp(s - new)
        keep = jnp.exp(old - new)
        top[...] = new
        total[...] = total[...] * keep + jnp.sum(p, axis=0, keepdims=True)
        acc[...] = acc[...] * keep + dot_f32(vt[:, pl.ds(at, BK)], p.astype(BF))

    three_loops(bounds_ref, i, block)
    o = acc[...] / total[...]
    o_ref[0] = heads_tall(o, group).astype(BF)
    lse_ref[0] = top[...] + jnp.log(total[...])


def backward_kernel(
    group, bounds_ref, q_ref, k_ref, kt_ref, v_ref, cos_ref, sin_ref, start_ref, o_ref, do_ref,
    lse_ref, dq_ref, dkv_ref, dk, dv, acc,
):
    i = pl.program_id(0)
    rows = q_ref.shape[1]
    wide = rows * group
    q4 = heads_wide(q_ref[...], group)
    g4 = heads_wide(do_ref[0], group)
    o4 = heads_wide(o_ref[0], group)
    delta = jnp.sum(g4.astype(F32) * o4.astype(F32), axis=0, keepdims=True)
    q4t = q4.T
    g4t = g4.T
    starts = start_ref[0]
    lse = lse_ref[0]
    acc[...] = jnp.zeros_like(acc)

    @pl.when(i == 0)
    def _():
        dk[...] = jnp.zeros_like(dk)
        dv[...] = jnp.zeros_like(dv)

    def block(j, masked):
        at = pl.multiple_of(j * BK, BK)
        s = dot_f32(k_ref[pl.ds(at, BK), :], q4)
        p = jnp.exp(s - lse)
        if masked:
            p = jnp.where(allowed_block(j, BK, i * rows, rows, wide, starts), p, 0.0)
        dp = dot_f32(v_ref[pl.ds(at, BK), :], g4)
        ds = (p * (dp - delta)).astype(BF)
        dv[pl.ds(at, BK), :] += dot_f32(p.astype(BF), g4t)
        dk[pl.ds(at, BK), :] += dot_f32(ds, q4t)
        acc[...] += dot_f32(kt_ref[:, pl.ds(at, BK)], ds)

    three_loops(bounds_ref, i, block)
    here = pl.ds(pl.multiple_of(i * rows, rows), rows)
    cosine, sine = cos_ref[:, here], sin_ref[:, here]
    for h in range(group):
        dq = acc[:, h * rows : (h + 1) * rows] * (HD**-0.5)
        dq_ref[h * HD : (h + 1) * HD, :] = turned_back(dq, cosine, sine).astype(BF)

    @pl.when(i == pl.num_programs(0) - 1)
    def _():
        for part in range(dk.shape[0] // BK):
            at = pl.ds(part * BK, BK)
            dk_t = turned_back(dk[at, :].T, cos_ref[:, at], sin_ref[:, at])
            dkv_ref[:HD, at] = dk_t.astype(BF)
            dkv_ref[HD:, at] = dv[at, :].T.astype(BF)


def whole_spec(shape):
    return pl.BlockSpec(shape, lambda i, b: (0,) * len(shape))


def attend(bounds, projected, cosine, sine, starts, group, senders, local):
    length = projected.shape[1]
    blocks = length // BQ
    per = local // BQ
    wide = group * HD
    piece = pl.BlockSpec((1, wide, BQ), lambda i, b: (i // per, 0, i % per))
    line = pl.BlockSpec((1, 1, group * BQ), lambda i, b: (i, 0, 0))
    flat = pl.BlockSpec((wide, BQ), lambda i, b: (0, i))
    return pl.pallas_call(
        functools.partial(forward_kernel, group),
        out_shape=(
            jax.ShapeDtypeStruct((senders, wide, local), BF),
            jax.ShapeDtypeStruct((blocks, 1, group * BQ), F32),
            jax.ShapeDtypeStruct((wide, length), BF),
            jax.ShapeDtypeStruct((HD, length), BF),
            jax.ShapeDtypeStruct((length, HD), BF),
            jax.ShapeDtypeStruct((length, HD), BF),
        ),
        grid_spec=pltpu.PrefetchScalarGridSpec(
            num_scalar_prefetch=1,
            grid=(blocks,),
            in_specs=[
                flat,
                pl.BlockSpec((2 * HD, length), lambda i, b: (wide // (2 * HD), 0)),
                whole_spec((HALF, length)),
                whole_spec((HALF, length)),
                line,
            ],
            out_specs=(
                piece,
                line,
                flat,
                whole_spec((HD, length)),
                whole_spec((length, HD)),
                whole_spec((length, HD)),
            ),
            scratch_shapes=[
                pltpu.VMEM((HD, length), BF),
                pltpu.VMEM((HD, group * BQ), F32),
                pltpu.VMEM((1, group * BQ), F32),
                pltpu.VMEM((1, group * BQ), F32),
            ],
        ),
        compiler_params=pltpu.CompilerParams(
            dimension_semantics=("arbitrary",), vmem_limit_bytes=VMEM_LIMIT
        ),
        cost_estimate=pl.CostEstimate(
            flops=40 * group * length * length * HD // 2,
            bytes_accessed=4 * group * length * HD * 2,
            transcendentals=group * length * length // 4,
        ),
        name="attend",
    )(bounds, projected, projected, cosine, sine, starts)


def attend_back(bounds, qt, k, kt, v, cosine, sine, starts, o, do, lse, group):
    length = k.shape[0]
    blocks = length // BQ
    senders, _, local = o.shape
    per = local // BQ
    piece = pl.BlockSpec((1, group * HD, BQ), lambda i, b: (i // per, 0, i % per))
    line = pl.BlockSpec((1, 1, group * BQ), lambda i, b: (i, 0, 0))
    flat = pl.BlockSpec((group * HD, BQ), lambda i, b: (0, i))
    return pl.pallas_call(
        functools.partial(backward_kernel, group),
        out_shape=(
            jax.ShapeDtypeStruct((group * HD, length), BF),
            jax.ShapeDtypeStruct((2 * HD, length), BF),
        ),
        grid_spec=pltpu.PrefetchScalarGridSpec(
            num_scalar_prefetch=1,
            grid=(blocks,),
            in_specs=[
                flat,
                whole_spec((length, HD)),
                whole_spec((HD, length)),
                whole_spec((length, HD)),
                whole_spec((HALF, length)),
                whole_spec((HALF, length)),
                line,
                piece,
                piece,
                line,
            ],
            out_specs=(flat, whole_spec((2 * HD, length))),
            scratch_shapes=[
                pltpu.VMEM((length, HD), F32),
                pltpu.VMEM((length, HD), F32),
                pltpu.VMEM((HD, group * BQ), F32),
            ],
        ),
        compiler_params=pltpu.CompilerParams(
            dimension_semantics=("arbitrary",), vmem_limit_bytes=VMEM_LIMIT
        ),
        cost_estimate=pl.CostEstimate(
            flops=50 * group * length * length * HD // 2,
            bytes_accessed=8 * group * length * HD,
            transcendentals=group * length * length // 4,
        ),
        name="attend_back",
    )(bounds, qt, k, kt, v, cosine, sine, starts, o, do, lse)


def project_kernel(cols, x_ref, w_ref, n_ref, p_ref, wt_ref):
    @pl.when(pl.program_id(0) == 0)
    def _():
        wt_ref[...] = w_ref[...].T

    wide = x_ref[0].astype(F32)
    scale = lax.rsqrt(jnp.mean(wide * wide, axis=-1, keepdims=True) + EPS)
    gain = wt_ref[pl.ds(cols, 8), :].astype(F32)[0:1]
    normed = (wide * scale * gain).astype(BF)
    n_ref[0] = normed
    p_ref[...] = lax.dot_general(
        wt_ref[:cols, :], normed, (((1,), (1,)), ((), ())), preferred_element_type=F32
    )


def project(x_all, w_ext, cols):
    count, local, width = x_all.shape
    wide = w_ext.shape[1]
    block = pl.BlockSpec((1, local, width), lambda i: (i, 0, 0))
    return pl.pallas_call(
        functools.partial(project_kernel, cols),
        out_shape=(
            jax.ShapeDtypeStruct(x_all.shape, BF),
            jax.ShapeDtypeStruct((cols, count * local), F32),
            jax.ShapeDtypeStruct((wide, width), BF),
        ),
        grid=(count,),
        in_specs=[block, pl.BlockSpec((width, wide), lambda i: (0, 0))],
        out_specs=(
            block,
            pl.BlockSpec((cols, local), lambda i: (0, i)),
            pl.BlockSpec((wide, width), lambda i: (0, 0)),
        ),
        compiler_params=pltpu.CompilerParams(
            dimension_semantics=("arbitrary",), vmem_limit_bytes=VMEM_LIMIT
        ),
        cost_estimate=pl.CostEstimate(
            flops=2 * cols * width * count * local,
            bytes_accessed=4 * width * count * local,
            transcendentals=0,
        ),
        name="project",
    )(x_all, w_ext)


def ffn_kernel(
    places_ref, first_ref, second_ref, dy_ref, gate_ref, up_ref, down_ref, *rest
):
    act_ref, dg_ref, du_ref, n_ref, y_ref, pa_ref, pb_ref = rest[-7:]
    which = pl.program_id(0)
    n = jnp.where(which == 0, first_ref[...], second_ref[...])
    n_ref[0] = n
    dy = dy_ref[0]
    across = (((1,), (1,)), ((), ()))
    gate = dot_f32(n, gate_ref[...])
    up = dot_f32(n, up_ref[...])
    d_act = lax.dot_general(dy, down_ref[...], across, preferred_element_type=F32)
    sig = jax.nn.sigmoid(gate)
    silu = gate * sig
    act = (silu * up).astype(BF)
    d_gate = (d_act * up * sig * (1.0 + gate * (1.0 - sig))).astype(BF)
    d_up = (d_act * silu).astype(BF)
    act_ref[0] = act
    dg_ref[0] = d_gate
    du_ref[0] = d_up
    y_ref[0] = dot_f32(act, down_ref[...]).astype(BF)
    part = lax.dot_general(d_gate, gate_ref[...], across, preferred_element_type=F32)
    part += lax.dot_general(d_up, up_ref[...], across, preferred_element_type=F32)
    part = part.astype(BF)

    @pl.when(which == 0)
    def _():
        pa_ref[...] = part

    @pl.when(which == 1)
    def _():
        pb_ref[...] = part


def ffn_chunk(places, first, second, dy_all, gate_w, up_w, down_w, kept):
    local, width = first.shape
    hidden = gate_w.shape[1]
    tall = min(512, local)
    tiles = local // tall
    count = dy_all.shape[0]

    def at_place(last):
        return pl.BlockSpec((1, tall, last), lambda i, t, p: (p[i], t, 0))

    ahead = pl.BlockSpec((tall, width), lambda i, t, p: (jnp.where(i == 0, t, tiles - 1), 0))
    behind = pl.BlockSpec((tall, width), lambda i, t, p: (jnp.where(i == 0, 0, t), 0))

    def held(shape):
        return pl.BlockSpec(shape, lambda i, t, p: (0, 0), pipeline_mode=pl.Buffered(1))

    in_specs = [
        ahead, behind, at_place(width), held((width, hidden)), held((width, hidden)),
        held((hidden, width)),
    ]
    arrays = [first, second, dy_all, gate_w, up_w, down_w]
    aliases = {}
    if kept is not None:
        in_specs += [pl.BlockSpec(memory_space=pl.ANY)] * 5
        arrays += list(kept)
        aliases = {7 + n: n for n in range(5)}
    narrow = jax.ShapeDtypeStruct((count, local, hidden), BF)
    broad = jax.ShapeDtypeStruct((count, local, width), BF)
    single = jax.ShapeDtypeStruct((local, width), BF)
    outs = pl.pallas_call(
        ffn_kernel,
        out_shape=(narrow, narrow, narrow, broad, broad, single, single),
        grid_spec=pltpu.PrefetchScalarGridSpec(
            num_scalar_prefetch=1,
            grid=(2, tiles),
            in_specs=in_specs,
            out_specs=(
                at_place(hidden), at_place(hidden), at_place(hidden), at_place(width),
                at_place(width), ahead, behind,
            ),
        ),
        input_output_aliases=aliases,
        compiler_params=pltpu.CompilerParams(
            dimension_semantics=("arbitrary", "arbitrary"), vmem_limit_bytes=VMEM_LIMIT
        ),
        cost_estimate=pl.CostEstimate(
            flops=2 * 6 * 2 * local * width * hidden,
            bytes_accessed=2 * (5 * 2 * local * width + 3 * width * hidden),
            transcendentals=2 * local * hidden,
        ),
        name="ffn",
    )(places, *arrays)
    return outs[:5], outs[5], outs[6]


def start_kernel(
    count, parts, x_ref, attn_ref, ffn_ref, x_all, attn_all, ffn_all, attn_mid, ffn_mid,
    send, arrive, local_sem,
):
    me = lax.axis_index("seq")
    z = lax.axis_index("fsdp")
    after_z, before_z = (z + 1) % parts, (z + parts - 1) % parts
    half = x_ref.shape[0] // 2
    barrier = pltpu.get_barrier_semaphore()
    for bit in (1, 2, 4):
        pl.semaphore_signal(barrier, inc=1, device_id=(me ^ bit, z), device_id_type=MESH)
    for other in (after_z, before_z):
        pl.semaphore_signal(barrier, inc=1, device_id=(me, other), device_id_type=MESH)
    pl.semaphore_wait(barrier, 5)
    made = {}

    def start(name, source, target, device):
        n = len(made)
        copy = pltpu.make_async_remote_copy(
            src_ref=source, dst_ref=target, send_sem=send.at[n], recv_sem=arrive.at[n],
            device_id=device, device_id_type=MESH,
        )
        made[name] = copy
        copy.start()

    def to_bit(name, bit, source, target):
        start(name, source, target, (me ^ bit, z))

    def arrived(*names):
        for name in names:
            made[name].wait_recv()

    held = [
        pltpu.make_async_copy(x_ref, x_all.at[me], local_sem.at[0]),
        pltpu.make_async_copy(attn_ref.at[me], attn_all.at[z, me], local_sem.at[1]),
        pltpu.make_async_copy(ffn_ref.at[me], ffn_all.at[z, me], local_sem.at[2]),
    ]
    for copy in held:
        copy.start()

    def swap_first(tag, source, final, mid):
        to_bit(tag + "b3", 2, source.at[me ^ 6], mid.at[4])
        to_bit(tag + "a2", 1, source.at[me ^ 3], mid.at[1])
        to_bit(tag + "a4", 1, source.at[me ^ 7], mid.at[3])
        to_bit(tag + "a3", 1, source.at[me ^ 5], mid.at[2])
        to_bit(tag + "a1", 1, source.at[me ^ 1], final.at[z, me])
        to_bit(tag + "b1", 2, source.at[me ^ 2], final.at[z, me])
        to_bit(tag + "c1", 4, source.at[me ^ 4], final.at[z, me])

    def swap_rest(tag, final, mid):
        arrived(tag + "a2", tag + "a4", tag + "a3")
        to_bit(tag + "b4", 2, mid.at[3], mid.at[5])
        to_bit(tag + "b2", 2, mid.at[1], final.at[z, me ^ 1])
        to_bit(tag + "c2", 4, mid.at[2], final.at[z, me ^ 1])
        arrived(tag + "b3")
        to_bit(tag + "c3", 4, mid.at[4], final.at[z, me ^ 2])
        arrived(tag + "b4")
        to_bit(tag + "c4", 4, mid.at[5], final.at[z, me ^ 3])

    def swap_end(tag):
        arrived(*[tag + n for n in ("a1", "b1", "c1", "b2", "c2", "c3", "c4")])

    swap_first("attn", attn_ref, attn_all, attn_mid)
    to_bit("x1", 1, x_ref, x_all.at[me])
    to_bit("x2", 2, x_ref, x_all.at[me])
    to_bit("x4", 4, x_ref, x_all.at[me])
    swap_rest("attn", attn_all, attn_mid)
    swap_first("ffn", ffn_ref, ffn_all, ffn_mid)
    swap_end("attn")
    held[1].wait()
    start("z1", attn_all.at[z], attn_all.at[z], (me, after_z))
    arrived("x2")
    to_bit("x3", 1, x_all.at[me ^ 2], x_all.at[me ^ 2])
    to_bit("f1", 4, x_all.at[me ^ 2, pl.ds(0, half)], x_all.at[me ^ 2, pl.ds(0, half)])
    arrived("x4")
    to_bit("x5", 1, x_all.at[me ^ 4], x_all.at[me ^ 4])
    to_bit("f2", 2, x_all.at[me ^ 4, pl.ds(half, half)], x_all.at[me ^ 4, pl.ds(half, half)])
    swap_rest("ffn", ffn_all, ffn_mid)
    for step in range(2, parts):
        arrived("z" + str(step - 1))
        at = (z + parts + 1 - step) % parts
        start("z" + str(step), attn_all.at[at], attn_all.at[at], (me, after_z))
    swap_end("ffn")
    held[2].wait()
    start("zffn", ffn_all.at[z], ffn_all.at[z], (me, after_z))
    arrived("f1", "f2")
    to_bit("x7", 1, x_all.at[me ^ 6], x_all.at[me ^ 6])
    arrived("x1", "x3", "x5", "x7", "z" + str(parts - 1), "zffn")
    for copy in made.values():
        copy.wait_send()
    held[0].wait()


def start_gather(x, attn_send, ffn_send, count, parts):
    anyspace = pl.BlockSpec(memory_space=pl.ANY)
    copies = 8 + 2 * 12 + parts
    shapes = (
        jax.ShapeDtypeStruct((count,) + x.shape, BF),
        jax.ShapeDtypeStruct((parts,) + attn_send.shape, BF),
        jax.ShapeDtypeStruct((parts,) + ffn_send.shape, BF),
        jax.ShapeDtypeStruct((6,) + attn_send.shape[1:], BF),
        jax.ShapeDtypeStruct((6,) + ffn_send.shape[1:], BF),
    )
    return pl.pallas_call(
        functools.partial(start_kernel, count, parts),
        out_shape=shapes,
        in_specs=[anyspace] * 3,
        out_specs=(anyspace,) * 5,
        scratch_shapes=[
            pltpu.SemaphoreType.DMA((copies,)),
            pltpu.SemaphoreType.DMA((copies,)),
            pltpu.SemaphoreType.DMA((3,)),
        ],
        compiler_params=pltpu.CompilerParams(
            collective_id=0, has_side_effects=True, vmem_limit_bytes=8 * 1024 * 1024
        ),
        name="start_gather",
    )(x, attn_send, ffn_send)[:3]


def ring(axis):
    count = lax.axis_size(axis)
    return [(n, (n + 1) % count) for n in range(count)]


def hop(*blocks):
    return [lax.ppermute(block, "fsdp", ring("fsdp")) for block in blocks]


def collect(pieces, axis):
    count = lax.axis_size(axis)
    me = lax.axis_index(axis)
    whole = jnp.zeros((count,) + pieces[0].shape, pieces[0].dtype)
    for back, piece in enumerate(pieces):
        whole = lax.dynamic_update_index_in_dim(whole, piece, (me + count - back) % count, 0)
    return whole


def term_of(terms, step):
    count = lax.axis_size("fsdp")
    me = lax.axis_index("fsdp")
    return lax.dynamic_index_in_dim(terms, (me + 2 * count - 1 - step) % count, 1, False)


def ring_step(states, terms, step):
    moved = hop(*[state.astype(BF) for state in states])
    return [m.astype(F32) + term_of(t, step).astype(F32) for m, t in zip(moved, terms)]


def ring_finish(states, terms, step):
    for n in range(step, lax.axis_size("fsdp")):
        states = ring_step(states, terms, n)
    return states


def fence(*values):
    return lax.optimization_barrier(values)


def swap(block, bit):
    count = lax.axis_size("seq")
    return lax.ppermute(block, "seq", [(n, n ^ bit) for n in range(count)])


def gather_plain(block):
    me = lax.axis_index("seq")
    whole = lax.all_gather(block, "seq", axis=0, tiled=False)
    return [lax.dynamic_index_in_dim(whole, me ^ c, 0, False) for c in range(whole.shape[0])]


def scatter_plain(parts):
    me = lax.axis_index("seq")
    whole = jnp.zeros((len(parts),) + parts[0].shape, BF)
    for c, part in enumerate(parts):
        whole = lax.dynamic_update_index_in_dim(whole, part.astype(BF), me ^ c, 0)
    return lax.psum_scatter(whole, "seq", scatter_dimension=0, tiled=False).astype(F32)


def far_halves(over_x, over_y):
    half = over_x.shape[0] // 2
    return swap(over_x[:half], 4), swap(over_y[half:], 2)


def chip_sum(own, other):
    return own.astype(F32) + swap(other, 1).astype(F32)


def exchange(array):
    return lax.all_to_all(array, "seq", split_axis=0, concat_axis=0, tiled=True)


def document_starts(flags_all):
    length = flags_all.shape[0]
    lanes = 128
    table = flags_all.reshape(length // lanes, lanes)
    place = jnp.arange(length, dtype=jnp.int32).reshape(table.shape)
    marked = jnp.where((table != 0) & (place > 0), place, 0)
    inside = jnp.arange(lanes)[None, :] <= jnp.arange(lanes)[:, None]
    local = jnp.max(jnp.where(inside[None], marked[:, None, :], 0), axis=-1)
    rows = jnp.max(marked, axis=1)
    count = length // lanes
    before = jnp.arange(count)[None, :] < jnp.arange(count)[:, None]
    carried = jnp.max(jnp.where(before, rows[None, :], 0), axis=-1)
    return jnp.maximum(local, carried[:, None]).reshape(length)


def body(
    tokens, doc_starts, gain_attn, w_query, w_key, w_value, w_out, gain_ffn, w_gate, w_up, w_down,
    cotangent,
):
    streams, local, width = tokens.shape
    assert streams == 1
    count = lax.axis_size("seq")
    parts = lax.axis_size("fsdp")
    me = lax.axis_index("seq")
    cube = count == 8
    length = local * count
    half = local // 2
    group = H // count
    share = (H // KV) // group
    rows = w_query.shape[0]
    hidden = w_gate.shape[1] // count
    group_width = group * HD
    attn_cols = group_width + 2 * HD
    flag_cols = local // rows
    extra_cols = 128
    sheet = (length, width)

    own = tokens[0]
    attn_send = jnp.concatenate(
        [
            w_query.reshape(rows, count, group_width),
            jnp.repeat(w_key.reshape(rows, KV, HD), share, axis=1),
            jnp.repeat(w_value.reshape(rows, KV, HD), share, axis=1),
        ],
        axis=2,
    ).transpose(1, 0, 2)
    extra = jnp.concatenate(
        [
            gain_attn[:, None],
            gain_ffn[:, None],
            doc_starts[0].astype(BF).reshape(rows, flag_cols),
            jnp.zeros((rows, extra_cols - 2 - flag_cols), BF),
        ],
        axis=1,
    )
    attn_send = jnp.concatenate(
        [attn_send, jnp.broadcast_to(extra[None], (count,) + extra.shape)], axis=2
    )
    ffn_send = jnp.concatenate(
        [w_gate.reshape(rows, count, hidden), w_up.reshape(rows, count, hidden)], axis=0
    ).transpose(1, 0, 2)
    down_w = lax.all_gather(w_down, "fsdp", axis=0, tiled=True)
    z = lax.axis_index("fsdp")
    if cube:
        x_all, attn_all, ffn_all = start_gather(own, attn_send, ffn_send, count, parts)
        ffn_pieces = [
            lax.dynamic_index_in_dim(ffn_all, (z + parts - back) % parts, 0, False)
            for back in range(min(2, parts))
        ]
    else:
        x_all = lax.all_gather(own, "seq", axis=0, tiled=False)
        attn_all = lax.all_gather(exchange(attn_send), "fsdp", axis=0, tiled=False)
        ffn_pieces = [exchange(ffn_send)]
    dy = cotangent[0]
    own, x_all, attn_all, ffn_pieces, dy = fence(own, x_all, attn_all, ffn_pieces, dy)
    ffn_pieces = [piece.reshape(count, 2, rows, hidden) for piece in ffn_pieces]

    dy_all = lax.all_gather(dy, "seq", axis=0, tiled=False)
    if len(ffn_pieces) < parts:
        ffn_pieces += hop(ffn_pieces[-1])
    flags = lax.dynamic_index_in_dim(attn_all, z, 0, False)
    flags = flags[:, :, attn_cols + 2 : attn_cols + 2 + flag_cols].reshape(length)
    last = document_starts(flags)
    position = (jnp.arange(length, dtype=jnp.int32) - last).astype(F32)
    frequency = jnp.exp(jnp.arange(HALF, dtype=F32) * (-2.0 * math.log(10000.0) / HD))
    angle = frequency[:, None] * position[None, :]
    cosine, sine = jnp.cos(angle), jnp.sin(angle)
    blocks = length // BQ
    by_block = last.reshape(blocks, BQ)
    starts = jnp.tile(by_block, (1, group)).reshape(blocks, 1, group * BQ)
    first_row = jnp.arange(blocks, dtype=jnp.int32) * BQ
    low = by_block[:, 0] // BK
    high = (first_row + BQ + BK - 1) // BK
    begin = jnp.minimum((by_block[:, -1] + BK - 1) // BK, high)
    end = jnp.maximum((first_row + 1) // BK, begin)
    bounds = jnp.stack([low, begin, end, high], axis=1)
    w_ext = attn_all.transpose(1, 0, 2, 3).reshape(width, attn_cols + extra_cols)
    n1_all, projected, wt_ext = project(x_all, w_ext, attn_cols)
    attn_t = wt_ext[:attn_cols]
    gain_one = wt_ext[attn_cols].astype(F32)
    gain_two = wt_ext[attn_cols + 1].astype(F32)
    projected, cosine, sine, starts, bounds, ffn_last, w_out, down_w = fence(
        projected, cosine, sine, starts, bounds, ffn_pieces[-1], w_out, down_w
    )
    ffn_pieces[-1] = ffn_last

    out_w = lax.all_gather(w_out, ("seq", "fsdp"), axis=0, tiled=True)
    if len(ffn_pieces) < parts:
        ffn_pieces += hop(ffn_pieces[-1])
    o_heads, lse, q_t, k_t, k_n, v_n = attend(
        bounds, projected, cosine, sine, starts, group, count, local
    )
    o_heads, lse, q_t, k_t, k_n, v_n, ffn_last, dy_all = fence(
        o_heads, lse, q_t, k_t, k_n, v_n, ffn_pieces[-1], dy_all
    )
    ffn_pieces[-1] = ffn_last

    while len(ffn_pieces) < parts:
        ffn_pieces += hop(ffn_pieces[-1])
    o_t = exchange(o_heads).reshape(count * group_width, local)
    o_t, ffn_pieces = fence(o_t, ffn_pieces)

    ffn_w = collect(ffn_pieces, "fsdp").transpose(2, 1, 0, 3, 4).reshape(2, width, hidden)
    gate_w, up_w = ffn_w[0], ffn_w[1]
    x = own.astype(F32)
    r1 = lax.rsqrt(jnp.mean(x * x, axis=-1, keepdims=True) + EPS)
    h1 = x + jnp.einsum("et,ed->td", o_t, out_w, preferred_element_type=F32)
    r2 = lax.rsqrt(jnp.mean(h1 * h1, axis=-1, keepdims=True) + EPS)
    n2 = (h1 * r2 * gain_two).astype(BF)
    n2, h1, r2 = fence(n2, h1, r2)

    kept = None

    def chunk(kept, first, second, c):
        places = jnp.stack([me ^ c, me ^ (c + 1)]).astype(jnp.int32)
        return ffn_chunk(places, first, second, dy_all, gate_w, up_w, down_w, kept)

    if cube:
        side, over_x, over_y = swap(n2, 1), swap(n2, 2), swap(n2, 4)
        side, gate_w, up_w = fence(side, gate_w, up_w)
        kept, own_a, own_b = chunk(kept, n2, side, 0)
        kept, own_a, own_b, over_x, over_y = fence(kept, own_a, own_b, over_x, over_y)

        far_a, far_b = far_halves(over_x, over_y)
        side_x, side_y, own_c = swap(over_x, 1), swap(over_y, 1), swap(own_b, 1)
        side_x, side_y, over_x, over_y, kept = fence(side_x, side_y, over_x, over_y, kept)
        kept, x_a, x_b = chunk(kept, over_x, side_x, 2)
        kept, x_a, x_b, far_a, far_b, own_c = fence(kept, x_a, x_b, far_a, far_b, own_c)

        far = jnp.concatenate([far_a, far_b], axis=0)
        side_far = swap(far, 1)
        x_sum = chip_sum(x_a, x_b)
        x_first = swap(x_sum[:half].astype(BF), 2)
        kept, y_a, y_b = chunk(kept, over_y, side_y, 4)
        kept, y_a, y_b, far, side_far, x_sum = fence(kept, y_a, y_b, far, side_far, x_sum)

        y_sum = chip_sum(y_a, y_b)
        y_second = swap(y_sum[half:].astype(BF), 4)
        kept, far_one, far_two = chunk(kept, far, side_far, 6)
        kept, far_one, far_two, x_first, y_second, y_sum = fence(
            kept, far_one, far_two, x_first, y_second, y_sum
        )
        act, d_gate, d_up, n2_all, y_part = kept
        n2_all, dy_rows = n2_all.reshape(sheet), dy_all.reshape(sheet)
        act, d_gate, d_up = [a.reshape(length, hidden) for a in (act, d_gate, d_up)]

        far_sum = chip_sum(far_one, far_two).astype(BF)
        x_far, y_far = swap(far_sum[:half], 2), swap(far_sum[half:], 4)
        term_gate = jnp.einsum("td,tf->df", n2_all, d_gate, preferred_element_type=F32)
        x_far, y_far, term_gate = fence(x_far, y_far, term_gate)

        x_second = swap((x_sum[half:] + y_far.astype(F32)).astype(BF), 2)
        y_first = swap((y_sum[:half] + x_far.astype(F32)).astype(BF), 4)
        term_up = jnp.einsum("td,tf->df", n2_all, d_up, preferred_element_type=F32)
        x_second, y_first, term_up = fence(x_second, y_first, term_up)
        own_sum = own_a.astype(F32) + own_c.astype(F32)
        first = own_sum[:half] + x_first.astype(F32) + y_first.astype(F32)
        second = own_sum[half:] + x_second.astype(F32) + y_second.astype(F32)
        dn2 = jnp.concatenate([first, second], axis=0)
    else:
        n2_blocks = gather_plain(n2)
        dn2_parts = []
        for c in range(0, count, 2):
            kept, part_a, part_b = chunk(kept, n2_blocks[c], n2_blocks[c + 1], c)
            dn2_parts += [part_a, part_b]
        act, d_gate, d_up, n2_all, y_part = kept
        n2_all, dy_rows = n2_all.reshape(sheet), dy_all.reshape(sheet)
        act, d_gate, d_up = [a.reshape(length, hidden) for a in (act, d_gate, d_up)]
        dn2 = scatter_plain(dn2_parts)
        term_gate = jnp.einsum("td,tf->df", n2_all, d_gate, preferred_element_type=F32)
        term_up = jnp.einsum("td,tf->df", n2_all, d_up, preferred_element_type=F32)
    y_part = y_part.reshape(sheet)

    m2 = h1 * r2
    e2 = dn2 * gain_two
    dh1 = dy.astype(F32) + r2 * (e2 - m2 * jnp.mean(e2 * m2, axis=-1, keepdims=True))
    db = dh1.astype(BF)
    do_t = jnp.einsum("ed,td->et", out_w, db, preferred_element_type=F32).astype(BF)
    do_t, db, dh1, term_gate, term_up, y_part = fence(
        do_t, db, dh1, term_gate, term_up, y_part
    )
    y = lax.psum_scatter(y_part, "seq", scatter_dimension=0, tiled=True)
    gate_up = [
        term_gate.reshape(count, parts, rows, hidden),
        term_up.reshape(count, parts, rows, hidden),
    ]
    moved = hop(*[term_of(term, 0).astype(BF) for term in gate_up])
    do_heads = exchange(do_t.reshape(count, group_width, local))
    term_out = dot_f32(o_t, db).astype(BF)
    do_heads, term_out, moved = fence(do_heads, term_out, moved)

    part_out = lax.psum_scatter(term_out, "seq", scatter_dimension=0, tiled=True)
    states = [m.astype(F32) + term_of(t, 1) for m, t in zip(moved, gate_up)]
    if parts > 2:
        moved = hop(*[state.astype(BF) for state in states])
    dq_t, dkv_t = attend_back(
        bounds, q_t, k_n, k_t, v_n, cosine, sine, starts, o_heads, do_heads, lse, group
    )
    dq_t, dkv_t, moved, states, act = fence(dq_t, dkv_t, moved, states, act)

    d_t = jnp.concatenate([dq_t, dkv_t], axis=0)

    def pair_of(c):
        return jnp.concatenate(
            [lax.dynamic_slice_in_dim(d_t, (me ^ n) * local, local, 1) for n in (c, c + 1)], axis=1
        )

    def dn1_chunk(c):
        part = jnp.einsum("et,ed->td", pair_of(c), attn_t, preferred_element_type=F32).astype(BF)
        return part[:local], part[local:]

    term_down = jnp.einsum("tf,td->fd", act, dy_rows, preferred_element_type=F32)
    if parts > 2:
        states = [m.astype(F32) + term_of(t, 2) for m, t in zip(moved, gate_up)]
    if cube:
        far_sum = chip_sum(*dn1_chunk(6)).astype(BF)
        x_sum = chip_sum(*dn1_chunk(2))
        y_sum = chip_sum(*dn1_chunk(4))
        far_sum, x_sum, y_sum = fence(far_sum, x_sum, y_sum)
        x_far, y_far = swap(far_sum[:half], 2), swap(far_sum[half:], 4)
        x_first = swap(x_sum[:half].astype(BF), 2)
        y_second = swap(y_sum[half:].astype(BF), 4)
        own_sum = chip_sum(*dn1_chunk(0))
        term_attn = jnp.einsum(
            "td,et->de", n1_all.reshape(sheet), d_t, preferred_element_type=F32
        )
        states = ring_finish(states, gate_up, 3)
        x_far, y_far, own_sum, term_attn, states, term_down = fence(
            x_far, y_far, own_sum, term_attn, states, term_down
        )
        x_second = swap((x_sum[half:] + y_far.astype(F32)).astype(BF), 2)
        y_first = swap((y_sum[:half] + x_far.astype(F32)).astype(BF), 4)
        first = own_sum[:half] + x_first.astype(F32) + y_first.astype(F32)
        second = own_sum[half:] + x_second.astype(F32) + y_second.astype(F32)
        dn1 = jnp.concatenate([first, second], axis=0)
    else:
        dn1 = scatter_plain([piece for c in range(0, count, 2) for piece in dn1_chunk(c)])
        term_attn = jnp.einsum(
            "td,et->de", n1_all.reshape(sheet), d_t, preferred_element_type=F32
        )
        states = ring_finish(states, gate_up, 3)
    part_gate, part_up = states
    output = (h1 + y.astype(F32)).astype(BF)
    down_terms = [term_down.reshape(1, parts, hidden // parts, width)]
    (grad_down,) = ring_finish([term_of(down_terms[0], 0)], down_terms, 1)
    grad_down = grad_down.reshape(hidden // parts, width)
    attn_terms = [term_attn.reshape(count, parts, rows, attn_cols)]
    (part_attn,) = ring_finish([term_of(attn_terms[0], 0)], attn_terms, 1)
    out_terms = [part_out.reshape(1, parts, rows, width)]
    (grad_out,) = ring_finish([term_of(out_terms[0], 0)], out_terms, 1)
    grad_out = grad_out.reshape(rows, width)
    m1 = x * r1
    e1 = dn1 * gain_one
    grad_tokens = dh1 + r1 * (e1 - m1 * jnp.mean(e1 * m1, axis=-1, keepdims=True))

    ffn_back = exchange(jnp.stack([part_gate, part_up], axis=1).astype(BF)).astype(F32)
    grad_gate = ffn_back[:, 0].transpose(1, 0, 2).reshape(rows, count * hidden)
    grad_up = ffn_back[:, 1].transpose(1, 0, 2).reshape(rows, count * hidden)
    attn_back = exchange(part_attn.astype(BF)).astype(F32)
    grad_query = attn_back[:, :, :group_width].transpose(1, 0, 2).reshape(rows, H * HD)
    pair = attn_back[:, :, group_width:].reshape(KV, share, rows, 2 * HD).sum(axis=1)
    grad_key = pair[:, :, :HD].transpose(1, 0, 2).reshape(rows, KV * HD)
    grad_value = pair[:, :, HD:].transpose(1, 0, 2).reshape(rows, KV * HD)

    def along(weight, grad):
        return jnp.sum(weight.astype(F32) * grad, axis=1)

    grad_gain_attn = (
        along(w_query, grad_query) + along(w_key, grad_key) + along(w_value, grad_value)
    ) / gain_attn.astype(F32)
    grad_gain_ffn = (along(w_gate, grad_gate) + along(w_up, grad_up)) / gain_ffn.astype(F32)
    return (
        output[None],
        grad_tokens[None],
        grad_gain_attn,
        grad_query,
        grad_key,
        grad_value,
        grad_out,
        grad_gain_ffn,
        grad_gate,
        grad_up,
        grad_down,
    )


def solution(mesh):
    sheet = P("fsdp", "seq", None)
    line = P(("seq", "fsdp"))
    matrix = P(("seq", "fsdp"), None)
    return jax.shard_map(
        body,
        mesh=mesh,
        in_specs=(
            sheet, P("fsdp", "seq"), line, matrix, matrix, matrix, matrix, line, matrix, matrix,
            matrix, sheet,
        ),
        out_specs=(
            sheet, sheet, line, matrix, matrix, matrix, matrix, line, matrix, matrix, matrix,
        ),
        check_vma=False,
    )
```

time: 1350 us -> 1030 us (0.76)
  waiting for transfers between devices: 574 us -> 257 us
  Pallas kernels: 165 us -> 376 us
  blocking collectives: 169 us -> 0 us
  matrix products: 254 us -> 98.4 us
  starting transfers between devices: 21.1 us -> 91.9 us
  local copies, waits for them, and re-layouts: 59.8 us -> 92.9 us
  other arithmetic: 77.3 us -> 91 us
    pallas_call x0 -> x6, Pallas kernels: none -> 295 us  [the longest x1 151 us: start_gather(): pl.pallas_call(functools.partial(start_kernel, count, parts), out_shape=s...]
    reduce_scatter x3 -> x1, waiting for transfers between devices: 207 us -> 0.01 us  [body(): y = lax.psum_scatter(y_part, 'seq', scatter_dimension=0, tiled=True)]
    ppermute x24 -> x45, waiting for transfers between devices: 306 us -> 147 us  [the longest x17 89.8 us: hop(): return [lax.ppermute(block, 'fsdp', ring('fsdp')) for block in blocks]]
    dot_general x7 -> x6, matrix products: 130 us -> 37.4 us  [the longest x1 14.8 us: body(): jnp.einsum('tf,td->fd', act, dy_rows, preferred_element_type=F32)]
    all_gather x2 -> x0, blocking collectives: 84.8 us -> none  [the longest x1 69.3 us: body(): lax.all_gather(jnp.stack([gain_attn, gain_ffn]), both, axis=1, tiled=True)]
    all_to_all x2 -> x0, blocking collectives: 84 us -> none  [exchange(): return lax.all_to_all(array, 'seq', split_axis=0, concat_axis=0, tiled=True)]
    ppermute x24 -> x45, starting transfers between devices: 4.98 us -> 76 us  [the longest x17 54.6 us: hop(): return [lax.ppermute(block, 'fsdp', ring('fsdp')) for block in blocks]]
    dot_general x4 -> x1, matrix products: 65.6 us -> 8.32 us  [dot_f32(): return jnp.dot(a, b, preferred_element_type=F32)]
  transfers between devices with their start and end apart: 36 -> 54, of which waited for: 25 -> 26; matrix products, arithmetic and copies ran while one was open for 20% -> 21% of each run, Pallas kernels for 12% -> 37%
where the time goes in v2:
time: 1030 us; the launch traced here: 1020 us
  Pallas kernels  376 us (37%)
  waiting for transfers between devices  257 us (25%)
  matrix products  98.4 us (10%)
  local copies, waits for them, and re-layouts  92.9 us (9%)
  starting transfers between devices  91.9 us (9%)
  other arithmetic  91 us (9%)
  between operations  15.5 us (2%)
    pallas_call x1, Pallas kernels, start_gather(): pl.pallas_call(functools.partial(start_kernel, count, parts), out_shape=s...  151 us
    pallas_call x4, Pallas kernels, ffn_chunk(): pl.pallas_call(ffn_kernel, out_shape=(narrow, narrow, narrow, broad, broa...  126 us
    ppermute x17, waiting for transfers between devices, hop(): return [lax.ppermute(block, 'fsdp', ring('fsdp')) for block in blocks]  89.8 us
    all_gather x1, waiting for transfers between devices, body(): out_w = lax.all_gather(w_out, ('seq', 'fsdp'), axis=0, tiled=True)  59.8 us
    ppermute x28, waiting for transfers between devices, swap(): return lax.ppermute(block, 'seq', [(n, n ^ bit) for n in range(count)])  57.6 us
    ppermute x17, starting transfers between devices, hop(): return [lax.ppermute(block, 'fsdp', ring('fsdp')) for block in blocks]  54.6 us
    pallas_call x1, Pallas kernels, attend_back(): pl.pallas_call(functools.partial(backward_kernel, group), out_shape=(jax....  45.4 us
    pallas_call x1, Pallas kernels, attend(): pl.pallas_call(functools.partial(forward_kernel, group), out_shape=(jax.S...  35.2 us
  transfers between devices with their start and end apart: 54, of which 26 were waited for; matrix products, arithmetic and copies ran while one was open for 21% of the time, Pallas kernels for 37%

profile of v2, /device:TPU:0, one launch (start us, length us, event | category | flops | bytes accessed | tf_op | source)
XLA Modules:
  0.0 1023.0 jit_solution(11385954218520407869)
XLA Ops:
  17.7 151.1 %start_gather.1 = (bf16[8,512,2048]{2,1,0:T(8,128)(2,1)S(1)}, bf16[4,8,64,512]{3,2,1,0:T(8,128)(2,1)S(1)}, bf16[4,8,128,704]{3,2,1,0:T(8,128)(2,1)S(1)}, bf16[6,64,512]{2,1,0:T(8,128)(2,1)}, bf16[6,128,704]{2,1,0:T(8,128)(2,1)}) custom-call(bf16[512,2048]{1,0:T(8,128)(2,1)S(1)} %bitcast.184, bf16[8,64,512]{2,1,0:T(8,128)(2,1)S(1)} %pad_maximum_fusion.1.attn_ref, ...), custom_call_target="tpu_custom_call" | custom-call | tf_op jit(solution)/shard_map/start_gather/pallas_call | solution.py:510
  170.1 5.8 copy-done.4
  178.4 3.1 copy.150
  185.8 18.7 %project.1 = (bf16[8,512,2048]{2,1,0:T(8,128)(2,1)}, f32[384,4096]{1,0:T(8,128)}, bf16[512,2048]{1,0:T(8,128)(2,1)}) custom-call(bf16[8,512,2048]{2,1,0:T(8,128)(2,1)} %copy-done.4, bf16[2048,512]{1,0:T(8,128)(2,1)} %bitcast.236), custom_call_target="tpu_custom_call" | custom-call | flops 6442450944 | bytes 33554432 | tf_op jit(solution)/shard_map/project/pallas_call | solution.py:292
  207.3 4.8 collective-permute-done
  213.2 35.2 %attend.1 = (bf16[8,256,512]{2,1,0:T(8,128)(2,1)}, f32[16,1,1024]{2,1,0:T(1,128)}, bf16[256,4096]{1,0:T(8,128)(2,1)}, bf16[64,4096]{1,0:T(8,128)(2,1)}, bf16[409...) custom-call(s32[16,4]{1,0:T(8,128)} %copy.155.bounds_ref, f32[384,4096]{1,0:T(8,128)} %get-tuple-element.174.q_ref.kv_ref, ...), custom_call_target="tpu_custom_call" | custom-call | flops 85899345920 | bytes 8388608 | tf_op jit(solution)/shard_map/attend/pallas_call | solution.py:178
  248.4 16.6 %all-gather.9.cloned.1.call-done = bf16[4096,2048]{1,0:T(8,128)(2,1)} async-done(((bf16[512,2048]{1,0:T(8,128)(2,1)}), bf16[4096,2048]{1,0:T(8,128)(2,1)}) %all-gather.9.cloned.1.call-update) | async-done | bytes 16777232 | tf_op jit(solution)/shard_map/all_gather | solution.py:675
  265.0 4.3 all-to-all-start
  270.8 27.0 %all-to-all-done = bf16[8,256,512]{2,1,0:T(8,128)(2,1)} async-done(((bf16[8,256,512]{2,1,0:T(8,128)(2,1)}), bf16[8,256,512]{2,1,0:T(8,128)(2,1)}, u32[]{:S(2)}, u32[]{:S(2)}) %all-to-all-start) | async-done | bytes 2097184 | tf_op jit(solution)/shard_map/all_to_all | solution.py:595
  297.9 59.8 %all-gather.7.cloned.1.call-done = bf16[2048,2048]{1,0:T(8,128)(2,1)} async-done(((bf16[64,2048]{1,0:T(8,128)(2,1)}), bf16[2048,2048]{1,0:T(8,128)(2,1)}) %all-gather.7.cloned.1.call-update) | async-done | bytes 8388624 | tf_op jit(solution)/shard_map/all_gather | solution.py:704
  357.7 7.8 multiply_reduce_fusion.1
  379.6 31.1 %ffn.4 = (bf16[8,512,704]{2,1,0:T(8,128)(2,1)}, bf16[8,512,704]{2,1,0:T(8,128)(2,1)}, bf16[8,512,704]{2,1,0:T(8,128)(2,1)}, bf16[8,512,2048]{2,1,0:T(8,128)(2,1)...) custom-call(s32[2]{0:T(128)} %get-tuple-element.357.places_ref, ...), custom_call_target="tpu_custom_call" | custom-call | flops 17716740096 | bytes 29622272 | tf_op jit(solution)/shard_map/ffn/pallas_call | solution.py:381
  410.7 6.3 collective-permute-done.3.first_ref
  428.0 31.5 %ffn.5 = (bf16[8,512,704]{2,1,0:T(8,128)(2,1)}, bf16[8,512,704]{2,1,0:T(8,128)(2,1)}, bf16[8,512,704]{2,1,0:T(8,128)(2,1)}, bf16[8,512,2048]{2,1,0:T(8,128)(2,1)...) custom-call(s32[2]{0:T(128)} %get-tuple-element.358.places_ref, ...), custom_call_target="tpu_custom_call", output_to_operand_aliasing={{0}: (7, {}), {1}: (8, {}), {2}: (9, {}), {3}: (10, {}), {4... | custom-call | flops 17716740096 | bytes 29622272 | tf_op jit(solution)/shard_map/ffn/pallas_call | solution.py:381
  460.4 31.7 %ffn.6 = (bf16[8,512,704]{2,1,0:T(8,128)(2,1)}, bf16[8,512,704]{2,1,0:T(8,128)(2,1)}, bf16[8,512,704]{2,1,0:T(8,128)(2,1)}, bf16[8,512,2048]{2,1,0:T(8,128)(2,1)...) custom-call(s32[2]{0:T(128)} %get-tuple-element.360.places_ref, ...), custom_call_target="tpu_custom_call", output_to_operand_aliasing={{0}: (7, {}), {1}: (8, {}), {2}: (9, {}), {3}: (10, {}), {4... | custom-call | flops 17716740096 | bytes 29622272 | tf_op jit(solution)/shard_map/ffn/pallas_call | solution.py:381
  503.3 31.3 %ffn.7 = (bf16[8,512,704]{2,1,0:T(8,128)(2,1)}, bf16[8,512,704]{2,1,0:T(8,128)(2,1)}, bf16[8,512,704]{2,1,0:T(8,128)(2,1)}, bf16[8,512,2048]{2,1,0:T(8,128)(2,1)...) custom-call(s32[2]{0:T(128)} %get-tuple-element.359.places_ref, ...), custom_call_target="tpu_custom_call", output_to_operand_aliasing={{0}: (7, {}), {1}: (8, {}), {2}: (9, {}), {3}: (10, {}), {4... | custom-call | flops 17716740096 | bytes 29622272 | tf_op jit(solution)/shard_map/ffn/pallas_call | solution.py:381
  535.7 4.6 convert_add_fusion.6
  544.7 17.6 %convolution_bitcast_fusion.1 = f32[2048,704]{0,1:T(8,128)} fusion(bf16[8,512,2048]{2,1,0:T(8,128)(2,1)} %get-tuple-element.273, bf16[8,512,704]{2,1,0:T(8,128)(2,1)S(1)} %bitcast.201), kind=kOutput, calls=%fused_computation.32 | convolution fusion | flops 11811160064 | bytes 28311552 | tf_op jit(solution)/shard_map/td,tf->df/dot_general | solution.py:766
  562.4 6.2 collective-permute-done.16
  569.5 3.2 add_convert_fusion.6
  577.9 18.0 %convolution_bitcast_fusion = f32[2048,704]{0,1:T(8,128)} fusion(bf16[8,512,2048]{2,1,0:T(8,128)(2,1)} %get-tuple-element.273, bf16[8,512,704]{2,1,0:T(8,128)(2,1)S(1)} %bitcast.203), kind=kOutput, calls=%fused_computation.31 | convolution fusion | flops 11811160064 | bytes 28311552 | tf_op jit(solution)/shard_map/td,tf->df/dot_general | solution.py:771
  597.5 3.2 collective-permute-done.19
  605.1 4.1 fusion.66
  609.2 9.2 convolution_convert_fusion.5
  618.5 4.4 all-to-all-start.1
  622.9 6.6 copy.162
  632.5 6.4 copy.163
  642.3 8.3 convolution_convert_fusion
  653.3 16.2 %collective-permute-done.21 = bf16[8,64,704]{2,1,0:T(8,128)(2,1)} collective-permute-done((bf16[8,64,704]{2,1,0:T(8,128)(2,1)}, bf16[8,64,704]{2,1,0:T(8,128)(2,1)}, u32[]{:S(2)}, u32[]{:S(2)}) %collective-permute-start.21) | collective-permute-done | bytes 720928 | tf_op jit(solution)/shard_map/ppermute | solution.py:533
  675.1 45.4 %attend_back.1 = (bf16[256,4096]{1,0:T(8,128)(2,1)}, bf16[128,4096]{1,0:T(8,128)(2,1)}) custom-call(s32[16,4]{1,0:T(8,128)} %copy.155.bounds_ref, bf16[256,4096]{1,0:T(8,128)(2,1)} %get-tuple-element.287.q_ref, bf16[4096,64]{1,0:T(8,128)(2,1)} %get-tuple-element.288.k_ref, bf16[64,4096]{1,0:T(8,128)(2,1)} %get-tuple-element.289.kt_ref, ...), custom_call_target="tpu_custom_call" | custom-call | flops 107374182400 | bytes 8388608 | tf_op jit(solution)/shard_map/attend_back/pallas_call | solution.py:233
  751.2 50.1 %collective-permute-start.30 = (bf16[8,64,704]{2,1,0:T(8,128)(2,1)}, bf16[8,64,704]{2,1,0:T(8,128)(2,1)}, u32[]{:S(2)}, u32[]{:S(2)}) collective-permute-start(bf16[8,64,704]{2,1,0:T(8,128)(2,1)} %fusion.12), channel_id=1, source_target_pairs={{0,1},{1,2},{2,3},{3,0},{4,5},{5,6},{6,7},{7,4},{8,9},{9,10},{10,1... | collective-permute-start | bytes 2162696 | tf_op jit(solution)/shard_map/ppermute | solution.py:533
  801.3 14.8 %fusion.72 = f32[704,2048]{1,0:T(8,128)} fusion(bf16[4096,704]{1,0:T(8,128)(2,1)S(1)} %bitcast.199, bf16[4096,2048]{1,0:T(8,128)(2,1)S(1)} %bitcast.196), kind=kOutput, calls=%fused_computation.218 | convolution fusion | flops 11811160064 | bytes 28311552 | tf_op jit(solution)/shard_map/tf,td->fd/dot_general | solution.py:829
  816.1 13.0 %fusion.71 = f32[2048,384]{1,0:T(8,128)S(1)} fusion(bf16[4096,2048]{1,0:T(8,128)(2,1)} %bitcast.257, bf16[384,4096]{1,0:T(8,128)(2,1)} %copy-done.13), kind=kOutput, calls=%fused_computation.217 | convolution fusion | flops 6442450944 | bytes 23068672 | tf_op jit(solution)/shard_map/td,et->de/dot_general | solution.py:841
  845.3 8.3 collective-permute-done.31
  860.6 4.4 convert_add_fusion.1
  865.1 8.9 collective-permute-done.27
  873.9 3.5 collective-permute-done.28
  885.0 10.1 collective-permute-done.36
  897.1 3.6 all-to-all-start.3
  907.0 8.4 collective-permute-done.37
  916.7 18.6 %collective-permute-done.33 = bf16[256,2048]{1,0:T(8,128)(2,1)} collective-permute-done((bf16[256,2048]{1,0:T(8,128)(2,1)}, bf16[256,2048]{1,0:T(8,128)(2,1)}, u32[]{:S(2)}, u32[]{:S(2)}) %collective-permute-start.33) | collective-permute-done | bytes 1048608 | tf_op jit(solution)/shard_map/ppermute | solution.py:568
  940.5 3.2 fusion.6
  945.7 5.6 all-to-all-done.3
  951.3 3.5 all-to-all-start.2
  968.1 22.8 %collective-permute-done.39 = bf16[1,64,2048]{2,1,0:T(8,128)(2,1)} collective-permute-done((bf16[1,64,2048]{2,1,0:T(8,128)(2,1)S(1)}, bf16[1,64,2048]{2,1,0:T(8,128)(2,1)}, u32[]{:S(2)}, u32[]{:S(2)}) %collective-permute-start.39) | collective-permute-done | bytes 262176 | tf_op jit(solution)/shard_map/ppermute | solution.py:533
  993.4 8.2 collective-permute-done.40
  1004.6 5.9 collective-permute-done.41
  1011.3 4.9 fusion.8
  (383 shorter events, 190.2 us)
Async XLA Ops:
  7.2 204.9 %all-gather.5.cloned.1.call-start = ((), (), s32[]{:S(2)}) async-start(), calls=%async_computation.6 | async-start | bytes 3604480 | tf_op jit(solution)/shard_map/all_gather | solution.py:659
  7.9 257.1 %all-gather.9.cloned.1.call-start = ((), (), s32[]{:S(2)}) async-start(), calls=%async_computation.10 | async-start | bytes 18874368 | tf_op jit(solution)/shard_map/all_gather | solution.py:675
  177.8 179.9 %all-gather.7.cloned.1.call-start = ((), (), s32[]{:S(2)}) async-start(), calls=%async_computation.7 | async-start | bytes 8650752 | tf_op jit(solution)/shard_map/all_gather | solution.py:704
  177.8 34.2 %collective-permute-start = (bf16[8,2,64,704]{3,2,1,0:T(8,128)(2,1)}, bf16[8,2,64,704]{3,2,1,0:T(8,128)(2,1)}, u32[]{:S(2)}, u32[]{:S(2)}) collective-permute-start(bf16[8,2,64,704]{3,2,1,0:T(8,128)(2,1)} %bitcast.223), channel_id=1, source_target_pairs={{0,1},{1,2},{2,3},{3,0},{4,5},{5,6},{6,7},{7,4},{8,9},{9,10},{10,1... | collective-permute-start | bytes 4325384 | tf_op jit(solution)/shard_map/ppermute | solution.py:533
  212.8 35.7 %collective-permute-start.1 = (bf16[8,2,64,704]{3,2,1,0:T(8,128)(2,1)}, bf16[8,2,64,704]{3,2,1,0:T(8,128)(2,1)}, u32[]{:S(2)}, u32[]{:S(2)}) collective-permute-start(bf16[8,2,64,704]{3,2,1,0:T(8,128)(2,1)} %collective-permute-done), channel_id=1, source_target_pairs={{0,1},{1,2},{2,3},{3,0},{4,5},{5,6},{6,7},{7,4},{8,9},{9,10},{10,1... | collective-permute-start | bytes 4325384 | tf_op jit(solution)/shard_map/ppermute | solution.py:533
  265.0 32.8 %all-to-all-start = ((bf16[8,256,512]{2,1,0:T(8,128)(2,1)}), bf16[8,256,512]{2,1,0:T(8,128)(2,1)}, u32[]{:S(2)}, u32[]{:S(2)}) async-start(bf16[8,256,512]{2,1,0:T(8,128)(2,1)} %get-tuple-element.186.o_ref), calls=%async_computation | async-start | bytes 4194304 | tf_op jit(solution)/shard_map/all_to_all | solution.py:595
  368.1 11.6 %collective-permute-start.2 = (bf16[512,2048]{1,0:T(8,128)(2,1)}, bf16[512,2048]{1,0:T(8,128)(2,1)}, u32[]{:S(2)}, u32[]{:S(2)}) collective-permute-start(bf16[512,2048]{1,0:T(8,128)(2,1)} %multiply_convert_fusion.first_ref), channel_id=1, source_target_pairs={{0,4},{4,0},{8,12},{12,8},{16,20},{20,16},{24,28},{28,24},{1,5},{5... | collective-permute-start | bytes 6291464 | tf_op jit(solution)/shard_map/ppermute | solution.py:568
  368.9 48.1 %collective-permute-start.3 = (bf16[512,2048]{1,0:T(8,128)(2,1)}, bf16[512,2048]{1,0:T(8,128)(2,1)}, u32[]{:S(2)}, u32[]{:S(2)}) collective-permute-start(bf16[512,2048]{1,0:T(8,128)(2,1)} %multiply_convert_fusion.first_ref), channel_id=1, source_target_pairs={{0,8},{4,12},{8,0},{12,4},{16,24},{20,28},{24,16},{28,20},{1,9},{5... | collective-permute-start | bytes 6291464 | tf_op jit(solution)/shard_map/ppermute | solution.py:568
  370.3 47.7 %collective-permute-start.4 = (bf16[512,2048]{1,0:T(8,128)(2,1)}, bf16[512,2048]{1,0:T(8,128)(2,1)S(1)}, u32[]{:S(2)}, u32[]{:S(2)}) collective-permute-start(bf16[512,2048]{1,0:T(8,128)(2,1)} %multiply_convert_fusion.first_ref), channel_id=1, source_target_pairs={{0,16},{4,20},{8,24},{12,28},{16,0},{20,4},{24,8},{28,12},{1,17},{... | collective-permute-start | bytes 6291464 | tf_op jit(solution)/shard_map/ppermute | solution.py:568
  418.6 40.9 %collective-permute-start.9 = (bf16[512,2048]{1,0:T(8,128)(2,1)}, bf16[512,2048]{1,0:T(8,128)(2,1)}, u32[]{:S(2)}, u32[]{:S(2)}) collective-permute-start(bf16[512,2048]{1,0:T(8,128)(2,1)} %get-tuple-element.233), channel_id=1, source_target_pairs={{0,4},{4,0},{8,12},{12,8},{16,20},{20,16},{24,28},{28,24},{1,5},{5... | collective-permute-start | bytes 6291464 | tf_op jit(solution)/shard_map/ppermute | solution.py:568
  420.7 38.8 %collective-permute-start.7 = (bf16[256,2048]{1,0:T(8,128)(2,1)S(1)}, bf16[256,2048]{1,0:T(8,128)(2,1)S(1)}, u32[]{:S(2)}, u32[]{:S(2)}) collective-permute-start(bf16[256,2048]{1,0:T(8,128)(2,1)S(1)} %slice.132), channel_id=1, source_target_pairs={{0,16},{4,20},{8,24},{12,28},{16,0},{20,4},{24,8},{28,12},{1,17},{... | collective-permute-start | bytes 3145736 | tf_op jit(solution)/shard_map/ppermute | solution.py:568
  421.4 38.1 %collective-permute-start.8 = (bf16[256,2048]{1,0:T(8,128)(2,1)S(1)}, bf16[256,2048]{1,0:T(8,128)(2,1)S(1)}, u32[]{:S(2)}, u32[]{:S(2)}) collective-permute-start(bf16[256,2048]{1,0:T(8,128)(2,1)S(1)} %slice.133), channel_id=1, source_target_pairs={{0,8},{4,12},{8,0},{12,4},{16,24},{20,28},{24,16},{28,20},{1,9},{5... | collective-permute-start | bytes 3145736 | tf_op jit(solution)/shard_map/ppermute | solution.py:568
  459.5 32.6 %collective-permute-start.11 = (bf16[512,2048]{1,0:T(8,128)(2,1)}, bf16[512,2048]{1,0:T(8,128)(2,1)}, u32[]{:S(2)}, u32[]{:S(2)}) collective-permute-start(bf16[512,2048]{1,0:T(8,128)(2,1)} %get-tuple-element.252), channel_id=1, source_target_pairs={{0,4},{4,0},{8,12},{12,8},{16,20},{20,16},{24,28},{28,24},{1,5},{5... | collective-permute-start | bytes 6291464 | tf_op jit(solution)/shard_map/ppermute | solution.py:568
  459.8 34.8 %collective-permute-start.10 = (bf16[512,2048]{1,0:T(8,128)(2,1)S(1)}, bf16[512,2048]{1,0:T(8,128)(2,1)S(1)}, u32[]{:S(2)}, u32[]{:S(2)}) collective-permute-start(bf16[512,2048]{1,0:T(8,128)(2,1)S(1)} %constant_dynamic-update-slice_fusion.first_ref), channel_id=1, source_target_pairs={{0,4},{4,0},{8,12},{12,8},{16,20},{20,16},{24,28},{28,24},{1,5},{5... | collective-permute-start | bytes 6291464 | tf_op jit(solution)/shard_map/ppermute | solution.py:568
  494.9 39.7 %collective-permute-start.12 = (bf16[256,2048]{1,0:T(8,128)(2,1)S(1)}, bf16[256,2048]{1,0:T(8,128)(2,1)S(1)}, u32[]{:S(2)}, u32[]{:S(2)}) collective-permute-start(bf16[256,2048]{1,0:T(8,128)(2,1)S(1)} %slice.237), channel_id=1, source_target_pairs={{0,8},{4,12},{8,0},{12,4},{16,24},{20,28},{24,16},{28,20},{1,9},{5... | collective-permute-start | bytes 3145736 | tf_op jit(solution)/shard_map/ppermute | solution.py:568
  502.9 31.7 %collective-permute-start.14 = (bf16[256,2048]{1,0:T(8,128)(2,1)}, bf16[256,2048]{1,0:T(8,128)(2,1)S(1)}, u32[]{:S(2)}, u32[]{:S(2)}) collective-permute-start(bf16[256,2048]{1,0:T(8,128)(2,1)} %slice.236), channel_id=1, source_target_pairs={{0,16},{4,20},{8,24},{12,28},{16,0},{20,4},{24,8},{28,12},{1,17},{... | collective-permute-start | bytes 3145736 | tf_op jit(solution)/shard_map/ppermute | solution.py:568
  542.7 25.8 %collective-permute-start.16 = (bf16[256,2048]{1,0:T(8,128)(2,1)}, bf16[256,2048]{1,0:T(8,128)(2,1)}, u32[]{:S(2)}, u32[]{:S(2)}) collective-permute-start(bf16[256,2048]{1,0:T(8,128)(2,1)} %get-tuple-element.348), channel_id=1, source_target_pairs={{0,8},{4,12},{8,0},{12,4},{16,24},{20,28},{24,16},{28,20},{1,9},{5... | collective-permute-start | bytes 3145736 | tf_op jit(solution)/shard_map/ppermute | solution.py:568
  543.9 25.6 %collective-permute-start.17 = (bf16[256,2048]{1,0:T(8,128)(2,1)}, bf16[256,2048]{1,0:T(8,128)(2,1)}, u32[]{:S(2)}, u32[]{:S(2)}) collective-permute-start(bf16[256,2048]{1,0:T(8,128)(2,1)} %get-tuple-element.347), channel_id=1, source_target_pairs={{0,16},{4,20},{8,24},{12,28},{16,0},{20,4},{24,8},{28,12},{1,17},{... | collective-permute-start | bytes 3145736 | tf_op jit(solution)/shard_map/ppermute | solution.py:568
  572.7 24.8 %collective-permute-start.18 = (bf16[256,2048]{1,0:T(8,128)(2,1)}, bf16[256,2048]{1,0:T(8,128)(2,1)}, u32[]{:S(2)}, u32[]{:S(2)}) collective-permute-start(bf16[256,2048]{1,0:T(8,128)(2,1)} %add_convert_fusion.6), channel_id=1, source_target_pairs={{0,8},{4,12},{8,0},{12,4},{16,24},{20,28},{24,16},{28,20},{1,9},{5... | collective-permute-start | bytes 3145736 | tf_op jit(solution)/shard_map/ppermute | solution.py:568
  576.1 24.6 %collective-permute-start.19 = (bf16[256,2048]{1,0:T(8,128)(2,1)}, bf16[256,2048]{1,0:T(8,128)(2,1)}, u32[]{:S(2)}, u32[]{:S(2)}) collective-permute-start(bf16[256,2048]{1,0:T(8,128)(2,1)} %add_convert_fusion.5), channel_id=1, source_target_pairs={{0,16},{4,20},{8,24},{12,28},{16,0},{20,4},{24,8},{28,12},{1,17},{... | collective-permute-start | bytes 3145736 | tf_op jit(solution)/shard_map/ppermute | solution.py:568
  618.5 51.1 %all-to-all-start.1 = ((bf16[8,256,512]{2,1,0:T(8,128)(2,1)}), bf16[8,256,512]{2,1,0:T(8,128)(2,1)}, u32[]{:S(2)}, u32[]{:S(2)}) async-start(bf16[8,256,512]{2,1,0:T(8,128)(2,1)} %bitcast.237), calls=%async_computation.2 | async-start | bytes 4194304 | tf_op jit(solution)/shard_map/all_to_all | solution.py:595
  622.8 342.4 %reduce-scatter.5.cloned.1.call-start = ((), (), s32[]{:S(2)}) async-start(), calls=%async_computation.9 | async-start | bytes 9437184 | tf_op jit(solution)/shard_map/reduce_scatter | solution.py:809
  631.0 22.3 %collective-permute-start.20 = (bf16[8,64,704]{2,1,0:T(8,128)(2,1)S(1)}, bf16[8,64,704]{2,1,0:T(8,128)(2,1)}, u32[]{:S(2)}, u32[]{:S(2)}) collective-permute-start(bf16[8,64,704]{2,1,0:T(8,128)(2,1)S(1)} %fusion.20), channel_id=1, source_target_pairs={{0,1},{1,2},{2,3},{3,0},{4,5},{5,6},{6,7},{7,4},{8,9},{9,10},{10,1... | collective-permute-start | bytes 2162696 | tf_op jit(solution)/shard_map/ppermute | solution.py:533
  641.3 28.2 %collective-permute-start.21 = (bf16[8,64,704]{2,1,0:T(8,128)(2,1)}, bf16[8,64,704]{2,1,0:T(8,128)(2,1)}, u32[]{:S(2)}, u32[]{:S(2)}) collective-permute-start(bf16[8,64,704]{2,1,0:T(8,128)(2,1)} %fusion.21), channel_id=1, source_target_pairs={{0,1},{1,2},{2,3},{3,0},{4,5},{5,6},{6,7},{7,4},{8,9},{9,10},{10,1... | collective-permute-start | bytes 2162696 | tf_op jit(solution)/shard_map/ppermute | solution.py:533
  669.6 341.8 %reduce-scatter.3.cloned.1.call-start = ((), (), s32[]{:S(2)}) async-start(), calls=%async_computation.8 | async-start | bytes 18874368 | tf_op jit(solution)/shard_map/reduce_scatter | solution.py:799
  672.6 48.0 %collective-permute-start.22 = (bf16[8,64,704]{2,1,0:T(8,128)(2,1)S(1)}, bf16[8,64,704]{2,1,0:T(8,128)(2,1)S(1)}, u32[]{:S(2)}, u32[]{:S(2)}) collective-permute-start(bf16[8,64,704]{2,1,0:T(8,128)(2,1)S(1)} %bitcast_add_fusion.5), channel_id=1, source_target_pairs={{0,1},{1,2},{2,3},{3,0},{4,5},{5,6},{6,7},{7,4},{8,9},{9,10},{10,1... | collective-permute-start | bytes 2162696 | tf_op jit(solution)/shard_map/ppermute | solution.py:533
  675.0 45.6 %collective-permute-start.23 = (bf16[8,64,704]{2,1,0:T(8,128)(2,1)S(1)}, bf16[8,64,704]{2,1,0:T(8,128)(2,1)S(1)}, u32[]{:S(2)}, u32[]{:S(2)}) collective-permute-start(bf16[8,64,704]{2,1,0:T(8,128)(2,1)S(1)} %bitcast_add_fusion.4), channel_id=1, source_target_pairs={{0,1},{1,2},{2,3},{3,0},{4,5},{5,6},{6,7},{7,4},{8,9},{9,10},{10,1... | collective-permute-start | bytes 2162696 | tf_op jit(solution)/shard_map/ppermute | solution.py:533
  730.8 106.5 %collective-permute-start.24 = (bf16[512,2048]{1,0:T(8,128)(2,1)}, bf16[512,2048]{1,0:T(8,128)(2,1)}, u32[]{:S(2)}, u32[]{:S(2)}) collective-permute-start(bf16[512,2048]{1,0:T(8,128)(2,1)} %slice.178), channel_id=1, source_target_pairs={{0,4},{4,0},{8,12},{12,8},{16,20},{20,16},{24,28},{28,24},{1,5},{5... | collective-permute-start | bytes 6291464 | tf_op jit(solution)/shard_map/ppermute | solution.py:568
  735.9 96.0 %collective-permute-start.25 = (bf16[512,2048]{1,0:T(8,128)(2,1)}, bf16[512,2048]{1,0:T(8,128)(2,1)}, u32[]{:S(2)}, u32[]{:S(2)}) collective-permute-start(bf16[512,2048]{1,0:T(8,128)(2,1)} %slice.180), channel_id=1, source_target_pairs={{0,4},{4,0},{8,12},{12,8},{16,20},{20,16},{24,28},{28,24},{1,5},{5... | collective-permute-start | bytes 6291464 | tf_op jit(solution)/shard_map/ppermute | solution.py:568
  742.0 92.6 %collective-permute-start.26 = (bf16[512,2048]{1,0:T(8,128)(2,1)}, bf16[512,2048]{1,0:T(8,128)(2,1)}, u32[]{:S(2)}, u32[]{:S(2)}) collective-permute-start(bf16[512,2048]{1,0:T(8,128)(2,1)} %slice.182), channel_id=1, source_target_pairs={{0,4},{4,0},{8,12},{12,8},{16,20},{20,16},{24,28},{28,24},{1,5},{5... | collective-permute-start | bytes 6291464 | tf_op jit(solution)/shard_map/ppermute | solution.py:568
  747.5 113.1 %collective-permute-start.29 = (bf16[512,2048]{1,0:T(8,128)(2,1)}, bf16[512,2048]{1,0:T(8,128)(2,1)}, u32[]{:S(2)}, u32[]{:S(2)}) collective-permute-start(bf16[512,2048]{1,0:T(8,128)(2,1)} %slice.184), channel_id=1, source_target_pairs={{0,4},{4,0},{8,12},{12,8},{16,20},{20,16},{24,28},{28,24},{1,5},{5... | collective-permute-start | bytes 6291464 | tf_op jit(solution)/shard_map/ppermute | solution.py:568
  751.2 92.3 %collective-permute-start.30 = (bf16[8,64,704]{2,1,0:T(8,128)(2,1)}, bf16[8,64,704]{2,1,0:T(8,128)(2,1)}, u32[]{:S(2)}, u32[]{:S(2)}) collective-permute-start(bf16[8,64,704]{2,1,0:T(8,128)(2,1)} %fusion.12), channel_id=1, source_target_pairs={{0,1},{1,2},{2,3},{3,0},{4,5},{5,6},{6,7},{7,4},{8,9},{9,10},{10,1... | collective-permute-start | bytes 2162696 | tf_op jit(solution)/shard_map/ppermute | solution.py:533
  832.0 21.6 %collective-permute-start.31 = (bf16[8,64,704]{2,1,0:T(8,128)(2,1)S(1)}, bf16[8,64,704]{2,1,0:T(8,128)(2,1)S(1)}, u32[]{:S(2)}, u32[]{:S(2)}) collective-permute-start(bf16[8,64,704]{2,1,0:T(8,128)(2,1)S(1)} %fusion.11), channel_id=1, source_target_pairs={{0,1},{1,2},{2,3},{3,0},{4,5},{5,6},{6,7},{7,4},{8,9},{9,10},{10,1... | collective-permute-start | bytes 2162696 | tf_op jit(solution)/shard_map/ppermute | solution.py:533
  840.1 33.8 %collective-permute-start.27 = (bf16[256,2048]{1,0:T(8,128)(2,1)S(1)}, bf16[256,2048]{1,0:T(8,128)(2,1)S(1)}, u32[]{:S(2)}, u32[]{:S(2)}) collective-permute-start(bf16[256,2048]{1,0:T(8,128)(2,1)S(1)} %get-tuple-element.346), channel_id=1, source_target_pairs={{0,8},{4,12},{8,0},{12,4},{16,24},{20,28},{24,16},{28,20},{1,9},{5... | collective-permute-start | bytes 3145736 | tf_op jit(solution)/shard_map/ppermute | solution.py:568
  841.8 35.6 %collective-permute-start.28 = (bf16[256,2048]{1,0:T(8,128)(2,1)S(1)}, bf16[256,2048]{1,0:T(8,128)(2,1)S(1)}, u32[]{:S(2)}, u32[]{:S(2)}) collective-permute-start(bf16[256,2048]{1,0:T(8,128)(2,1)S(1)} %get-tuple-element.345), channel_id=1, source_target_pairs={{0,16},{4,20},{8,24},{12,28},{16,0},{20,4},{24,8},{28,12},{1,17},{... | collective-permute-start | bytes 3145736 | tf_op jit(solution)/shard_map/ppermute | solution.py:568
  856.4 60.2 %collective-permute-start.32 = (bf16[256,2048]{1,0:T(8,128)(2,1)}, bf16[256,2048]{1,0:T(8,128)(2,1)S(1)}, u32[]{:S(2)}, u32[]{:S(2)}) collective-permute-start(bf16[256,2048]{1,0:T(8,128)(2,1)} %slice.235), channel_id=1, source_target_pairs={{0,8},{4,12},{8,0},{12,4},{16,24},{20,28},{24,16},{28,20},{1,9},{5... | collective-permute-start | bytes 3145736 | tf_op jit(solution)/shard_map/ppermute | solution.py:568
  859.4 57.3 %collective-permute-start.35 = (bf16[256,2048]{1,0:T(8,128)(2,1)}, bf16[256,2048]{1,0:T(8,128)(2,1)}, u32[]{:S(2)}, u32[]{:S(2)}) collective-permute-start(bf16[256,2048]{1,0:T(8,128)(2,1)} %slice.234), channel_id=1, source_target_pairs={{0,16},{4,20},{8,24},{12,28},{16,0},{20,4},{24,8},{28,12},{1,17},{... | collective-permute-start | bytes 3145736 | tf_op jit(solution)/shard_map/ppermute | solution.py:568
  878.7 56.7 %collective-permute-start.33 = (bf16[256,2048]{1,0:T(8,128)(2,1)}, bf16[256,2048]{1,0:T(8,128)(2,1)}, u32[]{:S(2)}, u32[]{:S(2)}) collective-permute-start(bf16[256,2048]{1,0:T(8,128)(2,1)} %add_convert_fusion.4), channel_id=1, source_target_pairs={{0,16},{4,20},{8,24},{12,28},{16,0},{20,4},{24,8},{28,12},{1,17},{... | collective-permute-start | bytes 3145736 | tf_op jit(solution)/shard_map/ppermute | solution.py:568
  881.2 13.9 %collective-permute-start.36 = (bf16[8,64,384]{2,1,0:T(8,128)(2,1)S(1)}, bf16[8,64,384]{2,1,0:T(8,128)(2,1)S(1)}, u32[]{:S(2)}, u32[]{:S(2)}) collective-permute-start(bf16[8,64,384]{2,1,0:T(8,128)(2,1)S(1)} %fusion.41), channel_id=1, source_target_pairs={{0,1},{1,2},{2,3},{3,0},{4,5},{5,6},{6,7},{7,4},{8,9},{9,10},{10,1... | collective-permute-start | bytes 1179656 | tf_op jit(solution)/shard_map/ppermute | solution.py:533
  883.6 20.9 %collective-permute-start.42 = (bf16[1,176,2048]{2,1,0:T(8,128)(2,1)}, bf16[1,176,2048]{2,1,0:T(8,128)(2,1)S(1)}, u32[]{:S(2)}, u32[]{:S(2)}) collective-permute-start(bf16[1,176,2048]{2,1,0:T(8,128)(2,1)} %fusion.37), channel_id=1, source_target_pairs={{0,1},{1,2},{2,3},{3,0},{4,5},{5,6},{6,7},{7,4},{8,9},{9,10},{10,1... | collective-permute-start | bytes 2162696 | tf_op jit(solution)/shard_map/ppermute | solution.py:533
  895.1 40.2 %collective-permute-start.34 = (bf16[256,2048]{1,0:T(8,128)(2,1)}, bf16[256,2048]{1,0:T(8,128)(2,1)}, u32[]{:S(2)}, u32[]{:S(2)}) collective-permute-start(bf16[256,2048]{1,0:T(8,128)(2,1)} %add_convert_fusion.3), channel_id=1, source_target_pairs={{0,8},{4,12},{8,0},{12,4},{16,24},{20,28},{24,16},{28,20},{1,9},{5... | collective-permute-start | bytes 3145736 | tf_op jit(solution)/shard_map/ppermute | solution.py:568
  897.1 54.2 %all-to-all-start.3 = ((bf16[8,2,64,704]{3,2,1,0:T(8,128)(2,1)}), bf16[8,2,64,704]{3,2,1,0:T(8,128)(2,1)S(1)}, u32[]{:S(2)}, u32[]{:S(2)}) async-start(bf16[8,2,64,704]{3,2,1,0:T(8,128)(2,1)} %copy.169), calls=%async_computation.5 | async-start | bytes 3145728 | tf_op jit(solution)/shard_map/all_to_all | solution.py:595
  904.5 10.8 %collective-permute-start.37 = (bf16[8,64,384]{2,1,0:T(8,128)(2,1)S(1)}, bf16[8,64,384]{2,1,0:T(8,128)(2,1)S(1)}, u32[]{:S(2)}, u32[]{:S(2)}) collective-permute-start(bf16[8,64,384]{2,1,0:T(8,128)(2,1)S(1)} %fusion.36), channel_id=1, source_target_pairs={{0,1},{1,2},{2,3},{3,0},{4,5},{5,6},{6,7},{7,4},{8,9},{9,10},{10,1... | collective-permute-start | bytes 1179656 | tf_op jit(solution)/shard_map/ppermute | solution.py:533
  915.3 47.8 %collective-permute-start.43 = (bf16[1,176,2048]{2,1,0:T(8,128)(2,1)}, bf16[1,176,2048]{2,1,0:T(8,128)(2,1)}, u32[]{:S(2)}, u32[]{:S(2)}) collective-permute-start(bf16[1,176,2048]{2,1,0:T(8,128)(2,1)} %fusion.15), channel_id=1, source_target_pairs={{0,1},{1,2},{2,3},{3,0},{4,5},{5,6},{6,7},{7,4},{8,9},{9,10},{10,1... | collective-permute-start | bytes 2162696 | tf_op jit(solution)/shard_map/ppermute | solution.py:533
  916.6 27.1 %collective-permute-start.38 = (bf16[8,64,384]{2,1,0:T(8,128)(2,1)S(1)}, bf16[8,64,384]{2,1,0:T(8,128)(2,1)S(1)}, u32[]{:S(2)}, u32[]{:S(2)}) collective-permute-start(bf16[8,64,384]{2,1,0:T(8,128)(2,1)S(1)} %fusion.35), channel_id=1, source_target_pairs={{0,1},{1,2},{2,3},{3,0},{4,5},{5,6},{6,7},{7,4},{8,9},{9,10},{10,1... | collective-permute-start | bytes 1179656 | tf_op jit(solution)/shard_map/ppermute | solution.py:533
  951.3 13.8 %all-to-all-start.2 = ((bf16[8,64,384]{2,1,0:T(8,128)(2,1)}), bf16[8,64,384]{2,1,0:T(8,128)(2,1)S(1)}, u32[]{:S(2)}, u32[]{:S(2)}) async-start(bf16[8,64,384]{2,1,0:T(8,128)(2,1)} %fusion.34), calls=%async_computation.3 | async-start | bytes 786432 | tf_op jit(solution)/shard_map/all_to_all | solution.py:595
  964.9 36.9 %collective-permute-start.44 = (bf16[1,176,2048]{2,1,0:T(8,128)(2,1)S(1)}, bf16[1,176,2048]{2,1,0:T(8,128)(2,1)}, u32[]{:S(2)}, u32[]{:S(2)}) collective-permute-start(bf16[1,176,2048]{2,1,0:T(8,128)(2,1)S(1)} %fusion.14), channel_id=1, source_target_pairs={{0,1},{1,2},{2,3},{3,0},{4,5},{5,6},{6,7},{7,4},{8,9},{9,10},{10,1... | collective-permute-start | bytes 2162696 | tf_op jit(solution)/shard_map/ppermute | solution.py:533
  966.3 24.6 %collective-permute-start.39 = (bf16[1,64,2048]{2,1,0:T(8,128)(2,1)S(1)}, bf16[1,64,2048]{2,1,0:T(8,128)(2,1)}, u32[]{:S(2)}, u32[]{:S(2)}) collective-permute-start(bf16[1,64,2048]{2,1,0:T(8,128)(2,1)S(1)} %dynamic-slice_bitcast_fusion.3), channel_id=1, source_target_pairs={{0,1},{1,2},{2,3},{3,0},{4,5},{5,6},{6,7},{7,4},{8,9},{9,10},{10,1... | collective-permute-start | bytes 786440 | tf_op jit(solution)/shard_map/ppermute | solution.py:533
  (78 other events, 1257.0 us)
Sparse Core Ops, SparseCore 0:
  9.6 61.8 all-gather.4
  177.9 87.0 all-gather.8
  268.0 89.6 all-gather.6
  669.7 69.6 reduce-scatter.4
  743.2 162.0 reduce-scatter.2

commit v3 on v2

--- a/solution.py
+++ b/solution.py
@@ -114,10 +114,15 @@
 
 
 def backward_kernel(
-    group, bounds_ref, q_ref, k_ref, kt_ref, v_ref, cos_ref, sin_ref, start_ref, o_ref, do_ref,
-    lse_ref, dq_ref, dkv_ref, dk, dv, acc,
+    group, skip, final, bounds_ref, q_ref, k_ref, kt_ref, v_ref, cos_ref, sin_ref, start_ref,
+    o_ref, do_ref, lse_ref, *rest
 ):
-    i = pl.program_id(0)
+    if final:
+        dk_before, dv_before, dq_ref, dkv_ref, dk, dv, acc = rest
+    else:
+        dq_ref, dk, dv, acc = rest
+    step = pl.program_id(0)
+    i = step + skip
     rows = q_ref.shape[1]
     wide = rows * group
     q4 = heads_wide(q_ref[...], group)
@@ -130,10 +135,10 @@
     lse = lse_ref[0]
     acc[...] = jnp.zeros_like(acc)
 
-    @pl.when(i == 0)
+    @pl.when(step == 0)
     def _():
-        dk[...] = jnp.zeros_like(dk)
-        dv[...] = jnp.zeros_like(dv)
+        dk[...] = dk_before[...] if final else jnp.zeros_like(dk)
+        dv[...] = dv_before[...] if final else jnp.zeros_like(dv)
 
     def block(j, masked):
         at = pl.multiple_of(j * BK, BK)
@@ -154,13 +159,15 @@
         dq = acc[:, h * rows : (h + 1) * rows] * (HD**-0.5)
         dq_ref[h * HD : (h + 1) * HD, :] = turned_back(dq, cosine, sine).astype(BF)
 
-    @pl.when(i == pl.num_programs(0) - 1)
-    def _():
-        for part in range(dk.shape[0] // BK):
-            at = pl.ds(part * BK, BK)
-            dk_t = turned_back(dk[at, :].T, cos_ref[:, at], sin_ref[:, at])
-            dkv_ref[:HD, at] = dk_t.astype(BF)
-            dkv_ref[HD:, at] = dv[at, :].T.astype(BF)
+    if final:
+
+        @pl.when(step == pl.num_programs(0) - 1)
+        def _():
+            for part in range(dk.shape[0] // BK):
+                at = pl.ds(part * BK, BK)
+                dk_t = turned_back(dk[at, :].T, cos_ref[:, at], sin_ref[:, at])
+                dkv_ref[:HD, at] = dk_t.astype(BF)
+                dkv_ref[HD:, at] = dv[at, :].T.astype(BF)
 
 
 def whole_spec(shape):
@@ -222,52 +229,62 @@
     )(bounds, projected, projected, cosine, sine, starts)
 
 
-def attend_back(bounds, qt, k, kt, v, cosine, sine, starts, o, do, lse, group):
+def attend_back(
+    bounds, qt, k, kt, v, cosine, sine, starts, o, do, lse, group, skip, blocks, before
+):
     length = k.shape[0]
-    blocks = length // BQ
     senders, _, local = o.shape
     per = local // BQ
-    piece = pl.BlockSpec((1, group * HD, BQ), lambda i, b: (i // per, 0, i % per))
-    line = pl.BlockSpec((1, 1, group * BQ), lambda i, b: (i, 0, 0))
-    flat = pl.BlockSpec((group * HD, BQ), lambda i, b: (0, i))
+    final = before is not None
+    wide = group * HD
+    piece = pl.BlockSpec((1, wide, BQ), lambda i, b: ((i + skip) // per, 0, (i + skip) % per))
+    line = pl.BlockSpec((1, 1, group * BQ), lambda i, b: (i + skip, 0, 0))
+    tall = whole_spec((length, HD))
+    arrays = [qt, k, kt, v, cosine, sine, starts, o, do, lse]
+    in_specs = [
+        pl.BlockSpec((wide, BQ), lambda i, b: (0, i + skip)),
+        tall,
+        whole_spec((HD, length)),
+        tall,
+        whole_spec((HALF, length)),
+        whole_spec((HALF, length)),
+        line,
+        piece,
+        piece,
+        line,
+    ]
+    out_specs = [pl.BlockSpec((wide, BQ), lambda i, b: (0, i))]
+    out_shape = [jax.ShapeDtypeStruct((wide, blocks * BQ), BF)]
+    scratch = [pltpu.VMEM((HD, group * BQ), F32)]
+    if final:
+        arrays += list(before)
+        in_specs += [tall, tall]
+        out_specs += [whole_spec((2 * HD, length))]
+        out_shape += [jax.ShapeDtypeStruct((2 * HD, length), BF)]
+        scratch = [pltpu.VMEM((length, HD), F32), pltpu.VMEM((length, HD), F32)] + scratch
+    else:
+        out_specs += [tall, tall]
+        out_shape += [jax.ShapeDtypeStruct((length, HD), F32)] * 2
     return pl.pallas_call(
-        functools.partial(backward_kernel, group),
-        out_shape=(
-            jax.ShapeDtypeStruct((group * HD, length), BF),
-            jax.ShapeDtypeStruct((2 * HD, length), BF),
-        ),
+        functools.partial(backward_kernel, group, skip, final),
+        out_shape=out_shape,
         grid_spec=pltpu.PrefetchScalarGridSpec(
             num_scalar_prefetch=1,
             grid=(blocks,),
-            in_specs=[
-                flat,
-                whole_spec((length, HD)),
-                whole_spec((HD, length)),
-                whole_spec((length, HD)),
-                whole_spec((HALF, length)),
-                whole_spec((HALF, length)),
-                line,
-                piece,
-                piece,
-                line,
-            ],
-            out_specs=(flat, whole_spec((2 * HD, length))),
-            scratch_shapes=[
-                pltpu.VMEM((length, HD), F32),
-                pltpu.VMEM((length, HD), F32),
-                pltpu.VMEM((HD, group * BQ), F32),
-            ],
+            in_specs=in_specs,
+            out_specs=out_specs,
+            scratch_shapes=scratch,
         ),
         compiler_params=pltpu.CompilerParams(
             dimension_semantics=("arbitrary",), vmem_limit_bytes=VMEM_LIMIT
         ),
         cost_estimate=pl.CostEstimate(
-            flops=50 * group * length * length * HD // 2,
+            flops=25 * group * length * length * HD // 2,
             bytes_accessed=8 * group * length * HD,
-            transcendentals=group * length * length // 4,
+            transcendentals=group * length * length // 8,
         ),
         name="attend_back",
-    )(bounds, qt, k, kt, v, cosine, sine, starts, o, do, lse)
+    )(bounds, *arrays)
 
 
 def project_kernel(cols, x_ref, w_ref, n_ref, p_ref, wt_ref):
@@ -318,7 +335,7 @@
 def ffn_kernel(
     places_ref, first_ref, second_ref, dy_ref, gate_ref, up_ref, down_ref, *rest
 ):
-    act_ref, dg_ref, du_ref, n_ref, y_ref, pa_ref, pb_ref = rest[-7:]
+    act_ref, dg_ref, du_ref, n_ref, ya_ref, yb_ref, pa_ref, pb_ref = rest[-8:]
     which = pl.program_id(0)
     n = jnp.where(which == 0, first_ref[...], second_ref[...])
     n_ref[0] = n
@@ -335,7 +352,9 @@
     act_ref[0] = act
     dg_ref[0] = d_gate
     du_ref[0] = d_up
-    y_ref[0] = dot_f32(act, down_ref[...]).astype(BF)
+    split = ya_ref.shape[-1]
+    ya_ref[0] = dot_f32(act, down_ref[:, :split]).astype(BF)
+    yb_ref[0] = dot_f32(act, down_ref[:, split:]).astype(BF)
     part = lax.dot_general(d_gate, gate_ref[...], across, preferred_element_type=F32)
     part += lax.dot_general(d_up, up_ref[...], across, preferred_element_type=F32)
     part = part.astype(BF)
@@ -372,22 +391,23 @@
     arrays = [first, second, dy_all, gate_w, up_w, down_w]
     aliases = {}
     if kept is not None:
-        in_specs += [pl.BlockSpec(memory_space=pl.ANY)] * 5
+        in_specs += [pl.BlockSpec(memory_space=pl.ANY)] * 6
         arrays += list(kept)
-        aliases = {7 + n: n for n in range(5)}
+        aliases = {7 + n: n for n in range(6)}
     narrow = jax.ShapeDtypeStruct((count, local, hidden), BF)
     broad = jax.ShapeDtypeStruct((count, local, width), BF)
+    part = jax.ShapeDtypeStruct((count, local, width // 2), BF)
     single = jax.ShapeDtypeStruct((local, width), BF)
     outs = pl.pallas_call(
         ffn_kernel,
-        out_shape=(narrow, narrow, narrow, broad, broad, single, single),
+        out_shape=(narrow, narrow, narrow, broad, part, part, single, single),
         grid_spec=pltpu.PrefetchScalarGridSpec(
             num_scalar_prefetch=1,
             grid=(2, tiles),
             in_specs=in_specs,
             out_specs=(
                 at_place(hidden), at_place(hidden), at_place(hidden), at_place(width),
-                at_place(width), ahead, behind,
+                at_place(width // 2), at_place(width // 2), ahead, behind,
             ),
         ),
         input_output_aliases=aliases,
@@ -401,12 +421,324 @@
         ),
         name="ffn",
     )(places, *arrays)
-    return outs[:5], outs[5], outs[6]
+    return outs[:6], outs[6], outs[7]
+
+
+def spread(out_ref, value, per, parts, rows):
+    for s in range(per):
+        for f in range(parts):
+            at = (s * parts + f) * rows
+            out_ref[f, s] = value[at : at + rows].astype(BF)
+
+
+def side_kernel(per, parts, rows, n_ref, d_ref, t_ref):
+    spread(t_ref, dot_f32(n_ref[...].T, d_ref[...]), per, parts, rows)
+
+
+def side_terms(n2, d, count, parts):
+    length, width = n2.shape
+    hidden = d.shape[1]
+    rows = width // (count * parts)
+    per = max(1, 512 // (parts * rows))
+    wide = per * parts * rows
+    return pl.pallas_call(
+        functools.partial(side_kernel, per, parts, rows),
+        out_shape=jax.ShapeDtypeStruct((parts, count, rows, hidden), BF),
+        grid=(width // wide,),
+        in_specs=[
+            pl.BlockSpec((length, wide), lambda i: (0, i)),
+            pl.BlockSpec((length, hidden), lambda i: (0, 0), pipeline_mode=pl.Buffered(1)),
+        ],
+        out_specs=pl.BlockSpec((parts, per, rows, hidden), lambda i: (0, i, 0, 0)),
+        compiler_params=pltpu.CompilerParams(
+            dimension_semantics=("arbitrary",), vmem_limit_bytes=VMEM_LIMIT
+        ),
+        cost_estimate=pl.CostEstimate(
+            flops=2 * length * width * hidden,
+            bytes_accessed=2 * length * (width + 2 * hidden),
+            transcendentals=0,
+        ),
+        name="side_terms",
+    )(n2, d)
+
+
+def down_kernel(a_ref, dy_ref, t_ref, a_t):
+    @pl.when(pl.program_id(0) == 0)
+    def _():
+        a_t[...] = a_ref[...].T
+
+    t_ref[...] = dot_f32(a_t[...], dy_ref[...]).astype(BF)
+
+
+def down_terms_of(act, dy):
+    length, width = dy.shape
+    hidden = act.shape[1]
+    wide = min(512, width)
+    return pl.pallas_call(
+        down_kernel,
+        out_shape=jax.ShapeDtypeStruct((hidden, width), BF),
+        grid=(width // wide,),
+        in_specs=[
+            pl.BlockSpec((length, hidden), lambda i: (0, 0), pipeline_mode=pl.Buffered(1)),
+            pl.BlockSpec((length, wide), lambda i: (0, i)),
+        ],
+        out_specs=pl.BlockSpec((hidden, wide), lambda i: (0, i)),
+        scratch_shapes=[pltpu.VMEM((hidden, length), BF)],
+        compiler_params=pltpu.CompilerParams(
+            dimension_semantics=("arbitrary",), vmem_limit_bytes=VMEM_LIMIT
+        ),
+        cost_estimate=pl.CostEstimate(
+            flops=2 * length * width * hidden,
+            bytes_accessed=2 * length * (width + hidden),
+            transcendentals=0,
+        ),
+        name="down_terms",
+    )(act, dy)
+
+
+def attn_kernel(per, parts, rows, d_ref, n_ref, t_ref):
+    spread(t_ref, dot_f32(d_ref[...], n_ref[...]).T, per, parts, rows)
+
+
+def attn_terms_of(d_t, n1, count, parts):
+    cols, length = d_t.shape
+    width = n1.shape[1]
+    rows = width // (count * parts)
+    per = max(1, 512 // (parts * rows))
+    wide = per * parts * rows
+    return pl.pallas_call(
+        functools.partial(attn_kernel, per, parts, rows),
+        out_shape=jax.ShapeDtypeStruct((parts, count, rows, cols), BF),
+        grid=(width // wide,),
+        in_specs=[
+            pl.BlockSpec((cols, length), lambda i: (0, 0), pipeline_mode=pl.Buffered(1)),
+            pl.BlockSpec((length, wide), lambda i: (0, i)),
+        ],
+        out_specs=pl.BlockSpec((parts, per, rows, cols), lambda i: (0, i, 0, 0)),
+        compiler_params=pltpu.CompilerParams(
+            dimension_semantics=("arbitrary",), vmem_limit_bytes=VMEM_LIMIT
+        ),
+        cost_estimate=pl.CostEstimate(
+            flops=2 * length * width * cols,
+            bytes_accessed=2 * length * (width + cols),
+            transcendentals=0,
+        ),
+        name="attn_terms",
+    )(d_t, n1)
+
+
+def tail_kernel(
+    parts, cols, d_ref, w_ref, x_ref, dh_ref, n_ref, grad_ref, back_ref,
+    even, side_send, side_recv, landing, n_buf, terms, hop_send, hop_recv, last, mid,
+    send, arrive, n_sem, own_sem,
+):
+    me = lax.axis_index("seq")
+    z = lax.axis_index("fsdp")
+    after_z, before_z = (z + 1) % parts, (z + parts - 1) % parts
+    local, width = x_ref.shape
+    half = local // 2
+    low, high = pl.ds(0, half), pl.ds(half, half)
+    barrier = pltpu.get_barrier_semaphore()
+    for bit in (1, 2, 4):
+        pl.semaphore_signal(barrier, inc=1, device_id=(me ^ bit, z), device_id_type=MESH)
+    for other in (after_z, before_z):
+        pl.semaphore_signal(barrier, inc=1, device_id=(me, other), device_id_type=MESH)
+    pl.semaphore_wait(barrier, 5)
+    made = {}
+
+    def start(name, source, target, device):
+        n = len(made)
+        copy = pltpu.make_async_remote_copy(
+            src_ref=source, dst_ref=target, send_sem=send.at[n], recv_sem=arrive.at[n],
+            device_id=device, device_id_type=MESH,
+        )
+        made[name] = copy
+        copy.start()
+
+    def to_bit(name, bit, source, target):
+        start(name, source, target, (me ^ bit, z))
+
+    def arrived(*names):
+        for name in names:
+            made[name].wait_recv()
+
+    chunk = n_buf.shape[2]
+    chunks = width // chunk
+
+    def fetch(i):
+        return pltpu.make_async_copy(
+            n_ref.at[:, pl.ds(i * chunk, chunk)], n_buf.at[i % 2], n_sem.at[i % 2]
+        )
+
+    fetch(0).start()
+    tile = 512
+
+    def product(c, out):
+        at = pl.multiple_of((me ^ c) * local, local)
+        d = d_ref[:, pl.ds(at, local)].T
+
+        def one(t, carry):
+            here = pl.ds(pl.multiple_of(t * tile, tile), tile)
+            out[:, here] = dot_f32(d, w_ref[pl.ds(0, cols), here]).astype(BF)
+            return carry
+
+        lax.fori_loop(0, width // tile, one, 0)
+
+    def chip(pair):
+        product(2 * pair + 1, side_send.at[pair])
+        to_bit("s" + str(pair), 1, side_send.at[pair], side_recv.at[pair])
+        product(2 * pair, even.at[pair])
+
+    def add_side(pair, part):
+        even[pair, part] = (
+            even[pair, part].astype(F32) + side_recv[pair, part].astype(F32)
+        ).astype(BF)
+
+    chip(3)
+    chip(1)
+    arrived("s3")
+    add_side(3, low)
+    to_bit("far_x", 2, even.at[3, low], landing.at[0])
+    add_side(3, high)
+    to_bit("far_y", 4, even.at[3, high], landing.at[1])
+    chip(2)
+    arrived("s1")
+    add_side(1, low)
+    to_bit("first_x", 2, even.at[1, low], landing.at[2])
+    add_side(1, high)
+    chip(0)
+    arrived("s2")
+    add_side(2, high)
+    to_bit("second_y", 4, even.at[2, high], landing.at[3])
+    add_side(2, low)
+
+    count, rows = back_ref.shape[0], back_ref.shape[1]
+    per = chunk // (parts * rows)
+    for i in range(chunks):
+        if i + 1 < chunks:
+            fetch(i + 1).start()
+        fetch(i).wait()
+        value = dot_f32(d_ref[...], n_buf[i % 2]).T
+        for s in range(per):
+            for f in range(parts):
+                at = (s * parts + f) * rows
+                terms[f, i * per + s] = value[at : at + rows].astype(BF)
+    start("r1", terms.at[before_z], hop_recv.at[0], (me, after_z))
+
+    def add_far(pair, part, slot):
+        even[pair, part] = (even[pair, part].astype(F32) + landing[slot].astype(F32)).astype(BF)
+
+    arrived("far_x")
+    add_far(2, low, 0)
+    to_bit("first_y", 4, even.at[2, low], landing.at[4])
+    arrived("far_y")
+    add_far(1, high, 1)
+    to_bit("second_x", 2, even.at[1, high], landing.at[5])
+    arrived("s0")
+    for step in range(1, parts):
+        arrived("r" + str(step))
+        state = hop_recv[step - 1].astype(F32)
+        state = state + terms[(z + 2 * parts - 1 - step) % parts].astype(F32)
+        if step < parts - 1:
+            hop_send[step - 1] = state.astype(BF)
+            start("r" + str(step + 1), hop_send.at[step - 1], hop_recv.at[step], (me, after_z))
+        else:
+            last[...] = state.astype(BF)
+
+    mine = pltpu.make_async_copy(last.at[me], back_ref.at[me], own_sem.at[0])
+    mine.start()
+    to_bit("b3", 2, last.at[me ^ 6], mid.at[4])
+    to_bit("a2", 1, last.at[me ^ 3], mid.at[1])
+    to_bit("a4", 1, last.at[me ^ 7], mid.at[3])
+    to_bit("a3", 1, last.at[me ^ 5], mid.at[2])
+    to_bit("a1", 1, last.at[me ^ 1], back_ref.at[me])
+    to_bit("b1", 2, last.at[me ^ 2], back_ref.at[me])
+    to_bit("c1", 4, last.at[me ^ 4], back_ref.at[me])
+    arrived("a4", "a2", "a3")
+    to_bit("b4", 2, mid.at[3], mid.at[5])
+    to_bit("b2", 2, mid.at[1], back_ref.at[me ^ 1])
+    to_bit("c2", 4, mid.at[2], back_ref.at[me ^ 1])
+    arrived("b3")
+    to_bit("c3", 4, mid.at[4], back_ref.at[me ^ 2])
+    arrived("b4")
+    to_bit("c4", 4, mid.at[5], back_ref.at[me ^ 3])
+
+    arrived("first_x", "second_y", "first_y", "second_x")
+    gain = w_ref[pl.ds(cols, 8), :].astype(F32)[0:1]
+    tall = 64
+
+    def finish(first_slot, second_slot, offset):
+        def one(t, carry):
+            from_half = pl.ds(pl.multiple_of(t * tall, tall), tall)
+            at = pl.ds(pl.multiple_of(t * tall + offset, tall), tall)
+            dn = even[0, at].astype(F32) + side_recv[0, at].astype(F32)
+            dn = dn + landing[first_slot, from_half].astype(F32)
+            dn = dn + landing[second_slot, from_half].astype(F32)
+            x = x_ref[at].astype(F32)
+            r = lax.rsqrt(jnp.mean(x * x, axis=-1, keepdims=True) + EPS)
+            m = x * r
+            e = dn * gain
+            inner = jnp.mean(e * m, axis=-1, keepdims=True)
+            grad_ref[at] = dh_ref[at] + r * (e - m * inner)
+            return carry
+
+        lax.fori_loop(0, half // tall, one, 0)
+
+    finish(2, 4, 0)
+    finish(3, 5, half)
+    arrived("a1", "b1", "c1", "b2", "c2", "c3", "c4")
+    mine.wait()
+    for copy in made.values():
+        copy.wait_send()
+
+
+def tail(d_t, wt_ext, x, dh1, n1, cols, count, parts):
+    local, width = x.shape
+    length = n1.shape[0]
+    rows = width // (count * parts)
+    half = local // 2
+    chunk = 512
+    anyspace = pl.BlockSpec(memory_space=pl.ANY)
+    vmem = pl.BlockSpec(memory_space=pltpu.VMEM)
+    copies = 4 + 6 + parts - 1 + 12
+    block = (count, rows, cols)
+    return pl.pallas_call(
+        functools.partial(tail_kernel, parts, cols),
+        out_shape=(
+            jax.ShapeDtypeStruct((local, width), F32),
+            jax.ShapeDtypeStruct(block, BF),
+        ),
+        in_specs=[vmem, vmem, vmem, vmem, anyspace],
+        out_specs=(vmem, anyspace),
+        scratch_shapes=[
+            pltpu.VMEM((4, local, width), BF),
+            pltpu.VMEM((4, local, width), BF),
+            pltpu.VMEM((4, local, width), BF),
+            pltpu.VMEM((6, half, width), BF),
+            pltpu.VMEM((2, length, chunk), BF),
+            pltpu.VMEM((parts,) + block, BF),
+            pltpu.VMEM((max(1, parts - 2),) + block, BF),
+            pltpu.VMEM((parts - 1,) + block, BF),
+            pltpu.VMEM(block, BF),
+            pltpu.VMEM((6, rows, cols), BF),
+            pltpu.SemaphoreType.DMA((copies,)),
+            pltpu.SemaphoreType.DMA((copies,)),
+            pltpu.SemaphoreType.DMA((2,)),
+            pltpu.SemaphoreType.DMA((1,)),
+        ],
+        compiler_params=pltpu.CompilerParams(
+            collective_id=1, has_side_effects=True, vmem_limit_bytes=62 * 1024 * 1024
+        ),
+        cost_estimate=pl.CostEstimate(
+            flops=1 << 30, bytes_accessed=1 << 20, transcendentals=0
+        ),
+        name="tail",
+    )(d_t, wt_ext, x, dh1, n1)
 
 
 def start_kernel(
-    count, parts, x_ref, attn_ref, ffn_ref, x_all, attn_all, ffn_all, attn_mid, ffn_mid,
-    send, arrive, local_sem,
+    parts, x_ref, attn_ref, ffn_ref, out_ref, down_ref, x_all, attn_all, ffn_mine, out_all,
+    down_all, attn_mid, ffn_mid, send, arrive, local_sem,
 ):
     me = lax.axis_index("seq")
     z = lax.axis_index("fsdp")
@@ -439,89 +771,111 @@
     held = [
         pltpu.make_async_copy(x_ref, x_all.at[me], local_sem.at[0]),
         pltpu.make_async_copy(attn_ref.at[me], attn_all.at[z, me], local_sem.at[1]),
-        pltpu.make_async_copy(ffn_ref.at[me], ffn_all.at[z, me], local_sem.at[2]),
+        pltpu.make_async_copy(ffn_ref.at[me], ffn_mine.at[me], local_sem.at[2]),
+        pltpu.make_async_copy(out_ref, out_all.at[z], local_sem.at[3]),
+        pltpu.make_async_copy(down_ref, down_all.at[z], local_sem.at[4]),
     ]
     for copy in held:
         copy.start()
 
     def swap_first(tag, source, final, mid):
-        to_bit(tag + "b3", 2, source.at[me ^ 6], mid.at[4])
         to_bit(tag + "a2", 1, source.at[me ^ 3], mid.at[1])
         to_bit(tag + "a4", 1, source.at[me ^ 7], mid.at[3])
         to_bit(tag + "a3", 1, source.at[me ^ 5], mid.at[2])
-        to_bit(tag + "a1", 1, source.at[me ^ 1], final.at[z, me])
-        to_bit(tag + "b1", 2, source.at[me ^ 2], final.at[z, me])
-        to_bit(tag + "c1", 4, source.at[me ^ 4], final.at[z, me])
-
-    def swap_rest(tag, final, mid):
-        arrived(tag + "a2", tag + "a4", tag + "a3")
+        to_bit(tag + "a1", 1, source.at[me ^ 1], final.at[me])
+
+    def swap_second(tag, source, final, mid):
+        to_bit(tag + "b3", 2, source.at[me ^ 6], mid.at[4])
+        to_bit(tag + "b1", 2, source.at[me ^ 2], final.at[me])
+        arrived(tag + "a4", tag + "a2")
         to_bit(tag + "b4", 2, mid.at[3], mid.at[5])
-        to_bit(tag + "b2", 2, mid.at[1], final.at[z, me ^ 1])
-        to_bit(tag + "c2", 4, mid.at[2], final.at[z, me ^ 1])
+        to_bit(tag + "b2", 2, mid.at[1], final.at[me ^ 1])
+
+    def swap_third(tag, source, final, mid):
+        to_bit(tag + "c1", 4, source.at[me ^ 4], final.at[me])
+        arrived(tag + "a3")
+        to_bit(tag + "c2", 4, mid.at[2], final.at[me ^ 1])
         arrived(tag + "b3")
-        to_bit(tag + "c3", 4, mid.at[4], final.at[z, me ^ 2])
+        to_bit(tag + "c3", 4, mid.at[4], final.at[me ^ 2])
         arrived(tag + "b4")
-        to_bit(tag + "c4", 4, mid.at[5], final.at[z, me ^ 3])
+        to_bit(tag + "c4", 4, mid.at[5], final.at[me ^ 3])
 
     def swap_end(tag):
         arrived(*[tag + n for n in ("a1", "b1", "c1", "b2", "c2", "c3", "c4")])
 
-    swap_first("attn", attn_ref, attn_all, attn_mid)
+    def around(tag, step, whole):
+        if step > 1:
+            arrived(tag + str(step - 1))
+        at = (z + parts + 1 - step) % parts
+        start(tag + str(step), whole.at[at], whole.at[at], (me, after_z))
+
+    attn_sets = (attn_ref, attn_all.at[z], attn_mid)
+    ffn_sets = (ffn_ref, ffn_mine, ffn_mid)
+    start("o1", out_ref, out_all.at[z], (me, after_z))
+    swap_first("attn", *attn_sets)
+    swap_second("attn", *attn_sets)
+    to_bit("x2", 2, x_ref, x_all.at[me])
+    swap_third("attn", *attn_sets)
+    to_bit("x4", 4, x_ref, x_all.at[me])
     to_bit("x1", 1, x_ref, x_all.at[me])
-    to_bit("x2", 2, x_ref, x_all.at[me])
-    to_bit("x4", 4, x_ref, x_all.at[me])
-    swap_rest("attn", attn_all, attn_mid)
-    swap_first("ffn", ffn_ref, ffn_all, ffn_mid)
+    swap_first("ffn", *ffn_sets)
     swap_end("attn")
     held[1].wait()
-    start("z1", attn_all.at[z], attn_all.at[z], (me, after_z))
+    around("z", 1, attn_all)
+    held[4].wait()
+    around("d", 1, down_all)
+    for step in range(2, parts):
+        around("o", step, out_all)
+        around("z", step, attn_all)
     arrived("x2")
     to_bit("x3", 1, x_all.at[me ^ 2], x_all.at[me ^ 2])
     to_bit("f1", 4, x_all.at[me ^ 2, pl.ds(0, half)], x_all.at[me ^ 2, pl.ds(0, half)])
     arrived("x4")
     to_bit("x5", 1, x_all.at[me ^ 4], x_all.at[me ^ 4])
     to_bit("f2", 2, x_all.at[me ^ 4, pl.ds(half, half)], x_all.at[me ^ 4, pl.ds(half, half)])
-    swap_rest("ffn", ffn_all, ffn_mid)
-    for step in range(2, parts):
-        arrived("z" + str(step - 1))
-        at = (z + parts + 1 - step) % parts
-        start("z" + str(step), attn_all.at[at], attn_all.at[at], (me, after_z))
-    swap_end("ffn")
-    held[2].wait()
-    start("zffn", ffn_all.at[z], ffn_all.at[z], (me, after_z))
+    around("d", 2, down_all)
+    swap_second("ffn", *ffn_sets)
+    swap_third("ffn", *ffn_sets)
+    for step in range(3, parts):
+        around("d", step, down_all)
     arrived("f1", "f2")
     to_bit("x7", 1, x_all.at[me ^ 6], x_all.at[me ^ 6])
-    arrived("x1", "x3", "x5", "x7", "z" + str(parts - 1), "zffn")
+    swap_end("ffn")
+    arrived("x1", "x3", "x5", "x7", "z" + str(parts - 1), "o" + str(parts - 1))
+    arrived("d" + str(parts - 1))
     for copy in made.values():
         copy.wait_send()
-    held[0].wait()
-
-
-def start_gather(x, attn_send, ffn_send, count, parts):
+    for copy in (held[0], held[2], held[3]):
+        copy.wait()
+
+
+def start_gather(x, attn_send, ffn_send, w_out, w_down, count, parts):
     anyspace = pl.BlockSpec(memory_space=pl.ANY)
-    copies = 8 + 2 * 12 + parts
+    copies = 8 + 2 * 12 + 3 * (parts - 1)
     shapes = (
         jax.ShapeDtypeStruct((count,) + x.shape, BF),
         jax.ShapeDtypeStruct((parts,) + attn_send.shape, BF),
-        jax.ShapeDtypeStruct((parts,) + ffn_send.shape, BF),
+        jax.ShapeDtypeStruct(ffn_send.shape, BF),
+        jax.ShapeDtypeStruct((parts,) + w_out.shape, BF),
+        jax.ShapeDtypeStruct((parts,) + w_down.shape, BF),
         jax.ShapeDtypeStruct((6,) + attn_send.shape[1:], BF),
         jax.ShapeDtypeStruct((6,) + ffn_send.shape[1:], BF),
     )
     return pl.pallas_call(
-        functools.partial(start_kernel, count, parts),
+        functools.partial(start_kernel, parts),
         out_shape=shapes,
-        in_specs=[anyspace] * 3,
-        out_specs=(anyspace,) * 5,
+        in_specs=[anyspace] * 5,
+        out_specs=(anyspace,) * 7,
         scratch_shapes=[
             pltpu.SemaphoreType.DMA((copies,)),
             pltpu.SemaphoreType.DMA((copies,)),
-            pltpu.SemaphoreType.DMA((3,)),
+            pltpu.SemaphoreType.DMA((5,)),
         ],
         compiler_params=pltpu.CompilerParams(
             collective_id=0, has_side_effects=True, vmem_limit_bytes=8 * 1024 * 1024
         ),
         name="start_gather",
-    )(x, attn_send, ffn_send)[:3]
+    )(x, attn_send, ffn_send, w_out, w_down)[:5]
 
 
 def ring(axis):
@@ -545,17 +899,21 @@
 def term_of(terms, step):
     count = lax.axis_size("fsdp")
     me = lax.axis_index("fsdp")
-    return lax.dynamic_index_in_dim(terms, (me + 2 * count - 1 - step) % count, 1, False)
-
-
-def ring_step(states, terms, step):
-    moved = hop(*[state.astype(BF) for state in states])
+    return lax.dynamic_index_in_dim(terms, (me + 2 * count - 1 - step) % count, 0, False)
+
+
+def launch(states):
+    return hop(*[state.astype(BF) for state in states])
+
+
+def landed(moved, terms, step):
     return [m.astype(F32) + term_of(t, step).astype(F32) for m, t in zip(moved, terms)]
 
 
-def ring_finish(states, terms, step):
-    for n in range(step, lax.axis_size("fsdp")):
-        states = ring_step(states, terms, n)
+def ring_finish(moved, terms, step):
+    states = landed(moved, terms, step)
+    for n in range(step + 1, lax.axis_size("fsdp")):
+        states = landed(launch(states), terms, n)
     return states
 
 
@@ -656,25 +1014,27 @@
     ffn_send = jnp.concatenate(
         [w_gate.reshape(rows, count, hidden), w_up.reshape(rows, count, hidden)], axis=0
     ).transpose(1, 0, 2)
-    down_w = lax.all_gather(w_down, "fsdp", axis=0, tiled=True)
     z = lax.axis_index("fsdp")
     if cube:
-        x_all, attn_all, ffn_all = start_gather(own, attn_send, ffn_send, count, parts)
-        ffn_pieces = [
-            lax.dynamic_index_in_dim(ffn_all, (z + parts - back) % parts, 0, False)
-            for back in range(min(2, parts))
-        ]
+        x_all, attn_all, ffn_part, out_part, down_w = start_gather(
+            own, attn_send, ffn_send, w_out, w_down, count, parts
+        )
     else:
         x_all = lax.all_gather(own, "seq", axis=0, tiled=False)
         attn_all = lax.all_gather(exchange(attn_send), "fsdp", axis=0, tiled=False)
-        ffn_pieces = [exchange(ffn_send)]
+        ffn_part = exchange(ffn_send)
+        out_part = lax.all_gather(w_out, "fsdp", axis=0, tiled=False)
+        down_w = lax.all_gather(w_down, "fsdp", axis=0, tiled=False)
+    down_w = down_w.reshape(hidden, width)
     dy = cotangent[0]
-    own, x_all, attn_all, ffn_pieces, dy = fence(own, x_all, attn_all, ffn_pieces, dy)
-    ffn_pieces = [piece.reshape(count, 2, rows, hidden) for piece in ffn_pieces]
+    own, x_all, attn_all, ffn_part, out_part, dy = fence(
+        own, x_all, attn_all, ffn_part, out_part, dy
+    )
+    ffn_pieces = [[ffn_part.reshape(count, 2, rows, hidden)]]
 
     dy_all = lax.all_gather(dy, "seq", axis=0, tiled=False)
     if len(ffn_pieces) < parts:
-        ffn_pieces += hop(ffn_pieces[-1])
+        ffn_pieces.append(hop(*ffn_pieces[-1]))
     flags = lax.dynamic_index_in_dim(attn_all, z, 0, False)
     flags = flags[:, :, attn_cols + 2 : attn_cols + 2 + flag_cols].reshape(length)
     last = document_starts(flags)
@@ -696,14 +1056,14 @@
     attn_t = wt_ext[:attn_cols]
     gain_one = wt_ext[attn_cols].astype(F32)
     gain_two = wt_ext[attn_cols + 1].astype(F32)
-    projected, cosine, sine, starts, bounds, ffn_last, w_out, down_w = fence(
-        projected, cosine, sine, starts, bounds, ffn_pieces[-1], w_out, down_w
+    projected, cosine, sine, starts, bounds, ffn_last, out_part = fence(
+        projected, cosine, sine, starts, bounds, ffn_pieces[-1], out_part
     )
     ffn_pieces[-1] = ffn_last
 
-    out_w = lax.all_gather(w_out, ("seq", "fsdp"), axis=0, tiled=True)
+    out_w = lax.all_gather(out_part.reshape(parts * rows, width), "seq", axis=0, tiled=True)
     if len(ffn_pieces) < parts:
-        ffn_pieces += hop(ffn_pieces[-1])
+        ffn_pieces.append(hop(*ffn_pieces[-1]))
     o_heads, lse, q_t, k_t, k_n, v_n = attend(
         bounds, projected, cosine, sine, starts, group, count, local
     )
@@ -713,11 +1073,11 @@
     ffn_pieces[-1] = ffn_last
 
     while len(ffn_pieces) < parts:
-        ffn_pieces += hop(ffn_pieces[-1])
+        ffn_pieces.append(hop(*ffn_pieces[-1]))
     o_t = exchange(o_heads).reshape(count * group_width, local)
     o_t, ffn_pieces = fence(o_t, ffn_pieces)
 
-    ffn_w = collect(ffn_pieces, "fsdp").transpose(2, 1, 0, 3, 4).reshape(2, width, hidden)
+    ffn_w = collect([piece[0] for piece in ffn_pieces], "fsdp").transpose(2, 1, 0, 3, 4).reshape(2, width, hidden)
     gate_w, up_w = ffn_w[0], ffn_w[1]
     x = own.astype(F32)
     r1 = lax.rsqrt(jnp.mean(x * x, axis=-1, keepdims=True) + EPS)
@@ -726,6 +1086,10 @@
     n2 = (h1 * r2 * gain_two).astype(BF)
     n2, h1, r2 = fence(n2, h1, r2)
 
+    def over_seq(part):
+        whole = part.reshape(-1, part.shape[-1])
+        return lax.psum_scatter(whole, "seq", scatter_dimension=0, tiled=True)
+
     kept = None
 
     def chunk(kept, first, second, c):
@@ -757,19 +1121,21 @@
         kept, far_one, far_two, x_first, y_second, y_sum = fence(
             kept, far_one, far_two, x_first, y_second, y_sum
         )
-        act, d_gate, d_up, n2_all, y_part = kept
+        act, d_gate, d_up, n2_all, y_one, y_two = kept
         n2_all, dy_rows = n2_all.reshape(sheet), dy_all.reshape(sheet)
         act, d_gate, d_up = [a.reshape(length, hidden) for a in (act, d_gate, d_up)]
 
         far_sum = chip_sum(far_one, far_two).astype(BF)
         x_far, y_far = swap(far_sum[:half], 2), swap(far_sum[half:], 4)
-        term_gate = jnp.einsum("td,tf->df", n2_all, d_gate, preferred_element_type=F32)
-        x_far, y_far, term_gate = fence(x_far, y_far, term_gate)
+        gate_t = side_terms(n2_all, d_gate, count, parts)
+        x_far, y_far, gate_t, y_one = fence(x_far, y_far, gate_t, y_one)
 
         x_second = swap((x_sum[half:] + y_far.astype(F32)).astype(BF), 2)
         y_first = swap((y_sum[:half] + x_far.astype(F32)).astype(BF), 4)
-        term_up = jnp.einsum("td,tf->df", n2_all, d_up, preferred_element_type=F32)
-        x_second, y_first, term_up = fence(x_second, y_first, term_up)
+        (gate_moved,) = launch([term_of(gate_t, 0)])
+        y_one = over_seq(y_one)
+        up_t = side_terms(n2_all, d_up, count, parts)
+        x_second, y_first, up_t, gate_moved, act = fence(x_second, y_first, up_t, gate_moved, act)
         own_sum = own_a.astype(F32) + own_c.astype(F32)
         first = own_sum[:half] + x_first.astype(F32) + y_first.astype(F32)
         second = own_sum[half:] + x_second.astype(F32) + y_second.astype(F32)
@@ -780,43 +1146,62 @@
         for c in range(0, count, 2):
             kept, part_a, part_b = chunk(kept, n2_blocks[c], n2_blocks[c + 1], c)
             dn2_parts += [part_a, part_b]
-        act, d_gate, d_up, n2_all, y_part = kept
+        act, d_gate, d_up, n2_all, y_one, y_two = kept
         n2_all, dy_rows = n2_all.reshape(sheet), dy_all.reshape(sheet)
         act, d_gate, d_up = [a.reshape(length, hidden) for a in (act, d_gate, d_up)]
         dn2 = scatter_plain(dn2_parts)
-        term_gate = jnp.einsum("td,tf->df", n2_all, d_gate, preferred_element_type=F32)
-        term_up = jnp.einsum("td,tf->df", n2_all, d_up, preferred_element_type=F32)
-    y_part = y_part.reshape(sheet)
+        gate_t = side_terms(n2_all, d_gate, count, parts)
+        up_t = side_terms(n2_all, d_up, count, parts)
+        (gate_moved,) = launch([term_of(gate_t, 0)])
+        y_one = over_seq(y_one)
 
     m2 = h1 * r2
     e2 = dn2 * gain_two
     dh1 = dy.astype(F32) + r2 * (e2 - m2 * jnp.mean(e2 * m2, axis=-1, keepdims=True))
     db = dh1.astype(BF)
     do_t = jnp.einsum("ed,td->et", out_w, db, preferred_element_type=F32).astype(BF)
-    do_t, db, dh1, term_gate, term_up, y_part = fence(
-        do_t, db, dh1, term_gate, term_up, y_part
-    )
-    y = lax.psum_scatter(y_part, "seq", scatter_dimension=0, tiled=True)
-    gate_up = [
-        term_gate.reshape(count, parts, rows, hidden),
-        term_up.reshape(count, parts, rows, hidden),
-    ]
-    moved = hop(*[term_of(term, 0).astype(BF) for term in gate_up])
+    (up_moved,) = launch([term_of(up_t, 0)])
+    (gate_state,) = landed([gate_moved], [gate_t], 1)
+    if parts > 2:
+        (gate_moved,) = launch([gate_state])
+    do_t, db, dh1, up_moved, gate_moved, gate_state = fence(
+        do_t, db, dh1, up_moved, gate_moved, gate_state
+    )
     do_heads = exchange(do_t.reshape(count, group_width, local))
     term_out = dot_f32(o_t, db).astype(BF)
-    do_heads, term_out, moved = fence(do_heads, term_out, moved)
-
-    part_out = lax.psum_scatter(term_out, "seq", scatter_dimension=0, tiled=True)
-    states = [m.astype(F32) + term_of(t, 1) for m, t in zip(moved, gate_up)]
+    term_down = down_terms_of(act, dy_rows).reshape(parts, hidden // parts, width)
+    (up_state,) = landed([up_moved], [up_t], 1)
     if parts > 2:
-        moved = hop(*[state.astype(BF) for state in states])
-    dq_t, dkv_t = attend_back(
-        bounds, q_t, k_n, k_t, v_n, cosine, sine, starts, o_heads, do_heads, lse, group
-    )
-    dq_t, dkv_t, moved, states, act = fence(dq_t, dkv_t, moved, states, act)
-
-    d_t = jnp.concatenate([dq_t, dkv_t], axis=0)
-
+        (up_moved,) = launch([up_state])
+    do_heads, term_out, term_down, y_one, up_moved, up_state = fence(
+        do_heads, term_out, term_down, y_one, up_moved, up_state
+    )
+
+    part_out = over_seq(term_out)
+    pair_t = [gate_t, up_t]
+    pair = [gate_state, up_state]
+    if parts > 2:
+        pair = landed([gate_moved, up_moved], pair_t, 2)
+    moved = launch((pair if parts > 3 else []) + [term_of(term_down, 0)])
+    cut = blocks * 11 // 16
+    saved = (bounds, q_t, k_n, k_t, v_n, cosine, sine, starts, o_heads, do_heads, lse, group)
+    dq_one, dk, dv = attend_back(*saved, 0, cut, None)
+    dq_one, dk, dv, moved, pair, do_heads, y_two, part_out = fence(
+        dq_one, dk, dv, moved, pair, do_heads, y_two, part_out
+    )
+    y_two = over_seq(y_two)
+    down_state = landed(moved[-1:], [term_down], 1)
+    if parts > 3:
+        pair = ring_finish(moved[:2], pair_t, 3)
+    ffn_back = exchange(jnp.stack(pair, axis=1).astype(BF))
+    moved = launch(down_state if parts > 2 else [])
+    saved = (bounds, q_t, k_n, k_t, v_n, cosine, sine, starts, o_heads, do_heads, lse, group)
+    dq_two, dkv_t = attend_back(*saved, cut, blocks - cut, (dk, dv))
+    dq_two, dkv_t, moved, down_state, part_out, ffn_back = fence(
+        dq_two, dkv_t, moved, down_state, part_out, ffn_back
+    )
+
+    d_t = jnp.concatenate([jnp.concatenate([dq_one, dq_two], axis=1), dkv_t], axis=0)
     def pair_of(c):
         return jnp.concatenate(
             [lax.dynamic_slice_in_dim(d_t, (me ^ n) * local, local, 1) for n in (c, c + 1)], axis=1
@@ -826,54 +1211,33 @@
         part = jnp.einsum("et,ed->td", pair_of(c), attn_t, preferred_element_type=F32).astype(BF)
         return part[:local], part[local:]
 
-    term_down = jnp.einsum("tf,td->fd", act, dy_rows, preferred_element_type=F32)
+    n1_rows = n1_all.reshape(sheet)
     if parts > 2:
-        states = [m.astype(F32) + term_of(t, 2) for m, t in zip(moved, gate_up)]
+        down_state = landed(moved, [term_down], 2)
+    moved = launch(down_state if parts > 3 else [])
+    grad_out = lax.psum_scatter(part_out, "fsdp", scatter_dimension=0, tiled=True).astype(F32)
     if cube:
-        far_sum = chip_sum(*dn1_chunk(6)).astype(BF)
-        x_sum = chip_sum(*dn1_chunk(2))
-        y_sum = chip_sum(*dn1_chunk(4))
-        far_sum, x_sum, y_sum = fence(far_sum, x_sum, y_sum)
-        x_far, y_far = swap(far_sum[:half], 2), swap(far_sum[half:], 4)
-        x_first = swap(x_sum[:half].astype(BF), 2)
-        y_second = swap(y_sum[half:].astype(BF), 4)
-        own_sum = chip_sum(*dn1_chunk(0))
-        term_attn = jnp.einsum(
-            "td,et->de", n1_all.reshape(sheet), d_t, preferred_element_type=F32
-        )
-        states = ring_finish(states, gate_up, 3)
-        x_far, y_far, own_sum, term_attn, states, term_down = fence(
-            x_far, y_far, own_sum, term_attn, states, term_down
-        )
-        x_second = swap((x_sum[half:] + y_far.astype(F32)).astype(BF), 2)
-        y_first = swap((y_sum[:half] + x_far.astype(F32)).astype(BF), 4)
-        first = own_sum[:half] + x_first.astype(F32) + y_first.astype(F32)
-        second = own_sum[half:] + x_second.astype(F32) + y_second.astype(F32)
-        dn1 = jnp.concatenate([first, second], axis=0)
+        grad_tokens, attn_back = tail(d_t, wt_ext, own, dh1, n1_rows, attn_cols, count, parts)
     else:
         dn1 = scatter_plain([piece for c in range(0, count, 2) for piece in dn1_chunk(c)])
-        term_attn = jnp.einsum(
-            "td,et->de", n1_all.reshape(sheet), d_t, preferred_element_type=F32
-        )
-        states = ring_finish(states, gate_up, 3)
-    part_gate, part_up = states
-    output = (h1 + y.astype(F32)).astype(BF)
-    down_terms = [term_down.reshape(1, parts, hidden // parts, width)]
-    (grad_down,) = ring_finish([term_of(down_terms[0], 0)], down_terms, 1)
-    grad_down = grad_down.reshape(hidden // parts, width)
-    attn_terms = [term_attn.reshape(count, parts, rows, attn_cols)]
-    (part_attn,) = ring_finish([term_of(attn_terms[0], 0)], attn_terms, 1)
-    out_terms = [part_out.reshape(1, parts, rows, width)]
-    (grad_out,) = ring_finish([term_of(out_terms[0], 0)], out_terms, 1)
-    grad_out = grad_out.reshape(rows, width)
-    m1 = x * r1
-    e1 = dn1 * gain_one
-    grad_tokens = dh1 + r1 * (e1 - m1 * jnp.mean(e1 * m1, axis=-1, keepdims=True))
-
-    ffn_back = exchange(jnp.stack([part_gate, part_up], axis=1).astype(BF)).astype(F32)
+        attn_terms = [attn_terms_of(d_t, n1_rows, count, parts)]
+        (part_attn,) = ring_finish(launch([term_of(attn_terms[0], 0)]), attn_terms, 1)
+        attn_back = exchange(part_attn.astype(BF))
+        m1 = x * r1
+        e1 = dn1 * gain_one
+        grad_tokens = dh1 + r1 * (e1 - m1 * jnp.mean(e1 * m1, axis=-1, keepdims=True))
+    grad_tokens, attn_back, moved, ffn_back, y_one, y_two, grad_out = fence(
+        grad_tokens, attn_back, moved, ffn_back, y_one, y_two, grad_out
+    )
+    if parts > 3:
+        down_state = ring_finish(moved, [term_down], 3)
+    grad_down = down_state[0].reshape(hidden // parts, width)
+    output = (h1 + jnp.concatenate([y_one, y_two], axis=1).astype(F32)).astype(BF)
+
+    ffn_back = ffn_back.astype(F32)
     grad_gate = ffn_back[:, 0].transpose(1, 0, 2).reshape(rows, count * hidden)
     grad_up = ffn_back[:, 1].transpose(1, 0, 2).reshape(rows, count * hidden)
-    attn_back = exchange(part_attn.astype(BF)).astype(F32)
+    attn_back = attn_back.astype(F32)
     grad_query = attn_back[:, :, :group_width].transpose(1, 0, 2).reshape(rows, H * HD)
     pair = attn_back[:, :, group_width:].reshape(KV, share, rows, 2 * HD).sum(axis=1)
     grad_key = pair[:, :, :HD].transpose(1, 0, 2).reshape(rows, KV * HD)

time: 1030 us -> 936 us (0.909)
  Pallas kernels: 376 us -> 542 us
  waiting for transfers between devices: 257 us -> 169 us
  matrix products: 98.4 us -> 26.7 us
  local copies, waits for them, and re-layouts: 92.9 us -> 57.6 us
  starting transfers between devices: 91.9 us -> 57.4 us
  other arithmetic: 91 us -> 62.2 us
    pallas_call x6 -> x11, Pallas kernels: 322 us -> 488 us  [the longest x1 142 us: tail(): pl.pallas_call(functools.partial(tail_kernel, parts, cols), out_shape=(ja...]
    dot_general x8 -> x0, matrix products: 73.1 us -> none  [the longest x1 18 us: body(): term_up = jnp.einsum('td,tf->df', n2_all, d_up, preferred_element_type=F32)]
    all_to_all x4 -> x3, waiting for transfers between devices: 32.7 us -> 1.11 us  [exchange(): return lax.all_to_all(array, 'seq', split_axis=0, concat_axis=0, tiled=True)]
    all_gather x2 -> x1, waiting for transfers between devices: 59.8 us -> 30.1 us  [body(): lax.all_gather(out_part.reshape(parts * rows, width), 'seq', axis=0, tile...]
    ppermute x28 -> x18, waiting for transfers between devices: 57.6 us -> 30 us  [swap(): return lax.ppermute(block, 'seq', [(n, n ^ bit) for n in range(count)])]
    reduce_scatter x2 -> x4, waiting for transfers between devices: 0.02 us -> 23.7 us  [the longest x3 23.7 us: over_seq(): return lax.psum_scatter(whole, 'seq', scatter_dimension=0, tiled=True)]
    ppermute x17 -> x12, waiting for transfers between devices: 89.8 us -> 68.5 us  [hop(): return [lax.ppermute(block, 'fsdp', ring('fsdp')) for block in blocks]]
    ppermute x17 -> x12, starting transfers between devices: 54.6 us -> 34 us  [hop(): return [lax.ppermute(block, 'fsdp', ring('fsdp')) for block in blocks]]
  transfers between devices with their start and end apart: 54 -> 39, of which waited for: 26 -> 19; matrix products, arithmetic and copies ran while one was open for 21% -> 9% of each run, Pallas kernels for 37% -> 47%
where the time goes in v3:
time: 936 us; the launch traced here: 931 us
  Pallas kernels  542 us (58%)
  waiting for transfers between devices  169 us (18%)
  other arithmetic  62.2 us (7%)
  local copies, waits for them, and re-layouts  57.6 us (6%)
  starting transfers between devices  57.4 us (6%)
  matrix products  26.7 us (3%)
  between operations  15.6 us (2%)
    pallas_call x1, Pallas kernels, tail(): pl.pallas_call(functools.partial(tail_kernel, parts, cols), out_shape=(ja...  142 us
    pallas_call x4, Pallas kernels, ffn_chunk(): pl.pallas_call(ffn_kernel, out_shape=(narrow, narrow, narrow, broad, part...  125 us
    pallas_call x1, Pallas kernels, start_gather(): pl.pallas_call(functools.partial(start_kernel, parts), out_shape=shapes,...  109 us
    ppermute x12, waiting for transfers between devices, hop(): return [lax.ppermute(block, 'fsdp', ring('fsdp')) for block in blocks]  68.5 us
    pallas_call x2, Pallas kernels, attend_back(): pl.pallas_call(functools.partial(backward_kernel, group, skip, final), ou...  52.2 us
    pallas_call x2, Pallas kernels, side_terms(): pl.pallas_call(functools.partial(side_kernel, per, parts, rows), out_shap...  39.8 us
    pallas_call x1, Pallas kernels, attend(): pl.pallas_call(functools.partial(forward_kernel, group), out_shape=(jax.S...  35.8 us
    ppermute x12, starting transfers between devices, hop(): return [lax.ppermute(block, 'fsdp', ring('fsdp')) for block in blocks]  34 us
  transfers between devices with their start and end apart: 39, of which 19 were waited for; matrix products, arithmetic and copies ran while one was open for 9% of the time, Pallas kernels for 47%

profile of v3, /device:TPU:0, one launch (start us, length us, event | category | flops | bytes accessed | tf_op | source)
XLA Modules:
  0.0 931.2 jit_solution(10274416019189148940)
XLA Ops:
  17.4 109.1 %start_gather.1 = (bf16[8,512,2048]{2,1,0:T(8,128)(2,1)S(1)}, bf16[4,8,64,512]{3,2,1,0:T(8,128)(2,1)S(1)}, bf16[8,128,704]{2,1,0:T(8,128)(2,1)S(1)}, bf16[4,64,2...) custom-call(bf16[512,2048]{1,0:T(8,128)(2,1)S(1)} %bitcast.136, ...), custom_call_target="tpu_custom_call" | custom-call | tf_op jit(solution)/shard_map/start_gather/pallas_call | solution.py:864
  130.5 5.8 copy-done.8
  136.4 2.9 copy.123
  146.7 18.3 %project.1 = (bf16[8,512,2048]{2,1,0:T(8,128)(2,1)}, f32[384,4096]{1,0:T(8,128)}, bf16[512,2048]{1,0:T(8,128)(2,1)}) custom-call(bf16[8,512,2048]{2,1,0:T(8,128)(2,1)} %copy-done.8, bf16[2048,512]{1,0:T(8,128)(2,1)} %bitcast.169), custom_call_target="tpu_custom_call" | custom-call | flops 6442450944 | bytes 33554432 | tf_op jit(solution)/shard_map/project/pallas_call | solution.py:309
  165.1 2.8 multiply_sine_fusion
  167.8 5.1 collective-permute-done
  173.8 35.8 %attend.1 = (bf16[8,256,512]{2,1,0:T(8,128)(2,1)}, f32[16,1,1024]{2,1,0:T(1,128)}, bf16[256,4096]{1,0:T(8,128)(2,1)}, bf16[64,4096]{1,0:T(8,128)(2,1)}, bf16[409...) custom-call(s32[16,4]{1,0:T(8,128)} %copy.124.bounds_ref, f32[384,4096]{1,0:T(8,128)} %get-tuple-element.200.q_ref.kv_ref, ...), custom_call_target="tpu_custom_call" | custom-call | flops 85899345920 | bytes 8388608 | tf_op jit(solution)/shard_map/attend/pallas_call | solution.py:185
  209.6 15.1 %all-gather.6.cloned.1.call-done = bf16[4096,2048]{1,0:T(8,128)(2,1)} async-done(((bf16[512,2048]{1,0:T(8,128)(2,1)}), bf16[4096,2048]{1,0:T(8,128)(2,1)}) %all-gather.6.cloned.1.call-update) | async-done | bytes 16777232 | tf_op jit(solution)/shard_map/all_gather | solution.py:1035
  224.7 4.3 all-to-all-start
  231.4 36.4 %collective-permute-done.2 = bf16[8,2,64,704]{3,2,0,1:T(8,128)(2,1)} collective-permute-done((bf16[8,2,64,704]{3,2,0,1:T(8,128)(2,1)}, bf16[8,2,64,704]{3,2,0,1:T(8,128)(2,1)}, u32[]{:S(2)}, u32[]{:S(2)}) %collective-permute-start.2) | collective-permute-done | bytes 1441824 | tf_op jit(solution)/shard_map/ppermute | solution.py:887
  267.8 30.1 %all-gather.4.cloned.1.call-done = bf16[2048,2048]{1,0:T(8,128)(2,1)} async-done(((bf16[256,2048]{1,0:T(8,128)(2,1)}), bf16[2048,2048]{1,0:T(8,128)(2,1)}) %all-gather.4.cloned.1.call-update) | async-done | bytes 8388624 | tf_op jit(solution)/shard_map/all_gather | solution.py:1064
  298.0 7.8 multiply_reduce_fusion.1
  317.1 3.0 fusion.30
  320.2 31.4 %ffn.4 = (bf16[8,512,704]{2,1,0:T(8,128)(2,1)}, bf16[8,512,704]{2,1,0:T(8,128)(2,1)}, bf16[8,512,704]{2,1,0:T(8,128)(2,1)}, bf16[8,512,2048]{2,1,0:T(8,128)(2,1)...) custom-call(s32[2]{0:T(128)} %get-tuple-element.389.places_ref, ...), custom_call_target="tpu_custom_call" | custom-call | flops 17716740096 | bytes 29622272 | tf_op jit(solution)/shard_map/ffn/pallas_call | solution.py:401
  351.5 5.9 collective-permute-done.4.first_ref
  362.9 3.1 collective-permute-done.6.second_ref
  368.4 31.1 %ffn.5 = (bf16[8,512,704]{2,1,0:T(8,128)(2,1)}, bf16[8,512,704]{2,1,0:T(8,128)(2,1)}, bf16[8,512,704]{2,1,0:T(8,128)(2,1)}, bf16[8,512,2048]{2,1,0:T(8,128)(2,1)...) custom-call(s32[2]{0:T(128)} %get-tuple-element.390.places_ref, ...), custom_call_target="tpu_custom_call", output_to_operand_aliasing={{0}: (7, {}), {1}: (8, {}), {2}: (9, {}), {3}: (10, {}), {4... | custom-call | flops 17716740096 | bytes 29622272 | tf_op jit(solution)/shard_map/ffn/pallas_call | solution.py:401
  400.4 31.5 %ffn.6 = (bf16[8,512,704]{2,1,0:T(8,128)(2,1)}, bf16[8,512,704]{2,1,0:T(8,128)(2,1)}, bf16[8,512,704]{2,1,0:T(8,128)(2,1)}, bf16[8,512,2048]{2,1,0:T(8,128)(2,1)...) custom-call(s32[2]{0:T(128)} %get-tuple-element.392.places_ref, ...), custom_call_target="tpu_custom_call", output_to_operand_aliasing={{0}: (7, {}), {1}: (8, {}), {2}: (9, {}), {3}: (10, {}), {4... | custom-call | flops 17716740096 | bytes 29622272 | tf_op jit(solution)/shard_map/ffn/pallas_call | solution.py:401
  431.9 2.5 convert_add_fusion.1
  442.3 31.3 %ffn.7 = (bf16[8,512,704]{2,1,0:T(8,128)(2,1)}, bf16[8,512,704]{2,1,0:T(8,128)(2,1)}, bf16[8,512,704]{2,1,0:T(8,128)(2,1)}, bf16[8,512,2048]{2,1,0:T(8,128)(2,1)...) custom-call(s32[2]{0:T(128)} %get-tuple-element.391.places_ref, ...), custom_call_target="tpu_custom_call", output_to_operand_aliasing={{0}: (7, {}), {1}: (8, {}), {2}: (9, {}), {3}: (10, {}), {4... | custom-call | flops 17716740096 | bytes 29622272 | tf_op jit(solution)/shard_map/ffn/pallas_call | solution.py:401
  473.8 4.3 collective-permute-done.16
  482.7 19.2 %side_terms.2 = bf16[4,8,64,704]{3,2,1,0:T(8,128)(2,1)} custom-call(bf16[4096,2048]{1,0:T(8,128)(2,1)} %bitcast.145, bf16[4096,704]{1,0:T(8,128)(2,1)} %bitcast.150), custom_call_target="tpu_custom_call" | custom-call | flops 11811160064 | bytes 28311552 | tf_op jit(solution)/shard_map/side_terms/pallas_call | solution.py:444
  502.0 4.0 collective-permute-done.17
  513.6 2.7 add_convert_fusion.2
  519.8 20.6 %side_terms.3 = bf16[4,8,64,704]{3,2,1,0:T(8,128)(2,1)} custom-call(bf16[4096,2048]{1,0:T(8,128)(2,1)} %bitcast.146, bf16[4096,704]{1,0:T(8,128)(2,1)} %bitcast.151), custom_call_target="tpu_custom_call" | custom-call | flops 11811160064 | bytes 28311552 | tf_op jit(solution)/shard_map/side_terms/pallas_call | solution.py:444
  540.3 6.4 collective-permute-done.20
  552.4 9.8 %collective-permute-start.23 = (bf16[8,64,704]{2,1,0:T(8,128)(2,1)}, bf16[8,64,704]{2,1,0:T(8,128)(2,1)}, u32[]{:S(2)}, u32[]{:S(2)}) collective-permute-start(bf16[8,64,704]{2,1,0:T(8,128)(2,1)} %convert_add_fusion.9), channel_id=1, source_target_pairs={{0,1},{1,2},{2,3},{3,0},{4,5},{5,6},{6,7},{7,4},{8,9},{9,10},{10,1... | collective-permute-start | bytes 2162696 | tf_op jit(solution)/shard_map/ppermute | solution.py:887
  562.3 2.6 fusion.2
  566.8 4.2 fusion.28
  571.0 10.6 %convolution_convert_fusion.1 = bf16[2048,512]{1,0:T(8,128)(2,1)} fusion(bf16[2048,2048]{1,0:T(8,128)(2,1)} %all-gather.4.cloned.1.call-done, bf16[512,2048]{1,0:T(8,128)(2,1)S(1)} %get-tuple-element.325), kind=kOutput, calls=%fused_computation.13 | convolution fusion | flops 4296015872 | bytes 12582912 | tf_op jit(solution)/shard_map/ed,td->et/dot_general | solution.py:1162
  581.6 4.4 all-to-all-start.1
  586.0 19.6 %down_terms.1 = bf16[704,2048]{1,0:T(8,128)(2,1)} custom-call(bf16[4096,704]{1,0:T(8,128)(2,1)} %bitcast.149, bf16[4096,2048]{1,0:T(8,128)(2,1)} %all-gather.6.cloned.1.call-done), custom_call_target="tpu_custom_call" | custom-call | flops 11811160064 | bytes 22544384 | tf_op jit(solution)/shard_map/down_terms/pallas_call | solution.py:477
  605.6 2.6 convert_add_fusion.8
  608.2 6.0 collective-permute-start.24
  614.2 8.3 convolution_convert_fusion
  622.6 11.6 %collective-permute-done.24 = bf16[8,64,704]{2,1,0:T(8,128)(2,1)} collective-permute-done((bf16[8,64,704]{2,1,0:T(8,128)(2,1)}, bf16[8,64,704]{2,1,0:T(8,128)(2,1)}, u32[]{:S(2)}, u32[]{:S(2)}) %collective-permute-start.24) | collective-permute-done | bytes 720928 | tf_op jit(solution)/shard_map/ppermute | solution.py:887
  637.3 2.5 collective-permute-start.26
  641.3 32.4 %attend_back.2 = (bf16[256,2816]{1,0:T(8,128)(2,1)}, f32[4096,64]{1,0:T(8,128)}, f32[4096,64]{1,0:T(8,128)}) custom-call(s32[16,4]{1,0:T(8,128)} %copy.124.bounds_ref, bf16[256,4096]{1,0:T(8,128)(2,1)} %get-tuple-element.218.q_ref, bf16[4096,64]{1,0:T(8,128)(2,1)} %get-tuple-element.219.k_ref, bf16[64,4096]{1,0:T(8,128)(2,1)} %get-tuple-element.220.kt_ref, ...), custom_call_target="tpu_custom_call" | custom-call | flops 53687091200 | bytes 8388608 | tf_op jit(solution)/shard_map/attend_back/pallas_call | solution.py:268
  674.8 14.3 %collective-permute-done.27 = bf16[176,2048]{1,0:T(8,128)(2,1)} collective-permute-done((bf16[176,2048]{1,0:T(8,128)(2,1)S(1)}, bf16[176,2048]{1,0:T(8,128)(2,1)}, u32[]{:S(2)}, u32[]{:S(2)}) %collective-permute-start.27) | collective-permute-done | bytes 720928 | tf_op jit(solution)/shard_map/ppermute | solution.py:887
  689.1 16.4 %reduce-scatter.7.cloned.1.call-done = bf16[256,2048]{1,0:T(8,128)(2,1)} async-done(((bf16[2048,2048]{1,0:T(8,128)(2,1)}), bf16[256,2048]{1,0:T(8,128)(2,1)}) %reduce-scatter.7.cloned.1.call-update) | async-done | bytes 1048592 | tf_op jit(solution)/shard_map/reduce_scatter | solution.py:1091
  713.8 3.6 all-to-all-start.2
  717.4 19.8 %attend_back.3 = (bf16[256,1280]{1,0:T(8,128)(2,1)}, bf16[128,4096]{1,0:T(8,128)(2,1)}) custom-call(s32[16,4]{1,0:T(8,128)} %copy.124.bounds_ref, bf16[256,4096]{1,0:T(8,128)(2,1)} %get-tuple-element.218.q_ref, bf16[4096,64]{1,0:T(8,128)(2,1)} %get-tuple-element.219.k_ref, bf16[64,4096]{1,0:T(8,128)(2,1)} %get-tuple-element.220.kt_ref, ...), custom_call_target="tpu_custom_call" | custom-call | flops 53687091200 | bytes 8388608 | tf_op jit(solution)/shard_map/attend_back/pallas_call | solution.py:268
  739.0 2.6 fusion.5
  741.5 7.6 collective-permute-start.29
  751.1 142.4 %tail.1 = (f32[512,2048]{1,0:T(8,128)}, bf16[8,64,384]{2,1,0:T(8,128)(2,1)}) custom-call(bf16[384,4096]{1,0:T(8,128)(2,1)} %pad_maximum_fusion.d_ref, bf16[512,2048]{1,0:T(8,128)(2,1)} %get-tuple-element.216.w_ref, bf16[512,2048]{1,0:T(8,128)(2,1)} %bitcast.135, f32[512,2048]{1,0:T(8,128)} %get-tuple-element.351.dh_ref, bf16[4096,2048]{1,0:T(8,128)(2,1)} %bitcast.161), custom_call_target="tpu_custom_call" | custom-call | flops 1073741824 | bytes 1048576 | tf_op jit(solution)/shard_map/tail/pallas_call | solution.py:705
  895.4 7.3 reduce-scatter.9.cloned.1.call-done
  914.3 2.7 convert_add_fusion.10
  917.0 3.8 fusion
  (264 shorter events, 109.8 us)
Async XLA Ops:
  7.2 217.5 %all-gather.6.cloned.1.call-start = ((), (), s32[]{:S(2)}) async-start(), calls=%async_computation.12 | async-start | bytes 18874368 | tf_op jit(solution)/shard_map/all_gather | solution.py:1035
  136.3 161.6 %all-gather.4.cloned.1.call-start = ((), (), s32[]{:S(2)}) async-start(), calls=%async_computation.7 | async-start | bytes 9437184 | tf_op jit(solution)/shard_map/all_gather | solution.py:1064
  139.3 33.7 %collective-permute-start = (bf16[8,2,64,704]{3,2,0,1:T(8,128)(2,1)}, bf16[8,2,64,704]{3,2,0,1:T(8,128)(2,1)}, u32[]{:S(2)}, u32[]{:S(2)}) collective-permute-start(bf16[8,2,64,704]{3,2,0,1:T(8,128)(2,1)} %copy.123), channel_id=1, source_target_pairs={{0,1},{1,2},{2,3},{3,0},{4,5},{5,6},{6,7},{7,4},{8,9},{9,10},{10,1... | collective-permute-start | bytes 4325384 | tf_op jit(solution)/shard_map/ppermute | solution.py:887
  173.6 36.0 %collective-permute-start.1 = (bf16[8,2,64,704]{3,2,0,1:T(8,128)(2,1)}, bf16[8,2,64,704]{3,2,0,1:T(8,128)(2,1)}, u32[]{:S(2)}, u32[]{:S(2)}) collective-permute-start(bf16[8,2,64,704]{3,2,0,1:T(8,128)(2,1)} %collective-permute-done), channel_id=1, source_target_pairs={{0,1},{1,2},{2,3},{3,0},{4,5},{5,6},{6,7},{7,4},{8,9},{9,10},{10,1... | collective-permute-start | bytes 4325384 | tf_op jit(solution)/shard_map/ppermute | solution.py:887
  224.7 43.2 %all-to-all-start = ((bf16[8,256,512]{2,1,0:T(8,128)(2,1)}), bf16[8,256,512]{2,1,0:T(8,128)(2,1)}, u32[]{:S(2)}, u32[]{:S(2)}) async-start(bf16[8,256,512]{2,1,0:T(8,128)(2,1)} %get-tuple-element.212.o_ref), calls=%async_computation | async-start | bytes 4194304 | tf_op jit(solution)/shard_map/all_to_all | solution.py:953
  229.0 405.2 %reduce-scatter.5.cloned.1.call-start = ((), (), s32[]{:S(2)}) async-start(), calls=%async_computation.8 | async-start | bytes 9437184 | tf_op jit(solution)/shard_map/reduce_scatter | solution.py:1091
  229.1 38.7 %collective-permute-start.2 = (bf16[8,2,64,704]{3,2,0,1:T(8,128)(2,1)}, bf16[8,2,64,704]{3,2,0,1:T(8,128)(2,1)}, u32[]{:S(2)}, u32[]{:S(2)}) collective-permute-start(bf16[8,2,64,704]{3,2,0,1:T(8,128)(2,1)} %collective-permute-done.1), channel_id=1, source_target_pairs={{0,1},{1,2},{2,3},{3,0},{4,5},{5,6},{6,7},{7,4},{8,9},{9,10},{10,1... | collective-permute-start | bytes 4325384 | tf_op jit(solution)/shard_map/ppermute | solution.py:887
  308.4 11.8 %collective-permute-start.3 = (bf16[512,2048]{1,0:T(8,128)(2,1)}, bf16[512,2048]{1,0:T(8,128)(2,1)}, u32[]{:S(2)}, u32[]{:S(2)}) collective-permute-start(bf16[512,2048]{1,0:T(8,128)(2,1)} %multiply_convert_fusion.first_ref), channel_id=1, source_target_pairs={{0,4},{4,0},{8,12},{12,8},{16,20},{20,16},{24,28},{28,24},{1,5},{5... | collective-permute-start | bytes 6291464 | tf_op jit(solution)/shard_map/ppermute | solution.py:926
  309.3 48.1 %collective-permute-start.4 = (bf16[512,2048]{1,0:T(8,128)(2,1)}, bf16[512,2048]{1,0:T(8,128)(2,1)}, u32[]{:S(2)}, u32[]{:S(2)}) collective-permute-start(bf16[512,2048]{1,0:T(8,128)(2,1)} %multiply_convert_fusion.first_ref), channel_id=1, source_target_pairs={{0,8},{4,12},{8,0},{12,4},{16,24},{20,28},{24,16},{28,20},{1,9},{5... | collective-permute-start | bytes 6291464 | tf_op jit(solution)/shard_map/ppermute | solution.py:926
  310.8 47.7 %collective-permute-start.5 = (bf16[512,2048]{1,0:T(8,128)(2,1)}, bf16[512,2048]{1,0:T(8,128)(2,1)S(1)}, u32[]{:S(2)}, u32[]{:S(2)}) collective-permute-start(bf16[512,2048]{1,0:T(8,128)(2,1)} %multiply_convert_fusion.first_ref), channel_id=1, source_target_pairs={{0,16},{4,20},{8,24},{12,28},{16,0},{20,4},{24,8},{28,12},{1,17},{... | collective-permute-start | bytes 6291464 | tf_op jit(solution)/shard_map/ppermute | solution.py:926
  358.5 7.5 collective-permute-start.6
  358.5 9.9 %collective-permute-start.7 = (bf16[512,2048]{1,0:T(8,128)(2,1)S(1)}, bf16[512,2048]{1,0:T(8,128)(2,1)}, u32[]{:S(2)}, u32[]{:S(2)}) collective-permute-start(bf16[512,2048]{1,0:T(8,128)(2,1)S(1)} %collective-permute-done.5.first_ref), channel_id=1, source_target_pairs={{0,4},{4,0},{8,12},{12,8},{16,20},{20,16},{24,28},{28,24},{1,5},{5... | collective-permute-start | bytes 6291464 | tf_op jit(solution)/shard_map/ppermute | solution.py:926
  359.0 40.5 %collective-permute-start.10 = (bf16[512,2048]{1,0:T(8,128)(2,1)}, bf16[512,2048]{1,0:T(8,128)(2,1)}, u32[]{:S(2)}, u32[]{:S(2)}) collective-permute-start(bf16[512,2048]{1,0:T(8,128)(2,1)} %get-tuple-element.266), channel_id=1, source_target_pairs={{0,4},{4,0},{8,12},{12,8},{16,20},{20,16},{24,28},{28,24},{1,5},{5... | collective-permute-start | bytes 6291464 | tf_op jit(solution)/shard_map/ppermute | solution.py:926
  361.2 38.3 %collective-permute-start.8 = (bf16[256,2048]{1,0:T(8,128)(2,1)S(1)}, bf16[256,2048]{1,0:T(8,128)(2,1)S(1)}, u32[]{:S(2)}, u32[]{:S(2)}) collective-permute-start(bf16[256,2048]{1,0:T(8,128)(2,1)S(1)} %slice.76), channel_id=1, source_target_pairs={{0,16},{4,20},{8,24},{12,28},{16,0},{20,4},{24,8},{28,12},{1,17},{... | collective-permute-start | bytes 3145736 | tf_op jit(solution)/shard_map/ppermute | solution.py:926
  361.8 37.7 %collective-permute-start.9 = (bf16[256,2048]{1,0:T(8,128)(2,1)S(1)}, bf16[256,2048]{1,0:T(8,128)(2,1)S(1)}, u32[]{:S(2)}, u32[]{:S(2)}) collective-permute-start(bf16[256,2048]{1,0:T(8,128)(2,1)S(1)} %slice.77), channel_id=1, source_target_pairs={{0,8},{4,12},{8,0},{12,4},{16,24},{20,28},{24,16},{28,20},{1,9},{5... | collective-permute-start | bytes 3145736 | tf_op jit(solution)/shard_map/ppermute | solution.py:926
  399.5 32.4 %collective-permute-start.12 = (bf16[512,2048]{1,0:T(8,128)(2,1)}, bf16[512,2048]{1,0:T(8,128)(2,1)}, u32[]{:S(2)}, u32[]{:S(2)}) collective-permute-start(bf16[512,2048]{1,0:T(8,128)(2,1)} %get-tuple-element.287), channel_id=1, source_target_pairs={{0,4},{4,0},{8,12},{12,8},{16,20},{20,16},{24,28},{28,24},{1,5},{5... | collective-permute-start | bytes 6291464 | tf_op jit(solution)/shard_map/ppermute | solution.py:926
  400.2 31.7 %copy-start.19 = (bf16[512,2048]{1,0:T(8,128)(2,1)}, bf16[512,2048]{1,0:T(8,128)(2,1)S(1)}, u32[]{:S(2)}) copy-start(bf16[512,2048]{1,0:T(8,128)(2,1)S(1)} %constant_dynamic-update-slice_fusion.first_ref) | copy-start | bytes 6291460
  400.2 34.3 %collective-permute-start.11 = (bf16[512,2048]{1,0:T(8,128)(2,1)S(1)}, bf16[512,2048]{1,0:T(8,128)(2,1)S(1)}, u32[]{:S(2)}, u32[]{:S(2)}) collective-permute-start(bf16[512,2048]{1,0:T(8,128)(2,1)S(1)} %constant_dynamic-update-slice_fusion.first_ref), channel_id=1, source_target_pairs={{0,4},{4,0},{8,12},{12,8},{16,20},{20,16},{24,28},{28,24},{1,5},{5... | collective-permute-start | bytes 6291464 | tf_op jit(solution)/shard_map/ppermute | solution.py:926
  400.4 31.5 %copy-start.28 = (bf16[512,2048]{1,0:T(8,128)(2,1)S(1)}, bf16[512,2048]{1,0:T(8,128)(2,1)}, u32[]{:S(2)}) copy-start(bf16[512,2048]{1,0:T(8,128)(2,1)} %get-tuple-element.286) | copy-start | bytes 6291460
  434.5 4.2 collective-permute-start.14
  434.9 38.7 %collective-permute-start.13 = (bf16[256,2048]{1,0:T(8,128)(2,1)S(1)}, bf16[256,2048]{1,0:T(8,128)(2,1)S(1)}, u32[]{:S(2)}, u32[]{:S(2)}) collective-permute-start(bf16[256,2048]{1,0:T(8,128)(2,1)S(1)} %slice.132), channel_id=1, source_target_pairs={{0,8},{4,12},{8,0},{12,4},{16,24},{20,28},{24,16},{28,20},{1,9},{5... | collective-permute-start | bytes 3145736 | tf_op jit(solution)/shard_map/ppermute | solution.py:926
  441.7 32.0 %collective-permute-start.15 = (bf16[256,2048]{1,0:T(8,128)(2,1)S(1)}, bf16[256,2048]{1,0:T(8,128)(2,1)S(1)}, u32[]{:S(2)}, u32[]{:S(2)}) collective-permute-start(bf16[256,2048]{1,0:T(8,128)(2,1)S(1)} %slice.131), channel_id=1, source_target_pairs={{0,16},{4,20},{8,24},{12,28},{16,0},{20,4},{24,8},{28,12},{1,17},{... | collective-permute-start | bytes 3145736 | tf_op jit(solution)/shard_map/ppermute | solution.py:926
  473.7 4.4 collective-permute-start.16
  480.6 25.4 %collective-permute-start.17 = (bf16[256,2048]{1,0:T(8,128)(2,1)S(1)}, bf16[256,2048]{1,0:T(8,128)(2,1)}, u32[]{:S(2)}, u32[]{:S(2)}) collective-permute-start(bf16[256,2048]{1,0:T(8,128)(2,1)S(1)} %get-tuple-element.380), channel_id=1, source_target_pairs={{0,8},{4,12},{8,0},{12,4},{16,24},{20,28},{24,16},{28,20},{1,9},{5... | collective-permute-start | bytes 3145736 | tf_op jit(solution)/shard_map/ppermute | solution.py:926
  481.7 24.9 %collective-permute-start.18 = (bf16[256,2048]{1,0:T(8,128)(2,1)S(1)}, bf16[256,2048]{1,0:T(8,128)(2,1)S(1)}, u32[]{:S(2)}, u32[]{:S(2)}) collective-permute-start(bf16[256,2048]{1,0:T(8,128)(2,1)S(1)} %get-tuple-element.379), channel_id=1, source_target_pairs={{0,16},{4,20},{8,24},{12,28},{16,0},{20,4},{24,8},{28,12},{1,17},{... | collective-permute-start | bytes 3145736 | tf_op jit(solution)/shard_map/ppermute | solution.py:926
  512.4 28.0 %collective-permute-start.19 = (bf16[256,2048]{1,0:T(8,128)(2,1)}, bf16[256,2048]{1,0:T(8,128)(2,1)}, u32[]{:S(2)}, u32[]{:S(2)}) collective-permute-start(bf16[256,2048]{1,0:T(8,128)(2,1)} %add_convert_fusion.3), channel_id=1, source_target_pairs={{0,8},{4,12},{8,0},{12,4},{16,24},{20,28},{24,16},{28,20},{1,9},{5... | collective-permute-start | bytes 3145736 | tf_op jit(solution)/shard_map/ppermute | solution.py:926
  516.4 30.4 %collective-permute-start.20 = (bf16[256,2048]{1,0:T(8,128)(2,1)}, bf16[256,2048]{1,0:T(8,128)(2,1)}, u32[]{:S(2)}, u32[]{:S(2)}) collective-permute-start(bf16[256,2048]{1,0:T(8,128)(2,1)} %add_convert_fusion.2), channel_id=1, source_target_pairs={{0,16},{4,20},{8,24},{12,28},{16,0},{20,4},{24,8},{28,12},{1,17},{... | collective-permute-start | bytes 3145736 | tf_op jit(solution)/shard_map/ppermute | solution.py:926
  518.3 22.1 %collective-permute-start.21 = (bf16[8,64,704]{2,1,0:T(8,128)(2,1)}, bf16[8,64,704]{2,1,0:T(8,128)(2,1)}, u32[]{:S(2)}, u32[]{:S(2)}) collective-permute-start(bf16[8,64,704]{2,1,0:T(8,128)(2,1)} %dynamic-slice_bitcast_fusion.1), channel_id=1, source_target_pairs={{0,1},{1,2},{2,3},{3,0},{4,5},{5,6},{6,7},{7,4},{8,9},{9,10},{10,1... | collective-permute-start | bytes 2162696 | tf_op jit(solution)/shard_map/ppermute | solution.py:887
  540.3 22.0 %copy-start.32 = (bf16[256,2048]{1,0:T(8,128)(2,1)S(1)}, bf16[256,2048]{1,0:T(8,128)(2,1)}, u32[]{:S(2)}) copy-start(bf16[256,2048]{1,0:T(8,128)(2,1)} %copy-done.31) | copy-start | bytes 3145732
  540.3 22.0 %copy-start.34 = (bf16[256,2048]{1,0:T(8,128)(2,1)S(1)}, bf16[256,2048]{1,0:T(8,128)(2,1)}, u32[]{:S(2)}) copy-start(bf16[256,2048]{1,0:T(8,128)(2,1)} %copy-done.33) | copy-start | bytes 3145732
  548.9 32.6 %collective-permute-start.22 = (bf16[8,64,704]{2,1,0:T(8,128)(2,1)}, bf16[8,64,704]{2,1,0:T(8,128)(2,1)}, u32[]{:S(2)}, u32[]{:S(2)}) collective-permute-start(bf16[8,64,704]{2,1,0:T(8,128)(2,1)} %dynamic-slice_bitcast_fusion), channel_id=1, source_target_pairs={{0,1},{1,2},{2,3},{3,0},{4,5},{5,6},{6,7},{7,4},{8,9},{9,10},{10,1... | collective-permute-start | bytes 2162696 | tf_op jit(solution)/shard_map/ppermute | solution.py:887
  552.4 29.1 %collective-permute-start.23 = (bf16[8,64,704]{2,1,0:T(8,128)(2,1)}, bf16[8,64,704]{2,1,0:T(8,128)(2,1)}, u32[]{:S(2)}, u32[]{:S(2)}) collective-permute-start(bf16[8,64,704]{2,1,0:T(8,128)(2,1)} %convert_add_fusion.9), channel_id=1, source_target_pairs={{0,1},{1,2},{2,3},{3,0},{4,5},{5,6},{6,7},{7,4},{8,9},{9,10},{10,1... | collective-permute-start | bytes 2162696 | tf_op jit(solution)/shard_map/ppermute | solution.py:887
  571.0 10.6 %copy-start.24 = (bf16[512,2048]{1,0:T(8,128)(2,1)}, bf16[512,2048]{1,0:T(8,128)(2,1)S(1)}, u32[]{:S(2)}) copy-start(bf16[512,2048]{1,0:T(8,128)(2,1)S(1)} %get-tuple-element.325) | copy-start | bytes 6291460
  581.6 52.6 %all-to-all-start.1 = ((bf16[8,256,512]{2,1,0:T(8,128)(2,1)}), bf16[8,256,512]{2,1,0:T(8,128)(2,1)}, u32[]{:S(2)}, u32[]{:S(2)}) async-start(bf16[8,256,512]{2,1,0:T(8,128)(2,1)} %bitcast.170), calls=%async_computation.1 | async-start | bytes 4194304 | tf_op jit(solution)/shard_map/all_to_all | solution.py:953
  586.0 119.6 %reduce-scatter.7.cloned.1.call-start = ((), (), s32[]{:S(2)}) async-start(), calls=%async_computation.9 | async-start | bytes 9437184 | tf_op jit(solution)/shard_map/reduce_scatter | solution.py:1091
  608.2 26.0 %collective-permute-start.24 = (bf16[8,64,704]{2,1,0:T(8,128)(2,1)}, bf16[8,64,704]{2,1,0:T(8,128)(2,1)}, u32[]{:S(2)}, u32[]{:S(2)}) collective-permute-start(bf16[8,64,704]{2,1,0:T(8,128)(2,1)} %convert_add_fusion.8), channel_id=1, source_target_pairs={{0,1},{1,2},{2,3},{3,0},{4,5},{5,6},{6,7},{7,4},{8,9},{9,10},{10,1... | collective-permute-start | bytes 2162696 | tf_op jit(solution)/shard_map/ppermute | solution.py:887
  635.6 38.2 %collective-permute-start.25 = (bf16[8,64,704]{2,1,0:T(8,128)(2,1)S(1)}, bf16[8,64,704]{2,1,0:T(8,128)(2,1)}, u32[]{:S(2)}, u32[]{:S(2)}) collective-permute-start(bf16[8,64,704]{2,1,0:T(8,128)(2,1)S(1)} %convert_add_fusion.7), channel_id=1, source_target_pairs={{0,1},{1,2},{2,3},{3,0},{4,5},{5,6},{6,7},{7,4},{8,9},{9,10},{10,1... | collective-permute-start | bytes 2162696 | tf_op jit(solution)/shard_map/ppermute | solution.py:887
  637.3 37.5 %collective-permute-start.26 = (bf16[8,64,704]{2,1,0:T(8,128)(2,1)S(1)}, bf16[8,64,704]{2,1,0:T(8,128)(2,1)}, u32[]{:S(2)}, u32[]{:S(2)}) collective-permute-start(bf16[8,64,704]{2,1,0:T(8,128)(2,1)S(1)} %convert_add_fusion.6), channel_id=1, source_target_pairs={{0,1},{1,2},{2,3},{3,0},{4,5},{5,6},{6,7},{7,4},{8,9},{9,10},{10,1... | collective-permute-start | bytes 2162696 | tf_op jit(solution)/shard_map/ppermute | solution.py:887
  641.0 48.1 %collective-permute-start.27 = (bf16[176,2048]{1,0:T(8,128)(2,1)S(1)}, bf16[176,2048]{1,0:T(8,128)(2,1)}, u32[]{:S(2)}, u32[]{:S(2)}) collective-permute-start(bf16[176,2048]{1,0:T(8,128)(2,1)S(1)} %dynamic-slice_bitcast_fusion.2), channel_id=1, source_target_pairs={{0,1},{1,2},{2,3},{3,0},{4,5},{5,6},{6,7},{7,4},{8,9},{9,10},{10,1... | collective-permute-start | bytes 2162696 | tf_op jit(solution)/shard_map/ppermute | solution.py:887
  708.0 29.3 %collective-permute-start.28 = (bf16[176,2048]{1,0:T(8,128)(2,1)}, bf16[176,2048]{1,0:T(8,128)(2,1)}, u32[]{:S(2)}, u32[]{:S(2)}) collective-permute-start(bf16[176,2048]{1,0:T(8,128)(2,1)} %convert_add_fusion.12), channel_id=1, source_target_pairs={{0,1},{1,2},{2,3},{3,0},{4,5},{5,6},{6,7},{7,4},{8,9},{9,10},{10,1... | collective-permute-start | bytes 2162696 | tf_op jit(solution)/shard_map/ppermute | solution.py:887
  713.8 24.5 %all-to-all-start.2 = ((bf16[8,2,64,704]{3,2,1,0:T(8,128)(2,1)}), bf16[8,2,64,704]{3,2,1,0:T(8,128)(2,1)S(1)}, u32[]{:S(2)}, u32[]{:S(2)}) async-start(bf16[8,2,64,704]{3,2,1,0:T(8,128)(2,1)} %copy.130), calls=%async_computation.4 | async-start | bytes 3145728 | tf_op jit(solution)/shard_map/all_to_all | solution.py:953
  717.4 176.2 %reduce-scatter.11.cloned.1.call-start = ((), (), s32[]{:S(2)}) async-start(), calls=%async_computation.11 | async-start | bytes 1310720 | tf_op jit(solution)/shard_map/reduce_scatter | solution.py:1218
  738.4 164.3 %reduce-scatter.9.cloned.1.call-start = ((), (), s32[]{:S(2)}) async-start(), calls=%async_computation.10 | async-start | bytes 9437184 | tf_op jit(solution)/shard_map/reduce_scatter | solution.py:1091
  738.4 10.7 %copy-start.36 = (bf16[128,4096]{1,0:T(8,128)(2,1)S(1)}, bf16[128,4096]{1,0:T(8,128)(2,1)}, u32[]{:S(2)}) copy-start(bf16[128,4096]{1,0:T(8,128)(2,1)} %get-tuple-element.350) | copy-start | bytes 3145732
  738.9 10.2 %copy-start.30 = (bf16[256,2816]{1,0:T(8,128)(2,1)S(1)}, bf16[256,2816]{1,0:T(8,128)(2,1)}, u32[]{:S(2)}) copy-start(bf16[256,2816]{1,0:T(8,128)(2,1)} %get-tuple-element.339) | copy-start | bytes 4325380
  739.0 10.2 %copy-start.37 = (bf16[256,1280]{1,0:T(8,128)(2,1)S(1)}, bf16[256,1280]{1,0:T(8,128)(2,1)}, u32[]{:S(2)}) copy-start(bf16[256,1280]{1,0:T(8,128)(2,1)} %get-tuple-element.349) | copy-start | bytes 1966084
  741.5 153.8 %collective-permute-start.29 = (bf16[176,2048]{1,0:T(8,128)(2,1)}, bf16[176,2048]{1,0:T(8,128)(2,1)}, u32[]{:S(2)}, u32[]{:S(2)}) collective-permute-start(bf16[176,2048]{1,0:T(8,128)(2,1)} %fusion.5), channel_id=1, source_target_pairs={{0,1},{1,2},{2,3},{3,0},{4,5},{5,6},{6,7},{7,4},{8,9},{9,10},{10,1... | collective-permute-start | bytes 2162696 | tf_op jit(solution)/shard_map/ppermute | solution.py:887
  893.5 10.6 %copy-start.40 = (bf16[64,256]{1,0:T(8,128)(2,1)S(1)}, bf16[64,256]{1,0:T(8,128)(2,1)}, u32[]{:S(2)}) copy-start(bf16[64,256]{1,0:T(8,128)(2,1)} %param.17) | copy-start | bytes 98308
  (36 other events, 119.3 us)
Sparse Core Ops, SparseCore 0:
  136.5 88.1 all-gather.5
  226.6 71.3 all-gather.3
  506.8 80.9 reduce-scatter.4
  634.4 71.1 reduce-scatter.6
  738.5 65.0 reduce-scatter.10
  807.3 95.2 reduce-scatter.8

commit v4 on v3

--- a/solution.py
+++ b/solution.py
@@ -19,6 +19,7 @@
 BF = jnp.bfloat16
 F32 = jnp.float32
 VMEM_LIMIT = 56 * 1024 * 1024
+FFN_VMEM = 34 * 1024 * 1024
 MESH = pl.DeviceIdType.MESH
 
 
@@ -63,25 +64,31 @@
 
 
 def forward_kernel(
-    group, bounds_ref, q_ref, kv_ref, cos_ref, sin_ref, start_ref,
-    o_ref, lse_ref, qt_ref, kt_ref, kn_ref, vn_ref, vt, acc, top, total,
+    group, skip, final, bounds_ref, q_ref, kv_ref, cos_ref, sin_ref, start_ref, *rest
 ):
-    i = pl.program_id(0)
+    if final:
+        kn_ref, vt, o_ref, lse_ref, qt_ref, acc, top, total = rest
+    else:
+        o_ref, lse_ref, qt_ref, kt_ref, kn_ref, vn_ref, vt, acc, top, total = rest
+    step = pl.program_id(0)
+    i = step + skip
     rows = q_ref.shape[1]
     wide = rows * group
     here = pl.ds(pl.multiple_of(i * rows, rows), rows)
     cosine, sine = cos_ref[:, here], sin_ref[:, here]
 
-    @pl.when(i == 0)
-    def _():
-        for part in range(kv_ref.shape[1] // BK):
-            at = pl.ds(part * BK, BK)
-            k = turned(kv_ref[:HD, at], cos_ref[:, at], sin_ref[:, at]).astype(BF)
-            v = kv_ref[HD:, at].astype(BF)
-            kt_ref[:, at] = k
-            vt[:, at] = v
-            kn_ref[at, :] = k.T
-            vn_ref[at, :] = v.T
+    if not final:
+
+        @pl.when(step == 0)
+        def _():
+            for part in range(kv_ref.shape[1] // BK):
+                at = pl.ds(part * BK, BK)
+                k = turned(kv_ref[:HD, at], cos_ref[:, at], sin_ref[:, at]).astype(BF)
+                v = kv_ref[HD:, at].astype(BF)
+                kt_ref[:, at] = k
+                vt[:, at] = v
+                kn_ref[at, :] = k.T
+                vn_ref[at, :] = v.T
 
     heads = [
         turned(q_ref[h * HD : (h + 1) * HD, :], cosine, sine).astype(BF) * BF(HD**-0.5)
@@ -174,59 +181,77 @@
     return pl.BlockSpec(shape, lambda i, b: (0,) * len(shape))
 
 
-def attend(bounds, projected, cosine, sine, starts, group, senders, local):
+def attend(
+    bounds, projected, cosine, sine, starts, group, senders, local, skip, blocks, before
+):
     length = projected.shape[1]
-    blocks = length // BQ
     per = local // BQ
     wide = group * HD
-    piece = pl.BlockSpec((1, wide, BQ), lambda i, b: (i // per, 0, i % per))
-    line = pl.BlockSpec((1, 1, group * BQ), lambda i, b: (i, 0, 0))
-    flat = pl.BlockSpec((wide, BQ), lambda i, b: (0, i))
-    return pl.pallas_call(
-        functools.partial(forward_kernel, group),
-        out_shape=(
-            jax.ShapeDtypeStruct((senders, wide, local), BF),
-            jax.ShapeDtypeStruct((blocks, 1, group * BQ), F32),
-            jax.ShapeDtypeStruct((wide, length), BF),
+    final = before is not None
+    line = pl.BlockSpec((1, 1, group * BQ), lambda i, b: (i + skip, 0, 0))
+    piece = pl.BlockSpec((1, wide, BQ), lambda i, b: ((i + skip) // per, 0, (i + skip) % per))
+    own_line = pl.BlockSpec((1, 1, group * BQ), lambda i, b: (i, 0, 0))
+    tall, flat = whole_spec((length, HD)), whole_spec((HD, length))
+    arrays = [projected, projected, cosine, sine, starts]
+    in_specs = [
+        pl.BlockSpec((wide, BQ), lambda i, b: (0, i + skip)),
+        pl.BlockSpec((2 * HD, length), lambda i, b: (wide // (2 * HD), 0)),
+        whole_spec((HALF, length)),
+        whole_spec((HALF, length)),
+        line,
+    ]
+    out_shape = [
+        jax.ShapeDtypeStruct((senders, wide, local), BF),
+        jax.ShapeDtypeStruct((blocks, 1, group * BQ), F32),
+        jax.ShapeDtypeStruct((wide, blocks * BQ), BF),
+    ]
+    out_specs = [piece, own_line, pl.BlockSpec((wide, BQ), lambda i, b: (0, i))]
+    scratch = [
+        pltpu.VMEM((HD, group * BQ), F32),
+        pltpu.VMEM((1, group * BQ), F32),
+        pltpu.VMEM((1, group * BQ), F32),
+    ]
+    aliases = {}
+    kernel = functools.partial(forward_kernel, group, skip, final)
+    if final:
+        o_before, kn, vt = before
+        arrays += [kn, vt, o_before]
+        in_specs += [tall, flat, pl.BlockSpec(memory_space=pl.ANY)]
+        aliases = {8: 0}
+        inner = kernel
+
+        def kernel(*refs):
+            return inner(*refs[:8], *refs[9:])
+
+    else:
+        out_shape += [
             jax.ShapeDtypeStruct((HD, length), BF),
             jax.ShapeDtypeStruct((length, HD), BF),
             jax.ShapeDtypeStruct((length, HD), BF),
-        ),
+            jax.ShapeDtypeStruct((HD, length), BF),
+        ]
+        out_specs += [flat, tall, tall, flat]
+    return pl.pallas_call(
+        kernel,
+        out_shape=out_shape,
         grid_spec=pltpu.PrefetchScalarGridSpec(
             num_scalar_prefetch=1,
             grid=(blocks,),
-            in_specs=[
-                flat,
-                pl.BlockSpec((2 * HD, length), lambda i, b: (wide // (2 * HD), 0)),
-                whole_spec((HALF, length)),
-                whole_spec((HALF, length)),
-                line,
-            ],
-            out_specs=(
-                piece,
-                line,
-                flat,
-                whole_spec((HD, length)),
-                whole_spec((length, HD)),
-                whole_spec((length, HD)),
-            ),
-            scratch_shapes=[
-                pltpu.VMEM((HD, length), BF),
-                pltpu.VMEM((HD, group * BQ), F32),
-                pltpu.VMEM((1, group * BQ), F32),
-                pltpu.VMEM((1, group * BQ), F32),
-            ],
-        ),
+            in_specs=in_specs,
+            out_specs=out_specs,
+            scratch_shapes=scratch,
+        ),
+        input_output_aliases=aliases,
         compiler_params=pltpu.CompilerParams(
             dimension_semantics=("arbitrary",), vmem_limit_bytes=VMEM_LIMIT
         ),
         cost_estimate=pl.CostEstimate(
-            flops=40 * group * length * length * HD // 2,
-            bytes_accessed=4 * group * length * HD * 2,
-            transcendentals=group * length * length // 4,
+            flops=20 * group * length * length * HD // 2,
+            bytes_accessed=4 * group * length * HD,
+            transcendentals=group * length * length // 8,
         ),
         name="attend",
-    )(bounds, projected, projected, cosine, sine, starts)
+    )(bounds, *arrays)
 
 
 def attend_back(
@@ -242,7 +267,7 @@
     tall = whole_spec((length, HD))
     arrays = [qt, k, kt, v, cosine, sine, starts, o, do, lse]
     in_specs = [
-        pl.BlockSpec((wide, BQ), lambda i, b: (0, i + skip)),
+        pl.BlockSpec((wide, BQ), lambda i, b: (0, i)),
         tall,
         whole_spec((HD, length)),
         tall,
@@ -251,7 +276,7 @@
         line,
         piece,
         piece,
-        line,
+        pl.BlockSpec((1, 1, group * BQ), lambda i, b: (i, 0, 0)),
     ]
     out_specs = [pl.BlockSpec((wide, BQ), lambda i, b: (0, i))]
     out_shape = [jax.ShapeDtypeStruct((wide, blocks * BQ), BF)]
@@ -371,7 +396,7 @@
 def ffn_chunk(places, first, second, dy_all, gate_w, up_w, down_w, kept):
     local, width = first.shape
     hidden = gate_w.shape[1]
-    tall = min(512, local)
+    tall = min(256, local)
     tiles = local // tall
     count = dy_all.shape[0]
 
@@ -381,13 +406,8 @@
     ahead = pl.BlockSpec((tall, width), lambda i, t, p: (jnp.where(i == 0, t, tiles - 1), 0))
     behind = pl.BlockSpec((tall, width), lambda i, t, p: (jnp.where(i == 0, 0, t), 0))
 
-    def held(shape):
-        return pl.BlockSpec(shape, lambda i, t, p: (0, 0), pipeline_mode=pl.Buffered(1))
-
-    in_specs = [
-        ahead, behind, at_place(width), held((width, hidden)), held((width, hidden)),
-        held((hidden, width)),
-    ]
+    held = pl.BlockSpec(memory_space=pltpu.VMEM)
+    in_specs = [ahead, behind, at_place(width), held, held, held]
     arrays = [first, second, dy_all, gate_w, up_w, down_w]
     aliases = {}
     if kept is not None:
@@ -412,7 +432,7 @@
         ),
         input_output_aliases=aliases,
         compiler_params=pltpu.CompilerParams(
-            dimension_semantics=("arbitrary", "arbitrary"), vmem_limit_bytes=VMEM_LIMIT
+            dimension_semantics=("arbitrary", "arbitrary"), vmem_limit_bytes=FFN_VMEM
         ),
         cost_estimate=pl.CostEstimate(
             flops=2 * 6 * 2 * local * width * hidden,
@@ -1032,7 +1052,7 @@
     )
     ffn_pieces = [[ffn_part.reshape(count, 2, rows, hidden)]]
 
-    dy_all = lax.all_gather(dy, "seq", axis=0, tiled=False)
+    out_w = lax.all_gather(out_part.reshape(parts * rows, width), "seq", axis=0, tiled=True)
     if len(ffn_pieces) < parts:
         ffn_pieces.append(hop(*ffn_pieces[-1]))
     flags = lax.dynamic_index_in_dim(attn_all, z, 0, False)
@@ -1056,26 +1076,30 @@
     attn_t = wt_ext[:attn_cols]
     gain_one = wt_ext[attn_cols].astype(F32)
     gain_two = wt_ext[attn_cols + 1].astype(F32)
-    projected, cosine, sine, starts, bounds, ffn_last, out_part = fence(
-        projected, cosine, sine, starts, bounds, ffn_pieces[-1], out_part
+    projected, cosine, sine, starts, bounds, ffn_last, dy = fence(
+        projected, cosine, sine, starts, bounds, ffn_pieces[-1], dy
     )
     ffn_pieces[-1] = ffn_last
 
-    out_w = lax.all_gather(out_part.reshape(parts * rows, width), "seq", axis=0, tiled=True)
+    dy_all = lax.all_gather(dy, "seq", axis=0, tiled=False)
+    cut = blocks * 11 // 16
+    ready = (bounds, projected, cosine, sine, starts, group, count, local)
     if len(ffn_pieces) < parts:
         ffn_pieces.append(hop(*ffn_pieces[-1]))
-    o_heads, lse, q_t, k_t, k_n, v_n = attend(
-        bounds, projected, cosine, sine, starts, group, count, local
-    )
-    o_heads, lse, q_t, k_t, k_n, v_n, ffn_last, dy_all = fence(
-        o_heads, lse, q_t, k_t, k_n, v_n, ffn_pieces[-1], dy_all
+    o_half, lse_one, qt_one, k_t, k_n, v_n, v_t = attend(*ready, 0, cut, None)
+    o_half, lse_one, qt_one, k_t, k_n, v_n, v_t, ffn_last, out_w = fence(
+        o_half, lse_one, qt_one, k_t, k_n, v_n, v_t, ffn_pieces[-1], out_w
     )
     ffn_pieces[-1] = ffn_last
-
     while len(ffn_pieces) < parts:
         ffn_pieces.append(hop(*ffn_pieces[-1]))
+    o_heads, lse_two, qt_two = attend(*ready, cut, blocks - cut, (o_half, k_n, v_t))
+    o_heads, lse_two, qt_two, ffn_pieces = fence(o_heads, lse_two, qt_two, ffn_pieces)
+
     o_t = exchange(o_heads).reshape(count * group_width, local)
-    o_t, ffn_pieces = fence(o_t, ffn_pieces)
+    o_t, dy_all, qt_one, qt_two, lse_one, lse_two = fence(
+        o_t, dy_all, qt_one, qt_two, lse_one, lse_two
+    )
 
     ffn_w = collect([piece[0] for piece in ffn_pieces], "fsdp").transpose(2, 1, 0, 3, 4).reshape(2, width, hidden)
     gate_w, up_w = ffn_w[0], ffn_w[1]
@@ -1164,9 +1188,10 @@
     (gate_state,) = landed([gate_moved], [gate_t], 1)
     if parts > 2:
         (gate_moved,) = launch([gate_state])
-    do_t, db, dh1, up_moved, gate_moved, gate_state = fence(
-        do_t, db, dh1, up_moved, gate_moved, gate_state
-    )
+    do_t, db, dh1, up_moved, gate_moved, gate_state, y_two = fence(
+        do_t, db, dh1, up_moved, gate_moved, gate_state, y_two
+    )
+    y_two = over_seq(y_two)
     do_heads = exchange(do_t.reshape(count, group_width, local))
     term_out = dot_f32(o_t, db).astype(BF)
     term_down = down_terms_of(act, dy_rows).reshape(parts, hidden // parts, width)
@@ -1177,25 +1202,23 @@
         do_heads, term_out, term_down, y_one, up_moved, up_state
     )
 
-    part_out = over_seq(term_out)
     pair_t = [gate_t, up_t]
     pair = [gate_state, up_state]
     if parts > 2:
         pair = landed([gate_moved, up_moved], pair_t, 2)
     moved = launch((pair if parts > 3 else []) + [term_of(term_down, 0)])
-    cut = blocks * 11 // 16
-    saved = (bounds, q_t, k_n, k_t, v_n, cosine, sine, starts, o_heads, do_heads, lse, group)
+    saved = (bounds, qt_one, k_n, k_t, v_n, cosine, sine, starts, o_heads, do_heads, lse_one, group)
     dq_one, dk, dv = attend_back(*saved, 0, cut, None)
-    dq_one, dk, dv, moved, pair, do_heads, y_two, part_out = fence(
-        dq_one, dk, dv, moved, pair, do_heads, y_two, part_out
-    )
-    y_two = over_seq(y_two)
+    dq_one, dk, dv, moved, pair, do_heads, y_two, term_out = fence(
+        dq_one, dk, dv, moved, pair, do_heads, y_two, term_out
+    )
+    part_out = over_seq(term_out)
     down_state = landed(moved[-1:], [term_down], 1)
     if parts > 3:
         pair = ring_finish(moved[:2], pair_t, 3)
     ffn_back = exchange(jnp.stack(pair, axis=1).astype(BF))
     moved = launch(down_state if parts > 2 else [])
-    saved = (bounds, q_t, k_n, k_t, v_n, cosine, sine, starts, o_heads, do_heads, lse, group)
+    saved = (bounds, qt_two, k_n, k_t, v_n, cosine, sine, starts, o_heads, do_heads, lse_two, group)
     dq_two, dkv_t = attend_back(*saved, cut, blocks - cut, (dk, dv))
     dq_two, dkv_t, moved, down_state, part_out, ffn_back = fence(
         dq_two, dkv_t, moved, down_state, part_out, ffn_back

time: 936 us -> 901 us (0.963)
  Pallas kernels: 542 us -> 480 us
  waiting for transfers between devices: 169 us -> 221 us
  starting transfers between devices: 57.4 us -> 32.7 us
    pallas_call x1, Pallas kernels: 142 us -> 93.4 us  [tail(): pl.pallas_call(functools.partial(tail_kernel, parts, cols), out_shape=(ja...]
    all_to_all x3, waiting for transfers between devices: 1.11 us -> 49.8 us  [exchange(): return lax.all_to_all(array, 'seq', split_axis=0, concat_axis=0, tiled=True)]
    reduce_scatter x3, waiting for transfers between devices: 23.7 us -> 59 us  [over_seq(): return lax.psum_scatter(whole, 'seq', scatter_dimension=0, tiled=True)]
    all_gather x1, waiting for transfers between devices: 30.1 us -> 0.01 us  [body(): lax.all_gather(out_part.reshape(parts * rows, width), 'seq', axis=0, tile...]
    ppermute x12, starting transfers between devices: 34 us -> 10 us  [hop(): return [lax.ppermute(block, 'fsdp', ring('fsdp')) for block in blocks]]
    pallas_call x4, Pallas kernels: 125 us -> 105 us  [ffn_chunk(): pl.pallas_call(ffn_kernel, out_shape=(narrow, narrow, narrow, broad, part...]
    ppermute x18, waiting for transfers between devices: 30 us -> 42.9 us  [swap(): return lax.ppermute(block, 'seq', [(n, n ^ bit) for n in range(count)])]
    ppermute x12, waiting for transfers between devices: 68.5 us -> 58.8 us  [hop(): return [lax.ppermute(block, 'fsdp', ring('fsdp')) for block in blocks]]
  transfers between devices with their start and end apart: 39 -> 39, of which waited for: 19 -> 19; matrix products, arithmetic and copies ran while one was open for 9% -> 9% of each run, Pallas kernels for 47% -> 41%
where the time goes in v4:
time: 901 us; the launch traced here: 895 us
  Pallas kernels  480 us (53%)
  waiting for transfers between devices  221 us (25%)
  local copies, waits for them, and re-layouts  60.5 us (7%)
  other arithmetic  58.6 us (7%)
  starting transfers between devices  32.7 us (4%)
  matrix products  26.3 us (3%)
  between operations  15.3 us (2%)
    pallas_call x1, Pallas kernels, start_gather(): pl.pallas_call(functools.partial(start_kernel, parts), out_shape=shapes,...  109 us
    pallas_call x4, Pallas kernels, ffn_chunk(): pl.pallas_call(ffn_kernel, out_shape=(narrow, narrow, narrow, broad, part...  105 us
    pallas_call x1, Pallas kernels, tail(): pl.pallas_call(functools.partial(tail_kernel, parts, cols), out_shape=(ja...  93.4 us
    reduce_scatter x3, waiting for transfers between devices, over_seq(): return lax.psum_scatter(whole, 'seq', scatter_dimension=0, tiled=True)  59 us
    ppermute x12, waiting for transfers between devices, hop(): return [lax.ppermute(block, 'fsdp', ring('fsdp')) for block in blocks]  58.8 us
    pallas_call x2, Pallas kernels, attend_back(): pl.pallas_call(functools.partial(backward_kernel, group, skip, final), ou...  54 us
    all_to_all x3, waiting for transfers between devices, exchange(): return lax.all_to_all(array, 'seq', split_axis=0, concat_axis=0, tiled=True)  49.8 us
    ppermute x18, waiting for transfers between devices, swap(): return lax.ppermute(block, 'seq', [(n, n ^ bit) for n in range(count)])  42.9 us
  transfers between devices with their start and end apart: 39, of which 19 were waited for; matrix products, arithmetic and copies ran while one was open for 9% of the time, Pallas kernels for 41%

profile of v4, /device:TPU:0, one launch (start us, length us, event | category | flops | bytes accessed | tf_op | source)
XLA Modules:
  0.0 894.5 jit_solution(5701160067998063994)
XLA Ops:
  17.4 109.1 %start_gather.1 = (bf16[8,512,2048]{2,1,0:T(8,128)(2,1)S(1)}, bf16[4,8,64,512]{3,2,1,0:T(8,128)(2,1)S(1)}, bf16[8,128,704]{2,1,0:T(8,128)(2,1)S(1)}, bf16[4,64,2...) custom-call(bf16[512,2048]{1,0:T(8,128)(2,1)S(1)} %bitcast.144, ...), custom_call_target="tpu_custom_call" | custom-call | tf_op jit(solution)/shard_map/start_gather/pallas_call | solution.py:884
  130.6 5.8 copy-done.14
  136.5 2.9 copy.126
  146.8 18.9 %project.1 = (bf16[8,512,2048]{2,1,0:T(8,128)(2,1)}, f32[384,4096]{1,0:T(8,128)}, bf16[512,2048]{1,0:T(8,128)(2,1)}) custom-call(bf16[8,512,2048]{2,1,0:T(8,128)(2,1)} %copy-done.14, bf16[2048,512]{1,0:T(8,128)(2,1)} %bitcast.170), custom_call_target="tpu_custom_call" | custom-call | flops 6442450944 | bytes 33554432 | tf_op jit(solution)/shard_map/project/pallas_call | solution.py:334
  165.7 2.8 multiply_sine_fusion
  168.5 4.2 collective-permute-done
  174.0 27.3 %attend.2 = (bf16[8,256,512]{2,1,0:T(8,128)(2,1)}, f32[11,1,1024]{2,1,0:T(1,128)}, bf16[256,2816]{1,0:T(8,128)(2,1)}, bf16[64,4096]{1,0:T(8,128)(2,1)}, bf16[409...) custom-call(s32[16,4]{1,0:T(8,128)} %copy.128.bounds_ref.refs_0_, ...), custom_call_target="tpu_custom_call" | custom-call | flops 42949672960 | bytes 4194304 | tf_op jit(solution)/shard_map/attend/pallas_call | solution.py:234
  201.3 7.2 collective-permute-done.1
  208.5 13.8 %attend.3 = (bf16[8,256,512]{2,1,0:T(8,128)(2,1)}, f32[5,1,1024]{2,1,0:T(1,128)}, bf16[256,1280]{1,0:T(8,128)(2,1)}) custom-call(s32[16,4]{1,0:T(8,128)} %copy.128.bounds_ref.refs_0_, f32[384,4096]{1,0:T(8,128)} %get-tuple-element.214.q_ref.kv_ref.refs_1_.refs_2_, ...), custom_call_target="tpu_custom_call", output_to_operand_aliasing={{0}: (8, {})} | custom-call | flops 42949672960 | bytes 4194304 | tf_op jit(solution)/shard_map/attend/pallas_call | solution.py:234
  222.3 17.4 %collective-permute-done.2 = bf16[8,2,64,704]{3,2,0,1:T(8,128)(2,1)} collective-permute-done((bf16[8,2,64,704]{3,2,0,1:T(8,128)(2,1)}, bf16[8,2,64,704]{3,2,0,1:T(8,128)(2,1)}, u32[]{:S(2)}, u32[]{:S(2)}) %collective-permute-start.2) | collective-permute-done | bytes 1441824 | tf_op jit(solution)/shard_map/ppermute | solution.py:907
  239.7 4.4 all-to-all-start
  245.0 48.4 %all-to-all-done = bf16[8,256,512]{2,1,0:T(8,128)(2,1)} async-done(((bf16[8,256,512]{2,1,0:T(8,128)(2,1)}), bf16[8,256,512]{2,1,0:T(8,128)(2,1)}, u32[]{:S(2)}, u32[]{:S(2)}) %all-to-all-start) | async-done | bytes 2097184 | tf_op jit(solution)/shard_map/all_to_all | solution.py:973
  293.4 10.1 %all-gather.6.cloned.1.call-done = bf16[4096,2048]{1,0:T(8,128)(2,1)} async-done(((bf16[512,2048]{1,0:T(8,128)(2,1)}), bf16[4096,2048]{1,0:T(8,128)(2,1)}) %all-gather.6.cloned.1.call-update) | async-done | bytes 16777232 | tf_op jit(solution)/shard_map/all_gather | solution.py:1084
  303.5 7.8 multiply_reduce_fusion.1
  325.3 26.7 %ffn.4 = (bf16[8,512,704]{2,1,0:T(8,128)(2,1)}, bf16[8,512,704]{2,1,0:T(8,128)(2,1)}, bf16[8,512,704]{2,1,0:T(8,128)(2,1)}, bf16[8,512,2048]{2,1,0:T(8,128)(2,1)...) custom-call(s32[2]{0:T(128)S(1)} %get-tuple-element.417.places_ref, ...), custom_call_target="tpu_custom_call" | custom-call | flops 17716740096 | bytes 29622272 | tf_op jit(solution)/shard_map/ffn/pallas_call | solution.py:421
  353.3 15.6 %collective-permute-done.4.first_ref = bf16[512,2048]{1,0:T(8,128)(2,1)} collective-permute-done((bf16[512,2048]{1,0:T(8,128)(2,1)}, bf16[512,2048]{1,0:T(8,128)(2,1)}, u32[]{:S(2)}, u32[]{:S(2)}) %collective-permute-start.4) | collective-permute-done | bytes 2097184 | tf_op jit(solution)/shard_map/ppermute | solution.py:946
  374.8 2.8 collective-permute-done.7.second_ref
  379.4 26.5 %ffn.5 = (bf16[8,512,704]{2,1,0:T(8,128)(2,1)}, bf16[8,512,704]{2,1,0:T(8,128)(2,1)}, bf16[8,512,704]{2,1,0:T(8,128)(2,1)}, bf16[8,512,2048]{2,1,0:T(8,128)(2,1)...) custom-call(s32[2]{0:T(128)S(1)} %get-tuple-element.418.places_ref, ...), custom_call_target="tpu_custom_call", output_to_operand_aliasing={{0}: (7, {}), {1}: (8, {}), {2}: (9, {}), {3}: (10, {}), {4... | custom-call | flops 17716740096 | bytes 29622272 | tf_op jit(solution)/shard_map/ffn/pallas_call | solution.py:421
  406.8 26.3 %ffn.6 = (bf16[8,512,704]{2,1,0:T(8,128)(2,1)}, bf16[8,512,704]{2,1,0:T(8,128)(2,1)}, bf16[8,512,704]{2,1,0:T(8,128)(2,1)}, bf16[8,512,2048]{2,1,0:T(8,128)(2,1)...) custom-call(s32[2]{0:T(128)S(1)} %get-tuple-element.420.places_ref, ...), custom_call_target="tpu_custom_call", output_to_operand_aliasing={{0}: (7, {}), {1}: (8, {}), {2}: (9, {}), {3}: (10, {}), {4... | custom-call | flops 17716740096 | bytes 29622272 | tf_op jit(solution)/shard_map/ffn/pallas_call | solution.py:421
  434.9 3.3 collective-permute-done.14
  440.9 26.0 %ffn.7 = (bf16[8,512,704]{2,1,0:T(8,128)(2,1)}, bf16[8,512,704]{2,1,0:T(8,128)(2,1)}, bf16[8,512,704]{2,1,0:T(8,128)(2,1)}, bf16[8,512,2048]{2,1,0:T(8,128)(2,1)...) custom-call(s32[2]{0:T(128)S(1)} %get-tuple-element.419.places_ref, ...), custom_call_target="tpu_custom_call", output_to_operand_aliasing={{0}: (7, {}), {1}: (8, {}), {2}: (9, {}), {3}: (10, {}), {4... | custom-call | flops 17716740096 | bytes 29622272 | tf_op jit(solution)/shard_map/ffn/pallas_call | solution.py:421
  467.0 4.0 collective-permute-done.16
  473.4 18.9 %side_terms.2 = bf16[4,8,64,704]{3,2,1,0:T(8,128)(2,1)} custom-call(bf16[4096,2048]{1,0:T(8,128)(2,1)} %bitcast.153, bf16[4096,704]{1,0:T(8,128)(2,1)} %bitcast.158), custom_call_target="tpu_custom_call" | custom-call | flops 11811160064 | bytes 28311552 | tf_op jit(solution)/shard_map/side_terms/pallas_call | solution.py:464
  492.2 5.2 collective-permute-done.17
  499.1 2.5 convert_add_fusion.2
  505.0 3.0 add_convert_fusion.2
  510.9 19.9 %side_terms.3 = bf16[4,8,64,704]{3,2,1,0:T(8,128)(2,1)} custom-call(bf16[4096,2048]{1,0:T(8,128)(2,1)} %bitcast.154, bf16[4096,704]{1,0:T(8,128)(2,1)} %bitcast.159), custom_call_target="tpu_custom_call" | custom-call | flops 11811160064 | bytes 28311552 | tf_op jit(solution)/shard_map/side_terms/pallas_call | solution.py:464
  532.4 9.2 %collective-permute-done.20 = bf16[256,2048]{1,0:T(8,128)(2,1)} collective-permute-done((bf16[256,2048]{1,0:T(8,128)(2,1)}, bf16[256,2048]{1,0:T(8,128)(2,1)}, u32[]{:S(2)}, u32[]{:S(2)}) %collective-permute-start.20) | collective-permute-done | bytes 1048608 | tf_op jit(solution)/shard_map/ppermute | solution.py:946
  548.7 2.6 fusion.2
  553.2 4.2 fusion.28
  557.4 10.2 %convolution_convert_fusion.1 = bf16[2048,512]{1,0:T(8,128)(2,1)} fusion(bf16[2048,2048]{1,0:T(8,128)(2,1)} %all-gather.4.cloned.1.call-done, bf16[512,2048]{1,0:T(8,128)(2,1)S(1)} %get-tuple-element.351), kind=kOutput, calls=%fused_computation.13 | convolution fusion | flops 4296015872 | bytes 12582912 | tf_op jit(solution)/shard_map/ed,td->et/dot_general | solution.py:1186
  567.6 8.2 collective-permute-done.23
  575.9 4.4 all-to-all-start.1
  580.3 19.5 %down_terms.1 = bf16[704,2048]{1,0:T(8,128)(2,1)} custom-call(bf16[4096,704]{1,0:T(8,128)(2,1)} %bitcast.157, bf16[4096,2048]{1,0:T(8,128)(2,1)} %all-gather.6.cloned.1.call-done), custom_call_target="tpu_custom_call" | custom-call | flops 11811160064 | bytes 22544384 | tf_op jit(solution)/shard_map/down_terms/pallas_call | solution.py:497
  599.8 2.6 convert_add_fusion.8
  602.8 2.2 convert_add_fusion.7
  606.3 8.3 convolution_convert_fusion
  614.7 10.6 %collective-permute-done.24 = bf16[8,64,704]{2,1,0:T(8,128)(2,1)} collective-permute-done((bf16[8,64,704]{2,1,0:T(8,128)(2,1)}, bf16[8,64,704]{2,1,0:T(8,128)(2,1)}, u32[]{:S(2)}, u32[]{:S(2)}) %collective-permute-start.24) | collective-permute-done | bytes 720928 | tf_op jit(solution)/shard_map/ppermute | solution.py:907
  628.1 34.4 %attend_back.2 = (bf16[256,2816]{1,0:T(8,128)(2,1)}, f32[4096,64]{1,0:T(8,128)}, f32[4096,64]{1,0:T(8,128)}) custom-call(s32[16,4]{1,0:T(8,128)} %copy.128.bounds_ref.refs_0_, bf16[256,2816]{1,0:T(8,128)(2,1)} %get-tuple-element.244.q_ref, bf16[4096,64]{1,0:T(8,128)(2,1)} %get-tuple-element.227.refs_6_.k_ref, bf16[64,4096]{1,0:T(8,128)(2,1)} %get-tuple-element.245.kt_ref, ...), custom_call_target="tpu_custom_call" | custom-call | flops 53687091200 | bytes 8388608 | tf_op jit(solution)/shard_map/attend_back/pallas_call | solution.py:293
  662.6 11.2 %collective-permute-done.27 = bf16[176,2048]{1,0:T(8,128)(2,1)} collective-permute-done((bf16[176,2048]{1,0:T(8,128)(2,1)S(1)}, bf16[176,2048]{1,0:T(8,128)(2,1)}, u32[]{:S(2)}, u32[]{:S(2)}) %collective-permute-start.27) | collective-permute-done | bytes 720928 | tf_op jit(solution)/shard_map/ppermute | solution.py:907
  673.8 2.4 convert_add_fusion.12
  680.7 3.8 all-to-all-start.2
  684.5 19.5 %attend_back.3 = (bf16[256,1280]{1,0:T(8,128)(2,1)}, bf16[128,4096]{1,0:T(8,128)(2,1)}) custom-call(s32[16,4]{1,0:T(8,128)} %copy.128.bounds_ref.refs_0_, bf16[256,1280]{1,0:T(8,128)(2,1)} %get-tuple-element.366.q_ref, bf16[4096,64]{1,0:T(8,128)(2,1)} %get-tuple-element.227.refs_6_.k_ref, bf16[64,4096]{1,0:T(8,128)(2,1)} %get-tuple-element.245.kt_ref, ...), custom_call_target="tpu_custom_call" | custom-call | flops 53687091200 | bytes 8388608 | tf_op jit(solution)/shard_map/attend_back/pallas_call | solution.py:293
  705.5 59.0 %reduce-scatter.9.cloned.1.call-done = bf16[256,2048]{1,0:T(8,128)(2,1)} async-done(((bf16[2048,2048]{1,0:T(8,128)(2,1)}), bf16[256,2048]{1,0:T(8,128)(2,1)}) %reduce-scatter.9.cloned.1.call-update) | async-done | bytes 1048592 | tf_op jit(solution)/shard_map/reduce_scatter | solution.py:1115
  764.6 2.6 fusion.5
  770.9 93.4 %tail.1 = (f32[512,2048]{1,0:T(8,128)}, bf16[8,64,384]{2,1,0:T(8,128)(2,1)}) custom-call(bf16[384,4096]{1,0:T(8,128)(2,1)} %pad_maximum_fusion.d_ref, bf16[512,2048]{1,0:T(8,128)(2,1)} %get-tuple-element.242.w_ref, bf16[512,2048]{1,0:T(8,128)(2,1)} %bitcast.143, f32[512,2048]{1,0:T(8,128)} %get-tuple-element.379.dh_ref, bf16[4096,2048]{1,0:T(8,128)(2,1)} %bitcast.161), custom_call_target="tpu_custom_call" | custom-call | flops 1073741824 | bytes 1048576 | tf_op jit(solution)/shard_map/tail/pallas_call | solution.py:725
  877.8 2.7 convert_add_fusion.10
  880.6 3.8 fusion
  (263 shorter events, 103.5 us)
Async XLA Ops:
  7.2 7.2 copy-start.26
  7.2 201.3 %all-gather.4.cloned.1.call-start = ((), (), s32[]{:S(2)}) async-start(), calls=%async_computation.7 | async-start | bytes 9437184 | tf_op jit(solution)/shard_map/all_gather | solution.py:1055
  130.6 5.8 copy-start.14
  136.4 167.1 %all-gather.6.cloned.1.call-start = ((), (), s32[]{:S(2)}) async-start(), calls=%async_computation.12 | async-start | bytes 18874368 | tf_op jit(solution)/shard_map/all_gather | solution.py:1084
  139.4 33.4 %collective-permute-start = (bf16[8,2,64,704]{3,2,0,1:T(8,128)(2,1)}, bf16[8,2,64,704]{3,2,0,1:T(8,128)(2,1)}, u32[]{:S(2)}, u32[]{:S(2)}) collective-permute-start(bf16[8,2,64,704]{3,2,0,1:T(8,128)(2,1)} %copy.126), channel_id=1, source_target_pairs={{0,1},{1,2},{2,3},{3,0},{4,5},{5,6},{6,7},{7,4},{8,9},{9,10},{10,1... | collective-permute-start | bytes 4325384 | tf_op jit(solution)/shard_map/ppermute | solution.py:907
  173.4 35.1 %collective-permute-start.1 = (bf16[8,2,64,704]{3,2,0,1:T(8,128)(2,1)}, bf16[8,2,64,704]{3,2,0,1:T(8,128)(2,1)}, u32[]{:S(2)}, u32[]{:S(2)}) collective-permute-start(bf16[8,2,64,704]{3,2,0,1:T(8,128)(2,1)} %collective-permute-done), channel_id=1, source_target_pairs={{0,1},{1,2},{2,3},{3,0},{4,5},{5,6},{6,7},{7,4},{8,9},{9,10},{10,1... | collective-permute-start | bytes 4325384 | tf_op jit(solution)/shard_map/ppermute | solution.py:907
  208.5 31.2 %collective-permute-start.2 = (bf16[8,2,64,704]{3,2,0,1:T(8,128)(2,1)}, bf16[8,2,64,704]{3,2,0,1:T(8,128)(2,1)}, u32[]{:S(2)}, u32[]{:S(2)}) collective-permute-start(bf16[8,2,64,704]{3,2,0,1:T(8,128)(2,1)} %collective-permute-done.1), channel_id=1, source_target_pairs={{0,1},{1,2},{2,3},{3,0},{4,5},{5,6},{6,7},{7,4},{8,9},{9,10},{10,1... | collective-permute-start | bytes 4325384 | tf_op jit(solution)/shard_map/ppermute | solution.py:907
  239.7 53.8 %all-to-all-start = ((bf16[8,256,512]{2,1,0:T(8,128)(2,1)}), bf16[8,256,512]{2,1,0:T(8,128)(2,1)}, u32[]{:S(2)}, u32[]{:S(2)}) async-start(bf16[8,256,512]{2,1,0:T(8,128)(2,1)} %get-tuple-element.234.o_ref), calls=%async_computation | async-start | bytes 4194304 | tf_op jit(solution)/shard_map/all_to_all | solution.py:973
  244.0 381.2 %reduce-scatter.5.cloned.1.call-start = ((), (), s32[]{:S(2)}) async-start(), calls=%async_computation.8 | async-start | bytes 9437184 | tf_op jit(solution)/shard_map/reduce_scatter | solution.py:1115
  314.0 9.4 %collective-permute-start.3 = (bf16[512,2048]{1,0:T(8,128)(2,1)}, bf16[512,2048]{1,0:T(8,128)(2,1)}, u32[]{:S(2)}, u32[]{:S(2)}) collective-permute-start(bf16[512,2048]{1,0:T(8,128)(2,1)} %multiply_convert_fusion.first_ref), channel_id=1, source_target_pairs={{0,4},{4,0},{8,12},{12,8},{16,20},{20,16},{24,28},{28,24},{1,5},{5... | collective-permute-start | bytes 6291464 | tf_op jit(solution)/shard_map/ppermute | solution.py:946
  320.7 48.2 %collective-permute-start.4 = (bf16[512,2048]{1,0:T(8,128)(2,1)}, bf16[512,2048]{1,0:T(8,128)(2,1)}, u32[]{:S(2)}, u32[]{:S(2)}) collective-permute-start(bf16[512,2048]{1,0:T(8,128)(2,1)} %multiply_convert_fusion.first_ref), channel_id=1, source_target_pairs={{0,8},{4,12},{8,0},{12,4},{16,24},{20,28},{24,16},{28,20},{1,9},{5... | collective-permute-start | bytes 6291464 | tf_op jit(solution)/shard_map/ppermute | solution.py:946
  322.2 47.8 %collective-permute-start.5 = (bf16[512,2048]{1,0:T(8,128)(2,1)}, bf16[512,2048]{1,0:T(8,128)(2,1)}, u32[]{:S(2)}, u32[]{:S(2)}) collective-permute-start(bf16[512,2048]{1,0:T(8,128)(2,1)} %multiply_convert_fusion.first_ref), channel_id=1, source_target_pairs={{0,16},{4,20},{8,24},{12,28},{16,0},{20,4},{24,8},{28,12},{1,17},{... | collective-permute-start | bytes 6291464 | tf_op jit(solution)/shard_map/ppermute | solution.py:946
  323.3 28.6 %copy-start = (bf16[1,8,4,64,704]{4,3,2,1,0:T(8,128)(2,1)}, bf16[1,8,4,64,704]{4,3,2,1,0:T(8,128)(2,1)S(1)}, u32[]{:S(2)}) copy-start(bf16[1,8,4,64,704]{4,3,2,1,0:T(8,128)(2,1)S(1)} %get-tuple-element.402) | copy-start | bytes 8650756
  370.0 4.7 collective-permute-start.6
  370.1 7.5 collective-permute-start.7
  370.6 35.3 %collective-permute-start.10 = (bf16[512,2048]{1,0:T(8,128)(2,1)}, bf16[512,2048]{1,0:T(8,128)(2,1)}, u32[]{:S(2)}, u32[]{:S(2)}) collective-permute-start(bf16[512,2048]{1,0:T(8,128)(2,1)} %get-tuple-element.291), channel_id=1, source_target_pairs={{0,4},{4,0},{8,12},{12,8},{16,20},{20,16},{24,28},{28,24},{1,5},{5... | collective-permute-start | bytes 6291464 | tf_op jit(solution)/shard_map/ppermute | solution.py:946
  370.6 6.9 copy-start.1
  373.4 32.5 %collective-permute-start.8 = (bf16[256,2048]{1,0:T(8,128)(2,1)S(1)}, bf16[256,2048]{1,0:T(8,128)(2,1)S(1)}, u32[]{:S(2)}, u32[]{:S(2)}) collective-permute-start(bf16[256,2048]{1,0:T(8,128)(2,1)S(1)} %slice.76), channel_id=1, source_target_pairs={{0,16},{4,20},{8,24},{12,28},{16,0},{20,4},{24,8},{28,12},{1,17},{... | collective-permute-start | bytes 3145736 | tf_op jit(solution)/shard_map/ppermute | solution.py:946
  374.0 31.9 %collective-permute-start.9 = (bf16[256,2048]{1,0:T(8,128)(2,1)S(1)}, bf16[256,2048]{1,0:T(8,128)(2,1)S(1)}, u32[]{:S(2)}, u32[]{:S(2)}) collective-permute-start(bf16[256,2048]{1,0:T(8,128)(2,1)S(1)} %slice.77), channel_id=1, source_target_pairs={{0,8},{4,12},{8,0},{12,4},{16,24},{20,28},{24,16},{28,20},{1,9},{5... | collective-permute-start | bytes 3145736 | tf_op jit(solution)/shard_map/ppermute | solution.py:946
  405.9 27.2 %collective-permute-start.12 = (bf16[512,2048]{1,0:T(8,128)(2,1)S(1)}, bf16[512,2048]{1,0:T(8,128)(2,1)S(1)}, u32[]{:S(2)}, u32[]{:S(2)}) collective-permute-start(bf16[512,2048]{1,0:T(8,128)(2,1)S(1)} %get-tuple-element.312), channel_id=1, source_target_pairs={{0,4},{4,0},{8,12},{12,8},{16,20},{20,16},{24,28},{28,24},{1,5},{5... | collective-permute-start | bytes 6291464 | tf_op jit(solution)/shard_map/ppermute | solution.py:946
  406.3 27.6 %collective-permute-start.11 = (bf16[512,2048]{1,0:T(8,128)(2,1)S(1)}, bf16[512,2048]{1,0:T(8,128)(2,1)S(1)}, u32[]{:S(2)}, u32[]{:S(2)}) collective-permute-start(bf16[512,2048]{1,0:T(8,128)(2,1)S(1)} %constant_dynamic-update-slice_fusion.first_ref), channel_id=1, source_target_pairs={{0,4},{4,0},{8,12},{12,8},{16,20},{20,16},{24,28},{28,24},{1,5},{5... | collective-permute-start | bytes 6291464 | tf_op jit(solution)/shard_map/ppermute | solution.py:946
  433.9 4.2 collective-permute-start.14
  434.2 32.6 %collective-permute-start.13 = (bf16[256,2048]{1,0:T(8,128)(2,1)S(1)}, bf16[256,2048]{1,0:T(8,128)(2,1)S(1)}, u32[]{:S(2)}, u32[]{:S(2)}) collective-permute-start(bf16[256,2048]{1,0:T(8,128)(2,1)S(1)} %slice.132), channel_id=1, source_target_pairs={{0,8},{4,12},{8,0},{12,4},{16,24},{20,28},{24,16},{28,20},{1,9},{5... | collective-permute-start | bytes 3145736 | tf_op jit(solution)/shard_map/ppermute | solution.py:946
  439.1 27.8 %collective-permute-start.15 = (bf16[256,2048]{1,0:T(8,128)(2,1)S(1)}, bf16[256,2048]{1,0:T(8,128)(2,1)S(1)}, u32[]{:S(2)}, u32[]{:S(2)}) collective-permute-start(bf16[256,2048]{1,0:T(8,128)(2,1)S(1)} %slice.131), channel_id=1, source_target_pairs={{0,16},{4,20},{8,24},{12,28},{16,0},{20,4},{24,8},{28,12},{1,17},{... | collective-permute-start | bytes 3145736 | tf_op jit(solution)/shard_map/ppermute | solution.py:946
  466.9 4.2 collective-permute-start.16
  472.0 25.4 %collective-permute-start.17 = (bf16[256,2048]{1,0:T(8,128)(2,1)S(1)}, bf16[256,2048]{1,0:T(8,128)(2,1)}, u32[]{:S(2)}, u32[]{:S(2)}) collective-permute-start(bf16[256,2048]{1,0:T(8,128)(2,1)S(1)} %get-tuple-element.408), channel_id=1, source_target_pairs={{0,8},{4,12},{8,0},{12,4},{16,24},{20,28},{24,16},{28,20},{1,9},{5... | collective-permute-start | bytes 3145736 | tf_op jit(solution)/shard_map/ppermute | solution.py:946
  472.6 24.9 %collective-permute-start.18 = (bf16[256,2048]{1,0:T(8,128)(2,1)S(1)}, bf16[256,2048]{1,0:T(8,128)(2,1)S(1)}, u32[]{:S(2)}, u32[]{:S(2)}) collective-permute-start(bf16[256,2048]{1,0:T(8,128)(2,1)S(1)} %get-tuple-element.407), channel_id=1, source_target_pairs={{0,16},{4,20},{8,24},{12,28},{16,0},{20,4},{24,8},{28,12},{1,17},{... | collective-permute-start | bytes 3145736 | tf_op jit(solution)/shard_map/ppermute | solution.py:946
  497.6 176.2 %reduce-scatter.7.cloned.1.call-start = ((), (), s32[]{:S(2)}) async-start(), calls=%async_computation.9 | async-start | bytes 9437184 | tf_op jit(solution)/shard_map/reduce_scatter | solution.py:1115
  503.2 29.1 %collective-permute-start.19 = (bf16[256,2048]{1,0:T(8,128)(2,1)}, bf16[256,2048]{1,0:T(8,128)(2,1)}, u32[]{:S(2)}, u32[]{:S(2)}) collective-permute-start(bf16[256,2048]{1,0:T(8,128)(2,1)} %add_convert_fusion.3), channel_id=1, source_target_pairs={{0,8},{4,12},{8,0},{12,4},{16,24},{20,28},{24,16},{28,20},{1,9},{5... | collective-permute-start | bytes 3145736 | tf_op jit(solution)/shard_map/ppermute | solution.py:946
  508.0 33.6 %collective-permute-start.20 = (bf16[256,2048]{1,0:T(8,128)(2,1)}, bf16[256,2048]{1,0:T(8,128)(2,1)}, u32[]{:S(2)}, u32[]{:S(2)}) collective-permute-start(bf16[256,2048]{1,0:T(8,128)(2,1)} %add_convert_fusion.2), channel_id=1, source_target_pairs={{0,16},{4,20},{8,24},{12,28},{16,0},{20,4},{24,8},{28,12},{1,17},{... | collective-permute-start | bytes 3145736 | tf_op jit(solution)/shard_map/ppermute | solution.py:946
  509.4 21.4 %collective-permute-start.21 = (bf16[8,64,704]{2,1,0:T(8,128)(2,1)}, bf16[8,64,704]{2,1,0:T(8,128)(2,1)}, u32[]{:S(2)}, u32[]{:S(2)}) collective-permute-start(bf16[8,64,704]{2,1,0:T(8,128)(2,1)} %dynamic-slice_bitcast_fusion.1), channel_id=1, source_target_pairs={{0,1},{1,2},{2,3},{3,0},{4,5},{5,6},{6,7},{7,4},{8,9},{9,10},{10,1... | collective-permute-start | bytes 2162696 | tf_op jit(solution)/shard_map/ppermute | solution.py:907
  530.9 17.9 %copy-start.32 = (bf16[256,2048]{1,0:T(8,128)(2,1)S(1)}, bf16[256,2048]{1,0:T(8,128)(2,1)}, u32[]{:S(2)}) copy-start(bf16[256,2048]{1,0:T(8,128)(2,1)} %copy-done.31) | copy-start | bytes 3145732
  530.9 17.9 %copy-start.34 = (bf16[256,2048]{1,0:T(8,128)(2,1)S(1)}, bf16[256,2048]{1,0:T(8,128)(2,1)}, u32[]{:S(2)}) copy-start(bf16[256,2048]{1,0:T(8,128)(2,1)} %copy-done.33) | copy-start | bytes 3145732
  543.6 24.0 %collective-permute-start.22 = (bf16[8,64,704]{2,1,0:T(8,128)(2,1)}, bf16[8,64,704]{2,1,0:T(8,128)(2,1)}, u32[]{:S(2)}, u32[]{:S(2)}) collective-permute-start(bf16[8,64,704]{2,1,0:T(8,128)(2,1)} %dynamic-slice_bitcast_fusion), channel_id=1, source_target_pairs={{0,1},{1,2},{2,3},{3,0},{4,5},{5,6},{6,7},{7,4},{8,9},{9,10},{10,1... | collective-permute-start | bytes 2162696 | tf_op jit(solution)/shard_map/ppermute | solution.py:907
  547.3 28.5 %collective-permute-start.23 = (bf16[8,64,704]{2,1,0:T(8,128)(2,1)}, bf16[8,64,704]{2,1,0:T(8,128)(2,1)}, u32[]{:S(2)}, u32[]{:S(2)}) collective-permute-start(bf16[8,64,704]{2,1,0:T(8,128)(2,1)} %convert_add_fusion.9), channel_id=1, source_target_pairs={{0,1},{1,2},{2,3},{3,0},{4,5},{5,6},{6,7},{7,4},{8,9},{9,10},{10,1... | collective-permute-start | bytes 2162696 | tf_op jit(solution)/shard_map/ppermute | solution.py:907
  557.4 10.2 %copy-start.27 = (bf16[512,2048]{1,0:T(8,128)(2,1)}, bf16[512,2048]{1,0:T(8,128)(2,1)S(1)}, u32[]{:S(2)}) copy-start(bf16[512,2048]{1,0:T(8,128)(2,1)S(1)} %get-tuple-element.351) | copy-start | bytes 6291460
  575.9 49.4 %all-to-all-start.1 = ((bf16[8,256,512]{2,1,0:T(8,128)(2,1)}), bf16[8,256,512]{2,1,0:T(8,128)(2,1)}, u32[]{:S(2)}, u32[]{:S(2)}) async-start(bf16[8,256,512]{2,1,0:T(8,128)(2,1)} %bitcast.169), calls=%async_computation.1 | async-start | bytes 4194304 | tf_op jit(solution)/shard_map/all_to_all | solution.py:973
  580.2 184.3 %reduce-scatter.9.cloned.1.call-start = ((), (), s32[]{:S(2)}) async-start(), calls=%async_computation.10 | async-start | bytes 9437184 | tf_op jit(solution)/shard_map/reduce_scatter | solution.py:1115
  599.8 6.6 copy-start.28
  602.4 22.9 %collective-permute-start.24 = (bf16[8,64,704]{2,1,0:T(8,128)(2,1)}, bf16[8,64,704]{2,1,0:T(8,128)(2,1)}, u32[]{:S(2)}, u32[]{:S(2)}) collective-permute-start(bf16[8,64,704]{2,1,0:T(8,128)(2,1)} %convert_add_fusion.8), channel_id=1, source_target_pairs={{0,1},{1,2},{2,3},{3,0},{4,5},{5,6},{6,7},{7,4},{8,9},{9,10},{10,1... | collective-permute-start | bytes 2162696 | tf_op jit(solution)/shard_map/ppermute | solution.py:907
  605.0 57.6 %collective-permute-start.25 = (bf16[8,64,704]{2,1,0:T(8,128)(2,1)}, bf16[8,64,704]{2,1,0:T(8,128)(2,1)}, u32[]{:S(2)}, u32[]{:S(2)}) collective-permute-start(bf16[8,64,704]{2,1,0:T(8,128)(2,1)} %convert_add_fusion.7), channel_id=1, source_target_pairs={{0,1},{1,2},{2,3},{3,0},{4,5},{5,6},{6,7},{7,4},{8,9},{9,10},{10,1... | collective-permute-start | bytes 2162696 | tf_op jit(solution)/shard_map/ppermute | solution.py:907
  626.8 35.8 %collective-permute-start.26 = (bf16[8,64,704]{2,1,0:T(8,128)(2,1)S(1)}, bf16[8,64,704]{2,1,0:T(8,128)(2,1)}, u32[]{:S(2)}, u32[]{:S(2)}) collective-permute-start(bf16[8,64,704]{2,1,0:T(8,128)(2,1)S(1)} %convert_add_fusion.6), channel_id=1, source_target_pairs={{0,1},{1,2},{2,3},{3,0},{4,5},{5,6},{6,7},{7,4},{8,9},{9,10},{10,1... | collective-permute-start | bytes 2162696 | tf_op jit(solution)/shard_map/ppermute | solution.py:907
  628.1 45.8 %collective-permute-start.27 = (bf16[176,2048]{1,0:T(8,128)(2,1)S(1)}, bf16[176,2048]{1,0:T(8,128)(2,1)}, u32[]{:S(2)}, u32[]{:S(2)}) collective-permute-start(bf16[176,2048]{1,0:T(8,128)(2,1)S(1)} %dynamic-slice_bitcast_fusion.2), channel_id=1, source_target_pairs={{0,1},{1,2},{2,3},{3,0},{4,5},{5,6},{6,7},{7,4},{8,9},{9,10},{10,1... | collective-permute-start | bytes 2162696 | tf_op jit(solution)/shard_map/ppermute | solution.py:907
  676.3 27.8 %collective-permute-start.28 = (bf16[176,2048]{1,0:T(8,128)(2,1)}, bf16[176,2048]{1,0:T(8,128)(2,1)}, u32[]{:S(2)}, u32[]{:S(2)}) collective-permute-start(bf16[176,2048]{1,0:T(8,128)(2,1)} %convert_add_fusion.12), channel_id=1, source_target_pairs={{0,1},{1,2},{2,3},{3,0},{4,5},{5,6},{6,7},{7,4},{8,9},{9,10},{10,1... | collective-permute-start | bytes 2162696 | tf_op jit(solution)/shard_map/ppermute | solution.py:907
  680.7 24.9 %all-to-all-start.2 = ((bf16[8,2,64,704]{3,2,1,0:T(8,128)(2,1)}), bf16[8,2,64,704]{3,2,1,0:T(8,128)(2,1)S(1)}, u32[]{:S(2)}, u32[]{:S(2)}) async-start(bf16[8,2,64,704]{3,2,1,0:T(8,128)(2,1)} %copy.134), calls=%async_computation.5 | async-start | bytes 3145728 | tf_op jit(solution)/shard_map/all_to_all | solution.py:973
  684.5 179.9 %reduce-scatter.11.cloned.1.call-start = ((), (), s32[]{:S(2)}) async-start(), calls=%async_computation.11 | async-start | bytes 1310720 | tf_op jit(solution)/shard_map/reduce_scatter | solution.py:1241
  704.1 64.7 %copy-start.30 = (bf16[256,2816]{1,0:T(8,128)(2,1)S(1)}, bf16[256,2816]{1,0:T(8,128)(2,1)}, u32[]{:S(2)}) copy-start(bf16[256,2816]{1,0:T(8,128)(2,1)} %get-tuple-element.365) | copy-start | bytes 4325380
  767.1 99.1 %collective-permute-start.29 = (bf16[176,2048]{1,0:T(8,128)(2,1)}, bf16[176,2048]{1,0:T(8,128)(2,1)}, u32[]{:S(2)}, u32[]{:S(2)}) collective-permute-start(bf16[176,2048]{1,0:T(8,128)(2,1)} %fusion.5), channel_id=1, source_target_pairs={{0,1},{1,2},{2,3},{3,0},{4,5},{5,6},{6,7},{7,4},{8,9},{9,10},{10,1... | collective-permute-start | bytes 2162696 | tf_op jit(solution)/shard_map/ppermute | solution.py:907
  (35 other events, 99.3 us)
Sparse Core Ops, SparseCore 0:
  136.6 52.6 all-gather.3
  191.2 112.3 all-gather.5
  497.7 78.3 reduce-scatter.4
  579.8 71.2 reduce-scatter.6
  674.0 90.5 reduce-scatter.8
  766.8 38.1 reduce-scatter.10

commit v5 on v4

--- a/solution.py
+++ b/solution.py
@@ -19,7 +19,7 @@
 BF = jnp.bfloat16
 F32 = jnp.float32
 VMEM_LIMIT = 56 * 1024 * 1024
-FFN_VMEM = 34 * 1024 * 1024
+FFN_VMEM = 40 * 1024 * 1024
 MESH = pl.DeviceIdType.MESH
 
 
@@ -357,12 +357,14 @@
     )(x_all, w_ext)
 
 
-def ffn_kernel(
-    places_ref, first_ref, second_ref, dy_ref, gate_ref, up_ref, down_ref, *rest
-):
-    act_ref, dg_ref, du_ref, n_ref, ya_ref, yb_ref, pa_ref, pb_ref = rest[-8:]
+def ffn_kernel(tiles, places_ref, *refs):
+    n_refs, (dy_ref, gate_ref, up_ref, down_ref) = refs[:tiles], refs[tiles : tiles + 4]
+    outs = refs[-(6 + tiles) :]
+    act_ref, dg_ref, du_ref, n_ref, ya_ref, yb_ref = outs[:6]
     which = pl.program_id(0)
-    n = jnp.where(which == 0, first_ref[...], second_ref[...])
+    n = n_refs[0][...]
+    for t in range(1, tiles):
+        n = jnp.where(which == t, n_refs[t][...], n)
     n_ref[0] = n
     dy = dy_ref[0]
     across = (((1,), (1,)), ((), ()))
@@ -383,65 +385,65 @@
     part = lax.dot_general(d_gate, gate_ref[...], across, preferred_element_type=F32)
     part += lax.dot_general(d_up, up_ref[...], across, preferred_element_type=F32)
     part = part.astype(BF)
-
-    @pl.when(which == 0)
-    def _():
-        pa_ref[...] = part
-
-    @pl.when(which == 1)
-    def _():
-        pb_ref[...] = part
-
-
-def ffn_chunk(places, first, second, dy_all, gate_w, up_w, down_w, kept):
-    local, width = first.shape
+    for t in range(tiles):
+
+        @pl.when(which == t)
+        def _(t=t):
+            outs[6 + t][...] = part
+
+
+def ffn_chunk(tiles, dy_all, gate_w, up_w, down_w, kept):
+    count, local, width = dy_all.shape
     hidden = gate_w.shape[1]
     tall = min(256, local)
-    tiles = local // tall
-    count = dy_all.shape[0]
+    number = len(tiles)
+    places = jnp.stack(
+        [jnp.asarray(t[2], jnp.int32) for t in tiles] + [jnp.int32(t[3]) for t in tiles]
+    )
 
     def at_place(last):
-        return pl.BlockSpec((1, tall, last), lambda i, t, p: (p[i], t, 0))
-
-    ahead = pl.BlockSpec((tall, width), lambda i, t, p: (jnp.where(i == 0, t, tiles - 1), 0))
-    behind = pl.BlockSpec((tall, width), lambda i, t, p: (jnp.where(i == 0, 0, t), 0))
+        return pl.BlockSpec((1, tall, last), lambda i, p: (p[i], p[number + i], 0))
+
+    def fixed(n):
+        return pl.BlockSpec((tall, width), lambda i, p: (n, 0))
 
     held = pl.BlockSpec(memory_space=pltpu.VMEM)
-    in_specs = [ahead, behind, at_place(width), held, held, held]
-    arrays = [first, second, dy_all, gate_w, up_w, down_w]
+    in_specs = [fixed(t[1]) for t in tiles] + [at_place(width), held, held, held]
+    arrays = [t[0] for t in tiles] + [dy_all, gate_w, up_w, down_w]
     aliases = {}
     if kept is not None:
+        aliases = {1 + len(arrays) + n: n for n in range(6)}
         in_specs += [pl.BlockSpec(memory_space=pl.ANY)] * 6
         arrays += list(kept)
-        aliases = {7 + n: n for n in range(6)}
     narrow = jax.ShapeDtypeStruct((count, local, hidden), BF)
     broad = jax.ShapeDtypeStruct((count, local, width), BF)
     part = jax.ShapeDtypeStruct((count, local, width // 2), BF)
-    single = jax.ShapeDtypeStruct((local, width), BF)
+    single = jax.ShapeDtypeStruct((tall, width), BF)
     outs = pl.pallas_call(
-        ffn_kernel,
-        out_shape=(narrow, narrow, narrow, broad, part, part, single, single),
+        functools.partial(ffn_kernel, number),
+        out_shape=(narrow, narrow, narrow, broad, part, part) + (single,) * number,
         grid_spec=pltpu.PrefetchScalarGridSpec(
             num_scalar_prefetch=1,
-            grid=(2, tiles),
+            grid=(number,),
             in_specs=in_specs,
             out_specs=(
                 at_place(hidden), at_place(hidden), at_place(hidden), at_place(width),
-                at_place(width // 2), at_place(width // 2), ahead, behind,
-            ),
+                at_place(width // 2), at_place(width // 2),
+            )
+            + (fixed(0),) * number,
         ),
         input_output_aliases=aliases,
         compiler_params=pltpu.CompilerParams(
-            dimension_semantics=("arbitrary", "arbitrary"), vmem_limit_bytes=FFN_VMEM
+            dimension_semantics=("arbitrary",), vmem_limit_bytes=FFN_VMEM
         ),
         cost_estimate=pl.CostEstimate(
-            flops=2 * 6 * 2 * local * width * hidden,
-            bytes_accessed=2 * (5 * 2 * local * width + 3 * width * hidden),
-            transcendentals=2 * local * hidden,
+            flops=12 * number * tall * width * hidden,
+            bytes_accessed=2 * (5 * number * tall * width + 3 * width * hidden),
+            transcendentals=number * tall * hidden,
         ),
         name="ffn",
     )(places, *arrays)
-    return outs[:6], outs[6], outs[7]
+    return outs[:6], list(outs[6:])
 
 
 def spread(out_ref, value, per, parts, rows):
@@ -969,6 +971,17 @@
     return own.astype(F32) + swap(other, 1).astype(F32)
 
 
+def total_of(*terms):
+    total = terms[0].astype(F32)
+    for term in terms[1:]:
+        total = total + term.astype(F32)
+    return total
+
+
+def plus(*terms):
+    return total_of(*terms).astype(BF)
+
+
 def exchange(array):
     return lax.all_to_all(array, "seq", split_axis=0, concat_axis=0, tiled=True)
 
@@ -1116,60 +1129,98 @@
 
     kept = None
 
-    def chunk(kept, first, second, c):
-        places = jnp.stack([me ^ c, me ^ (c + 1)]).astype(jnp.int32)
-        return ffn_chunk(places, first, second, dy_all, gate_w, up_w, down_w, kept)
+    weights = (dy_all, gate_w, up_w, down_w)
 
     if cube:
-        side, over_x, over_y = swap(n2, 1), swap(n2, 2), swap(n2, 4)
+        side = swap(n2, 1)
+        low_n, high_n = n2[:half], n2[half:]
+        x_low, y_low = swap(low_n, 2), swap(low_n, 4)
+        x_high, y_high = swap(high_n, 2), swap(high_n, 4)
         side, gate_w, up_w = fence(side, gate_w, up_w)
-        kept, own_a, own_b = chunk(kept, n2, side, 0)
-        kept, own_a, own_b, over_x, over_y = fence(kept, own_a, own_b, over_x, over_y)
-
-        far_a, far_b = far_halves(over_x, over_y)
-        side_x, side_y, own_c = swap(over_x, 1), swap(over_y, 1), swap(own_b, 1)
-        side_x, side_y, over_x, over_y, kept = fence(side_x, side_y, over_x, over_y, kept)
-        kept, x_a, x_b = chunk(kept, over_x, side_x, 2)
-        kept, x_a, x_b, far_a, far_b, own_c = fence(kept, x_a, x_b, far_a, far_b, own_c)
-
-        far = jnp.concatenate([far_a, far_b], axis=0)
-        side_far = swap(far, 1)
-        x_sum = chip_sum(x_a, x_b)
-        x_first = swap(x_sum[:half].astype(BF), 2)
-        kept, y_a, y_b = chunk(kept, over_y, side_y, 4)
-        kept, y_a, y_b, far, side_far, x_sum = fence(kept, y_a, y_b, far, side_far, x_sum)
-
-        y_sum = chip_sum(y_a, y_b)
-        y_second = swap(y_sum[half:].astype(BF), 4)
-        kept, far_one, far_two = chunk(kept, far, side_far, 6)
-        kept, far_one, far_two, x_first, y_second, y_sum = fence(
-            kept, far_one, far_two, x_first, y_second, y_sum
+        weights = (dy_all, gate_w, up_w, down_w)
+        kept, (own_a, own_b, own_c, own_d) = ffn_chunk(
+            [(n2, 0, me, 0), (n2, 1, me, 1), (side, 0, me ^ 1, 0), (side, 1, me ^ 1, 1)],
+            *weights, kept,
+        )
+        kept, own_a, own_b, own_c, own_d, x_low, y_low = fence(
+            kept, own_a, own_b, own_c, own_d, x_low, y_low
+        )
+
+        far_a = swap(x_low, 4)
+        side_x, side_y = swap(x_low, 1), swap(y_low, 1)
+        own_c, own_d = swap(own_c, 1), swap(own_d, 1)
+        side_x, side_y, x_low, y_low, kept = fence(side_x, side_y, x_low, y_low, kept)
+        kept, (x_a, x_b, y_a, y_b) = ffn_chunk(
+            [(x_low, 0, me ^ 2, 0), (side_x, 0, me ^ 3, 0), (y_low, 0, me ^ 4, 0),
+             (side_y, 0, me ^ 5, 0)],
+            *weights, kept,
+        )
+        kept, x_a, x_b, y_a, y_b, x_high, y_high, own_c, own_d = fence(
+            kept, x_a, x_b, y_a, y_b, x_high, y_high, own_c, own_d
+        )
+
+        far_b = swap(y_high, 2)
+        side_x, side_y = swap(x_high, 1), swap(y_high, 1)
+        x_b, y_b = swap(x_b, 1), swap(y_b, 1)
+        side_x, side_y, x_high, y_high, kept, x_a, x_b = fence(
+            side_x, side_y, x_high, y_high, kept, x_a, x_b
+        )
+        x_first = swap(plus(x_a, x_b), 2)
+        kept, (x_c, x_d, y_c, y_d) = ffn_chunk(
+            [(x_high, 0, me ^ 2, 1), (side_x, 0, me ^ 3, 1), (y_high, 0, me ^ 4, 1),
+             (side_y, 0, me ^ 5, 1)],
+            *weights, kept,
+        )
+        kept, x_c, x_d, y_c, y_d, far_a, far_b, y_a, y_b = fence(
+            kept, x_c, x_d, y_c, y_d, far_a, far_b, y_a, y_b
+        )
+
+        side_far, side_more = swap(far_a, 1), swap(far_b, 1)
+        x_d, y_d = swap(x_d, 1), swap(y_d, 1)
+        side_far, side_more, y_c, y_d = fence(side_far, side_more, y_c, y_d)
+        y_second = swap(plus(y_c, y_d), 4)
+        kept, (far_one, far_two, far_three, far_four) = ffn_chunk(
+            [(far_a, 0, me ^ 6, 0), (far_b, 0, me ^ 6, 1), (side_far, 0, me ^ 7, 0),
+             (side_more, 0, me ^ 7, 1)],
+            *weights, kept,
+        )
+        kept, far_one, far_two, far_three, far_four, x_first, y_second, x_c, x_d = fence(
+            kept, far_one, far_two, far_three, far_four, x_first, y_second, x_c, x_d
         )
         act, d_gate, d_up, n2_all, y_one, y_two = kept
         n2_all, dy_rows = n2_all.reshape(sheet), dy_all.reshape(sheet)
         act, d_gate, d_up = [a.reshape(length, hidden) for a in (act, d_gate, d_up)]
 
-        far_sum = chip_sum(far_one, far_two).astype(BF)
-        x_far, y_far = swap(far_sum[:half], 2), swap(far_sum[half:], 4)
+        x_far = swap(plus(far_one, swap(far_three, 1)), 2)
+        y_far = swap(plus(far_two, swap(far_four, 1)), 4)
         gate_t = side_terms(n2_all, d_gate, count, parts)
         x_far, y_far, gate_t, y_one = fence(x_far, y_far, gate_t, y_one)
 
-        x_second = swap((x_sum[half:] + y_far.astype(F32)).astype(BF), 2)
-        y_first = swap((y_sum[:half] + x_far.astype(F32)).astype(BF), 4)
+        x_second = swap(plus(x_c, x_d, y_far), 2)
+        y_first = swap(plus(y_a, y_b, x_far), 4)
         (gate_moved,) = launch([term_of(gate_t, 0)])
         y_one = over_seq(y_one)
         up_t = side_terms(n2_all, d_up, count, parts)
         x_second, y_first, up_t, gate_moved, act = fence(x_second, y_first, up_t, gate_moved, act)
-        own_sum = own_a.astype(F32) + own_c.astype(F32)
-        first = own_sum[:half] + x_first.astype(F32) + y_first.astype(F32)
-        second = own_sum[half:] + x_second.astype(F32) + y_second.astype(F32)
-        dn2 = jnp.concatenate([first, second], axis=0)
+        dn2 = jnp.concatenate(
+            [
+                total_of(own_a, own_c, x_first, y_first),
+                total_of(own_b, own_d, x_second, y_second),
+            ],
+            axis=0,
+        )
     else:
         n2_blocks = gather_plain(n2)
         dn2_parts = []
         for c in range(0, count, 2):
-            kept, part_a, part_b = chunk(kept, n2_blocks[c], n2_blocks[c + 1], c)
-            dn2_parts += [part_a, part_b]
+            each = range(max(1, local // 256))
+            kept, found = ffn_chunk(
+                [(n2_blocks[n], t, me ^ n, t) for n in (c, c + 1) for t in each], *weights, kept
+            )
+            dn2_parts += [
+                jnp.concatenate(found[: len(each)], axis=0),
+                jnp.concatenate(found[len(each) :], axis=0),
+            ]
         act, d_gate, d_up, n2_all, y_one, y_two = kept
         n2_all, dy_rows = n2_all.reshape(sheet), dy_all.reshape(sheet)
         act, d_gate, d_up = [a.reshape(length, hidden) for a in (act, d_gate, d_up)]
@@ -1220,8 +1271,18 @@
     moved = launch(down_state if parts > 2 else [])
     saved = (bounds, qt_two, k_n, k_t, v_n, cosine, sine, starts, o_heads, do_heads, lse_two, group)
     dq_two, dkv_t = attend_back(*saved, cut, blocks - cut, (dk, dv))
-    dq_two, dkv_t, moved, down_state, part_out, ffn_back = fence(
-        dq_two, dkv_t, moved, down_state, part_out, ffn_back
+
+    def along(weight, grad):
+        return jnp.sum(weight.astype(F32) * grad, axis=1)
+
+    ffn_back, dq_two, dkv_t = fence(ffn_back, dq_two, dkv_t)
+    ffn_back = ffn_back.astype(F32)
+    grad_gate = ffn_back[:, 0].transpose(1, 0, 2).reshape(rows, count * hidden)
+    grad_up = ffn_back[:, 1].transpose(1, 0, 2).reshape(rows, count * hidden)
+    gain_sum = along(w_gate, grad_gate) + along(w_up, grad_up)
+    output = (h1 + jnp.concatenate([y_one, y_two], axis=1).astype(F32)).astype(BF)
+    dq_two, dkv_t, moved, down_state, part_out, grad_gate, grad_up, gain_sum, output = fence(
+        dq_two, dkv_t, moved, down_state, part_out, grad_gate, grad_up, gain_sum, output
     )
 
     d_t = jnp.concatenate([jnp.concatenate([dq_one, dq_two], axis=1), dkv_t], axis=0)
@@ -1249,30 +1310,21 @@
         m1 = x * r1
         e1 = dn1 * gain_one
         grad_tokens = dh1 + r1 * (e1 - m1 * jnp.mean(e1 * m1, axis=-1, keepdims=True))
-    grad_tokens, attn_back, moved, ffn_back, y_one, y_two, grad_out = fence(
-        grad_tokens, attn_back, moved, ffn_back, y_one, y_two, grad_out
-    )
+    grad_tokens, attn_back, moved, grad_out = fence(grad_tokens, attn_back, moved, grad_out)
     if parts > 3:
         down_state = ring_finish(moved, [term_down], 3)
     grad_down = down_state[0].reshape(hidden // parts, width)
-    output = (h1 + jnp.concatenate([y_one, y_two], axis=1).astype(F32)).astype(BF)
-
-    ffn_back = ffn_back.astype(F32)
-    grad_gate = ffn_back[:, 0].transpose(1, 0, 2).reshape(rows, count * hidden)
-    grad_up = ffn_back[:, 1].transpose(1, 0, 2).reshape(rows, count * hidden)
+
     attn_back = attn_back.astype(F32)
     grad_query = attn_back[:, :, :group_width].transpose(1, 0, 2).reshape(rows, H * HD)
     pair = attn_back[:, :, group_width:].reshape(KV, share, rows, 2 * HD).sum(axis=1)
     grad_key = pair[:, :, :HD].transpose(1, 0, 2).reshape(rows, KV * HD)
     grad_value = pair[:, :, HD:].transpose(1, 0, 2).reshape(rows, KV * HD)
 
-    def along(weight, grad):
-        return jnp.sum(weight.astype(F32) * grad, axis=1)
-
     grad_gain_attn = (
         along(w_query, grad_query) + along(w_key, grad_key) + along(w_value, grad_value)
     ) / gain_attn.astype(F32)
-    grad_gain_ffn = (along(w_gate, grad_gate) + along(w_up, grad_up)) / gain_ffn.astype(F32)
+    grad_gain_ffn = gain_sum / gain_ffn.astype(F32)
     return (
         output[None],
         grad_tokens[None],

time: 901 us -> 874 us (0.970)
  waiting for transfers between devices: 221 us -> 120 us
  Pallas kernels: 480 us -> 530 us
  starting transfers between devices: 32.7 us -> 47.8 us
  local copies, waits for them, and re-layouts: 60.5 us -> 72.2 us
    reduce_scatter x3, waiting for transfers between devices: 59 us -> 14.7 us  [over_seq(): return lax.psum_scatter(whole, 'seq', scatter_dimension=0, tiled=True)]
    ppermute x12, waiting for transfers between devices: 58.8 us -> 28.2 us  [hop(): return [lax.ppermute(block, 'fsdp', ring('fsdp')) for block in blocks]]
    pallas_call x2, Pallas kernels: 54 us -> 78.3 us  [attend_back(): pl.pallas_call(functools.partial(backward_kernel, group, skip, final), ou...]
    ppermute x18 -> x27, waiting for transfers between devices: 42.9 us -> 19.8 us  [swap(): return lax.ppermute(block, 'seq', [(n, n ^ bit) for n in range(count)])]
    pallas_call x2, Pallas kernels: 41.1 us -> 58.5 us  [attend(): pl.pallas_call(kernel, out_shape=out_shape, grid_spec=pltpu.PrefetchScala...]
    unnamed x91 -> x146, local copies, waits for them, and re-layouts: 25.4 us -> 37.4 us
    ppermute x12, starting transfers between devices: 10 us -> 20.5 us  [hop(): return [lax.ppermute(block, 'fsdp', ring('fsdp')) for block in blocks]]
  transfers between devices with their start and end apart: 39 -> 48, of which waited for: 19 -> 18; matrix products, arithmetic and copies ran while one was open for 9% -> 11% of each run, Pallas kernels for 41% -> 49%
where the time goes in v5:
time: 874 us; the launch traced here: 862 us
  Pallas kernels  530 us (61%)
  waiting for transfers between devices  120 us (14%)
  local copies, waits for them, and re-layouts  72.2 us (8%)
  other arithmetic  50 us (6%)
  starting transfers between devices  47.8 us (5%)
  matrix products  26 us (3%)
  between operations  15.8 us (2%)
    pallas_call x4, Pallas kernels, ffn_chunk(): pl.pallas_call(functools.partial(ffn_kernel, number), out_shape=(narrow,...  112 us
    pallas_call x1, Pallas kernels, start_gather(): pl.pallas_call(functools.partial(start_kernel, parts), out_shape=shapes,...  109 us
    pallas_call x1, Pallas kernels, tail(): pl.pallas_call(functools.partial(tail_kernel, parts, cols), out_shape=(ja...  93.3 us
    pallas_call x2, Pallas kernels, attend_back(): pl.pallas_call(functools.partial(backward_kernel, group, skip, final), ou...  78.3 us
    pallas_call x2, Pallas kernels, attend(): pl.pallas_call(kernel, out_shape=out_shape, grid_spec=pltpu.PrefetchScala...  58.5 us
    all_to_all x3, waiting for transfers between devices, exchange(): return lax.all_to_all(array, 'seq', split_axis=0, concat_axis=0, tiled=True)  48 us
    pallas_call x2, Pallas kernels, side_terms(): pl.pallas_call(functools.partial(side_kernel, per, parts, rows), out_shap...  40 us
    unnamed x146, local copies, waits for them, and re-layouts  37.4 us
  transfers between devices with their start and end apart: 48, of which 18 were waited for; matrix products, arithmetic and copies ran while one was open for 11% of the time, Pallas kernels for 49%

profile of v5, /device:TPU:0, one launch (start us, length us, event | category | flops | bytes accessed | tf_op | source)
XLA Modules:
  0.0 861.6 jit_solution(14773155025505063352)
XLA Ops:
  7.2 1.9 reshape.376
  13.8 109.1 %start_gather.1 = (bf16[8,512,2048]{2,1,0:T(8,128)(2,1)S(1)}, bf16[4,8,64,512]{3,2,1,0:T(8,128)(2,1)S(1)}, bf16[8,128,704]{2,1,0:T(8,128)(2,1)S(1)}, bf16[4,64,2...) custom-call(bf16[512,2048]{1,0:T(8,128)(2,1)S(1)} %bitcast.139, ...), custom_call_target="tpu_custom_call" | custom-call | tf_op jit(solution)/shard_map/start_gather/pallas_call | solution.py:886
  126.9 5.9 copy-done.22
  132.9 2.7 copy.126
  141.3 3.1 copy.121
  144.6 19.0 %project.1 = (bf16[8,512,2048]{2,1,0:T(8,128)(2,1)}, f32[384,4096]{1,0:T(8,128)}, bf16[512,2048]{1,0:T(8,128)(2,1)}) custom-call(bf16[8,512,2048]{2,1,0:T(8,128)(2,1)} %copy-done.22, bf16[2048,512]{1,0:T(8,128)(2,1)} %bitcast.169), custom_call_target="tpu_custom_call" | custom-call | flops 6442450944 | bytes 33554432 | tf_op jit(solution)/shard_map/project/pallas_call | solution.py:334
  163.6 2.8 multiply_sine_fusion
  166.3 2.9 collective-permute-done
  170.1 36.0 %attend.2 = (bf16[8,256,512]{2,1,0:T(8,128)(2,1)}, f32[11,1,1024]{2,1,0:T(1,128)}, bf16[256,2816]{1,0:T(8,128)(2,1)}, bf16[64,4096]{1,0:T(8,128)(2,1)}, bf16[409...) custom-call(s32[16,4]{1,0:T(8,128)} %copy.132.bounds_ref.refs_0_, ...), custom_call_target="tpu_custom_call" | custom-call | flops 42949672960 | bytes 4194304 | tf_op jit(solution)/shard_map/attend/pallas_call | solution.py:234
  206.2 2.8 collective-permute-start.2
  209.0 22.5 %attend.3 = (bf16[8,256,512]{2,1,0:T(8,128)(2,1)}, f32[5,1,1024]{2,1,0:T(1,128)}, bf16[256,1280]{1,0:T(8,128)(2,1)}) custom-call(s32[16,4]{1,0:T(8,128)} %copy.132.bounds_ref.refs_0_, f32[384,4096]{1,0:T(8,128)} %get-tuple-element.251.q_ref.kv_ref.refs_1_.refs_2_, ...), custom_call_target="tpu_custom_call", output_to_operand_aliasing={{0}: (8, {})} | custom-call | flops 42949672960 | bytes 4194304 | tf_op jit(solution)/shard_map/attend/pallas_call | solution.py:234
  231.5 6.0 collective-permute-done.2
  237.4 4.4 all-to-all-start
  243.2 48.0 %all-to-all-done = bf16[8,256,512]{2,1,0:T(8,128)(2,1)} async-done(((bf16[8,256,512]{2,1,0:T(8,128)(2,1)}), bf16[8,256,512]{2,1,0:T(8,128)(2,1)}, u32[]{:S(2)}, u32[]{:S(2)}) %all-to-all-start) | async-done | bytes 2097184 | tf_op jit(solution)/shard_map/all_to_all | solution.py:986
  291.2 8.7 %all-gather.6.cloned.1.call-done = bf16[4096,2048]{1,0:T(8,128)(2,1)} async-done(((bf16[512,2048]{1,0:T(8,128)(2,1)}), bf16[4096,2048]{1,0:T(8,128)(2,1)}) %all-gather.6.cloned.1.call-update) | async-done | bytes 16777232 | tf_op jit(solution)/shard_map/all_gather | solution.py:1097
  299.9 7.8 multiply_reduce_fusion.1
  316.1 2.3 fusion.27
  321.6 26.9 %ffn.4 = (bf16[8,512,704]{2,1,0:T(8,128)(2,1)}, bf16[8,512,704]{2,1,0:T(8,128)(2,1)}, bf16[8,512,704]{2,1,0:T(8,128)(2,1)}, bf16[8,512,2048]{2,1,0:T(8,128)(2,1)...) custom-call(s32[8]{0:T(128)S(1)} %stack.66.places_ref, ...), custom_call_target="tpu_custom_call" | custom-call | flops 17716740096 | bytes 29622272 | tf_op jit(solution)/shard_map/ffn/pallas_call | solution.py:422
  358.8 28.7 %ffn.5 = (bf16[8,512,704]{2,1,0:T(8,128)(2,1)}, bf16[8,512,704]{2,1,0:T(8,128)(2,1)}, bf16[8,512,704]{2,1,0:T(8,128)(2,1)}, bf16[8,512,2048]{2,1,0:T(8,128)(2,1)...) custom-call(s32[8]{0:T(128)S(1)} %stack.71.places_ref, ...), custom_call_target="tpu_custom_call", output_to_operand_aliasing={{0}: (9, {}), {1}: (10, {}), {2}: (11, {}), {3}: (12, {}), ... | custom-call | flops 17716740096 | bytes 29622272 | tf_op jit(solution)/shard_map/ffn/pallas_call | solution.py:422
  398.3 28.5 %ffn.6 = (bf16[8,512,704]{2,1,0:T(8,128)(2,1)}, bf16[8,512,704]{2,1,0:T(8,128)(2,1)}, bf16[8,512,704]{2,1,0:T(8,128)(2,1)}, bf16[8,512,2048]{2,1,0:T(8,128)(2,1)...) custom-call(s32[8]{0:T(128)S(1)} %stack.75.places_ref, ...), custom_call_target="tpu_custom_call", output_to_operand_aliasing={{0}: (9, {}), {1}: (10, {}), {2}: (11, {}), {3}: (12, {}), ... | custom-call | flops 17716740096 | bytes 29622272 | tf_op jit(solution)/shard_map/ffn/pallas_call | solution.py:422
  430.6 2.1 add_convert_fusion.6
  438.9 28.2 %ffn.7 = (bf16[8,512,704]{2,1,0:T(8,128)(2,1)}, bf16[8,512,704]{2,1,0:T(8,128)(2,1)}, bf16[8,512,704]{2,1,0:T(8,128)(2,1)}, bf16[8,512,2048]{2,1,0:T(8,128)(2,1)...) custom-call(s32[8]{0:T(128)S(1)} %stack.74.places_ref, ...), custom_call_target="tpu_custom_call", output_to_operand_aliasing={{0}: (9, {}), {1}: (10, {}), {2}: (11, {}), {3}: (12, {}), ... | custom-call | flops 17716740096 | bytes 29622272 | tf_op jit(solution)/shard_map/ffn/pallas_call | solution.py:422
  472.4 18.9 %side_terms.2 = bf16[4,8,64,704]{3,2,1,0:T(8,128)(2,1)} custom-call(bf16[4096,2048]{1,0:T(8,128)(2,1)} %bitcast.148, bf16[4096,704]{1,0:T(8,128)(2,1)} %bitcast.153), custom_call_target="tpu_custom_call" | custom-call | flops 11811160064 | bytes 28311552 | tf_op jit(solution)/shard_map/side_terms/pallas_call | solution.py:466
  491.3 4.2 collective-permute-done.27
  498.3 1.9 add_convert_fusion.1
  505.3 21.2 %side_terms.3 = bf16[4,8,64,704]{3,2,1,0:T(8,128)(2,1)} custom-call(bf16[4096,2048]{1,0:T(8,128)(2,1)} %bitcast.149, bf16[4096,704]{1,0:T(8,128)(2,1)} %bitcast.154), custom_call_target="tpu_custom_call" | custom-call | flops 11811160064 | bytes 28311552 | tf_op jit(solution)/shard_map/side_terms/pallas_call | solution.py:466
  526.5 5.1 collective-permute-done.28
  534.2 2.1 dynamic-slice_bitcast_fusion
  542.5 4.2 fusion.25
  546.6 10.0 %convolution_convert_fusion.1 = bf16[2048,512]{1,0:T(8,128)(2,1)} fusion(bf16[2048,2048]{1,0:T(8,128)(2,1)} %all-gather.4.cloned.1.call-done, bf16[512,2048]{1,0:T(8,128)(2,1)S(1)} %get-tuple-element.424), kind=kOutput, calls=%fused_computation.9 | convolution fusion | flops 4296015872 | bytes 12582912 | tf_op jit(solution)/shard_map/ed,td->et/dot_general | solution.py:1237
  557.5 7.2 collective-permute-done.31
  565.7 4.4 all-to-all-start.1
  570.1 19.8 %down_terms.1 = bf16[704,2048]{1,0:T(8,128)(2,1)} custom-call(bf16[4096,704]{1,0:T(8,128)(2,1)} %bitcast.152, bf16[4096,2048]{1,0:T(8,128)(2,1)} %all-gather.6.cloned.1.call-done), custom_call_target="tpu_custom_call" | custom-call | flops 11811160064 | bytes 22544384 | tf_op jit(solution)/shard_map/down_terms/pallas_call | solution.py:499
  590.0 2.4 convert_add_fusion.7
  594.5 8.3 convolution_convert_fusion
  602.8 12.1 %collective-permute-done.33 = bf16[8,64,704]{2,1,0:T(8,128)(2,1)} collective-permute-done((bf16[8,64,704]{2,1,0:T(8,128)(2,1)}, bf16[8,64,704]{2,1,0:T(8,128)(2,1)}, u32[]{:S(2)}, u32[]{:S(2)}) %collective-permute-start.33) | collective-permute-done | bytes 720928 | tf_op jit(solution)/shard_map/ppermute | solution.py:909
  617.7 45.9 %attend_back.2 = (bf16[256,2816]{1,0:T(8,128)(2,1)}, f32[4096,64]{1,0:T(8,128)}, f32[4096,64]{1,0:T(8,128)}) custom-call(s32[16,4]{1,0:T(8,128)} %copy.132.bounds_ref.refs_0_, bf16[256,2816]{1,0:T(8,128)(2,1)} %get-tuple-element.277.q_ref, bf16[4096,64]{1,0:T(8,128)(2,1)} %get-tuple-element.264.refs_6_.k_ref, bf16[64,4096]{1,0:T(8,128)(2,1)} %get-tuple-element.278.kt_ref, ...), custom_call_target="tpu_custom_call" | custom-call | flops 53687091200 | bytes 8388608 | tf_op jit(solution)/shard_map/attend_back/pallas_call | solution.py:293
  668.0 3.9 all-to-all-start.2
  672.0 2.8 convert_add_fusion.11
  674.8 3.1 collective-permute-start.37
  677.9 32.4 %attend_back.3 = (bf16[256,1280]{1,0:T(8,128)(2,1)}, bf16[128,4096]{1,0:T(8,128)(2,1)}) custom-call(s32[16,4]{1,0:T(8,128)} %copy.132.bounds_ref.refs_0_, bf16[256,1280]{1,0:T(8,128)(2,1)} %get-tuple-element.440.q_ref, bf16[4096,64]{1,0:T(8,128)(2,1)} %get-tuple-element.264.refs_6_.k_ref, bf16[64,4096]{1,0:T(8,128)(2,1)} %get-tuple-element.278.kt_ref, ...), custom_call_target="tpu_custom_call" | custom-call | flops 53687091200 | bytes 8388608 | tf_op jit(solution)/shard_map/attend_back/pallas_call | solution.py:293
  710.3 3.3 add_convert_fusion
  721.5 14.7 %reduce-scatter.9.cloned.1.call-done = bf16[256,2048]{1,0:T(8,128)(2,1)} async-done(((bf16[2048,2048]{1,0:T(8,128)(2,1)}), bf16[256,2048]{1,0:T(8,128)(2,1)}) %reduce-scatter.9.cloned.1.call-update) | async-done | bytes 1048592 | tf_op jit(solution)/shard_map/reduce_scatter | solution.py:1128
  737.8 7.5 collective-permute-start.38
  745.3 3.1 pad_maximum_fusion.d_ref
  748.4 93.3 %tail.1 = (f32[512,2048]{1,0:T(8,128)}, bf16[8,64,384]{2,1,0:T(8,128)(2,1)}) custom-call(bf16[384,4096]{1,0:T(8,128)(2,1)} %pad_maximum_fusion.d_ref, bf16[512,2048]{1,0:T(8,128)(2,1)} %get-tuple-element.283.w_ref, bf16[512,2048]{1,0:T(8,128)(2,1)} %bitcast.138, f32[512,2048]{1,0:T(8,128)} %get-tuple-element.458.dh_ref, bf16[4096,2048]{1,0:T(8,128)(2,1)} %bitcast.160), custom_call_target="tpu_custom_call" | custom-call | flops 1073741824 | bytes 1048576 | tf_op jit(solution)/shard_map/tail/pallas_call | solution.py:727
  845.2 2.7 convert_add_fusion.9
  849.6 4.7 copy.171
  (337 shorter events, 106.8 us)
Async XLA Ops:
  7.2 199.0 %all-gather.4.cloned.1.call-start = ((), (), s32[]{:S(2)}) async-start(), calls=%async_computation.7 | async-start | bytes 9437184 | tf_op jit(solution)/shard_map/all_gather | solution.py:1068
  132.8 167.1 %all-gather.6.cloned.1.call-start = ((), (), s32[]{:S(2)}) async-start(), calls=%async_computation.12 | async-start | bytes 18874368 | tf_op jit(solution)/shard_map/all_gather | solution.py:1097
  135.6 33.7 %collective-permute-start = (bf16[8,2,64,704]{3,2,0,1:T(8,128)(2,1)}, bf16[8,2,64,704]{3,2,0,1:T(8,128)(2,1)}, u32[]{:S(2)}, u32[]{:S(2)}) collective-permute-start(bf16[8,2,64,704]{3,2,0,1:T(8,128)(2,1)} %copy.126), channel_id=1, source_target_pairs={{0,1},{1,2},{2,3},{3,0},{4,5},{5,6},{6,7},{7,4},{8,9},{9,10},{10,1... | collective-permute-start | bytes 4325384 | tf_op jit(solution)/shard_map/ppermute | solution.py:909
  169.9 36.2 %collective-permute-start.1 = (bf16[8,2,64,704]{3,2,0,1:T(8,128)(2,1)}, bf16[8,2,64,704]{3,2,0,1:T(8,128)(2,1)}, u32[]{:S(2)}, u32[]{:S(2)}) collective-permute-start(bf16[8,2,64,704]{3,2,0,1:T(8,128)(2,1)} %collective-permute-done), channel_id=1, source_target_pairs={{0,1},{1,2},{2,3},{3,0},{4,5},{5,6},{6,7},{7,4},{8,9},{9,10},{10,1... | collective-permute-start | bytes 4325384 | tf_op jit(solution)/shard_map/ppermute | solution.py:909
  206.2 31.2 %collective-permute-start.2 = (bf16[8,2,64,704]{3,2,0,1:T(8,128)(2,1)}, bf16[8,2,64,704]{3,2,0,1:T(8,128)(2,1)}, u32[]{:S(2)}, u32[]{:S(2)}) collective-permute-start(bf16[8,2,64,704]{3,2,0,1:T(8,128)(2,1)} %collective-permute-done.1), channel_id=1, source_target_pairs={{0,1},{1,2},{2,3},{3,0},{4,5},{5,6},{6,7},{7,4},{8,9},{9,10},{10,1... | collective-permute-start | bytes 4325384 | tf_op jit(solution)/shard_map/ppermute | solution.py:909
  237.4 53.8 %all-to-all-start = ((bf16[8,256,512]{2,1,0:T(8,128)(2,1)}), bf16[8,256,512]{2,1,0:T(8,128)(2,1)}, u32[]{:S(2)}, u32[]{:S(2)}) async-start(bf16[8,256,512]{2,1,0:T(8,128)(2,1)} %get-tuple-element.271.o_ref), calls=%async_computation | async-start | bytes 4194304 | tf_op jit(solution)/shard_map/all_to_all | solution.py:986
  241.8 373.0 %reduce-scatter.5.cloned.1.call-start = ((), (), s32[]{:S(2)}) async-start(), calls=%async_computation.8 | async-start | bytes 9437184 | tf_op jit(solution)/shard_map/reduce_scatter | solution.py:1128
  309.7 11.9 %collective-permute-start.3 = (bf16[512,2048]{1,0:T(8,128)(2,1)S(1)}, bf16[512,2048]{1,0:T(8,128)(2,1)S(1)}, u32[]{:S(2)}, u32[]{:S(2)}) collective-permute-start(bf16[512,2048]{1,0:T(8,128)(2,1)S(1)} %multiply_convert_fusion.refs_0_.refs_1_), channel_id=1, source_target_pairs={{0,4},{4,0},{8,12},{12,8},{16,20},{20,16},{24,28},{28,24},{1,5},{5... | collective-permute-start | bytes 6291464 | tf_op jit(solution)/shard_map/ppermute | solution.py:948
  319.6 32.9 %collective-permute-start.4 = (bf16[256,2048]{1,0:T(8,128)(2,1)S(1)}, bf16[256,2048]{1,0:T(8,128)(2,1)}, u32[]{:S(2)}, u32[]{:S(2)}) collective-permute-start(bf16[256,2048]{1,0:T(8,128)(2,1)S(1)} %get-tuple-element.482), channel_id=1, source_target_pairs={{0,8},{4,12},{8,0},{12,4},{16,24},{20,28},{24,16},{28,20},{1,9},{5... | collective-permute-start | bytes 3145736 | tf_op jit(solution)/shard_map/ppermute | solution.py:948
  321.1 31.4 %collective-permute-start.5 = (bf16[256,2048]{1,0:T(8,128)(2,1)S(1)}, bf16[256,2048]{1,0:T(8,128)(2,1)}, u32[]{:S(2)}, u32[]{:S(2)}) collective-permute-start(bf16[256,2048]{1,0:T(8,128)(2,1)S(1)} %get-tuple-element.482), channel_id=1, source_target_pairs={{0,16},{4,20},{8,24},{12,28},{16,0},{20,4},{24,8},{28,12},{1,17},{... | collective-permute-start | bytes 3145736 | tf_op jit(solution)/shard_map/ppermute | solution.py:948
  352.5 3.0 collective-permute-start.6
  352.5 4.5 collective-permute-start.7
  353.1 37.3 %collective-permute-start.8 = (bf16[256,2048]{1,0:T(8,128)(2,1)}, bf16[256,2048]{1,0:T(8,128)(2,1)}, u32[]{:S(2)}, u32[]{:S(2)}) collective-permute-start(bf16[256,2048]{1,0:T(8,128)(2,1)} %get-tuple-element.481), channel_id=1, source_target_pairs={{0,8},{4,12},{8,0},{12,4},{16,24},{20,28},{24,16},{28,20},{1,9},{5... | collective-permute-start | bytes 3145736 | tf_op jit(solution)/shard_map/ppermute | solution.py:948
  353.8 36.6 %collective-permute-start.9 = (bf16[256,2048]{1,0:T(8,128)(2,1)}, bf16[256,2048]{1,0:T(8,128)(2,1)}, u32[]{:S(2)}, u32[]{:S(2)}) collective-permute-start(bf16[256,2048]{1,0:T(8,128)(2,1)} %get-tuple-element.481), channel_id=1, source_target_pairs={{0,16},{4,20},{8,24},{12,28},{16,0},{20,4},{24,8},{28,12},{1,17},{... | collective-permute-start | bytes 3145736 | tf_op jit(solution)/shard_map/ppermute | solution.py:948
  355.1 35.3 %collective-permute-start.10 = (bf16[256,2048]{1,0:T(8,128)(2,1)}, bf16[256,2048]{1,0:T(8,128)(2,1)S(1)}, u32[]{:S(2)}, u32[]{:S(2)}) collective-permute-start(bf16[256,2048]{1,0:T(8,128)(2,1)} %copy-done.27), channel_id=1, source_target_pairs={{0,4},{4,0},{8,12},{12,8},{16,20},{20,16},{24,28},{28,24},{1,5},{5... | collective-permute-start | bytes 3145736 | tf_op jit(solution)/shard_map/ppermute | solution.py:948
  355.5 34.9 %collective-permute-start.11 = (bf16[256,2048]{1,0:T(8,128)(2,1)}, bf16[256,2048]{1,0:T(8,128)(2,1)S(1)}, u32[]{:S(2)}, u32[]{:S(2)}) collective-permute-start(bf16[256,2048]{1,0:T(8,128)(2,1)} %copy-done.26), channel_id=1, source_target_pairs={{0,4},{4,0},{8,12},{12,8},{16,20},{20,16},{24,28},{28,24},{1,5},{5... | collective-permute-start | bytes 3145736 | tf_op jit(solution)/shard_map/ppermute | solution.py:948
  390.4 3.3 collective-permute-start.12
  390.6 4.4 collective-permute-start.13
  391.0 5.5 collective-permute-start.14
  391.8 37.9 %collective-permute-start.15 = (bf16[256,2048]{1,0:T(8,128)(2,1)}, bf16[256,2048]{1,0:T(8,128)(2,1)}, u32[]{:S(2)}, u32[]{:S(2)}) collective-permute-start(bf16[256,2048]{1,0:T(8,128)(2,1)} %collective-permute-done.4.refs_0_), channel_id=1, source_target_pairs={{0,16},{4,20},{8,24},{12,28},{16,0},{20,4},{24,8},{28,12},{1,17},{... | collective-permute-start | bytes 3145736 | tf_op jit(solution)/shard_map/ppermute | solution.py:948
  393.2 36.5 %collective-permute-start.16 = (bf16[256,2048]{1,0:T(8,128)(2,1)}, bf16[256,2048]{1,0:T(8,128)(2,1)}, u32[]{:S(2)}, u32[]{:S(2)}) collective-permute-start(bf16[256,2048]{1,0:T(8,128)(2,1)} %collective-permute-done.9.refs_2_), channel_id=1, source_target_pairs={{0,8},{4,12},{8,0},{12,4},{16,24},{20,28},{24,16},{28,20},{1,9},{5... | collective-permute-start | bytes 3145736 | tf_op jit(solution)/shard_map/ppermute | solution.py:948
  393.8 35.9 %collective-permute-start.17 = (bf16[256,2048]{1,0:T(8,128)(2,1)}, bf16[256,2048]{1,0:T(8,128)(2,1)}, u32[]{:S(2)}, u32[]{:S(2)}) collective-permute-start(bf16[256,2048]{1,0:T(8,128)(2,1)} %copy-done.25), channel_id=1, source_target_pairs={{0,4},{4,0},{8,12},{12,8},{16,20},{20,16},{24,28},{28,24},{1,5},{5... | collective-permute-start | bytes 3145736 | tf_op jit(solution)/shard_map/ppermute | solution.py:948
  429.7 3.8 collective-permute-start.18
  430.0 4.3 collective-permute-start.19
  430.3 5.5 collective-permute-start.20
  432.7 34.5 %collective-permute-start.21 = (bf16[256,2048]{1,0:T(8,128)(2,1)S(1)}, bf16[256,2048]{1,0:T(8,128)(2,1)S(1)}, u32[]{:S(2)}, u32[]{:S(2)}) collective-permute-start(bf16[256,2048]{1,0:T(8,128)(2,1)S(1)} %add_convert_fusion.6), channel_id=1, source_target_pairs={{0,8},{4,12},{8,0},{12,4},{16,24},{20,28},{24,16},{28,20},{1,9},{5... | collective-permute-start | bytes 3145736 | tf_op jit(solution)/shard_map/ppermute | solution.py:948
  433.4 33.7 %collective-permute-start.23 = (bf16[256,2048]{1,0:T(8,128)(2,1)S(1)}, bf16[256,2048]{1,0:T(8,128)(2,1)S(1)}, u32[]{:S(2)}, u32[]{:S(2)}) collective-permute-start(bf16[256,2048]{1,0:T(8,128)(2,1)S(1)} %copy-done.24), channel_id=1, source_target_pairs={{0,4},{4,0},{8,12},{12,8},{16,20},{20,16},{24,28},{28,24},{1,5},{5... | collective-permute-start | bytes 3145736 | tf_op jit(solution)/shard_map/ppermute | solution.py:948
  437.4 29.8 %collective-permute-start.22 = (bf16[256,2048]{1,0:T(8,128)(2,1)S(1)}, bf16[256,2048]{1,0:T(8,128)(2,1)S(1)}, u32[]{:S(2)}, u32[]{:S(2)}) collective-permute-start(bf16[256,2048]{1,0:T(8,128)(2,1)S(1)} %add_convert_fusion.5), channel_id=1, source_target_pairs={{0,16},{4,20},{8,24},{12,28},{16,0},{20,4},{24,8},{28,12},{1,17},{... | collective-permute-start | bytes 3145736 | tf_op jit(solution)/shard_map/ppermute | solution.py:948
  467.2 2.7 collective-permute-start.26
  467.2 4.1 collective-permute-start.24
  470.3 25.3 %collective-permute-start.27 = (bf16[256,2048]{1,0:T(8,128)(2,1)S(1)}, bf16[256,2048]{1,0:T(8,128)(2,1)S(1)}, u32[]{:S(2)}, u32[]{:S(2)}) collective-permute-start(bf16[256,2048]{1,0:T(8,128)(2,1)S(1)} %add_convert_fusion.3), channel_id=1, source_target_pairs={{0,16},{4,20},{8,24},{12,28},{16,0},{20,4},{24,8},{28,12},{1,17},{... | collective-permute-start | bytes 3145736 | tf_op jit(solution)/shard_map/ppermute | solution.py:948
  471.8 25.3 %collective-permute-start.25 = (bf16[256,2048]{1,0:T(8,128)(2,1)S(1)}, bf16[256,2048]{1,0:T(8,128)(2,1)S(1)}, u32[]{:S(2)}, u32[]{:S(2)}) collective-permute-start(bf16[256,2048]{1,0:T(8,128)(2,1)S(1)} %add_convert_fusion.4), channel_id=1, source_target_pairs={{0,8},{4,12},{8,0},{12,4},{16,24},{20,28},{24,16},{28,20},{1,9},{5... | collective-permute-start | bytes 3145736 | tf_op jit(solution)/shard_map/ppermute | solution.py:948
  497.1 166.6 %reduce-scatter.7.cloned.1.call-start = ((), (), s32[]{:S(2)}) async-start(), calls=%async_computation.9 | async-start | bytes 9437184 | tf_op jit(solution)/shard_map/reduce_scatter | solution.py:1128
  500.2 26.2 %collective-permute-start.29 = (bf16[256,2048]{1,0:T(8,128)(2,1)S(1)}, bf16[256,2048]{1,0:T(8,128)(2,1)S(1)}, u32[]{:S(2)}, u32[]{:S(2)}) collective-permute-start(bf16[256,2048]{1,0:T(8,128)(2,1)S(1)} %add_convert_fusion.1), channel_id=1, source_target_pairs={{0,16},{4,20},{8,24},{12,28},{16,0},{20,4},{24,8},{28,12},{1,17},{... | collective-permute-start | bytes 3145736 | tf_op jit(solution)/shard_map/ppermute | solution.py:948
  502.5 29.0 %collective-permute-start.28 = (bf16[256,2048]{1,0:T(8,128)(2,1)}, bf16[256,2048]{1,0:T(8,128)(2,1)S(1)}, u32[]{:S(2)}, u32[]{:S(2)}) collective-permute-start(bf16[256,2048]{1,0:T(8,128)(2,1)} %add_convert_fusion.2), channel_id=1, source_target_pairs={{0,8},{4,12},{8,0},{12,4},{16,24},{20,28},{24,16},{28,20},{1,9},{5... | collective-permute-start | bytes 3145736 | tf_op jit(solution)/shard_map/ppermute | solution.py:948
  504.1 22.3 %collective-permute-start.30 = (bf16[8,64,704]{2,1,0:T(8,128)(2,1)}, bf16[8,64,704]{2,1,0:T(8,128)(2,1)S(1)}, u32[]{:S(2)}, u32[]{:S(2)}) collective-permute-start(bf16[8,64,704]{2,1,0:T(8,128)(2,1)} %dynamic-slice_bitcast_fusion.1), channel_id=1, source_target_pairs={{0,1},{1,2},{2,3},{3,0},{4,5},{5,6},{6,7},{7,4},{8,9},{9,10},{10,1... | collective-permute-start | bytes 2162696 | tf_op jit(solution)/shard_map/ppermute | solution.py:909
  532.6 24.0 %collective-permute-start.32 = (bf16[8,64,704]{2,1,0:T(8,128)(2,1)}, bf16[8,64,704]{2,1,0:T(8,128)(2,1)S(1)}, u32[]{:S(2)}, u32[]{:S(2)}) collective-permute-start(bf16[8,64,704]{2,1,0:T(8,128)(2,1)} %convert_add_fusion.8), channel_id=1, source_target_pairs={{0,1},{1,2},{2,3},{3,0},{4,5},{5,6},{6,7},{7,4},{8,9},{9,10},{10,1... | collective-permute-start | bytes 2162696 | tf_op jit(solution)/shard_map/ppermute | solution.py:909
  536.2 28.5 %collective-permute-start.31 = (bf16[8,64,704]{2,1,0:T(8,128)(2,1)}, bf16[8,64,704]{2,1,0:T(8,128)(2,1)S(1)}, u32[]{:S(2)}, u32[]{:S(2)}) collective-permute-start(bf16[8,64,704]{2,1,0:T(8,128)(2,1)} %dynamic-slice_bitcast_fusion), channel_id=1, source_target_pairs={{0,1},{1,2},{2,3},{3,0},{4,5},{5,6},{6,7},{7,4},{8,9},{9,10},{10,1... | collective-permute-start | bytes 2162696 | tf_op jit(solution)/shard_map/ppermute | solution.py:909
  565.7 49.2 %all-to-all-start.1 = ((bf16[8,256,512]{2,1,0:T(8,128)(2,1)}), bf16[8,256,512]{2,1,0:T(8,128)(2,1)}, u32[]{:S(2)}, u32[]{:S(2)}) async-start(bf16[8,256,512]{2,1,0:T(8,128)(2,1)} %bitcast.168), calls=%async_computation.1 | async-start | bytes 4194304 | tf_op jit(solution)/shard_map/all_to_all | solution.py:986
  570.1 166.2 %reduce-scatter.9.cloned.1.call-start = ((), (), s32[]{:S(2)}) async-start(), calls=%async_computation.10 | async-start | bytes 9437184 | tf_op jit(solution)/shard_map/reduce_scatter | solution.py:1128
  592.3 22.5 %collective-permute-start.33 = (bf16[8,64,704]{2,1,0:T(8,128)(2,1)}, bf16[8,64,704]{2,1,0:T(8,128)(2,1)}, u32[]{:S(2)}, u32[]{:S(2)}) collective-permute-start(bf16[8,64,704]{2,1,0:T(8,128)(2,1)} %convert_add_fusion.7), channel_id=1, source_target_pairs={{0,1},{1,2},{2,3},{3,0},{4,5},{5,6},{6,7},{7,4},{8,9},{9,10},{10,1... | collective-permute-start | bytes 2162696 | tf_op jit(solution)/shard_map/ppermute | solution.py:909
  593.4 70.2 %collective-permute-start.34 = (bf16[8,64,704]{2,1,0:T(8,128)(2,1)}, bf16[8,64,704]{2,1,0:T(8,128)(2,1)}, u32[]{:S(2)}, u32[]{:S(2)}) collective-permute-start(bf16[8,64,704]{2,1,0:T(8,128)(2,1)} %convert_add_fusion.6), channel_id=1, source_target_pairs={{0,1},{1,2},{2,3},{3,0},{4,5},{5,6},{6,7},{7,4},{8,9},{9,10},{10,1... | collective-permute-start | bytes 2162696 | tf_op jit(solution)/shard_map/ppermute | solution.py:909
  616.4 47.2 %collective-permute-start.35 = (bf16[8,64,704]{2,1,0:T(8,128)(2,1)S(1)}, bf16[8,64,704]{2,1,0:T(8,128)(2,1)}, u32[]{:S(2)}, u32[]{:S(2)}) collective-permute-start(bf16[8,64,704]{2,1,0:T(8,128)(2,1)S(1)} %convert_add_fusion.5), channel_id=1, source_target_pairs={{0,1},{1,2},{2,3},{3,0},{4,5},{5,6},{6,7},{7,4},{8,9},{9,10},{10,1... | collective-permute-start | bytes 2162696 | tf_op jit(solution)/shard_map/ppermute | solution.py:909
  617.7 46.0 %collective-permute-start.36 = (bf16[176,2048]{1,0:T(8,128)(2,1)S(1)}, bf16[176,2048]{1,0:T(8,128)(2,1)}, u32[]{:S(2)}, u32[]{:S(2)}) collective-permute-start(bf16[176,2048]{1,0:T(8,128)(2,1)S(1)} %dynamic-slice_bitcast_fusion.2), channel_id=1, source_target_pairs={{0,1},{1,2},{2,3},{3,0},{4,5},{5,6},{6,7},{7,4},{8,9},{9,10},{10,1... | collective-permute-start | bytes 2162696 | tf_op jit(solution)/shard_map/ppermute | solution.py:909
  668.0 45.6 %all-to-all-start.2 = ((bf16[8,2,64,704]{3,2,1,0:T(8,128)(2,1)}), bf16[8,2,64,704]{3,2,1,0:T(8,128)(2,1)S(1)}, u32[]{:S(2)}, u32[]{:S(2)}) async-start(bf16[8,2,64,704]{3,2,1,0:T(8,128)(2,1)} %copy.133), calls=%async_computation.4 | async-start | bytes 3145728 | tf_op jit(solution)/shard_map/all_to_all | solution.py:986
  672.0 170.3 %reduce-scatter.11.cloned.1.call-start = ((), (), s32[]{:S(2)}) async-start(), calls=%async_computation.11 | async-start | bytes 1310720 | tf_op jit(solution)/shard_map/reduce_scatter | solution.py:1302
  674.8 46.7 %collective-permute-start.37 = (bf16[176,2048]{1,0:T(8,128)(2,1)}, bf16[176,2048]{1,0:T(8,128)(2,1)}, u32[]{:S(2)}, u32[]{:S(2)}) collective-permute-start(bf16[176,2048]{1,0:T(8,128)(2,1)} %convert_add_fusion.11), channel_id=1, source_target_pairs={{0,1},{1,2},{2,3},{3,0},{4,5},{5,6},{6,7},{7,4},{8,9},{9,10},{10,1... | collective-permute-start | bytes 2162696 | tf_op jit(solution)/shard_map/ppermute | solution.py:909
  737.8 106.2 %collective-permute-start.38 = (bf16[176,2048]{1,0:T(8,128)(2,1)S(1)}, bf16[176,2048]{1,0:T(8,128)(2,1)}, u32[]{:S(2)}, u32[]{:S(2)}) collective-permute-start(bf16[176,2048]{1,0:T(8,128)(2,1)S(1)} %fusion.2), channel_id=1, source_target_pairs={{0,1},{1,2},{2,3},{3,0},{4,5},{5,6},{6,7},{7,4},{8,9},{9,10},{10,1... | collective-permute-start | bytes 2162696 | tf_op jit(solution)/shard_map/ppermute | solution.py:909
  (72 other events, 430.9 us)
Sparse Core Ops, SparseCore 0:
  132.9 52.6 all-gather.3
  187.5 112.3 all-gather.5
  497.2 73.4 reduce-scatter.4
  574.5 71.2 reduce-scatter.6
  663.8 72.3 reduce-scatter.8
  738.5 40.5 reduce-scatter.10

commit v6 on v5

--- a/solution.py
+++ b/solution.py
@@ -95,24 +95,33 @@
         for h in range(group)
     ]
     qt_ref[...] = jnp.concatenate(heads, axis=0)
-    q4 = jnp.concatenate(heads, axis=1)
     starts = start_ref[0]
     acc[...] = jnp.zeros_like(acc)
     top[...] = jnp.full_like(top, NEG)
     total[...] = jnp.zeros_like(total)
 
+    parts_of = [pl.ds(h * rows, rows) for h in range(group)]
+    row = i * rows + lax.broadcasted_iota(jnp.int32, (1, rows), 1)
+    floor = starts[:, :rows]
+
     def block(j, masked):
         at = pl.multiple_of(j * BK, BK)
-        s = dot_f32(kn_ref[pl.ds(at, BK), :], q4)
+        k = kn_ref[pl.ds(at, BK), :]
+        v = vt[:, pl.ds(at, BK)]
+        scores = [dot_f32(k, q) for q in heads]
         if masked:
-            s = jnp.where(allowed_block(j, BK, i * rows, rows, wide, starts), s, NEG)
-        old = top[...]
-        new = jnp.maximum(old, jnp.max(s, axis=0, keepdims=True))
-        p = jnp.exp(s - new)
-        keep = jnp.exp(old - new)
-        top[...] = new
-        total[...] = total[...] * keep + jnp.sum(p, axis=0, keepdims=True)
-        acc[...] = acc[...] * keep + dot_f32(vt[:, pl.ds(at, BK)], p.astype(BF))
+            key = at + lax.broadcasted_iota(jnp.int32, (BK, 1), 0)
+            ok = (key <= row) & (key >= floor)
+        for part, s in zip(parts_of, scores):
+            if masked:
+                s = jnp.where(ok, s, NEG)
+            old = top[:, part]
+            new = jnp.maximum(old, jnp.max(s, axis=0, keepdims=True))
+            p = jnp.exp(s - new)
+            keep = jnp.exp(old - new)
+            top[:, part] = new
+            total[:, part] = total[:, part] * keep + jnp.sum(p, axis=0, keepdims=True)
+            acc[:, part] = acc[:, part] * keep + dot_f32(v, p.astype(BF))
 
     three_loops(bounds_ref, i, block)
     o = acc[...] / total[...]

time: 874 us -> 875 us (level)
  Pallas kernels: 530 us -> 568 us
  waiting for transfers between devices: 120 us -> 96.2 us
  starting transfers between devices: 47.8 us -> 34.6 us
    pallas_call x2, Pallas kernels: 78.3 us -> 102 us  [attend_back(): pl.pallas_call(functools.partial(backward_kernel, group, skip, final), ou...]
    reduce_scatter x3, waiting for transfers between devices: 14.7 us -> 0.04 us  [over_seq(): return lax.psum_scatter(whole, 'seq', scatter_dimension=0, tiled=True)]
    ppermute x12, starting transfers between devices: 20.5 us -> 7.68 us  [hop(): return [lax.ppermute(block, 'fsdp', ring('fsdp')) for block in blocks]]
    pallas_call x2, Pallas kernels: 58.5 us -> 69.7 us  [attend(): pl.pallas_call(kernel, out_shape=out_shape, grid_spec=pltpu.PrefetchScala...]
  transfers between devices with their start and end apart: 48 -> 48, of which waited for: 18 -> 16; matrix products, arithmetic and copies ran while one was open for 11% -> 11% of each run, Pallas kernels for 49% -> 53%
where the time goes in v6:
time: 875 us; the launch traced here: 863 us
  Pallas kernels  568 us (65%)
  waiting for transfers between devices  96.2 us (11%)
  local copies, waits for them, and re-layouts  72.3 us (8%)
  other arithmetic  49.9 us (6%)
  starting transfers between devices  34.6 us (4%)
  matrix products  26 us (3%)
  between operations  15.5 us (2%)
    pallas_call x4, Pallas kernels, ffn_chunk(): pl.pallas_call(functools.partial(ffn_kernel, number), out_shape=(narrow,...  112 us
    pallas_call x1, Pallas kernels, start_gather(): pl.pallas_call(functools.partial(start_kernel, parts), out_shape=shapes,...  109 us
    pallas_call x2, Pallas kernels, attend_back(): pl.pallas_call(functools.partial(backward_kernel, group, skip, final), ou...  102 us
    pallas_call x1, Pallas kernels, tail(): pl.pallas_call(functools.partial(tail_kernel, parts, cols), out_shape=(ja...  96 us
    pallas_call x2, Pallas kernels, attend(): pl.pallas_call(kernel, out_shape=out_shape, grid_spec=pltpu.PrefetchScala...  69.7 us
    all_to_all x3, waiting for transfers between devices, exchange(): return lax.all_to_all(array, 'seq', split_axis=0, concat_axis=0, tiled=True)  48.4 us
    pallas_call x2, Pallas kernels, side_terms(): pl.pallas_call(functools.partial(side_kernel, per, parts, rows), out_shap...  39.8 us
    unnamed x146, local copies, waits for them, and re-layouts  37.6 us
  transfers between devices with their start and end apart: 48, of which 16 were waited for; matrix products, arithmetic and copies ran while one was open for 11% of the time, Pallas kernels for 53%

profile of v6, /device:TPU:0, one launch (start us, length us, event | category | flops | bytes accessed | tf_op | source)
XLA Modules:
  0.0 862.6 jit_solution(14199731804414188790)
XLA Ops:
  7.2 1.9 reshape.376
  13.8 109.1 %start_gather.1 = (bf16[8,512,2048]{2,1,0:T(8,128)(2,1)S(1)}, bf16[4,8,64,512]{3,2,1,0:T(8,128)(2,1)S(1)}, bf16[8,128,704]{2,1,0:T(8,128)(2,1)S(1)}, bf16[4,64,2...) custom-call(bf16[512,2048]{1,0:T(8,128)(2,1)S(1)} %bitcast.139, ...), custom_call_target="tpu_custom_call" | custom-call | tf_op jit(solution)/shard_map/start_gather/pallas_call | solution.py:895
  126.9 5.9 copy-done.22
  132.9 2.7 copy.126
  141.3 3.1 copy.121
  144.6 19.0 %project.1 = (bf16[8,512,2048]{2,1,0:T(8,128)(2,1)}, f32[384,4096]{1,0:T(8,128)}, bf16[512,2048]{1,0:T(8,128)(2,1)}) custom-call(bf16[8,512,2048]{2,1,0:T(8,128)(2,1)} %copy-done.22, bf16[2048,512]{1,0:T(8,128)(2,1)} %bitcast.169), custom_call_target="tpu_custom_call" | custom-call | flops 6442450944 | bytes 33554432 | tf_op jit(solution)/shard_map/project/pallas_call | solution.py:343
  163.6 2.8 multiply_sine_fusion
  166.4 3.1 collective-permute-done
  170.1 34.9 %attend.2 = (bf16[8,256,512]{2,1,0:T(8,128)(2,1)}, f32[11,1,1024]{2,1,0:T(1,128)}, bf16[256,2816]{1,0:T(8,128)(2,1)}, bf16[64,4096]{1,0:T(8,128)(2,1)}, bf16[409...) custom-call(s32[16,4]{1,0:T(8,128)} %copy.132.bounds_ref.refs_0_, ...), custom_call_target="tpu_custom_call" | custom-call | flops 42949672960 | bytes 4194304 | tf_op jit(solution)/shard_map/attend/pallas_call | solution.py:243
  205.3 34.9 %attend.3 = (bf16[8,256,512]{2,1,0:T(8,128)(2,1)}, f32[5,1,1024]{2,1,0:T(1,128)}, bf16[256,1280]{1,0:T(8,128)(2,1)}) custom-call(s32[16,4]{1,0:T(8,128)} %copy.132.bounds_ref.refs_0_, f32[384,4096]{1,0:T(8,128)} %get-tuple-element.251.q_ref.kv_ref.refs_1_.refs_2_, ...), custom_call_target="tpu_custom_call", output_to_operand_aliasing={{0}: (8, {})} | custom-call | flops 42949672960 | bytes 4194304 | tf_op jit(solution)/shard_map/attend/pallas_call | solution.py:243
  240.1 4.4 all-to-all-start
  245.6 48.4 %all-to-all-done = bf16[8,256,512]{2,1,0:T(8,128)(2,1)} async-done(((bf16[8,256,512]{2,1,0:T(8,128)(2,1)}), bf16[8,256,512]{2,1,0:T(8,128)(2,1)}, u32[]{:S(2)}, u32[]{:S(2)}) %all-to-all-start) | async-done | bytes 2097184 | tf_op jit(solution)/shard_map/all_to_all | solution.py:995
  294.0 5.9 all-gather.6.cloned.1.call-done
  299.9 7.8 multiply_reduce_fusion.1
  316.1 2.3 fusion.27
  321.7 26.9 %ffn.4 = (bf16[8,512,704]{2,1,0:T(8,128)(2,1)}, bf16[8,512,704]{2,1,0:T(8,128)(2,1)}, bf16[8,512,704]{2,1,0:T(8,128)(2,1)}, bf16[8,512,2048]{2,1,0:T(8,128)(2,1)...) custom-call(s32[8]{0:T(128)S(1)} %stack.66.places_ref, ...), custom_call_target="tpu_custom_call" | custom-call | flops 17716740096 | bytes 29622272 | tf_op jit(solution)/shard_map/ffn/pallas_call | solution.py:431
  357.0 1.8 copy-done.2
  358.8 28.7 %ffn.5 = (bf16[8,512,704]{2,1,0:T(8,128)(2,1)}, bf16[8,512,704]{2,1,0:T(8,128)(2,1)}, bf16[8,512,704]{2,1,0:T(8,128)(2,1)}, bf16[8,512,2048]{2,1,0:T(8,128)(2,1)...) custom-call(s32[8]{0:T(128)S(1)} %stack.71.places_ref, ...), custom_call_target="tpu_custom_call", output_to_operand_aliasing={{0}: (9, {}), {1}: (10, {}), {2}: (11, {}), {3}: (12, {}), ... | custom-call | flops 17716740096 | bytes 29622272 | tf_op jit(solution)/shard_map/ffn/pallas_call | solution.py:431
  396.6 1.8 copy-done.3
  398.4 28.5 %ffn.6 = (bf16[8,512,704]{2,1,0:T(8,128)(2,1)}, bf16[8,512,704]{2,1,0:T(8,128)(2,1)}, bf16[8,512,704]{2,1,0:T(8,128)(2,1)}, bf16[8,512,2048]{2,1,0:T(8,128)(2,1)...) custom-call(s32[8]{0:T(128)S(1)} %stack.75.places_ref, ...), custom_call_target="tpu_custom_call", output_to_operand_aliasing={{0}: (9, {}), {1}: (10, {}), {2}: (11, {}), {3}: (12, {}), ... | custom-call | flops 17716740096 | bytes 29622272 | tf_op jit(solution)/shard_map/ffn/pallas_call | solution.py:431
  430.6 2.1 add_convert_fusion.6
  438.9 28.4 %ffn.7 = (bf16[8,512,704]{2,1,0:T(8,128)(2,1)}, bf16[8,512,704]{2,1,0:T(8,128)(2,1)}, bf16[8,512,704]{2,1,0:T(8,128)(2,1)}, bf16[8,512,2048]{2,1,0:T(8,128)(2,1)...) custom-call(s32[8]{0:T(128)S(1)} %stack.74.places_ref, ...), custom_call_target="tpu_custom_call", output_to_operand_aliasing={{0}: (9, {}), {1}: (10, {}), {2}: (11, {}), {3}: (12, {}), ... | custom-call | flops 17716740096 | bytes 29622272 | tf_op jit(solution)/shard_map/ffn/pallas_call | solution.py:431
  468.4 1.7 collective-permute-done.26
  472.7 18.9 %side_terms.2 = bf16[4,8,64,704]{3,2,1,0:T(8,128)(2,1)} custom-call(bf16[4096,2048]{1,0:T(8,128)(2,1)} %bitcast.148, bf16[4096,704]{1,0:T(8,128)(2,1)} %bitcast.153), custom_call_target="tpu_custom_call" | custom-call | flops 11811160064 | bytes 28311552 | tf_op jit(solution)/shard_map/side_terms/pallas_call | solution.py:475
  491.6 4.2 collective-permute-done.27
  498.5 1.9 add_convert_fusion.1
  505.9 20.9 %side_terms.3 = bf16[4,8,64,704]{3,2,1,0:T(8,128)(2,1)} custom-call(bf16[4096,2048]{1,0:T(8,128)(2,1)} %bitcast.149, bf16[4096,704]{1,0:T(8,128)(2,1)} %bitcast.154), custom_call_target="tpu_custom_call" | custom-call | flops 11811160064 | bytes 28311552 | tf_op jit(solution)/shard_map/side_terms/pallas_call | solution.py:475
  526.8 5.0 collective-permute-done.28
  534.4 2.1 dynamic-slice_bitcast_fusion
  539.3 1.8 copy-done.29
  542.7 4.2 fusion.25
  546.9 9.9 %convolution_convert_fusion.1 = bf16[2048,512]{1,0:T(8,128)(2,1)} fusion(bf16[2048,2048]{1,0:T(8,128)(2,1)} %all-gather.4.cloned.1.call-done, bf16[512,2048]{1,0:T(8,128)(2,1)S(1)} %get-tuple-element.424), kind=kOutput, calls=%fused_computation.9 | convolution fusion | flops 4296015872 | bytes 12582912 | tf_op jit(solution)/shard_map/ed,td->et/dot_general | solution.py:1246
  557.7 6.9 collective-permute-done.31
  565.6 4.4 all-to-all-start.1
  570.0 20.0 %down_terms.1 = bf16[704,2048]{1,0:T(8,128)(2,1)} custom-call(bf16[4096,704]{1,0:T(8,128)(2,1)} %bitcast.152, bf16[4096,2048]{1,0:T(8,128)(2,1)} %all-gather.6.cloned.1.call-done), custom_call_target="tpu_custom_call" | custom-call | flops 11811160064 | bytes 22544384 | tf_op jit(solution)/shard_map/down_terms/pallas_call | solution.py:508
  590.0 2.4 convert_add_fusion.7
  594.6 8.3 convolution_convert_fusion
  602.9 12.0 %collective-permute-done.33 = bf16[8,64,704]{2,1,0:T(8,128)(2,1)} collective-permute-done((bf16[8,64,704]{2,1,0:T(8,128)(2,1)}, bf16[8,64,704]{2,1,0:T(8,128)(2,1)}, u32[]{:S(2)}, u32[]{:S(2)}) %collective-permute-start.33) | collective-permute-done | bytes 720928 | tf_op jit(solution)/shard_map/ppermute | solution.py:918
  617.8 48.4 %attend_back.2 = (bf16[256,2816]{1,0:T(8,128)(2,1)}, f32[4096,64]{1,0:T(8,128)}, f32[4096,64]{1,0:T(8,128)}) custom-call(s32[16,4]{1,0:T(8,128)} %copy.132.bounds_ref.refs_0_, bf16[256,2816]{1,0:T(8,128)(2,1)} %get-tuple-element.277.q_ref, bf16[4096,64]{1,0:T(8,128)(2,1)} %get-tuple-element.264.refs_6_.k_ref, bf16[64,4096]{1,0:T(8,128)(2,1)} %get-tuple-element.278.kt_ref, ...), custom_call_target="tpu_custom_call" | custom-call | flops 53687091200 | bytes 8388608 | tf_op jit(solution)/shard_map/attend_back/pallas_call | solution.py:302
  670.6 3.9 all-to-all-start.2
  674.5 2.6 convert_add_fusion.11
  677.1 53.6 %attend_back.3 = (bf16[256,1280]{1,0:T(8,128)(2,1)}, bf16[128,4096]{1,0:T(8,128)(2,1)}) custom-call(s32[16,4]{1,0:T(8,128)} %copy.132.bounds_ref.refs_0_, bf16[256,1280]{1,0:T(8,128)(2,1)} %get-tuple-element.440.q_ref, bf16[4096,64]{1,0:T(8,128)(2,1)} %get-tuple-element.264.refs_6_.k_ref, bf16[64,4096]{1,0:T(8,128)(2,1)} %get-tuple-element.278.kt_ref, ...), custom_call_target="tpu_custom_call" | custom-call | flops 53687091200 | bytes 8388608 | tf_op jit(solution)/shard_map/attend_back/pallas_call | solution.py:302
  730.8 3.2 add_convert_fusion
  744.0 3.1 pad_maximum_fusion.d_ref
  747.0 96.0 %tail.1 = (f32[512,2048]{1,0:T(8,128)}, bf16[8,64,384]{2,1,0:T(8,128)(2,1)}) custom-call(bf16[384,4096]{1,0:T(8,128)(2,1)} %pad_maximum_fusion.d_ref, bf16[512,2048]{1,0:T(8,128)(2,1)} %get-tuple-element.283.w_ref, bf16[512,2048]{1,0:T(8,128)(2,1)} %bitcast.138, f32[512,2048]{1,0:T(8,128)} %get-tuple-element.458.dh_ref, bf16[4096,2048]{1,0:T(8,128)(2,1)} %bitcast.160), custom_call_target="tpu_custom_call" | custom-call | flops 1073741824 | bytes 1048576 | tf_op jit(solution)/shard_map/tail/pallas_call | solution.py:736
  843.5 1.8 convert_element_type.326
  846.5 2.7 convert_add_fusion.9
  850.9 4.7 copy.171
  (337 shorter events, 98.3 us)
Async XLA Ops:
  7.2 197.8 %all-gather.4.cloned.1.call-start = ((), (), s32[]{:S(2)}) async-start(), calls=%async_computation.7 | async-start | bytes 9437184 | tf_op jit(solution)/shard_map/all_gather | solution.py:1077
  132.8 167.1 %all-gather.6.cloned.1.call-start = ((), (), s32[]{:S(2)}) async-start(), calls=%async_computation.12 | async-start | bytes 18874368 | tf_op jit(solution)/shard_map/all_gather | solution.py:1106
  135.6 33.9 %collective-permute-start = (bf16[8,2,64,704]{3,2,0,1:T(8,128)(2,1)}, bf16[8,2,64,704]{3,2,0,1:T(8,128)(2,1)}, u32[]{:S(2)}, u32[]{:S(2)}) collective-permute-start(bf16[8,2,64,704]{3,2,0,1:T(8,128)(2,1)} %copy.126), channel_id=1, source_target_pairs={{0,1},{1,2},{2,3},{3,0},{4,5},{5,6},{6,7},{7,4},{8,9},{9,10},{10,1... | collective-permute-start | bytes 4325384 | tf_op jit(solution)/shard_map/ppermute | solution.py:918
  170.1 34.9 %collective-permute-start.1 = (bf16[8,2,64,704]{3,2,0,1:T(8,128)(2,1)}, bf16[8,2,64,704]{3,2,0,1:T(8,128)(2,1)}, u32[]{:S(2)}, u32[]{:S(2)}) collective-permute-start(bf16[8,2,64,704]{3,2,0,1:T(8,128)(2,1)} %collective-permute-done), channel_id=1, source_target_pairs={{0,1},{1,2},{2,3},{3,0},{4,5},{5,6},{6,7},{7,4},{8,9},{9,10},{10,1... | collective-permute-start | bytes 4325384 | tf_op jit(solution)/shard_map/ppermute | solution.py:918
  205.0 35.1 %collective-permute-start.2 = (bf16[8,2,64,704]{3,2,0,1:T(8,128)(2,1)}, bf16[8,2,64,704]{3,2,0,1:T(8,128)(2,1)}, u32[]{:S(2)}, u32[]{:S(2)}) collective-permute-start(bf16[8,2,64,704]{3,2,0,1:T(8,128)(2,1)} %collective-permute-done.1), channel_id=1, source_target_pairs={{0,1},{1,2},{2,3},{3,0},{4,5},{5,6},{6,7},{7,4},{8,9},{9,10},{10,1... | collective-permute-start | bytes 4325384 | tf_op jit(solution)/shard_map/ppermute | solution.py:918
  240.1 53.9 %all-to-all-start = ((bf16[8,256,512]{2,1,0:T(8,128)(2,1)}), bf16[8,256,512]{2,1,0:T(8,128)(2,1)}, u32[]{:S(2)}, u32[]{:S(2)}) async-start(bf16[8,256,512]{2,1,0:T(8,128)(2,1)} %get-tuple-element.271.o_ref), calls=%async_computation | async-start | bytes 4194304 | tf_op jit(solution)/shard_map/all_to_all | solution.py:995
  244.6 370.3 %reduce-scatter.5.cloned.1.call-start = ((), (), s32[]{:S(2)}) async-start(), calls=%async_computation.8 | async-start | bytes 9437184 | tf_op jit(solution)/shard_map/reduce_scatter | solution.py:1137
  309.7 12.0 %collective-permute-start.3 = (bf16[512,2048]{1,0:T(8,128)(2,1)S(1)}, bf16[512,2048]{1,0:T(8,128)(2,1)S(1)}, u32[]{:S(2)}, u32[]{:S(2)}) collective-permute-start(bf16[512,2048]{1,0:T(8,128)(2,1)S(1)} %multiply_convert_fusion.refs_0_.refs_1_), channel_id=1, source_target_pairs={{0,4},{4,0},{8,12},{12,8},{16,20},{20,16},{24,28},{28,24},{1,5},{5... | collective-permute-start | bytes 6291464 | tf_op jit(solution)/shard_map/ppermute | solution.py:957
  319.6 32.9 %collective-permute-start.4 = (bf16[256,2048]{1,0:T(8,128)(2,1)S(1)}, bf16[256,2048]{1,0:T(8,128)(2,1)}, u32[]{:S(2)}, u32[]{:S(2)}) collective-permute-start(bf16[256,2048]{1,0:T(8,128)(2,1)S(1)} %get-tuple-element.482), channel_id=1, source_target_pairs={{0,8},{4,12},{8,0},{12,4},{16,24},{20,28},{24,16},{28,20},{1,9},{5... | collective-permute-start | bytes 3145736 | tf_op jit(solution)/shard_map/ppermute | solution.py:957
  321.1 31.4 %collective-permute-start.5 = (bf16[256,2048]{1,0:T(8,128)(2,1)S(1)}, bf16[256,2048]{1,0:T(8,128)(2,1)}, u32[]{:S(2)}, u32[]{:S(2)}) collective-permute-start(bf16[256,2048]{1,0:T(8,128)(2,1)S(1)} %get-tuple-element.482), channel_id=1, source_target_pairs={{0,16},{4,20},{8,24},{12,28},{16,0},{20,4},{24,8},{28,12},{1,17},{... | collective-permute-start | bytes 3145736 | tf_op jit(solution)/shard_map/ppermute | solution.py:957
  352.5 3.0 collective-permute-start.6
  352.5 4.5 collective-permute-start.7
  353.1 37.3 %collective-permute-start.8 = (bf16[256,2048]{1,0:T(8,128)(2,1)}, bf16[256,2048]{1,0:T(8,128)(2,1)}, u32[]{:S(2)}, u32[]{:S(2)}) collective-permute-start(bf16[256,2048]{1,0:T(8,128)(2,1)} %get-tuple-element.481), channel_id=1, source_target_pairs={{0,8},{4,12},{8,0},{12,4},{16,24},{20,28},{24,16},{28,20},{1,9},{5... | collective-permute-start | bytes 3145736 | tf_op jit(solution)/shard_map/ppermute | solution.py:957
  353.8 36.6 %collective-permute-start.9 = (bf16[256,2048]{1,0:T(8,128)(2,1)}, bf16[256,2048]{1,0:T(8,128)(2,1)}, u32[]{:S(2)}, u32[]{:S(2)}) collective-permute-start(bf16[256,2048]{1,0:T(8,128)(2,1)} %get-tuple-element.481), channel_id=1, source_target_pairs={{0,16},{4,20},{8,24},{12,28},{16,0},{20,4},{24,8},{28,12},{1,17},{... | collective-permute-start | bytes 3145736 | tf_op jit(solution)/shard_map/ppermute | solution.py:957
  355.1 35.4 %collective-permute-start.10 = (bf16[256,2048]{1,0:T(8,128)(2,1)}, bf16[256,2048]{1,0:T(8,128)(2,1)S(1)}, u32[]{:S(2)}, u32[]{:S(2)}) collective-permute-start(bf16[256,2048]{1,0:T(8,128)(2,1)} %copy-done.27), channel_id=1, source_target_pairs={{0,4},{4,0},{8,12},{12,8},{16,20},{20,16},{24,28},{28,24},{1,5},{5... | collective-permute-start | bytes 3145736 | tf_op jit(solution)/shard_map/ppermute | solution.py:957
  355.5 35.0 %collective-permute-start.11 = (bf16[256,2048]{1,0:T(8,128)(2,1)}, bf16[256,2048]{1,0:T(8,128)(2,1)S(1)}, u32[]{:S(2)}, u32[]{:S(2)}) collective-permute-start(bf16[256,2048]{1,0:T(8,128)(2,1)} %copy-done.26), channel_id=1, source_target_pairs={{0,4},{4,0},{8,12},{12,8},{16,20},{20,16},{24,28},{28,24},{1,5},{5... | collective-permute-start | bytes 3145736 | tf_op jit(solution)/shard_map/ppermute | solution.py:957
  390.5 3.3 collective-permute-start.12
  390.7 4.4 collective-permute-start.13
  391.1 5.5 collective-permute-start.14
  391.9 37.9 %collective-permute-start.15 = (bf16[256,2048]{1,0:T(8,128)(2,1)}, bf16[256,2048]{1,0:T(8,128)(2,1)}, u32[]{:S(2)}, u32[]{:S(2)}) collective-permute-start(bf16[256,2048]{1,0:T(8,128)(2,1)} %collective-permute-done.4.refs_0_), channel_id=1, source_target_pairs={{0,16},{4,20},{8,24},{12,28},{16,0},{20,4},{24,8},{28,12},{1,17},{... | collective-permute-start | bytes 3145736 | tf_op jit(solution)/shard_map/ppermute | solution.py:957
  393.3 36.5 %collective-permute-start.16 = (bf16[256,2048]{1,0:T(8,128)(2,1)}, bf16[256,2048]{1,0:T(8,128)(2,1)}, u32[]{:S(2)}, u32[]{:S(2)}) collective-permute-start(bf16[256,2048]{1,0:T(8,128)(2,1)} %collective-permute-done.9.refs_2_), channel_id=1, source_target_pairs={{0,8},{4,12},{8,0},{12,4},{16,24},{20,28},{24,16},{28,20},{1,9},{5... | collective-permute-start | bytes 3145736 | tf_op jit(solution)/shard_map/ppermute | solution.py:957
  393.8 35.9 %collective-permute-start.17 = (bf16[256,2048]{1,0:T(8,128)(2,1)}, bf16[256,2048]{1,0:T(8,128)(2,1)}, u32[]{:S(2)}, u32[]{:S(2)}) collective-permute-start(bf16[256,2048]{1,0:T(8,128)(2,1)} %copy-done.25), channel_id=1, source_target_pairs={{0,4},{4,0},{8,12},{12,8},{16,20},{20,16},{24,28},{28,24},{1,5},{5... | collective-permute-start | bytes 3145736 | tf_op jit(solution)/shard_map/ppermute | solution.py:957
  429.8 3.8 collective-permute-start.18
  430.0 4.3 collective-permute-start.19
  430.3 5.5 collective-permute-start.20
  432.7 34.6 %collective-permute-start.21 = (bf16[256,2048]{1,0:T(8,128)(2,1)S(1)}, bf16[256,2048]{1,0:T(8,128)(2,1)S(1)}, u32[]{:S(2)}, u32[]{:S(2)}) collective-permute-start(bf16[256,2048]{1,0:T(8,128)(2,1)S(1)} %add_convert_fusion.6), channel_id=1, source_target_pairs={{0,8},{4,12},{8,0},{12,4},{16,24},{20,28},{24,16},{28,20},{1,9},{5... | collective-permute-start | bytes 3145736 | tf_op jit(solution)/shard_map/ppermute | solution.py:957
  433.5 33.9 %collective-permute-start.23 = (bf16[256,2048]{1,0:T(8,128)(2,1)S(1)}, bf16[256,2048]{1,0:T(8,128)(2,1)S(1)}, u32[]{:S(2)}, u32[]{:S(2)}) collective-permute-start(bf16[256,2048]{1,0:T(8,128)(2,1)S(1)} %copy-done.24), channel_id=1, source_target_pairs={{0,4},{4,0},{8,12},{12,8},{16,20},{20,16},{24,28},{28,24},{1,5},{5... | collective-permute-start | bytes 3145736 | tf_op jit(solution)/shard_map/ppermute | solution.py:957
  437.4 29.9 %collective-permute-start.22 = (bf16[256,2048]{1,0:T(8,128)(2,1)S(1)}, bf16[256,2048]{1,0:T(8,128)(2,1)S(1)}, u32[]{:S(2)}, u32[]{:S(2)}) collective-permute-start(bf16[256,2048]{1,0:T(8,128)(2,1)S(1)} %add_convert_fusion.5), channel_id=1, source_target_pairs={{0,16},{4,20},{8,24},{12,28},{16,0},{20,4},{24,8},{28,12},{1,17},{... | collective-permute-start | bytes 3145736 | tf_op jit(solution)/shard_map/ppermute | solution.py:957
  467.4 2.7 collective-permute-start.26
  467.5 4.1 collective-permute-start.24
  470.5 25.3 %collective-permute-start.27 = (bf16[256,2048]{1,0:T(8,128)(2,1)S(1)}, bf16[256,2048]{1,0:T(8,128)(2,1)S(1)}, u32[]{:S(2)}, u32[]{:S(2)}) collective-permute-start(bf16[256,2048]{1,0:T(8,128)(2,1)S(1)} %add_convert_fusion.3), channel_id=1, source_target_pairs={{0,16},{4,20},{8,24},{12,28},{16,0},{20,4},{24,8},{28,12},{1,17},{... | collective-permute-start | bytes 3145736 | tf_op jit(solution)/shard_map/ppermute | solution.py:957
  472.0 25.3 %collective-permute-start.25 = (bf16[256,2048]{1,0:T(8,128)(2,1)S(1)}, bf16[256,2048]{1,0:T(8,128)(2,1)S(1)}, u32[]{:S(2)}, u32[]{:S(2)}) collective-permute-start(bf16[256,2048]{1,0:T(8,128)(2,1)S(1)} %add_convert_fusion.4), channel_id=1, source_target_pairs={{0,8},{4,12},{8,0},{12,4},{16,24},{20,28},{24,16},{28,20},{1,9},{5... | collective-permute-start | bytes 3145736 | tf_op jit(solution)/shard_map/ppermute | solution.py:957
  497.3 168.9 %reduce-scatter.7.cloned.1.call-start = ((), (), s32[]{:S(2)}) async-start(), calls=%async_computation.9 | async-start | bytes 9437184 | tf_op jit(solution)/shard_map/reduce_scatter | solution.py:1137
  500.5 26.3 %collective-permute-start.29 = (bf16[256,2048]{1,0:T(8,128)(2,1)S(1)}, bf16[256,2048]{1,0:T(8,128)(2,1)S(1)}, u32[]{:S(2)}, u32[]{:S(2)}) collective-permute-start(bf16[256,2048]{1,0:T(8,128)(2,1)S(1)} %add_convert_fusion.1), channel_id=1, source_target_pairs={{0,16},{4,20},{8,24},{12,28},{16,0},{20,4},{24,8},{28,12},{1,17},{... | collective-permute-start | bytes 3145736 | tf_op jit(solution)/shard_map/ppermute | solution.py:957
  502.8 29.0 %collective-permute-start.28 = (bf16[256,2048]{1,0:T(8,128)(2,1)}, bf16[256,2048]{1,0:T(8,128)(2,1)S(1)}, u32[]{:S(2)}, u32[]{:S(2)}) collective-permute-start(bf16[256,2048]{1,0:T(8,128)(2,1)} %add_convert_fusion.2), channel_id=1, source_target_pairs={{0,8},{4,12},{8,0},{12,4},{16,24},{20,28},{24,16},{28,20},{1,9},{5... | collective-permute-start | bytes 3145736 | tf_op jit(solution)/shard_map/ppermute | solution.py:957
  504.4 22.4 %collective-permute-start.30 = (bf16[8,64,704]{2,1,0:T(8,128)(2,1)}, bf16[8,64,704]{2,1,0:T(8,128)(2,1)S(1)}, u32[]{:S(2)}, u32[]{:S(2)}) collective-permute-start(bf16[8,64,704]{2,1,0:T(8,128)(2,1)} %dynamic-slice_bitcast_fusion.1), channel_id=1, source_target_pairs={{0,1},{1,2},{2,3},{3,0},{4,5},{5,6},{6,7},{7,4},{8,9},{9,10},{10,1... | collective-permute-start | bytes 2162696 | tf_op jit(solution)/shard_map/ppermute | solution.py:918
  532.8 24.0 %collective-permute-start.32 = (bf16[8,64,704]{2,1,0:T(8,128)(2,1)}, bf16[8,64,704]{2,1,0:T(8,128)(2,1)S(1)}, u32[]{:S(2)}, u32[]{:S(2)}) collective-permute-start(bf16[8,64,704]{2,1,0:T(8,128)(2,1)} %convert_add_fusion.8), channel_id=1, source_target_pairs={{0,1},{1,2},{2,3},{3,0},{4,5},{5,6},{6,7},{7,4},{8,9},{9,10},{10,1... | collective-permute-start | bytes 2162696 | tf_op jit(solution)/shard_map/ppermute | solution.py:918
  536.4 28.2 %collective-permute-start.31 = (bf16[8,64,704]{2,1,0:T(8,128)(2,1)}, bf16[8,64,704]{2,1,0:T(8,128)(2,1)S(1)}, u32[]{:S(2)}, u32[]{:S(2)}) collective-permute-start(bf16[8,64,704]{2,1,0:T(8,128)(2,1)} %dynamic-slice_bitcast_fusion), channel_id=1, source_target_pairs={{0,1},{1,2},{2,3},{3,0},{4,5},{5,6},{6,7},{7,4},{8,9},{9,10},{10,1... | collective-permute-start | bytes 2162696 | tf_op jit(solution)/shard_map/ppermute | solution.py:918
  565.6 49.3 %all-to-all-start.1 = ((bf16[8,256,512]{2,1,0:T(8,128)(2,1)}), bf16[8,256,512]{2,1,0:T(8,128)(2,1)}, u32[]{:S(2)}, u32[]{:S(2)}) async-start(bf16[8,256,512]{2,1,0:T(8,128)(2,1)} %bitcast.168), calls=%async_computation.1 | async-start | bytes 4194304 | tf_op jit(solution)/shard_map/all_to_all | solution.py:995
  570.0 172.0 %reduce-scatter.9.cloned.1.call-start = ((), (), s32[]{:S(2)}) async-start(), calls=%async_computation.10 | async-start | bytes 9437184 | tf_op jit(solution)/shard_map/reduce_scatter | solution.py:1137
  592.4 22.5 %collective-permute-start.33 = (bf16[8,64,704]{2,1,0:T(8,128)(2,1)}, bf16[8,64,704]{2,1,0:T(8,128)(2,1)}, u32[]{:S(2)}, u32[]{:S(2)}) collective-permute-start(bf16[8,64,704]{2,1,0:T(8,128)(2,1)} %convert_add_fusion.7), channel_id=1, source_target_pairs={{0,1},{1,2},{2,3},{3,0},{4,5},{5,6},{6,7},{7,4},{8,9},{9,10},{10,1... | collective-permute-start | bytes 2162696 | tf_op jit(solution)/shard_map/ppermute | solution.py:918
  593.4 72.7 %collective-permute-start.34 = (bf16[8,64,704]{2,1,0:T(8,128)(2,1)}, bf16[8,64,704]{2,1,0:T(8,128)(2,1)}, u32[]{:S(2)}, u32[]{:S(2)}) collective-permute-start(bf16[8,64,704]{2,1,0:T(8,128)(2,1)} %convert_add_fusion.6), channel_id=1, source_target_pairs={{0,1},{1,2},{2,3},{3,0},{4,5},{5,6},{6,7},{7,4},{8,9},{9,10},{10,1... | collective-permute-start | bytes 2162696 | tf_op jit(solution)/shard_map/ppermute | solution.py:918
  616.4 49.7 %collective-permute-start.35 = (bf16[8,64,704]{2,1,0:T(8,128)(2,1)S(1)}, bf16[8,64,704]{2,1,0:T(8,128)(2,1)}, u32[]{:S(2)}, u32[]{:S(2)}) collective-permute-start(bf16[8,64,704]{2,1,0:T(8,128)(2,1)S(1)} %convert_add_fusion.5), channel_id=1, source_target_pairs={{0,1},{1,2},{2,3},{3,0},{4,5},{5,6},{6,7},{7,4},{8,9},{9,10},{10,1... | collective-permute-start | bytes 2162696 | tf_op jit(solution)/shard_map/ppermute | solution.py:918
  617.7 48.4 %collective-permute-start.36 = (bf16[176,2048]{1,0:T(8,128)(2,1)S(1)}, bf16[176,2048]{1,0:T(8,128)(2,1)}, u32[]{:S(2)}, u32[]{:S(2)}) collective-permute-start(bf16[176,2048]{1,0:T(8,128)(2,1)S(1)} %dynamic-slice_bitcast_fusion.2), channel_id=1, source_target_pairs={{0,1},{1,2},{2,3},{3,0},{4,5},{5,6},{6,7},{7,4},{8,9},{9,10},{10,1... | collective-permute-start | bytes 2162696 | tf_op jit(solution)/shard_map/ppermute | solution.py:918
  670.6 63.5 %all-to-all-start.2 = ((bf16[8,2,64,704]{3,2,1,0:T(8,128)(2,1)}), bf16[8,2,64,704]{3,2,1,0:T(8,128)(2,1)S(1)}, u32[]{:S(2)}, u32[]{:S(2)}) async-start(bf16[8,2,64,704]{3,2,1,0:T(8,128)(2,1)} %copy.133), calls=%async_computation.4 | async-start | bytes 3145728 | tf_op jit(solution)/shard_map/all_to_all | solution.py:995
  674.4 169.1 %reduce-scatter.11.cloned.1.call-start = ((), (), s32[]{:S(2)}) async-start(), calls=%async_computation.11 | async-start | bytes 1310720 | tf_op jit(solution)/shard_map/reduce_scatter | solution.py:1311
  677.1 64.8 %collective-permute-start.37 = (bf16[176,2048]{1,0:T(8,128)(2,1)}, bf16[176,2048]{1,0:T(8,128)(2,1)}, u32[]{:S(2)}, u32[]{:S(2)}) collective-permute-start(bf16[176,2048]{1,0:T(8,128)(2,1)} %convert_add_fusion.11), channel_id=1, source_target_pairs={{0,1},{1,2},{2,3},{3,0},{4,5},{5,6},{6,7},{7,4},{8,9},{9,10},{10,1... | collective-permute-start | bytes 2162696 | tf_op jit(solution)/shard_map/ppermute | solution.py:918
  743.7 101.7 %collective-permute-start.38 = (bf16[176,2048]{1,0:T(8,128)(2,1)S(1)}, bf16[176,2048]{1,0:T(8,128)(2,1)}, u32[]{:S(2)}, u32[]{:S(2)}) collective-permute-start(bf16[176,2048]{1,0:T(8,128)(2,1)S(1)} %fusion.2), channel_id=1, source_target_pairs={{0,1},{1,2},{2,3},{3,0},{4,5},{5,6},{6,7},{7,4},{8,9},{9,10},{10,1... | collective-permute-start | bytes 2162696 | tf_op jit(solution)/shard_map/ppermute | solution.py:918
  (72 other events, 429.3 us)
Sparse Core Ops, SparseCore 0:
  132.9 52.6 all-gather.3
  187.5 112.3 all-gather.5
  497.5 73.4 reduce-scatter.4
  574.7 71.3 reduce-scatter.6
  666.3 69.7 reduce-scatter.8
  742.1 39.6 reduce-scatter.10
